TPU v7x, 32 devices: a whole 2x2x4 slice. The times are simulated.
32 devices in a mesh: dp: 8 (over y, x, core), fsdp: 4 (over z).
Axes of the slice: x: 2, y: 2, z: 4, core: 2. Of those that a mesh axis runs over, the one named last changes fastest.
Arguments:
- unit_states: bfloat16 [32, 768, 1024], P(('dp', 'fsdp')), may hold values from -6 to 6
- encoder_states: bfloat16 [32, 256, 1024], P(('dp', 'fsdp')), may hold values from -6 to 6
- cotangent: float32 [32, 768, 1024], P(('dp', 'fsdp')), may hold values from -6 to 6
- unit_lengths: int32 [32], P(('dp', 'fsdp')), may hold values from 384 to 768, as said below
- text_lengths: int32 [32], P(('dp', 'fsdp')), may hold values from 64 to 256, as said below
- self_project: float32 [1024, 3072], P(('dp', 'fsdp')), may hold values from -0.1875 to 0.1875
- self_output: float32 [1024, 1024], P(('dp', 'fsdp')), may hold values from -1.5 to 1.5
- cross_project: float32 [1024, 3072], P(('dp', 'fsdp')), may hold values from -0.1875 to 0.1875
- cross_output: float32 [1024, 1024], P(('dp', 'fsdp')), may hold values from -1.5 to 1.5
- feed_input: float32 [1024, 4096], P(('dp', 'fsdp')), may hold values from -0.375 to 0.375
- feed_output: float32 [4096, 1024], P(('dp', 'fsdp')), may hold values from -0.375 to 0.375
- norm_gains: bfloat16 [4, 1024], P(None, ('dp', 'fsdp')), may hold values from 0.5 to 1.5
- norm_biases: bfloat16 [4, 1024], P(None, ('dp', 'fsdp')), may hold values from -0.59765625 to 0.59765625
Outputs:
- block_output: bfloat16 [32, 768, 1024], P(('dp', 'fsdp'))
- grad_states: float32 [32, 768, 1024], P(('dp', 'fsdp'))
- grad_encoder: float32 [32, 256, 1024], P(('dp', 'fsdp'))
- grad_self_project: float32 [1024, 3072], P(('dp', 'fsdp'))
- grad_self_output: float32 [1024, 1024], P(('dp', 'fsdp'))
- grad_cross_project: float32 [1024, 3072], P(('dp', 'fsdp'))
- grad_cross_output: float32 [1024, 1024], P(('dp', 'fsdp'))
- grad_feed_input: float32 [1024, 4096], P(('dp', 'fsdp'))
- grad_feed_output: float32 [4096, 1024], P(('dp', 'fsdp'))
- grad_gains: float32 [4, 1024], P(None, ('dp', 'fsdp'))
- grad_biases: float32 [4, 1024], P(None, ('dp', 'fsdp'))
Inputs may be any that keep to these rules, and one draw needn't show every extreme that they name: `unit_lengths`: units of each sequence; slots at and past it are padding. Some sequence has exactly 768. `text_lengths`: encoder states that count for each sequence; some sequence has exactly 256.
All inputs are finite; a program needn't handle non-finite values.
Results may differ from a plain program's by a relative error of at most 0.02.
Values may be sent and summed in bfloat16 or wider, within the bound.
No kernel may reach another device: no remote copies, remote signals or barrier semaphores. Data moves between devices by JAX's collectives and lax.ppermute only.
A program may use at most 256 MiB of HBM per device.

v0:
```python
import jax
import jax.numpy as jnp
from jax import lax
from jax.sharding import PartitionSpec as P

HEAD = 64


def layer_norm(values, gain_row, bias_row):
    centre = values - jnp.mean(values, axis=-1, keepdims=True)
    spread = jnp.mean(centre * centre, axis=-1, keepdims=True)
    return centre * lax.rsqrt(spread + 1e-05) * gain_row + bias_row


def gelu_slope(values):
    normal_cdf = 0.5 * (1.0 + lax.erf(values * 2.0 ** (-0.5)))
    normal_pdf = jnp.exp(-0.5 * values * values) * (2.0 * jnp.pi) ** (-0.5)
    return normal_cdf + values * normal_pdf


def product(left, right):
    return jnp.dot(left, right, preferred_element_type=jnp.float32)


def contract_rows(left, right):
    return lax.dot_general(
        left, right, (((0,), (0,)), ((), ())), preferred_element_type=jnp.float32
    )


def times_transposed(left, right):
    return lax.dot_general(
        left, right, (((1,), (1,)), ((), ())), preferred_element_type=jnp.float32
    )


def head_block(matrix, pair_index):
    start_col = pair_index * (2 * HEAD)
    block = lax.dynamic_slice_in_dim(matrix, start_col, 2 * HEAD, 1)
    return block.reshape(matrix.shape[0], 2, HEAD)


def merge_pairs(stacked):
    return jnp.transpose(stacked, (1, 0, 2)).reshape(
        stacked.shape[1], stacked.shape[0] * stacked.shape[2]
    )


def pair_scores(query_pair, key_pair, visible):
    scores = jnp.einsum(
        "qhd,khd->hqk", query_pair, key_pair, preferred_element_type=jnp.float32
    ) * HEAD ** (-0.5)
    return jnp.where(visible[None], scores, -1e30)


def attention_forward(query_rows, key_rows, value_rows, visible):
    row_count = query_rows.shape[0]
    pair_count = query_rows.shape[1] // (2 * HEAD)

    def one_pair(pair_index):
        query_pair = head_block(query_rows, pair_index)
        key_pair = head_block(key_rows, pair_index)
        value_pair = head_block(value_rows, pair_index)
        scores = pair_scores(query_pair, key_pair, visible)
        highest = jnp.max(scores, axis=-1, keepdims=True)
        expanded = jnp.exp(scores - highest)
        denominator = jnp.sum(expanded, axis=-1, keepdims=True)
        weights = (expanded / denominator).astype(jnp.bfloat16)
        mixed_heads = jnp.einsum(
            "hqk,khd->qhd", weights, value_pair, preferred_element_type=jnp.float32
        )
        return (mixed_heads.reshape(row_count, 2 * HEAD), highest + jnp.log(denominator))

    mixed_all, log_totals = lax.map(one_pair, jnp.arange(pair_count))
    return (merge_pairs(mixed_all).astype(jnp.bfloat16), log_totals)


def attention_backward(query_rows, key_rows, value_rows, visible, log_totals, grad_mixed):
    row_count = query_rows.shape[0]
    key_count = key_rows.shape[0]
    pair_count = query_rows.shape[1] // (2 * HEAD)

    def one_pair(inputs_pair):
        pair_index, log_pair = inputs_pair
        query_pair = head_block(query_rows, pair_index)
        key_pair = head_block(key_rows, pair_index)
        value_pair = head_block(value_rows, pair_index)
        grad_pair = head_block(grad_mixed, pair_index)
        scores = pair_scores(query_pair, key_pair, visible)
        probabilities = jnp.exp(scores - log_pair)
        grad_values = jnp.einsum(
            "hqk,qhd->khd",
            probabilities.astype(jnp.bfloat16),
            grad_pair,
            preferred_element_type=jnp.float32,
        )
        grad_probs = jnp.einsum(
            "qhd,khd->hqk", grad_pair, value_pair, preferred_element_type=jnp.float32
        )
        inner_sums = jnp.sum(probabilities * grad_probs, axis=-1, keepdims=True)
        grad_scores = (probabilities * (grad_probs - inner_sums) * HEAD ** (-0.5)).astype(
            jnp.bfloat16
        )
        grad_queries = jnp.einsum(
            "hqk,khd->qhd", grad_scores, key_pair, preferred_element_type=jnp.float32
        )
        grad_keys = jnp.einsum(
            "hqk,qhd->khd", grad_scores, query_pair, preferred_element_type=jnp.float32
        )
        return (
            grad_queries.reshape(row_count, 2 * HEAD),
            grad_keys.reshape(key_count, 2 * HEAD),
            grad_values.reshape(key_count, 2 * HEAD),
        )

    grad_queries, grad_keys, grad_values = lax.map(one_pair, (jnp.arange(pair_count), log_totals))
    return (merge_pairs(grad_queries), merge_pairs(grad_keys), merge_pairs(grad_values))


def self_forward(layer_input, project_low, output_low, gain_row, bias_row, visible):
    model_width = layer_input.shape[1]
    normed = layer_norm(layer_input, gain_row, bias_row).astype(jnp.bfloat16)
    projected = product(normed, project_low).astype(jnp.bfloat16)
    mixed_heads, log_totals = attention_forward(
        projected[:, :model_width],
        projected[:, model_width : 2 * model_width],
        projected[:, 2 * model_width :],
        visible,
    )
    after_branch = layer_input + product(mixed_heads, output_low)
    return (after_branch, (normed, projected, mixed_heads, log_totals))


def self_backward(
    grad_after, layer_input, project_low, output_low, gain_row, bias_row, visible, saved_state
):
    normed, projected, mixed_heads, log_totals = saved_state
    model_width = layer_input.shape[1]
    grad_branch = grad_after.astype(jnp.bfloat16)
    grad_output_weight = contract_rows(mixed_heads, grad_branch)
    grad_mixed = times_transposed(grad_branch, output_low).astype(jnp.bfloat16)
    grad_queries, grad_keys, grad_values = attention_backward(
        projected[:, :model_width],
        projected[:, model_width : 2 * model_width],
        projected[:, 2 * model_width :],
        visible,
        log_totals,
        grad_mixed,
    )
    grad_projected = jnp.concatenate([grad_queries, grad_keys, grad_values], axis=1).astype(
        jnp.bfloat16
    )
    grad_project_weight = contract_rows(normed, grad_projected)
    grad_normed = times_transposed(grad_projected, project_low)
    _, pullback = jax.vjp(layer_norm, layer_input, gain_row, bias_row)
    grad_input, grad_gain, grad_bias = pullback(grad_normed)
    return (grad_after + grad_input, grad_project_weight, grad_output_weight, grad_gain, grad_bias)


def cross_forward(after_self, encoded, project_low, output_low, gain_row, bias_row, visible):
    model_width = after_self.shape[1]
    normed = layer_norm(after_self, gain_row, bias_row).astype(jnp.bfloat16)
    queries = product(normed, project_low[:, :model_width]).astype(jnp.bfloat16)
    key_values = product(encoded, project_low[:, model_width:]).astype(jnp.bfloat16)
    mixed_heads, log_totals = attention_forward(
        queries, key_values[:, :model_width], key_values[:, model_width:], visible
    )
    after_branch = after_self + product(mixed_heads, output_low)
    return (after_branch, (normed, queries, key_values, mixed_heads, log_totals))


def cross_backward(
    grad_after,
    after_self,
    encoded,
    project_low,
    output_low,
    gain_row,
    bias_row,
    visible,
    saved_state,
):
    normed, queries, key_values, mixed_heads, log_totals = saved_state
    model_width = after_self.shape[1]
    grad_branch = grad_after.astype(jnp.bfloat16)
    grad_output_weight = contract_rows(mixed_heads, grad_branch)
    grad_mixed = times_transposed(grad_branch, output_low).astype(jnp.bfloat16)
    grad_queries, grad_keys, grad_values = attention_backward(
        queries,
        key_values[:, :model_width],
        key_values[:, model_width:],
        visible,
        log_totals,
        grad_mixed,
    )
    grad_queries = grad_queries.astype(jnp.bfloat16)
    grad_key_values = jnp.concatenate([grad_keys, grad_values], axis=1).astype(jnp.bfloat16)
    grad_project_weight = jnp.concatenate(
        [contract_rows(normed, grad_queries), contract_rows(encoded, grad_key_values)], axis=1
    )
    grad_normed = times_transposed(grad_queries, project_low[:, :model_width])
    grad_encoded = times_transposed(grad_key_values, project_low[:, model_width:])
    _, pullback = jax.vjp(layer_norm, after_self, gain_row, bias_row)
    grad_input, grad_gain, grad_bias = pullback(grad_normed)
    return (
        grad_after + grad_input,
        grad_encoded,
        grad_project_weight,
        grad_output_weight,
        grad_gain,
        grad_bias,
    )


def feed_forward_part(after_cross, input_low, output_low, gain_row, bias_row):
    normed = layer_norm(after_cross, gain_row, bias_row).astype(jnp.bfloat16)
    hidden_pre = product(normed, input_low)
    hidden = jax.nn.gelu(hidden_pre, approximate=False).astype(jnp.bfloat16)
    after_branch = after_cross + product(hidden, output_low)
    return (after_branch, (normed, hidden_pre, hidden))


def feed_backward(grad_after, after_cross, input_low, output_low, gain_row, bias_row, saved_state):
    normed, hidden_pre, hidden = saved_state
    grad_branch = grad_after.astype(jnp.bfloat16)
    grad_output_weight = contract_rows(hidden, grad_branch)
    grad_hidden = times_transposed(grad_branch, output_low)
    grad_pre = (grad_hidden * gelu_slope(hidden_pre)).astype(jnp.bfloat16)
    grad_input_weight = contract_rows(normed, grad_pre)
    grad_normed = times_transposed(grad_pre, input_low)
    _, pullback = jax.vjp(layer_norm, after_cross, gain_row, bias_row)
    grad_input, grad_gain, grad_bias = pullback(grad_normed)
    return (grad_after + grad_input, grad_input_weight, grad_output_weight, grad_gain, grad_bias)


def body(
    unit_states,
    encoder_states,
    cotangent,
    unit_lengths,
    text_lengths,
    self_project,
    self_output,
    cross_project,
    cross_output,
    feed_input,
    feed_output,
    norm_gains,
    norm_biases,
):
    layer_input = unit_states[0].astype(jnp.float32)
    encoded = encoder_states[0]
    row_count = layer_input.shape[0]
    text_count = encoded.shape[0]
    position = jnp.arange(row_count, dtype=jnp.int32)
    unit_length = unit_lengths[0]
    causal = (position[None, :] <= position[:, None]) & (position[None, :] < unit_length)
    text_visible = jnp.broadcast_to(
        jnp.arange(text_count, dtype=jnp.int32)[None, :] < text_lengths[0], (row_count, text_count)
    )
    self_project_low, self_output_low, gain_table, bias_table = (
        lax.all_gather(self_project.astype(jnp.bfloat16), ("dp", "fsdp"), axis=0, tiled=True),
        lax.all_gather(self_output.astype(jnp.bfloat16), ("dp", "fsdp"), axis=0, tiled=True),
        lax.all_gather(norm_gains, ("dp", "fsdp"), axis=1, tiled=True),
        lax.all_gather(norm_biases, ("dp", "fsdp"), axis=1, tiled=True),
    )
    gain_table = gain_table.astype(jnp.float32)
    bias_table = bias_table.astype(jnp.float32)
    after_self, self_saved = self_forward(
        layer_input, self_project_low, self_output_low, gain_table[0], bias_table[0], causal
    )
    cross_project_low, cross_output_low = (
        lax.all_gather(cross_project.astype(jnp.bfloat16), ("dp", "fsdp"), axis=0, tiled=True),
        lax.all_gather(cross_output.astype(jnp.bfloat16), ("dp", "fsdp"), axis=0, tiled=True),
    )
    after_cross, cross_saved = cross_forward(
        after_self,
        encoded,
        cross_project_low,
        cross_output_low,
        gain_table[1],
        bias_table[1],
        text_visible,
    )
    feed_input_low, feed_output_low = (
        lax.all_gather(feed_input.astype(jnp.bfloat16), ("dp", "fsdp"), axis=0, tiled=True),
        lax.all_gather(feed_output.astype(jnp.bfloat16), ("dp", "fsdp"), axis=0, tiled=True),
    )
    after_feed, feed_saved = feed_forward_part(
        after_cross, feed_input_low, feed_output_low, gain_table[2], bias_table[2]
    )
    result, final_pullback = jax.vjp(layer_norm, after_feed, gain_table[3], bias_table[3])
    row_live = (position < unit_length).astype(jnp.float32)
    grad_feed_after, grad_gain_last, grad_bias_last = final_pullback(
        cotangent[0] * row_live[:, None]
    )
    feed_input_low, feed_output_low = (
        lax.all_gather(feed_input.astype(jnp.bfloat16), ("dp", "fsdp"), axis=0, tiled=True),
        lax.all_gather(feed_output.astype(jnp.bfloat16), ("dp", "fsdp"), axis=0, tiled=True),
    )
    _, feed_saved = feed_forward_part(
        after_cross, feed_input_low, feed_output_low, gain_table[2], bias_table[2]
    )
    grad_cross_after, grad_feed_in, grad_feed_out, grad_gain_feed, grad_bias_feed = feed_backward(
        grad_feed_after,
        after_cross,
        feed_input_low,
        feed_output_low,
        gain_table[2],
        bias_table[2],
        feed_saved,
    )
    feed_in_part, feed_out_part = (
        lax.psum_scatter(grad_feed_in, ("dp", "fsdp"), scatter_dimension=0, tiled=True),
        lax.psum_scatter(grad_feed_out, ("dp", "fsdp"), scatter_dimension=0, tiled=True),
    )
    cross_project_low, cross_output_low = (
        lax.all_gather(cross_project.astype(jnp.bfloat16), ("dp", "fsdp"), axis=0, tiled=True),
        lax.all_gather(cross_output.astype(jnp.bfloat16), ("dp", "fsdp"), axis=0, tiled=True),
    )
    _, cross_saved = cross_forward(
        after_self,
        encoded,
        cross_project_low,
        cross_output_low,
        gain_table[1],
        bias_table[1],
        text_visible,
    )
    (
        grad_self_after,
        grad_encoded,
        grad_cross_in,
        grad_cross_out,
        grad_gain_cross,
        grad_bias_cross,
    ) = cross_backward(
        grad_cross_after,
        after_self,
        encoded,
        cross_project_low,
        cross_output_low,
        gain_table[1],
        bias_table[1],
        text_visible,
        cross_saved,
    )
    cross_in_part, cross_out_part = (
        lax.psum_scatter(grad_cross_in, ("dp", "fsdp"), scatter_dimension=0, tiled=True),
        lax.psum_scatter(grad_cross_out, ("dp", "fsdp"), scatter_dimension=0, tiled=True),
    )
    self_project_low, self_output_low = (
        lax.all_gather(self_project.astype(jnp.bfloat16), ("dp", "fsdp"), axis=0, tiled=True),
        lax.all_gather(self_output.astype(jnp.bfloat16), ("dp", "fsdp"), axis=0, tiled=True),
    )
    _, self_saved = self_forward(
        layer_input, self_project_low, self_output_low, gain_table[0], bias_table[0], causal
    )
    grad_input, grad_self_in, grad_self_out, grad_gain_self, grad_bias_self = self_backward(
        grad_self_after,
        layer_input,
        self_project_low,
        self_output_low,
        gain_table[0],
        bias_table[0],
        causal,
        self_saved,
    )
    grad_gain_all = jnp.stack([grad_gain_self, grad_gain_cross, grad_gain_feed, grad_gain_last])
    grad_bias_all = jnp.stack([grad_bias_self, grad_bias_cross, grad_bias_feed, grad_bias_last])
    self_in_part, self_out_part, gain_part, bias_part = (
        lax.psum_scatter(grad_self_in, ("dp", "fsdp"), scatter_dimension=0, tiled=True),
        lax.psum_scatter(grad_self_out, ("dp", "fsdp"), scatter_dimension=0, tiled=True),
        lax.psum_scatter(grad_gain_all, ("dp", "fsdp"), scatter_dimension=1, tiled=True),
        lax.psum_scatter(grad_bias_all, ("dp", "fsdp"), scatter_dimension=1, tiled=True),
    )
    return (
        result.astype(jnp.bfloat16)[None],
        grad_input[None],
        grad_encoded[None],
        self_in_part,
        self_out_part,
        cross_in_part,
        cross_out_part,
        feed_in_part,
        feed_out_part,
        gain_part,
        bias_part,
    )


def solution(mesh):
    return jax.shard_map(
        body,
        mesh=mesh,
        in_specs=(
            P(("dp", "fsdp"), None, None),
            P(("dp", "fsdp"), None, None),
            P(("dp", "fsdp"), None, None),
            P(("dp", "fsdp")),
            P(("dp", "fsdp")),
            P(("dp", "fsdp"), None),
            P(("dp", "fsdp"), None),
            P(("dp", "fsdp"), None),
            P(("dp", "fsdp"), None),
            P(("dp", "fsdp"), None),
            P(("dp", "fsdp"), None),
            P(None, ("dp", "fsdp")),
            P(None, ("dp", "fsdp")),
        ),
        out_specs=(
            P(("dp", "fsdp"), None, None),
            P(("dp", "fsdp"), None, None),
            P(("dp", "fsdp"), None, None),
            P(("dp", "fsdp"), None),
            P(("dp", "fsdp"), None),
            P(("dp", "fsdp"), None),
            P(("dp", "fsdp"), None),
            P(("dp", "fsdp"), None),
            P(("dp", "fsdp"), None),
            P(None, ("dp", "fsdp")),
            P(None, ("dp", "fsdp")),
        ),
        check_vma=False,
    )
```

profile of v0, /device:TPU:0, one launch (start us, length us, event | category | flops | bytes accessed | tf_op | source)
XLA Modules:
  0.0 2558.3 jit_solution(8296971297200764941)
XLA Ops:
  16.9 70.0 %all-gather.1 = bf16[32,32,4]{1,2,0:T(4,128)(2,1)S(1)} all-gather(bf16[1,32,4]{1,2,0:T(4,128)(2,1)S(1)} %bitcast.460), channel_id=1, replica_groups=mesh['dp'=8,'fsdp'=4] {'dp','fsdp'}, dimensions={0}, use_global_device_ids=true | all-gather | bytes 8448 | tf_op jit(solution)/shard_map/all_gather | solution.py:265
  87.7 63.8 %all-gather = bf16[32,32,4]{1,2,0:T(4,128)(2,1)S(1)} all-gather(bf16[1,32,4]{1,2,0:T(4,128)(2,1)S(1)} %bitcast.461), channel_id=1, replica_groups=mesh['dp'=8,'fsdp'=4] {'dp','fsdp'}, dimensions={0}, use_global_device_ids=true | all-gather | bytes 8448 | tf_op jit(solution)/shard_map/all_gather | solution.py:264
  155.0 8.4 convolution_convert_fusion
  174.7 88.4 %while.78 = (s32[]{:T(128)}, bf16[8,768,128]{1,2,0:T(8,128)(2,1)}, s32[8]{0:T(128)S(1)}, bf16[768,1024]{0,1:T(8,128)(2,1)}, bf16[768,1024]{0,1:T(8,128)(2,1)}, /...) while((s32[]{:T(128)}, bf16[8,768,128]{1,2,0:T(8,128)(2,1)}, ...), condition=%wide.region_5.6_spmd.clone, body=%wide.region_2.5_spmd.clone.sunk | while | flops 310248192 | bytes 12989371 | solution.py:74
  178.2 4.0 fusion.270
  189.2 4.0 fusion.270
  200.3 4.0 fusion.270
  211.3 4.0 fusion.270
  222.4 4.0 fusion.270
  233.5 4.0 fusion.270
  244.5 4.0 fusion.270
  255.6 4.0 fusion.270
  263.1 3.4 fusion.108
  268.7 4.1 fusion.160
  274.5 3.5 fusion.118
  281.1 51.5 %while.79 = (s32[]{:T(128)}, bf16[8,768,128]{1,2,0:T(8,128)(2,1)}, s32[8]{0:T(128)S(1)}, bf16[256,1024]{0,1:T(8,128)(2,1)S(1)}, bf16[768,1024]{0,1:T(8,128)(2,1)...) while((s32[]{:T(128)}, bf16[8,768,128]{1,2,0:T(8,128)(2,1)}, ...), condition=%wide.region_11.12_spmd.clone, body=%wide.region_8.11_spmd.clone.sunk | while | flops 103022848 | bytes 4731323 | solution.py:74
  332.6 5.0 fusion.161
  341.7 63.5 %while.82 = (s32[]{:T(128)}, bf16[8,768,128]{1,2,0:T(8,128)(2,1)}, f32[8,2,768,1]{2,1,3,0:T(2,128)S(1)}, s32[8]{0:T(128)S(1)}, bf16[768,1024]{0,1:T(8,128)(2,1)}...) while((s32[]{:T(128)}, bf16[8,768,128]{1,2,0:T(8,128)(2,1)}, ...), condition=%wide.region_32.33_spmd.clone, body=%wide.region_29.32_spmd.clone.sunk | while | flops 317323776 | bytes 18924488 | solution.py:74
  406.5 32.1 %while.80 = (s32[]{:T(128)}, bf16[8,768,128]{1,2,0:T(8,128)(2,1)}, f32[8,2,768,1]{2,1,3,0:T(2,128)S(1)}, s32[8]{0:T(128)S(1)}, bf16[256,1024]{0,1:T(8,128)(2,1)S...) while((s32[]{:T(128)}, bf16[8,768,128]{1,2,0:T(8,128)(2,1)}, ...), condition=%wide.region_23.24_spmd.clone, body=%wide.region_20.23_spmd.clone.sunk | while | flops 103807488 | bytes 6341063 | solution.py:74
  438.7 38.4 %fusion.77 = (bf16[768,4096]{1,0:T(8,128)(2,1)}, f32[768,4096]{1,0:T(8,128)}) fusion(bf16[1024,4096]{1,0:T(8,128)(2,1)} %all-gather.17.cloned.1.call-done, f32[768,1024]{1,0:T(8,128)} %copy-done.1, f32[1024]{0:T(1024)S(1)} %bitcast.430, f32[1024]{0:T(1024)S(1)} %bitcast.426, f32[768]{0:T(1024)S(1)} %fusion.135, f32[768]{0:T(1024)S(1)} %broadcast_multiply_fusion.1), kind=kOutput, calls=%fused_computation.114 | convolution fusion | flops 6650855424 | bytes 30423040 | tf_op jit(solution)/shard_map/dot_general | solution.py:22
  477.2 11.6 fusion.162
  495.2 13.8 fusion.83
  509.1 12.4 multiply_reduce_fusion.3
  528.5 114.1 %while.81 = (s32[]{:T(128)}, bf16[8,768,128]{1,2,0:T(8,128)(2,1)}, bf16[8,256,128]{1,2,0:T(8,128)(2,1)S(1)}, bf16[8,256,128]{1,2,0:T(8,128)(2,1)}, s32[8]{0:T(12...) while((s32[]{:T(128)}, bf16[8,768,128]{1,2,0:T(8,128)(2,1)}, ...), condition=%wide.region_26.27_spmd.clone, body=%wide.region_24.26_spmd.clone.sunk | while | flops 257166848 | bytes 14436843 | solution.py:116
  642.7 6.0 multiply_reduce_fusion.4
  658.9 262.3 %while.83 = (s32[]{:T(128)}, bf16[8,768,128]{1,2,0:T(8,128)(2,1)}, bf16[8,768,128]{1,2,0:T(8,128)(2,1)}, bf16[8,768,128]{1,2,0:T(8,128)(2,1)}, s32[8]{0:T(128)S(...) while((s32[]{:T(128)}, bf16[8,768,128]{1,2,0:T(8,128)(2,1)}, ...), condition=%wide.region_35.36_spmd.clone, body=%wide.region_33.35_spmd.clone.sunk | while | flops 772674048 | bytes 39341036 | solution.py:116
  671.5 7.8 fusion.316
  683.2 7.7 fusion.318
  704.3 7.8 fusion.316
  716.0 7.8 fusion.318
  737.1 7.8 fusion.316
  748.8 7.7 fusion.318
  761.4 3.4 subtract_exponential_fusion.8
  769.9 7.8 fusion.316
  781.6 7.7 fusion.318
  794.2 3.4 subtract_exponential_fusion.8
  802.7 7.8 fusion.316
  814.4 7.7 fusion.318
  835.5 7.8 fusion.316
  847.1 7.7 fusion.318
  868.3 7.8 fusion.316
  879.9 7.8 fusion.318
  892.6 3.4 subtract_exponential_fusion.8
  901.0 7.8 fusion.316
  912.7 7.7 fusion.318
  921.3 9.6 fusion.149
  936.6 6.1 fusion.125
  942.8 6.2 fusion.128
  949.6 12.4 fusion.112
  963.1 4.5 convolution_bitcast_fusion
  967.6 4.1 fusion.146
  971.6 11.9 pad_maximum_fusion
  983.5 12.6 copy.164
  996.8 13.5 fusion.147
  1011.0 13.7 fusion.142
  1024.7 4.6 fusion.122
  1031.7 36.2 %reduce-scatter.27.cloned.1.call-done = f32[32,4]{1,0:T(8,128)} async-done(((f32[1024,4]{1,0:T(8,128)}), f32[32,4]{1,0:T(8,128)}) %reduce-scatter.27.cloned.1.call-update) | async-done | bytes 528
  1069.3 131.7 %reduce-scatter.29.cloned.1.call-done = f32[32,4]{1,0:T(8,128)} async-done(((f32[1024,4]{1,0:T(8,128)}), f32[32,4]{1,0:T(8,128)}) %reduce-scatter.29.cloned.1.call-update) | async-done | bytes 528
  1202.4 145.7 %reduce-scatter.17.cloned.1.call-done = f32[32,1024]{1,0:T(8,128)} async-done(((f32[1024,1024]{1,0:T(8,128)}), f32[32,1024]{1,0:T(8,128)}) %reduce-scatter.17.cloned.1.call-update) | async-done | bytes 131088 | tf_op jit(solution)/shard_map/reduce_scatter | solution.py:373
  1348.1 149.2 %reduce-scatter.19.cloned.1.call-done = f32[32,1024]{1,0:T(8,128)} async-done(((f32[1024,1024]{1,0:T(8,128)}), f32[32,1024]{1,0:T(8,128)}) %reduce-scatter.19.cloned.1.call-update) | async-done | bytes 131088 | tf_op jit(solution)/shard_map/reduce_scatter | solution.py:350
  1497.4 160.9 %reduce-scatter.15.cloned.1.call-done = f32[32,3072]{1,0:T(8,128)} async-done(((f32[1024,3072]{1,0:T(8,128)}), f32[32,3072]{1,0:T(8,128)}) %reduce-scatter.15.cloned.1.call-update) | async-done | bytes 393232 | tf_op jit(solution)/shard_map/reduce_scatter | solution.py:372
  1658.3 162.0 %reduce-scatter.25.cloned.1.call-done = f32[32,3072]{1,0:T(8,128)} async-done(((f32[1024,3072]{1,0:T(8,128)}), f32[32,3072]{1,0:T(8,128)}) %reduce-scatter.25.cloned.1.call-update) | async-done | bytes 393232
  1820.3 366.2 %reduce-scatter.21.cloned.1.call-done = f32[32,4096]{1,0:T(8,128)} async-done(((f32[1024,4096]{1,0:T(8,128)}), f32[32,4096]{1,0:T(8,128)}) %reduce-scatter.21.cloned.1.call-update) | async-done | bytes 524304 | tf_op jit(solution)/shard_map/reduce_scatter | solution.py:314
  2186.5 364.9 %reduce-scatter.23.cloned.1.call-done = f32[128,1024]{1,0:T(8,128)} async-done(((f32[4096,1024]{1,0:T(8,128)}), f32[128,1024]{1,0:T(8,128)}) %reduce-scatter.23.cloned.1.call-update) | async-done | bytes 524304 | tf_op jit(solution)/shard_map/reduce_scatter | solution.py:315
  (688 shorter events, 484.9 us)
Async XLA Ops:
  7.2 256.0 %copy-start = (bf16[1,256,1024]{2,1,0:T(8,128)(2,1)S(1)}, bf16[1,256,1024]{2,1,0:T(8,128)(2,1)}, u32[]{:S(2)}) copy-start(bf16[1,256,1024]{2,1,0:T(8,128)(2,1)} %param.26) | copy-start | bytes 1572868
  7.2 8.9 copy-start.22
  7.2 9.7 copy-start.59
  7.2 80.5 %copy-start.60 = (bf16[4,32]{1,0:T(4,128)(2,1)S(1)}, bf16[4,32]{1,0:T(4,128)(2,1)}, u32[]{:S(2)}) copy-start(bf16[4,32]{1,0:T(4,128)(2,1)} %param.36) | copy-start | bytes 772
  7.2 144.9 %copy-start.3 = (bf16[1,768,1024]{2,1,0:T(8,128)(2,1)S(1)}, bf16[1,768,1024]{2,1,0:T(8,128)(2,1)}, u32[]{:S(2)}) copy-start(bf16[1,768,1024]{2,1,0:T(8,128)(2,1)} %param.25) | copy-start | bytes 4718596
  7.2 147.7 %all-gather.9.cloned.1.call-start = ((), (), s32[]{:S(2)}) async-start(), calls=%async_computation.8 | async-start | bytes 6488064 | tf_op jit(solution)/shard_map/all_gather | solution.py:262
  9.2 254.0 %all-gather.13.cloned.1.call-start = ((), (), s32[]{:S(2)}) async-start(), calls=%async_computation.10 | async-start | bytes 6488064 | tf_op jit(solution)/shard_map/all_gather | solution.py:273
  10.9 257.8 %all-gather.11.cloned.1.call-start = ((), (), s32[]{:S(2)}) async-start(), calls=%async_computation.9 | async-start | bytes 2162688 | tf_op jit(solution)/shard_map/all_gather | solution.py:263
  12.5 320.0 %all-gather.15.cloned.1.call-start = ((), (), s32[]{:S(2)}) async-start(), calls=%async_computation.11 | async-start | bytes 2162688 | tf_op jit(solution)/shard_map/all_gather | solution.py:274
  14.2 424.5 %all-gather.17.cloned.1.call-start = ((), (), s32[]{:S(2)}) async-start(), calls=%async_computation.12 | async-start | bytes 8650752 | tf_op jit(solution)/shard_map/all_gather | solution.py:286
  16.0 461.2 %all-gather.19.cloned.1.call-start = ((), (), s32[]{:S(2)}) async-start(), calls=%async_computation.13 | async-start | bytes 8650752 | tf_op jit(solution)/shard_map/all_gather | solution.py:287
  16.8 1051.1 %reduce-scatter.27.cloned.1.call-start = ((), (), s32[]{:S(2)}) async-start(), calls=%async_computation.20 | async-start | bytes 540672
  87.7 75.7 %copy-start.57 = (f32[1,1024]{1,0:T(1,128)}, f32[1,1024]{1,0:T(1,128)S(1)}, u32[]{:S(2)}) copy-start(f32[1,1024]{1,0:T(1,128)S(1)} %get-tuple-element.831) | copy-start | bytes 12292
  87.7 185.7 %copy-start.55 = (f32[1,1024]{1,0:T(1,128)}, f32[1,1024]{1,0:T(1,128)S(1)}, u32[]{:S(2)}) copy-start(f32[1,1024]{1,0:T(1,128)S(1)} %get-tuple-element.830) | copy-start | bytes 12292
  152.2 11.2 copy-start.34
  152.2 121.2 %copy-start.50 = (f32[1,1024]{1,0:T(1,128)}, f32[1,1024]{1,0:T(1,128)S(1)}, u32[]{:S(2)}) copy-start(f32[1,1024]{1,0:T(1,128)S(1)} %get-tuple-element.826) | copy-start | bytes 12292
  152.5 10.9 copy-start.30
  153.0 10.3 copy-start.32
  272.9 5.1 copy-start.36
  273.3 4.7 copy-start.40
  273.3 4.7 copy-start.46
  406.5 32.2 %copy-start.23 = (f32[1,1024]{1,0:T(1,128)S(1)}, f32[1,1024]{1,0:T(1,128)}, u32[]{:S(2)}) copy-start(f32[1,1024]{1,0:T(1,128)} %get-tuple-element.825) | copy-start | bytes 12292
  406.5 32.2 %copy-start.24 = (f32[1,1024]{1,0:T(1,128)S(1)}, f32[1,1024]{1,0:T(1,128)}, u32[]{:S(2)}) copy-start(f32[1,1024]{1,0:T(1,128)} %get-tuple-element.829) | copy-start | bytes 12292
  438.6 38.5 %copy-start.17 = (bf16[256,1024]{0,1:T(8,128)(2,1)}, bf16[256,1024]{0,1:T(8,128)(2,1)S(1)}, u32[]{:S(2)}) copy-start(bf16[256,1024]{0,1:T(8,128)(2,1)S(1)} %get-tuple-element.1458) | copy-start | bytes 1572868
  438.6 38.5 %copy-start.18 = (bf16[256,1024]{0,1:T(8,128)(2,1)}, bf16[256,1024]{0,1:T(8,128)(2,1)S(1)}, u32[]{:S(2)}) copy-start(bf16[256,1024]{0,1:T(8,128)(2,1)S(1)} %get-tuple-element.1460) | copy-start | bytes 1572868
  438.6 38.5 %copy-start.29 = (f32[8,2,768,1]{2,1,3,0:T(2,128)}, f32[8,2,768,1]{2,1,3,0:T(2,128)S(1)}, u32[]{:S(2)}) copy-start(f32[8,2,768,1]{2,1,3,0:T(2,128)S(1)} %get-tuple-element.1310) | copy-start | bytes 147460
  438.6 38.5 %copy-start.53 = (pred[256]{0:T(512)(128)(4,1)}, pred[256]{0:T(512)(128)(4,1)S(1)}, u32[]{:S(2)}) copy-start(pred[256]{0:T(512)(128)(4,1)S(1)} %get-tuple-element.1486) | copy-start | bytes 772
  488.7 1.9 copy-start.10
  488.8 1.9 copy-start.44
  490.6 4.6 slice-start
  492.3 2.9 slice-start.1
  495.2 27.4 %copy-start.11 = (f32[768,1024]{1,0:T(8,128)}, f32[768,1024]{1,0:T(8,128)S(1)}, u32[]{:S(2)}) copy-start(f32[768,1024]{1,0:T(8,128)S(1)} %get-tuple-element.797) | copy-start | bytes 9437188
  495.2 27.4 %copy-start.48 = (f32[768]{0:T(1024)}, f32[768]{0:T(1024)S(1)}, u32[]{:S(2)}) copy-start(f32[768]{0:T(1024)S(1)} %negate_multiply_fusion.4) | copy-start | bytes 9220
  495.2 13.9 copy-start.2
  509.1 12.5 copy-start.16
  509.1 12.5 copy-start.43
  524.2 3.0 copy-start.12
  524.2 4.3 copy-start.20
  524.2 4.3 copy-start.54
  528.5 114.2 %copy-start.37 = (f32[768]{0:T(1024)S(1)}, f32[768]{0:T(1024)}, u32[]{:S(2)}) copy-start(f32[768]{0:T(1024)} %copy-done.36) | copy-start | bytes 9220
  528.5 114.2 %copy-start.47 = (f32[768]{0:T(1024)S(1)}, f32[768]{0:T(1024)}, u32[]{:S(2)}) copy-start(f32[768]{0:T(1024)} %copy-done.46) | copy-start | bytes 9220
  528.5 114.2 %copy-start.51 = (f32[1,1024]{1,0:T(1,128)S(1)}, f32[1,1024]{1,0:T(1,128)}, u32[]{:S(2)}) copy-start(f32[1,1024]{1,0:T(1,128)} %copy-done.50) | copy-start | bytes 12292
  642.7 6.0 copy-start.41
  642.7 6.0 copy-start.6
  648.7 1.9 copy-start.13
  652.2 3.0 copy-start.14
  655.2 3.8 copy-start.27
  658.9 262.3 %copy-start.4 = (bf16[1,768,1024]{2,1,0:T(8,128)(2,1)S(1)}, bf16[1,768,1024]{2,1,0:T(8,128)(2,1)}, u32[]{:S(2)}) copy-start(bf16[1,768,1024]{2,1,0:T(8,128)(2,1)} %param.25) | copy-start | bytes 4718596
  658.9 262.3 %copy-start.31 = (f32[768]{0:T(1024)S(1)}, f32[768]{0:T(1024)}, u32[]{:S(2)}) copy-start(f32[768]{0:T(1024)} %copy-done.30) | copy-start | bytes 9220
  658.9 262.3 %copy-start.35 = (f32[1,1024]{1,0:T(1,128)S(1)}, f32[1,1024]{1,0:T(1,128)}, u32[]{:S(2)}) copy-start(f32[1,1024]{1,0:T(1,128)} %copy-done.34) | copy-start | bytes 12292
  921.3 9.7 copy-start.39
  921.3 11.3 copy-start.33
  935.4 265.6 %reduce-scatter.29.cloned.1.call-start = ((), (), s32[]{:S(2)}) async-start(), calls=%async_computation.21 | async-start | bytes 540672
  936.6 411.6 %reduce-scatter.17.cloned.1.call-start = ((), (), s32[]{:S(2)}) async-start(), calls=%async_computation.15 | async-start | bytes 4325376 | tf_op jit(solution)/shard_map/reduce_scatter | solution.py:373
  942.8 554.6 %reduce-scatter.19.cloned.1.call-start = ((), (), s32[]{:S(2)}) async-start(), calls=%async_computation.16 | async-start | bytes 4325376 | tf_op jit(solution)/shard_map/reduce_scatter | solution.py:350
  949.0 709.3 %reduce-scatter.15.cloned.1.call-start = ((), (), s32[]{:S(2)}) async-start(), calls=%async_computation.14 | async-start | bytes 12976128 | tf_op jit(solution)/shard_map/reduce_scatter | solution.py:372
  962.1 858.2 %reduce-scatter.25.cloned.1.call-start = ((), (), s32[]{:S(2)}) async-start(), calls=%async_computation.19 | async-start | bytes 12976128
  963.1 4.5 copy-start.7
  963.1 4.5 copy-start.19
  963.1 4.5 copy-start.56
  996.1 1190.4 %reduce-scatter.21.cloned.1.call-start = ((), (), s32[]{:S(2)}) async-start(), calls=%async_computation.17 | async-start | bytes 17301504 | tf_op jit(solution)/shard_map/reduce_scatter | solution.py:314
  1010.3 1541.1 %reduce-scatter.23.cloned.1.call-start = ((), (), s32[]{:S(2)}) async-start(), calls=%async_computation.18 | async-start | bytes 17301504 | tf_op jit(solution)/shard_map/reduce_scatter | solution.py:315
  1024.7 4.6 copy-start.9
  1024.7 4.6 copy-start.15
  (15 other events, 18.8 us)
Sparse Core Ops, SparseCore 0:
  11.5 72.2 all-gather.8
  86.7 68.1 all-gather.12
  158.4 54.9 all-gather.10
  216.8 55.3 all-gather.14
  275.5 76.2 all-gather.16
  355.2 76.0 all-gather.18
  935.5 132.3 reduce-scatter.26
  1070.3 130.7 reduce-scatter.28
  1203.9 144.1 reduce-scatter.16
  1350.8 146.5 reduce-scatter.18
  1504.0 154.2 reduce-scatter.14
  1665.8 154.4 reduce-scatter.24
  1823.1 363.2 reduce-scatter.20
  2189.2 362.1 reduce-scatter.22
where the time goes:
time: 2570 us; the launch traced here: 2560 us
  waiting for transfers between devices  1520 us (59%)
  matrix products  556 us (22%)
  local copies, waits for them, and re-layouts  248 us (10%)
  blocking collectives  134 us (5%)
  other arithmetic  51.9 us (2%)
  loops' own time  33.7 us (1%)
    reduce_scatter x1, waiting for transfers between devices, body(): lax.psum_scatter(grad_feed_in, ('dp', 'fsdp'), scatter_dimension=0, tiled...  366 us
    reduce_scatter x1, waiting for transfers between devices, body(): lax.psum_scatter(grad_feed_out, ('dp', 'fsdp'), scatter_dimension=0, tile...  365 us
    unnamed x17, waiting for transfers between devices  330 us
    reduce_scatter x1, waiting for transfers between devices, body(): lax.psum_scatter(grad_self_in, ('dp', 'fsdp'), scatter_dimension=0, tiled...  161 us
    reduce_scatter x1, waiting for transfers between devices, body(): lax.psum_scatter(grad_cross_out, ('dp', 'fsdp'), scatter_dimension=0, til...  149 us
    reduce_scatter x1, waiting for transfers between devices, body(): lax.psum_scatter(grad_self_out, ('dp', 'fsdp'), scatter_dimension=0, tile...  146 us
    dynamic_slice x144, local copies, waits for them, and re-layouts, head_block(): block = lax.dynamic_slice_in_dim(matrix, start_col, 2 * HEAD, 1)  109 us
    dot_general x16, matrix products, one_pair(): jnp.einsum('hqk,khd->qhd', grad_scores, key_pair, preferred_element_type=...  81.5 us
  transfers between devices with their start and end apart: 14, of which 8 were waited for; matrix products, arithmetic and copies ran while one was open for 16% of the time, Pallas kernels for 0%

commit v1 on v0

v1 whole, which is shorter than its diff:
```python
import functools

import jax
import jax.numpy as jnp
from jax import lax
from jax.experimental import pallas as pl
from jax.experimental.pallas import tpu as pltpu
from jax.sharding import PartitionSpec as P

HEAD = 64
LANES = 128
BOTH = ("dp", "fsdp")
VMEM_BYTES = 60 * 1024 * 1024
TAIL_RATE = 0.2316419
TAIL_POLY = (
    0.09252224973357535,
    0.09042007971374488,
    0.10265042640370807,
    0.013551821473999732,
    0.2252533241128307,
    -0.2016603378863937,
    0.24768663093443657,
    -0.07042413008644138,
)


def product(left, right):
    return jnp.dot(left, right, preferred_element_type=jnp.float32)


def contract_rows(left, right):
    return lax.dot_general(
        left, right, (((0,), (0,)), ((), ())), preferred_element_type=jnp.float32
    )


def times_transposed(left, right):
    return lax.dot_general(
        left, right, (((1,), (1,)), ((), ())), preferred_element_type=jnp.float32
    )


def layer_norm(values, gain_row, bias_row):
    centre = values - jnp.mean(values, axis=-1, keepdims=True)
    spread = jnp.mean(centre * centre, axis=-1, keepdims=True)
    return centre * lax.rsqrt(spread + 1e-05) * gain_row + bias_row


def norm_backward(values, gain_row, grad):
    centre = values - jnp.mean(values, axis=-1, keepdims=True)
    rate = lax.rsqrt(jnp.mean(centre * centre, axis=-1, keepdims=True) + 1e-05)
    normed = centre * rate
    scaled = grad * gain_row
    grad_input = rate * (
        scaled
        - jnp.mean(scaled, axis=-1, keepdims=True)
        - normed * jnp.mean(scaled * normed, axis=-1, keepdims=True)
    )
    return grad_input, jnp.sum(grad * normed, axis=0), jnp.sum(grad, axis=0)


def masked_scores(keys, queries, key_limit, causal, query_start):
    scores = times_transposed(keys, queries)
    key_count, query_count = scores.shape
    if not causal:
        row = lax.broadcasted_iota(jnp.int32, scores.shape, 0)
        return jnp.where(row < key_limit, scores, -1e30)
    row = query_start + lax.broadcasted_iota(jnp.int32, (query_count, query_count), 0)
    column = query_start + lax.broadcasted_iota(jnp.int32, (query_count, query_count), 1)
    diagonal = jnp.where(
        (row <= column) & (row < key_limit), scores[query_start:, :], -1e30
    )
    if query_start == 0:
        return diagonal
    below_row = lax.broadcasted_iota(jnp.int32, (query_start, query_count), 0)
    below = jnp.where(below_row < key_limit, scores[:query_start, :], -1e30)
    return jnp.concatenate([below, diagonal], axis=0)


def query_blocks(row_count, key_count, causal):
    width = 256 if row_count % 256 == 0 else row_count
    return [
        (start, width, start + width if causal else key_count)
        for start in range(0, row_count, width)
    ]


def head_lanes(head, shape):
    lane = lax.broadcasted_iota(jnp.int32, shape, 1)
    return (lane >= head * HEAD) & (lane < (head + 1) * HEAD)


def attention_forward_kernel(causal, limit_ref, q_ref, k_ref, v_ref, mixed_ref, total_ref, mixed_turned):
    key_limit = limit_ref[0]
    row_count, key_count = q_ref.shape[0], k_ref.shape[0]
    values_turned = v_ref[...].T
    scaled = q_ref[...] * jnp.bfloat16(HEAD**-0.5)
    for head in range(2):
        own = jnp.where(head_lanes(head, scaled.shape), scaled, jnp.zeros_like(scaled))
        lanes = slice(head * HEAD, (head + 1) * HEAD)
        for start, width, stop in query_blocks(row_count, key_count, causal):
            scores = masked_scores(
                k_ref[:stop, :], own[start : start + width, :], key_limit, causal, start
            )
            highest = jnp.max(scores, axis=0, keepdims=True)
            expanded = jnp.exp(scores - highest)
            total = jnp.sum(expanded, axis=0, keepdims=True)
            mixed = product(values_turned[lanes, :stop], expanded.astype(jnp.bfloat16))
            mixed_turned[lanes, start : start + width] = mixed / total
            total_ref[0, head : head + 1, start : start + width] = highest + jnp.log(total)
    mixed_ref[...] = mixed_turned[...].T.astype(jnp.bfloat16)


def attention_forward(limit, queries, q_at, keys, k_at, values, v_at, causal):
    row_count, key_count = queries.shape[0], keys.shape[0]
    width = 1024
    pairs = width // LANES
    cost = pl.CostEstimate(
        flops=4 * row_count * key_count * width,
        transcendentals=row_count * key_count * pairs * 2,
        bytes_accessed=4 * row_count * width + 4 * key_count * width,
    )
    return pl.pallas_call(
        functools.partial(attention_forward_kernel, causal),
        grid_spec=pltpu.PrefetchScalarGridSpec(
            num_scalar_prefetch=1,
            grid=(pairs,),
            in_specs=[
                pl.BlockSpec((row_count, LANES), lambda p, s: (0, q_at + p)),
                pl.BlockSpec((key_count, LANES), lambda p, s: (0, k_at + p)),
                pl.BlockSpec((key_count, LANES), lambda p, s: (0, v_at + p)),
            ],
            out_specs=[
                pl.BlockSpec((row_count, LANES), lambda p, s: (0, p)),
                pl.BlockSpec((1, 2, row_count), lambda p, s: (p, 0, 0)),
            ],
            scratch_shapes=[pltpu.VMEM((LANES, row_count), jnp.float32)],
        ),
        out_shape=[
            jax.ShapeDtypeStruct((row_count, width), jnp.bfloat16),
            jax.ShapeDtypeStruct((pairs, 2, row_count), jnp.float32),
        ],
        compiler_params=pltpu.CompilerParams(vmem_limit_bytes=VMEM_BYTES),
        cost_estimate=cost,
        name="attention_forward",
    )(limit, queries, keys, values)


def attention_backward_kernel(
    causal,
    limit_ref,
    q_ref,
    k_ref,
    v_ref,
    mixed_ref,
    grad_ref,
    total_ref,
    grad_q_ref,
    grad_k_ref,
    grad_v_ref,
    grad_q_turned,
    grad_k_sum,
    grad_v_sum,
):
    key_limit = limit_ref[0]
    row_count, key_count = q_ref.shape[0], k_ref.shape[0]
    keys_turned = k_ref[...].T
    scaled = q_ref[...] * jnp.bfloat16(HEAD**-0.5)
    grad = grad_ref[...]
    inner_turned = (grad.astype(jnp.float32) * mixed_ref[...].astype(jnp.float32)).T
    grad_k_sum[...] = jnp.zeros_like(grad_k_sum)
    grad_v_sum[...] = jnp.zeros_like(grad_v_sum)
    for head in range(2):
        mask = head_lanes(head, scaled.shape)
        own = jnp.where(mask, scaled, jnp.zeros_like(scaled))
        own_grad = jnp.where(mask, grad, jnp.zeros_like(grad))
        lanes = slice(head * HEAD, (head + 1) * HEAD)
        inner = jnp.sum(inner_turned[lanes, :], axis=0, keepdims=True)
        for start, width, stop in query_blocks(row_count, key_count, causal):
            columns = slice(start, start + width)
            queries, grads = own[columns, :], own_grad[columns, :]
            scores = masked_scores(k_ref[:stop, :], queries, key_limit, causal, start)
            probs = jnp.exp(scores - total_ref[0, head : head + 1, columns])
            grad_v_sum[:stop, :] += product(probs.astype(jnp.bfloat16), grads)
            grad_probs = times_transposed(v_ref[:stop, :], grads)
            grad_scores = (probs * (grad_probs - inner[:, columns])).astype(jnp.bfloat16)
            grad_k_sum[:stop, :] += product(grad_scores, queries)
            grad_q_turned[lanes, columns] = product(keys_turned[lanes, :stop], grad_scores)
    grad_q_ref[...] = (grad_q_turned[...].T * HEAD**-0.5).astype(jnp.bfloat16)
    grad_k_ref[...] = grad_k_sum[...].astype(jnp.bfloat16)
    grad_v_ref[...] = grad_v_sum[...].astype(jnp.bfloat16)


def attention_backward(limit, queries, q_at, keys, k_at, values, v_at, mixed, grad_mixed, totals, causal):
    row_count, key_count = queries.shape[0], keys.shape[0]
    width = 1024
    pairs = width // LANES
    cost = pl.CostEstimate(
        flops=10 * row_count * key_count * width,
        transcendentals=row_count * key_count * pairs * 2,
        bytes_accessed=8 * row_count * width + 8 * key_count * width,
    )
    row_block = pl.BlockSpec((row_count, LANES), lambda p, s: (0, p))
    key_block = pl.BlockSpec((key_count, LANES), lambda p, s: (0, p))
    return pl.pallas_call(
        functools.partial(attention_backward_kernel, causal),
        grid_spec=pltpu.PrefetchScalarGridSpec(
            num_scalar_prefetch=1,
            grid=(pairs,),
            in_specs=[
                pl.BlockSpec((row_count, LANES), lambda p, s: (0, q_at + p)),
                pl.BlockSpec((key_count, LANES), lambda p, s: (0, k_at + p)),
                pl.BlockSpec((key_count, LANES), lambda p, s: (0, v_at + p)),
                row_block,
                row_block,
                pl.BlockSpec((1, 2, row_count), lambda p, s: (p, 0, 0)),
            ],
            out_specs=[row_block, key_block, key_block],
            scratch_shapes=[
                pltpu.VMEM((LANES, row_count), jnp.float32),
                pltpu.VMEM((key_count, LANES), jnp.float32),
                pltpu.VMEM((key_count, LANES), jnp.float32),
            ],
        ),
        out_shape=[
            jax.ShapeDtypeStruct((row_count, width), jnp.bfloat16),
            jax.ShapeDtypeStruct((key_count, width), jnp.bfloat16),
            jax.ShapeDtypeStruct((key_count, width), jnp.bfloat16),
        ],
        compiler_params=pltpu.CompilerParams(vmem_limit_bytes=VMEM_BYTES),
        cost_estimate=cost,
        name="attention_backward",
    )(limit, queries, keys, values, mixed, grad_mixed, totals)


def gelu_and_slope(values):
    size = jnp.abs(values)
    bell = jnp.exp(-0.5 * values * values)
    t = 1.0 / (1.0 + TAIL_RATE * size)
    poly = TAIL_POLY[-1] * t + TAIL_POLY[-2]
    for coefficient in TAIL_POLY[-3::-1]:
        poly = poly * t + coefficient
    tail = poly * t * bell
    normal_cdf = jnp.where(values >= 0, 1.0 - tail, tail)
    return values * normal_cdf, normal_cdf + values * (bell * (2.0 * jnp.pi) ** (-0.5))


def feed_forward_kernel(normed_ref, input_ref, output_ref, base_ref, hidden_ref, slope_ref, after_ref):
    @pl.when(pl.program_id(0) == 0)
    def _():
        after_ref[...] = base_ref[...]

    row_count = normed_ref.shape[0]
    step = 256 if row_count % 256 == 0 else row_count
    for start in range(0, row_count, step):
        rows = slice(start, start + step)
        hidden, slope = gelu_and_slope(product(normed_ref[rows, :], input_ref[...]))
        hidden = hidden.astype(jnp.bfloat16)
        hidden_ref[rows, :] = hidden
        slope_ref[rows, :] = slope.astype(jnp.bfloat16)
        after_ref[rows, :] += product(hidden, output_ref[...])


def feed_forward(normed, input_low, output_low, after_cross):
    row_count, width = normed.shape
    hidden_width = input_low.shape[1]
    tile = 512
    whole = pl.BlockSpec((row_count, width), lambda j: (0, 0))
    tall = pl.BlockSpec((row_count, tile), lambda j: (0, j))
    return pl.pallas_call(
        feed_forward_kernel,
        grid=(hidden_width // tile,),
        in_specs=[
            whole,
            pl.BlockSpec((width, tile), lambda j: (0, j)),
            pl.BlockSpec((tile, width), lambda j: (j, 0)),
            whole,
        ],
        out_specs=[tall, tall, whole],
        out_shape=[
            jax.ShapeDtypeStruct((row_count, hidden_width), jnp.bfloat16),
            jax.ShapeDtypeStruct((row_count, hidden_width), jnp.bfloat16),
            jax.ShapeDtypeStruct((row_count, width), jnp.float32),
        ],
        compiler_params=pltpu.CompilerParams(vmem_limit_bytes=VMEM_BYTES),
        cost_estimate=pl.CostEstimate(
            flops=4 * row_count * width * hidden_width,
            transcendentals=2 * row_count * hidden_width,
            bytes_accessed=4 * width * hidden_width + 4 * row_count * hidden_width,
        ),
        name="feed_forward",
    )(normed, input_low, output_low, after_cross)


def feed_backward_kernel(
    grad_ref,
    turned_ref,
    hidden_ref,
    slope_ref,
    input_ref,
    output_ref,
    grad_in_ref,
    grad_out_ref,
    grad_normed_ref,
):
    @pl.when(pl.program_id(0) == 0)
    def _():
        grad_normed_ref[...] = jnp.zeros_like(grad_normed_ref)

    grad_hidden = times_transposed(grad_ref[...], output_ref[...])
    grad_pre = (grad_hidden * slope_ref[...].astype(jnp.float32)).astype(jnp.bfloat16)
    grad_out_ref[...] = contract_rows(hidden_ref[...], grad_ref[...]).astype(jnp.bfloat16)
    grad_in_ref[...] = product(turned_ref[...], grad_pre).astype(jnp.bfloat16)
    grad_normed_ref[...] += times_transposed(grad_pre, input_ref[...])


def feed_backward(table, grad_branch, normed_turned, hidden, slope, input_low, output_low):
    row_count, width = grad_branch.shape
    hidden_width = hidden.shape[1]
    tile = hidden_width // table.shape[0]
    whole = pl.BlockSpec((row_count, width), lambda j, t: (0, 0))
    tall = pl.BlockSpec((row_count, tile), lambda j, t: (0, t[j]))
    return pl.pallas_call(
        lambda table_ref, *refs: feed_backward_kernel(*refs),
        grid_spec=pltpu.PrefetchScalarGridSpec(
            num_scalar_prefetch=1,
            grid=(hidden_width // tile,),
            in_specs=[
                whole,
                pl.BlockSpec((width, row_count), lambda j, t: (0, 0)),
                tall,
                tall,
                pl.BlockSpec((width, tile), lambda j, t: (0, t[j])),
                pl.BlockSpec((tile, width), lambda j, t: (t[j], 0)),
            ],
            out_specs=[
                pl.BlockSpec((width, tile), lambda j, t: (0, t[j])),
                pl.BlockSpec((tile, width), lambda j, t: (j, 0)),
                whole,
            ],
        ),
        out_shape=[
            jax.ShapeDtypeStruct((width, hidden_width), jnp.bfloat16),
            jax.ShapeDtypeStruct((hidden_width, width), jnp.bfloat16),
            jax.ShapeDtypeStruct((row_count, width), jnp.float32),
        ],
        compiler_params=pltpu.CompilerParams(vmem_limit_bytes=VMEM_BYTES),
        cost_estimate=pl.CostEstimate(
            flops=8 * row_count * width * hidden_width,
            transcendentals=0,
            bytes_accessed=8 * width * hidden_width + 4 * row_count * hidden_width,
        ),
        name="feed_backward",
    )(table, grad_branch, normed_turned, hidden, slope, input_low, output_low)


def place_rows_kernel(starts, table_ref, *refs):
    out_ref = refs[-1]
    step = pl.program_id(0)
    for index, ref in enumerate(refs[:-1]):

        @pl.when((step >= starts[index]) & (step < starts[index + 1]))
        def _(ref=ref):
            out_ref[...] = ref[...]


def place_rows(table, pieces, rows):
    starts = [0]
    for piece in pieces:
        starts.append(starts[-1] + piece.shape[0] // rows)
    columns = pieces[0].shape[1]

    def piece_spec(first, last):
        return pl.BlockSpec((rows, columns), lambda j, t: (jnp.clip(j - first, 0, last - first - 1), 0))

    return pl.pallas_call(
        functools.partial(place_rows_kernel, starts),
        grid_spec=pltpu.PrefetchScalarGridSpec(
            num_scalar_prefetch=1,
            grid=(starts[-1],),
            in_specs=[piece_spec(starts[i], starts[i + 1]) for i in range(len(pieces))],
            out_specs=pl.BlockSpec((rows, columns), lambda j, t: (t[j], 0)),
        ),
        out_shape=jax.ShapeDtypeStruct((starts[-1] * rows, columns), pieces[0].dtype),
        compiler_params=pltpu.CompilerParams(vmem_limit_bytes=VMEM_BYTES),
        cost_estimate=pl.CostEstimate(
            flops=0, transcendentals=0, bytes_accessed=4 * starts[-1] * rows * columns
        ),
        name="place_rows",
    )(table, *pieces)


def turn_blocks_kernel(table_ref, in_ref, out_ref):
    out_ref[...] = in_ref[...].T


def turn_blocks(table, matrix, block):
    row_count = matrix.shape[0]
    count = matrix.shape[1] // block
    return pl.pallas_call(
        turn_blocks_kernel,
        grid_spec=pltpu.PrefetchScalarGridSpec(
            num_scalar_prefetch=1,
            grid=(count,),
            in_specs=[pl.BlockSpec((row_count, block), lambda j, t: (0, t[j]))],
            out_specs=pl.BlockSpec((block, row_count), lambda j, t: (j, 0)),
        ),
        out_shape=jax.ShapeDtypeStruct((matrix.shape[1], row_count), matrix.dtype),
        compiler_params=pltpu.CompilerParams(vmem_limit_bytes=VMEM_BYTES),
        cost_estimate=pl.CostEstimate(flops=0, transcendentals=0, bytes_accessed=4 * matrix.size),
        name="turn_blocks",
    )(table, matrix)


class Links:
    def __init__(self, dp_count, fsdp_count, width):
        self.dp_count, self.fsdp_count = dp_count, fsdp_count
        power = (dp_count & (dp_count - 1)) == 0 and (fsdp_count & (fsdp_count - 1)) == 0
        self.pairwise = power and dp_count > 1 and (width // dp_count) % LANES == 0 and width // dp_count >= 16 * fsdp_count
        self.dp_index = lax.axis_index("dp")
        self.fsdp_index = lax.axis_index("fsdp")
        self.blocks = dp_count if self.pairwise else width // LANES
        self.high_bits = [1 << b for b in range(1, dp_count.bit_length() - 1)]
        if self.pairwise:
            self.fsdp_table = (self.fsdp_index ^ jnp.arange(fsdp_count, dtype=jnp.int32)).astype(jnp.int32)

    def order(self, flip):
        return self.high_bits[::-1] if flip else self.high_bits

    def table(self, masks):
        return (self.dp_index ^ jnp.asarray(masks, dtype=jnp.int32)).astype(jnp.int32)

    def swap(self, array, bit):
        return lax.ppermute(array, "dp", [(i, i ^ bit) for i in range(self.dp_count)])

    def swap_fsdp(self, array, bit):
        return lax.ppermute(array, "fsdp", [(i, i ^ bit) for i in range(self.fsdp_count)])

    def gather(self, shard, flip):
        if not self.pairwise:
            return lax.all_gather(shard, BOTH, axis=0, tiled=True)
        return self.spread(self.gather_fsdp(shard), flip)

    def gather_fsdp(self, shard):
        parts = [shard] + [self.swap_fsdp(shard, k) for k in range(1, self.fsdp_count)]
        return place_rows(self.fsdp_table, parts, shard.shape[0])

    def spread(self, block, flip):
        pieces, masks = [block], [0]
        for bit in self.order(flip) + [1]:
            pieces = pieces + [self.swap(piece, bit) for piece in pieces]
            masks = masks + [mask ^ bit for mask in masks]
        return place_rows(self.table(masks), pieces, block.shape[0])

    def row_masks(self, flip):
        if not self.pairwise:
            return None
        masks = [0]
        for bit in self.order(flip) + [1]:
            masks = [mask ^ bit for mask in masks] + masks
        return masks

    def row_table(self, flip):
        if not self.pairwise:
            return jnp.arange(self.blocks, dtype=jnp.int32)
        return self.table(self.row_masks(flip))

    def scatter(self, grad, flip):
        if not self.pairwise:
            part = lax.psum_scatter(grad.astype(jnp.float32), "dp", scatter_dimension=0, tiled=True)
            return lax.psum_scatter(part, "fsdp", scatter_dimension=0, tiled=True)
        for bit in [1] + self.order(flip)[::-1]:
            half = grad.shape[0] // 2
            other = self.swap(grad[:half], bit)
            grad = (grad[half:].astype(jnp.float32) + other.astype(jnp.float32)).astype(jnp.bfloat16)
        rows = grad.shape[0] // self.fsdp_count

        def block(index):
            return lax.dynamic_slice_in_dim(grad, index * rows, rows, 0)

        total = block(self.fsdp_index).astype(jnp.float32)
        for k in range(1, self.fsdp_count):
            total = total + self.swap_fsdp(block(self.fsdp_index ^ k), k).astype(jnp.float32)
        return total


def body(
    unit_states,
    encoder_states,
    cotangent,
    unit_lengths,
    text_lengths,
    self_project,
    self_output,
    cross_project,
    cross_output,
    feed_input,
    feed_output,
    norm_gains,
    norm_biases,
):
    low = jnp.bfloat16
    layer_input = unit_states[0].astype(jnp.float32)
    encoded = encoder_states[0]
    row_count, width = layer_input.shape
    links = Links(lax.axis_size("dp"), lax.axis_size("fsdp"), width)
    shard_rows = self_project.shape[0]

    tables = jnp.concatenate([norm_gains, norm_biases], axis=0).T
    tables = jnp.pad(tables, ((0, 0), (0, LANES - tables.shape[1])))
    self_shard = jnp.concatenate([self_project.astype(low), self_output.astype(low), tables], axis=1)
    cross_shard = jnp.concatenate([cross_project.astype(low), cross_output.astype(low)], axis=1)
    if links.pairwise:
        self_part = links.gather_fsdp(self_shard)
        cross_part = links.gather_fsdp(cross_shard)
        self_first = links.spread(self_part[:, : 2 * width], False)
        self_second = links.spread(self_part[:, 2 * width :], True)
        cross_first = links.spread(cross_part[:, width : 3 * width], False)
        cross_second = links.spread(
            jnp.concatenate([cross_part[:, :width], cross_part[:, 3 * width :]], axis=1), True
        )
    else:
        self_whole = links.gather(self_shard, False)
        cross_whole = links.gather(cross_shard, False)
        self_first, self_second = self_whole[:, : 2 * width], self_whole[:, 2 * width :]
        cross_first = cross_whole[:, width : 3 * width]
        cross_second = jnp.concatenate([cross_whole[:, :width], cross_whole[:, 3 * width :]], axis=1)
    feed_input_low = links.gather(feed_input.astype(low), False)
    feed_output_low = links.gather(feed_output.astype(low), True)

    self_value, self_output_low = self_second[:, :width], self_second[:, width : 2 * width]
    norm_rows = self_second[:, 2 * width : 2 * width + 8].astype(jnp.float32).T
    gain_table, bias_table = norm_rows[:4], norm_rows[4:]
    cross_query, cross_output_low = cross_second[:, :width], cross_second[:, width:]

    normed_self = layer_norm(layer_input, gain_table[0], bias_table[0]).astype(low)
    query_key = product(normed_self, self_first).astype(low)
    self_values = product(normed_self, self_value).astype(low)
    self_mixed, self_totals = attention_forward(
        unit_lengths, query_key, 0, query_key, width // LANES, self_values, 0, True
    )
    after_self = layer_input + product(self_mixed, self_output_low)
    normed_cross = layer_norm(after_self, gain_table[1], bias_table[1]).astype(low)
    cross_queries = product(normed_cross, cross_query).astype(low)
    cross_kv = product(encoded, cross_first).astype(low)
    cross_mixed, cross_totals = attention_forward(
        text_lengths, cross_queries, 0, cross_kv, 0, cross_kv, width // LANES, False
    )
    after_cross = after_self + product(cross_mixed, cross_output_low)
    normed_feed = layer_norm(after_cross, gain_table[2], bias_table[2]).astype(low)
    hidden, slope, after_feed = feed_forward(normed_feed, feed_input_low, feed_output_low, after_cross)
    block_output = layer_norm(after_feed, gain_table[3], bias_table[3]).astype(low)

    row_live = (jnp.arange(row_count, dtype=jnp.int32) < unit_lengths[0]).astype(jnp.float32)
    grad_y = cotangent[0] * row_live[:, None]
    grad_after_feed, grad_gain_3, grad_bias_3 = norm_backward(after_feed, gain_table[3], grad_y)
    first_rows, second_rows = links.row_table(False), links.row_table(True)
    lane_block = width // links.blocks
    grad_feed_in, grad_feed_out, grad_normed = feed_backward(
        first_rows,
        grad_after_feed.astype(low),
        turn_blocks(second_rows, normed_feed, lane_block),
        hidden,
        slope,
        feed_input_low,
        feed_output_low,
    )
    feed_out_part = links.scatter(grad_feed_out, False)
    feed_in_part = links.scatter(grad_feed_in, True)
    grad_input, grad_gain_2, grad_bias_2 = norm_backward(after_cross, gain_table[2], grad_normed)
    grad_after_cross = grad_after_feed + grad_input

    cross_branch = grad_after_cross.astype(low)
    grad_cross_mixed = times_transposed(cross_branch, cross_output_low).astype(low)
    grad_cross_out = product(turn_blocks(first_rows, cross_mixed, lane_block), cross_branch).astype(low)
    cross_out_part = links.scatter(grad_cross_out, False)
    grad_q, grad_k, grad_v = attention_backward(
        text_lengths,
        cross_queries,
        0,
        cross_kv,
        0,
        cross_kv,
        width // LANES,
        cross_mixed,
        grad_cross_mixed,
        cross_totals,
        False,
    )
    grad_kv = jnp.concatenate([grad_k, grad_v], axis=1)
    grad_cross_query = product(turn_blocks(first_rows, normed_cross, lane_block), grad_q).astype(low)
    grad_cross_kv = product(turn_blocks(second_rows, encoded, lane_block), grad_kv).astype(low)
    cross_query_part = links.scatter(grad_cross_query, False)
    cross_kv_part = links.scatter(grad_cross_kv, True)
    grad_normed = times_transposed(grad_q, cross_query)
    grad_encoded = times_transposed(grad_kv, cross_first)
    grad_input, grad_gain_1, grad_bias_1 = norm_backward(after_self, gain_table[1], grad_normed)
    grad_after_self = grad_after_cross + grad_input

    self_branch = grad_after_self.astype(low)
    grad_self_mixed = times_transposed(self_branch, self_output_low).astype(low)
    grad_self_out = product(turn_blocks(first_rows, self_mixed, lane_block), self_branch).astype(low)
    self_out_part = links.scatter(grad_self_out, False)
    grad_q, grad_k, grad_v = attention_backward(
        unit_lengths,
        query_key,
        0,
        query_key,
        width // LANES,
        self_values,
        0,
        self_mixed,
        grad_self_mixed,
        self_totals,
        True,
    )
    grad_qk = jnp.concatenate([grad_q, grad_k], axis=1)
    grad_normed = times_transposed(grad_qk, self_first) + times_transposed(grad_v, self_value)
    grad_input, grad_gain_0, grad_bias_0 = norm_backward(layer_input, gain_table[0], grad_normed)
    grad_states = grad_after_self + grad_input
    grad_tables = jnp.stack(
        [grad_gain_0, grad_gain_1, grad_gain_2, grad_gain_3, grad_bias_0, grad_bias_1, grad_bias_2, grad_bias_3]
    )
    grad_tables = jnp.pad(grad_tables.T, ((0, 0), (0, LANES - 8))).astype(low)
    self_turned = turn_blocks(first_rows, normed_self, lane_block)
    if links.pairwise:
        grad_tables = place_rows(jnp.arange(links.blocks, dtype=jnp.int32), [
            lax.dynamic_slice_in_dim(grad_tables, first_rows[j] * lane_block, lane_block, 0)
            for j in range(links.blocks)
        ], lane_block)
    grad_self_qk = product(self_turned, grad_qk).astype(low)
    grad_self_v = product(turn_blocks(second_rows, normed_self, lane_block), grad_v).astype(low)
    self_qk_part = links.scatter(grad_self_qk, False)
    self_v_part = links.scatter(grad_self_v, True)
    table_part = links.scatter(grad_tables, False)

    return (
        block_output[None],
        grad_states[None],
        grad_encoded[None],
        jnp.concatenate([self_qk_part, self_v_part], axis=1),
        self_out_part,
        jnp.concatenate([cross_query_part, cross_kv_part], axis=1),
        cross_out_part,
        feed_in_part,
        feed_out_part,
        table_part[:, :4].T,
        table_part[:, 4:8].T,
    )


def solution(mesh):
    return jax.shard_map(
        body,
        mesh=mesh,
        in_specs=(
            P(BOTH, None, None),
            P(BOTH, None, None),
            P(BOTH, None, None),
            P(BOTH),
            P(BOTH),
            P(BOTH, None),
            P(BOTH, None),
            P(BOTH, None),
            P(BOTH, None),
            P(BOTH, None),
            P(BOTH, None),
            P(None, BOTH),
            P(None, BOTH),
        ),
        out_specs=(
            P(BOTH, None, None),
            P(BOTH, None, None),
            P(BOTH, None, None),
            P(BOTH, None),
            P(BOTH, None),
            P(BOTH, None),
            P(BOTH, None),
            P(BOTH, None),
            P(BOTH, None),
            P(None, BOTH),
            P(None, BOTH),
        ),
        check_vma=False,
    )
```

time: 2570 us -> 825 us (0.32)
  waiting for transfers between devices: 1520 us -> 228 us
  matrix products: 556 us -> 69.3 us
  Pallas kernels: 0 us -> 257 us
  local copies, waits for them, and re-layouts: 248 us -> 43.3 us
  starting transfers between devices: 1.05 us -> 145 us
  blocking collectives: 134 us -> 0 us
  loops' own time: 33.7 us -> 0 us
    reduce_scatter x5 -> x0, waiting for transfers between devices: 1190 us -> none  [the longest x1 366 us: body(): lax.psum_scatter(grad_feed_in, ('dp', 'fsdp'), scatter_dimension=0, tiled...]
    dot_general x135 -> x0, matrix products: 383 us -> none  [the longest x16 81.5 us: one_pair(): jnp.einsum('hqk,khd->qhd', grad_scores, key_pair, preferred_element_type=...]
    unnamed x17 -> x0, waiting for transfers between devices: 330 us -> none
    pallas_call x0 -> x24, Pallas kernels: none -> 257 us  [the longest x11 61.9 us: place_rows(): pl.pallas_call(functools.partial(place_rows_kernel, starts), grid_spec=pl...]
    ppermute x0 -> x108, waiting for transfers between devices: none -> 228 us  [the longest x69 161 us: swap(): lax.ppermute(array, 'dp', [(i, i ^ bit) for i in range(self.dp_count)])]
    ppermute x0 -> x108, starting transfers between devices: none -> 145 us  [the longest x39 96.6 us: swap_fsdp(): lax.ppermute(array, 'fsdp', [(i, i ^ bit) for i in range(self.fsdp_count)])]
    dynamic_slice x192 -> x10, local copies, waits for them, and re-layouts: 137 us -> 1.76 us  [the longest x9 1.03 us: block(): return lax.dynamic_slice_in_dim(grad, index * rows, rows, 0)]
    all_gather x2 -> x0, blocking collectives: 134 us -> none  [the longest x1 70 us: body(): lax.all_gather(norm_biases, ('dp', 'fsdp'), axis=1, tiled=True)]
  transfers between devices with their start and end apart: 14 -> 108, of which waited for: 8 -> 38; matrix products, arithmetic and copies ran while one was open for 16% -> 13% of each run, Pallas kernels for 0% -> 16%
where the time goes in v1:
time: 825 us; the launch traced here: 814 us
  Pallas kernels  257 us (31%)
  waiting for transfers between devices  228 us (28%)
  starting transfers between devices  145 us (18%)
  matrix products  69.3 us (8%)
  other arithmetic  61.8 us (7%)
  local copies, waits for them, and re-layouts  43.3 us (5%)
  between operations  9.13 us (1%)
    ppermute x69, waiting for transfers between devices, swap(): lax.ppermute(array, 'dp', [(i, i ^ bit) for i in range(self.dp_count)])  161 us
    ppermute x39, starting transfers between devices, swap_fsdp(): lax.ppermute(array, 'fsdp', [(i, i ^ bit) for i in range(self.fsdp_count)])  96.6 us
    ppermute x39, waiting for transfers between devices, swap_fsdp(): lax.ppermute(array, 'fsdp', [(i, i ^ bit) for i in range(self.fsdp_count)])  67.4 us
    pallas_call x11, Pallas kernels, place_rows(): pl.pallas_call(functools.partial(place_rows_kernel, starts), grid_spec=pl...  61.9 us
    ppermute x69, starting transfers between devices, swap(): lax.ppermute(array, 'dp', [(i, i ^ bit) for i in range(self.dp_count)])  48.9 us
    pallas_call x7, Pallas kernels, turn_blocks(): pl.pallas_call(turn_blocks_kernel, grid_spec=pltpu.PrefetchScalarGridSpec...  44.6 us
    pallas_call x2, Pallas kernels, attention_backward(): pl.pallas_call(functools.partial(attention_backward_kernel, causal), grid...  44.1 us
    dot_general x12, matrix products, product(): return jnp.dot(left, right, preferred_element_type=jnp.float32)  43.9 us
  transfers between devices with their start and end apart: 108, of which 38 were waited for; matrix products, arithmetic and copies ran while one was open for 13% of the time, Pallas kernels for 16%

profile of v1, /device:TPU:0, one launch (start us, length us, event | category | flops | bytes accessed | tf_op | source)
XLA Modules:
  0.0 814.2 jit_solution(16372833021379268252)
XLA Ops:
  10.4 3.5 collective-permute-start.35
  17.8 4.6 collective-permute-start.36
  22.3 4.8 collective-permute-done.18.refs_2_
  27.7 17.9 %collective-permute-start.45 = (bf16[128,1024]{1,0:T(8,128)(2,1)S(1)}, bf16[128,1024]{1,0:T(8,128)(2,1)}, u32[]{:S(2)}, u32[]{:S(2)}) collective-permute-start(bf16[128,1024]{1,0:T(8,128)(2,1)S(1)} %convert_element_type.462.refs_0_), channel_id=1, source_target_pairs={{0,2},{1,3},{2,0},{3,1},{4,6},{5,7},{6,4},{7,5},{8,10},{9,11},{10,... | collective-permute-start | bytes 786440 | tf_op jit(solution)/shard_map/ppermute | solution.py:437
  50.2 5.1 collective-permute-done.35.refs_2_
  59.3 24.5 %collective-permute-done.45.refs_2_ = bf16[128,1024]{1,0:T(8,128)(2,1)} collective-permute-done((bf16[128,1024]{1,0:T(8,128)(2,1)S(1)}, bf16[128,1024]{1,0:T(8,128)(2,1)}, u32[]{:S(2)}, u32[]{:S(2)}) %collective-permute-start.45) | collective-permute-done | bytes 262176 | tf_op jit(solution)/shard_map/ppermute | solution.py:437
  92.6 5.8 collective-permute-done.20.refs_1_
  98.5 3.4 place_rows.11
  106.5 4.6 collective-permute-done.27.refs_1_
  113.8 8.5 %collective-permute-done.10.refs_1_ = bf16[128,2048]{1,0:T(8,128)(2,1)} collective-permute-done((bf16[128,2048]{1,0:T(8,128)(2,1)S(1)}, bf16[128,2048]{1,0:T(8,128)(2,1)}, u32[]{:S(2)}, u32[]{:S(2)}) %collective-permute-start.10) | collective-permute-done | bytes 524320 | tf_op jit(solution)/shard_map/ppermute | solution.py:434
  124.3 6.5 collective-permute-done.3.refs_1_
  134.2 8.8 %collective-permute-done.22.refs_3_ = bf16[128,2048]{1,0:T(8,128)(2,1)S(1)} collective-permute-done((bf16[128,2048]{1,0:T(8,128)(2,1)S(1)}, bf16[128,2048]{1,0:T(8,128)(2,1)S(1)}, u32[]{:S(2)}, u32[]{:S(2)}) %collective-permute-start.22) | collective-permute-done | bytes 524320 | tf_op jit(solution)/shard_map/ppermute | solution.py:434
  148.6 9.1 %collective-permute-done.12.refs_3_ = bf16[128,2048]{1,0:T(8,128)(2,1)} collective-permute-done((bf16[128,2048]{1,0:T(8,128)(2,1)}, bf16[128,2048]{1,0:T(8,128)(2,1)}, u32[]{:S(2)}, u32[]{:S(2)}) %collective-permute-start.12) | collective-permute-done | bytes 524320 | tf_op jit(solution)/shard_map/ppermute | solution.py:434
  158.8 3.4 place_rows.17.refs_0_
  172.4 5.7 turn_blocks.12
  178.1 3.4 place_rows.19.refs_0_
  181.5 6.4 place_rows.15
  188.0 6.6 place_rows.16
  194.6 4.4 fusion.19.k_ref.v_ref
  199.0 6.6 place_rows.13
  208.8 6.7 place_rows.12
  219.3 5.2 fusion.42.v_ref
  224.5 4.9 convolution_convert_fusion.2.q_ref.k_ref
  229.4 21.1 %attention_forward.2 = (bf16[768,1024]{1,0:T(8,128)(2,1)}, f32[8,2,768]{2,1,0:T(2,128)}) custom-call(s32[1]{0:T(128)} %copy.58.limit_ref, bf16[768,2048]{1,0:T(8,128)(2,1)} %convolution_convert_fusion.2.q_ref.k_ref, bf16[768,2048]{1,0:T(8,128)(2,1)} %convolution_convert_fusion.2.q_ref.k_ref, bf16[768,1024]{1,0:T(8,128)(2,1)} %fusion.42.v_ref), custom_call_target="tpu_custom_call" | custom-call | flops 2415919104 | bytes 6291456 | tf_op jit(solution)/shard_map/attention_forward/pallas_call | solution.py:123
  250.5 3.9 fusion.66
  261.8 17.4 %attention_forward.3 = (bf16[768,1024]{1,0:T(8,128)(2,1)}, f32[8,2,768]{2,1,0:T(2,128)}) custom-call(s32[1]{0:T(128)S(6)} %copy.59.limit_ref, bf16[768,1024]{1,0:T(8,128)(2,1)} %fusion.48.q_ref, bf16[256,2048]{1,0:T(8,128)(2,1)} %fusion.19.k_ref.v_ref, bf16[256,2048]{1,0:T(8,128)(2,1)} %fusion.19.k_ref.v_ref), custom_call_target="tpu_custom_call" | custom-call | flops 805306368 | bytes 4194304 | tf_op jit(solution)/shard_map/attention_forward/pallas_call | solution.py:123
  281.1 4.9 fusion.67
  286.0 6.6 turn_blocks.9
  292.7 6.5 turn_blocks.8
  299.1 6.5 turn_blocks.10
  305.6 6.4 turn_blocks.11
  312.0 6.4 turn_blocks.13
  320.7 6.5 turn_blocks.7.refs_1_
  327.1 9.0 %place_rows.18.input_ref.refs_4_ = bf16[1024,4096]{1,0:T(8,128)(2,1)} custom-call(s32[8]{0:T(128)} %broadcast_xor_fusion.2.table_ref, bf16[128,4096]{1,0:T(8,128)(2,1)} %place_rows.17.refs_0_, bf16[128,4096]{1,0:T(8,128)(2,1)} %collective-permute-done.37.refs_1_, bf16[128,4096]{1,0:T(8,128)(2,1)} %collective-permute-done.38.refs_2_, ...), custom_call_target="tpu_custom_call" | custom-call | bytes 16777216 | tf_op jit(solution)/shard_map/place_rows/pallas_call | solution.py:376
  336.2 8.8 %place_rows.20.output_ref.refs_5_ = bf16[4096,1024]{1,0:T(8,128)(2,1)} custom-call(s32[8]{0:T(128)} %broadcast_xor_fusion.3.table_ref, bf16[512,1024]{1,0:T(8,128)(2,1)} %place_rows.19.refs_0_, bf16[512,1024]{1,0:T(8,128)(2,1)} %collective-permute-done.47.refs_1_, bf16[512,1024]{1,0:T(8,128)(2,1)} %collective-permute-done.48.refs_2_, ...), custom_call_target="tpu_custom_call" | custom-call | bytes 16777216 | tf_op jit(solution)/shard_map/place_rows/pallas_call | solution.py:376
  344.9 33.2 %feed_forward.1 = (bf16[768,4096]{1,0:T(8,128)(2,1)}, bf16[768,4096]{1,0:T(8,128)(2,1)}, f32[768,1024]{1,0:T(8,128)}) custom-call(bf16[768,1024]{1,0:T(8,128)(2,1)} %add_convert_fusion.7.normed_ref.in_ref, bf16[1024,4096]{1,0:T(8,128)(2,1)} %place_rows.18.input_ref.refs_4_, bf16[4096,1024]{1,0:T(8,128)(2,1)} %place_rows.20.output_ref.refs_5_, ...), custom_call_target="tpu_custom_call" | custom-call | flops 12884901888 | bytes 29360128 | tf_op jit(solution)/shard_map/feed_forward/pallas_call | solution.py:270
  387.8 34.7 %feed_backward.1 = (bf16[1024,4096]{1,0:T(8,128)(2,1)}, bf16[4096,1024]{1,0:T(8,128)(2,1)}, f32[768,1024]{1,0:T(8,128)}) custom-call(s32[8]{0:T(128)} %copy-done.80, bf16[768,1024]{1,0:T(8,128)(2,1)} %get-tuple-element.100.refs_0_, bf16[1024,768]{1,0:T(8,128)(2,1)} %turn_blocks.7.refs_1_, bf16[768,4096]{1,0:T(8,128)(2,1)} %get-tuple-element.30.refs_2_, ...), custom_call_target="tpu_custom_call" | custom-call | flops 25769803776 | bytes 46137344 | tf_op jit(solution)/shard_map/feed_backward/pallas_call | solution.py:323
  431.5 17.9 %attention_backward.2 = (bf16[768,1024]{1,0:T(8,128)(2,1)}, bf16[256,1024]{1,0:T(8,128)(2,1)}, bf16[256,1024]{1,0:T(8,128)(2,1)}) custom-call(s32[1]{0:T(128)S(6)} %copy.59.limit_ref, bf16[768,1024]{1,0:T(8,128)(2,1)} %fusion.48.q_ref, bf16[256,2048]{1,0:T(8,128)(2,1)} %fusion.19.k_ref.v_ref, bf16[256,2048]{1,0:T(8,128)(2,1)} %fusion.19.k_ref.v_ref, ...), custom_call_target="tpu_custom_call" | custom-call | flops 2013265920 | bytes 8388608 | tf_op jit(solution)/shard_map/attention_backward/pallas_call | solution.py:205
  449.4 4.6 multiply_reduce_fusion.2
  455.2 5.7 fusion.45.grad_ref
  460.9 26.1 %attention_backward.3 = (bf16[768,1024]{1,0:T(8,128)(2,1)}, bf16[768,1024]{1,0:T(8,128)(2,1)}, bf16[768,1024]{1,0:T(8,128)(2,1)}) custom-call(s32[1]{0:T(128)} %copy.58.limit_ref, bf16[768,2048]{1,0:T(8,128)(2,1)} %convolution_convert_fusion.2.q_ref.k_ref, bf16[768,2048]{1,0:T(8,128)(2,1)} %convolution_convert_fusion.2.q_ref.k_ref, ...), custom_call_target="tpu_custom_call" | custom-call | flops 6039797760 | bytes 12582912 | tf_op jit(solution)/shard_map/attention_backward/pallas_call | solution.py:205
  487.1 4.0 fusion.33
  493.8 5.8 fusion.15
  502.9 5.1 convolution_convert_fusion.1
  515.8 4.0 place_rows.21
  521.3 4.9 fusion.14
  538.6 14.4 %collective-permute-start.106 = (bf16[32,128]{1,0:T(8,128)(2,1)S(1)}, bf16[32,128]{1,0:T(8,128)(2,1)S(1)}, u32[]{:S(2)}, u32[]{:S(2)}) collective-permute-start(bf16[32,128]{1,0:T(8,128)(2,1)S(1)} %get-tuple-element.139), channel_id=1, source_target_pairs={{0,2},{1,3},{2,0},{3,1},{4,6},{5,7},{6,4},{7,5},{8,10},{9,11},{10,... | collective-permute-start | bytes 24584 | tf_op jit(solution)/shard_map/ppermute | solution.py:437
  582.3 8.2 %collective-permute-done.61 = bf16[256,1024]{1,0:T(8,128)(2,1)S(1)} collective-permute-done((bf16[256,1024]{1,0:T(8,128)(2,1)S(1)}, bf16[256,1024]{1,0:T(8,128)(2,1)S(1)}, u32[]{:S(2)}, u32[]{:S(2)}) %collective-permute-start.61) | collective-permute-done | bytes 524320 | tf_op jit(solution)/shard_map/ppermute | solution.py:434
  595.6 9.8 %collective-permute-done.73 = bf16[256,1024]{1,0:T(8,128)(2,1)S(1)} collective-permute-done((bf16[256,1024]{1,0:T(8,128)(2,1)S(1)}, bf16[256,1024]{1,0:T(8,128)(2,1)S(1)}, u32[]{:S(2)}, u32[]{:S(2)}) %collective-permute-start.73) | collective-permute-done | bytes 524320 | tf_op jit(solution)/shard_map/ppermute | solution.py:434
  606.9 9.7 %collective-permute-done.85 = bf16[256,1024]{1,0:T(8,128)(2,1)S(1)} collective-permute-done((bf16[256,1024]{1,0:T(8,128)(2,1)S(1)}, bf16[256,1024]{1,0:T(8,128)(2,1)S(1)}, u32[]{:S(2)}, u32[]{:S(2)}) %collective-permute-start.85) | collective-permute-done | bytes 524320 | tf_op jit(solution)/shard_map/ppermute | solution.py:434
  617.9 3.7 collective-permute-done.62
  624.8 6.1 collective-permute-done.74
  667.4 3.5 collective-permute-done.55
  672.3 9.9 %collective-permute-done.79 = bf16[256,2048]{1,0:T(8,128)(2,1)S(1)} collective-permute-done((bf16[256,2048]{1,0:T(8,128)(2,1)S(1)}, bf16[256,2048]{1,0:T(8,128)(2,1)S(1)}, u32[]{:S(2)}, u32[]{:S(2)}) %collective-permute-start.79) | collective-permute-done | bytes 1048608 | tf_op jit(solution)/shard_map/ppermute | solution.py:434
  684.2 3.6 collective-permute-done.56
  695.3 3.7 add_convert_fusion.1
  708.1 4.3 add_convert_fusion
  713.6 27.1 %collective-permute-done.91 = bf16[256,4096]{1,0:T(8,128)(2,1)S(1)} collective-permute-done((bf16[256,4096]{1,0:T(8,128)(2,1)}, bf16[256,4096]{1,0:T(8,128)(2,1)S(1)}, u32[]{:S(2)}, u32[]{:S(2)}) %collective-permute-start.91) | collective-permute-done | bytes 2097184 | tf_op jit(solution)/shard_map/ppermute | solution.py:434
  744.0 17.3 %collective-permute-done.97 = bf16[1024,1024]{1,0:T(8,128)(2,1)S(1)} collective-permute-done((bf16[1024,1024]{1,0:T(8,128)(2,1)S(1)}, bf16[1024,1024]{1,0:T(8,128)(2,1)S(1)}, u32[]{:S(2)}, u32[]{:S(2)}) %collective-permute-start.97) | collective-permute-done | bytes 2097184 | tf_op jit(solution)/shard_map/ppermute | solution.py:434
  763.6 10.7 %collective-permute-done.92 = bf16[128,4096]{1,0:T(8,128)(2,1)S(1)} collective-permute-done((bf16[128,4096]{1,0:T(8,128)(2,1)S(1)}, bf16[128,4096]{1,0:T(8,128)(2,1)S(1)}, u32[]{:S(2)}, u32[]{:S(2)}) %collective-permute-start.92) | collective-permute-done | bytes 1048608 | tf_op jit(solution)/shard_map/ppermute | solution.py:434
  781.4 4.3 collective-permute-done.95
  785.7 9.7 %collective-permute-start.99 = (bf16[128,1024]{1,0:T(8,128)(2,1)S(1)}, bf16[128,1024]{1,0:T(8,128)(2,1)S(1)}, u32[]{:S(2)}, u32[]{:S(2)}) collective-permute-start(bf16[128,1024]{1,0:T(8,128)(2,1)S(1)} %get-tuple-element.103), channel_id=1, source_target_pairs={{0,1},{1,0},{2,3},{3,2},{4,5},{5,4},{6,7},{7,6},{8,9},{9,8},{10,11... | collective-permute-start | bytes 786440 | tf_op jit(solution)/shard_map/ppermute | solution.py:437
  795.4 10.7 %collective-permute-done.94 = bf16[32,4096]{1,0:T(8,128)(2,1)S(1)} collective-permute-done((bf16[32,4096]{1,0:T(8,128)(2,1)S(1)}, bf16[32,4096]{1,0:T(8,128)(2,1)S(1)}, u32[]{:S(2)}, u32[]{:S(2)}) %collective-permute-start.94) | collective-permute-done | bytes 262176 | tf_op jit(solution)/shard_map/ppermute | solution.py:437
  807.0 5.8 collective-permute-done.100
  (534 shorter events, 231.9 us)
Async XLA Ops:
  5.8 21.4 %collective-permute-start.18 = (bf16[32,4096]{1,0:T(8,128)(2,1)S(1)}, bf16[32,4096]{1,0:T(8,128)(2,1)S(1)}, u32[]{:S(2)}, u32[]{:S(2)}) collective-permute-start(bf16[32,4096]{1,0:T(8,128)(2,1)S(1)} %pad_maximum_fusion.3.refs_0_), channel_id=1, source_target_pairs={{0,2},{1,3},{2,0},{3,1},{4,6},{5,7},{6,4},{7,5},{8,10},{9,11},{10,... | collective-permute-start | bytes 786440 | tf_op jit(solution)/shard_map/ppermute | solution.py:437
  8.4 19.4 %collective-permute-start.19 = (bf16[32,4096]{1,0:T(8,128)(2,1)S(1)}, bf16[32,4096]{1,0:T(8,128)(2,1)S(1)}, u32[]{:S(2)}, u32[]{:S(2)}) collective-permute-start(bf16[32,4096]{1,0:T(8,128)(2,1)S(1)} %pad_maximum_fusion.3.refs_0_), channel_id=1, source_target_pairs={{0,3},{1,2},{2,1},{3,0},{4,7},{5,6},{6,5},{7,4},{8,11},{9,10},{10,... | collective-permute-start | bytes 786440 | tf_op jit(solution)/shard_map/ppermute | solution.py:437
  9.4 40.7 %collective-permute-start.34 = (bf16[32,4096]{1,0:T(8,128)(2,1)S(1)}, bf16[32,4096]{1,0:T(8,128)(2,1)S(1)}, u32[]{:S(2)}, u32[]{:S(2)}) collective-permute-start(bf16[32,4096]{1,0:T(8,128)(2,1)S(1)} %convert_element_type.461.refs_0_), channel_id=1, source_target_pairs={{0,1},{1,0},{2,3},{3,2},{4,5},{5,4},{6,7},{7,6},{8,9},{9,8},{10,11... | collective-permute-start | bytes 786440 | tf_op jit(solution)/shard_map/ppermute | solution.py:437
  10.4 44.9 %collective-permute-start.35 = (bf16[32,4096]{1,0:T(8,128)(2,1)S(1)}, bf16[32,4096]{1,0:T(8,128)(2,1)S(1)}, u32[]{:S(2)}, u32[]{:S(2)}) collective-permute-start(bf16[32,4096]{1,0:T(8,128)(2,1)S(1)} %convert_element_type.461.refs_0_), channel_id=1, source_target_pairs={{0,2},{1,3},{2,0},{3,1},{4,6},{5,7},{6,4},{7,5},{8,10},{9,11},{10,... | collective-permute-start | bytes 786440 | tf_op jit(solution)/shard_map/ppermute | solution.py:437
  17.8 37.6 %collective-permute-start.36 = (bf16[32,4096]{1,0:T(8,128)(2,1)S(1)}, bf16[32,4096]{1,0:T(8,128)(2,1)S(1)}, u32[]{:S(2)}, u32[]{:S(2)}) collective-permute-start(bf16[32,4096]{1,0:T(8,128)(2,1)S(1)} %convert_element_type.461.refs_0_), channel_id=1, source_target_pairs={{0,3},{1,2},{2,1},{3,0},{4,7},{5,6},{6,5},{7,4},{8,11},{9,10},{10,... | collective-permute-start | bytes 786440 | tf_op jit(solution)/shard_map/ppermute | solution.py:437
  27.2 30.7 %collective-permute-start.44 = (bf16[128,1024]{1,0:T(8,128)(2,1)S(1)}, bf16[128,1024]{1,0:T(8,128)(2,1)S(1)}, u32[]{:S(2)}, u32[]{:S(2)}) collective-permute-start(bf16[128,1024]{1,0:T(8,128)(2,1)S(1)} %convert_element_type.462.refs_0_), channel_id=1, source_target_pairs={{0,1},{1,0},{2,3},{3,2},{4,5},{5,4},{6,7},{7,6},{8,9},{9,8},{10,11... | collective-permute-start | bytes 786440 | tf_op jit(solution)/shard_map/ppermute | solution.py:437
  27.7 56.1 %collective-permute-start.45 = (bf16[128,1024]{1,0:T(8,128)(2,1)S(1)}, bf16[128,1024]{1,0:T(8,128)(2,1)}, u32[]{:S(2)}, u32[]{:S(2)}) collective-permute-start(bf16[128,1024]{1,0:T(8,128)(2,1)S(1)} %convert_element_type.462.refs_0_), channel_id=1, source_target_pairs={{0,2},{1,3},{2,0},{3,1},{4,6},{5,7},{6,4},{7,5},{8,10},{9,11},{10,... | collective-permute-start | bytes 786440 | tf_op jit(solution)/shard_map/ppermute | solution.py:437
  50.2 37.9 %collective-permute-start = (bf16[32,4224]{1,0:T(8,128)(2,1)S(1)}, bf16[32,4224]{1,0:T(8,128)(2,1)S(1)}, u32[]{:S(2)}, u32[]{:S(2)}) collective-permute-start(bf16[32,4224]{1,0:T(8,128)(2,1)S(1)} %fusion.60.refs_0_), channel_id=1, source_target_pairs={{0,1},{1,0},{2,3},{3,2},{4,5},{5,4},{6,7},{7,6},{8,9},{9,8},{10,11... | collective-permute-start | bytes 811016 | tf_op jit(solution)/shard_map/ppermute | solution.py:437
  55.3 34.2 %collective-permute-start.1 = (bf16[32,4224]{1,0:T(8,128)(2,1)S(1)}, bf16[32,4224]{1,0:T(8,128)(2,1)S(1)}, u32[]{:S(2)}, u32[]{:S(2)}) collective-permute-start(bf16[32,4224]{1,0:T(8,128)(2,1)S(1)} %fusion.60.refs_0_), channel_id=1, source_target_pairs={{0,2},{1,3},{2,0},{3,1},{4,6},{5,7},{6,4},{7,5},{8,10},{9,11},{10,... | collective-permute-start | bytes 811016 | tf_op jit(solution)/shard_map/ppermute | solution.py:437
  55.3 35.7 %collective-permute-start.2 = (bf16[32,4224]{1,0:T(8,128)(2,1)S(1)}, bf16[32,4224]{1,0:T(8,128)(2,1)S(1)}, u32[]{:S(2)}, u32[]{:S(2)}) collective-permute-start(bf16[32,4224]{1,0:T(8,128)(2,1)S(1)} %fusion.60.refs_0_), channel_id=1, source_target_pairs={{0,3},{1,2},{2,1},{3,0},{4,7},{5,6},{6,5},{7,4},{8,11},{9,10},{10,... | collective-permute-start | bytes 811016 | tf_op jit(solution)/shard_map/ppermute | solution.py:437
  57.9 28.6 %collective-permute-start.46 = (bf16[128,1024]{1,0:T(8,128)(2,1)S(1)}, bf16[128,1024]{1,0:T(8,128)(2,1)S(1)}, u32[]{:S(2)}, u32[]{:S(2)}) collective-permute-start(bf16[128,1024]{1,0:T(8,128)(2,1)S(1)} %convert_element_type.462.refs_0_), channel_id=1, source_target_pairs={{0,3},{1,2},{2,1},{3,0},{4,7},{5,6},{6,5},{7,4},{8,11},{9,10},{10,... | collective-permute-start | bytes 786440 | tf_op jit(solution)/shard_map/ppermute | solution.py:437
  86.5 16.6 %collective-permute-start.21 = (bf16[128,2048]{1,0:T(8,128)(2,1)S(1)}, bf16[128,2048]{1,0:T(8,128)(2,1)}, u32[]{:S(2)}, u32[]{:S(2)}) collective-permute-start(bf16[128,2048]{1,0:T(8,128)(2,1)S(1)} %pad_maximum_fusion.refs_0_), channel_id=1, source_target_pairs={{0,8},{4,12},{8,0},{12,4},{16,24},{20,28},{24,16},{28,20},{1,9},{5... | collective-permute-start | bytes 1572872 | tf_op jit(solution)/shard_map/ppermute | solution.py:434
  88.1 16.6 %collective-permute-start.23 = (bf16[128,2048]{1,0:T(8,128)(2,1)S(1)}, bf16[128,2048]{1,0:T(8,128)(2,1)}, u32[]{:S(2)}, u32[]{:S(2)}) collective-permute-start(bf16[128,2048]{1,0:T(8,128)(2,1)S(1)} %pad_maximum_fusion.refs_0_), channel_id=1, source_target_pairs={{0,4},{4,0},{8,12},{12,8},{16,20},{20,16},{24,28},{28,24},{1,5},{5... | collective-permute-start | bytes 1572872 | tf_op jit(solution)/shard_map/ppermute | solution.py:434
  89.5 21.5 %collective-permute-start.27 = (bf16[128,2048]{1,0:T(8,128)(2,1)S(1)}, bf16[128,2048]{1,0:T(8,128)(2,1)}, u32[]{:S(2)}, u32[]{:S(2)}) collective-permute-start(bf16[128,2048]{1,0:T(8,128)(2,1)S(1)} %slice.354.refs_0_), channel_id=1, source_target_pairs={{0,8},{4,12},{8,0},{12,4},{16,24},{20,28},{24,16},{28,20},{1,9},{5... | collective-permute-start | bytes 1572872 | tf_op jit(solution)/shard_map/ppermute | solution.py:434
  91.0 21.1 %collective-permute-start.28 = (bf16[128,2048]{1,0:T(8,128)(2,1)S(1)}, bf16[128,2048]{1,0:T(8,128)(2,1)}, u32[]{:S(2)}, u32[]{:S(2)}) collective-permute-start(bf16[128,2048]{1,0:T(8,128)(2,1)S(1)} %slice.354.refs_0_), channel_id=1, source_target_pairs={{0,16},{4,20},{8,24},{12,28},{16,0},{20,4},{24,8},{28,12},{1,17},{... | collective-permute-start | bytes 1572872 | tf_op jit(solution)/shard_map/ppermute | solution.py:434
  103.1 19.2 %collective-permute-start.10 = (bf16[128,2048]{1,0:T(8,128)(2,1)S(1)}, bf16[128,2048]{1,0:T(8,128)(2,1)}, u32[]{:S(2)}, u32[]{:S(2)}) collective-permute-start(bf16[128,2048]{1,0:T(8,128)(2,1)S(1)} %slice.346.refs_0_), channel_id=1, source_target_pairs={{0,8},{4,12},{8,0},{12,4},{16,24},{20,28},{24,16},{28,20},{1,9},{5... | collective-permute-start | bytes 1572872 | tf_op jit(solution)/shard_map/ppermute | solution.py:434
  104.6 19.1 %collective-permute-start.11 = (bf16[128,2048]{1,0:T(8,128)(2,1)S(1)}, bf16[128,2048]{1,0:T(8,128)(2,1)S(1)}, u32[]{:S(2)}, u32[]{:S(2)}) collective-permute-start(bf16[128,2048]{1,0:T(8,128)(2,1)S(1)} %slice.346.refs_0_), channel_id=1, source_target_pairs={{0,16},{4,20},{8,24},{12,28},{16,0},{20,4},{24,8},{28,12},{1,17},{... | collective-permute-start | bytes 1572872 | tf_op jit(solution)/shard_map/ppermute | solution.py:434
  112.2 18.6 %collective-permute-start.3 = (bf16[128,2176]{1,0:T(8,128)(2,1)S(1)}, bf16[128,2176]{1,0:T(8,128)(2,1)}, u32[]{:S(2)}, u32[]{:S(2)}) collective-permute-start(bf16[128,2176]{1,0:T(8,128)(2,1)S(1)} %slice.342.refs_0_), channel_id=1, source_target_pairs={{0,16},{4,20},{8,24},{12,28},{16,0},{20,4},{24,8},{28,12},{1,17},{... | collective-permute-start | bytes 1671176 | tf_op jit(solution)/shard_map/ppermute | solution.py:434
  112.3 22.0 %collective-permute-start.4 = (bf16[128,2176]{1,0:T(8,128)(2,1)S(1)}, bf16[128,2176]{1,0:T(8,128)(2,1)}, u32[]{:S(2)}, u32[]{:S(2)}) collective-permute-start(bf16[128,2176]{1,0:T(8,128)(2,1)S(1)} %slice.342.refs_0_), channel_id=1, source_target_pairs={{0,8},{4,12},{8,0},{12,4},{16,24},{20,28},{24,16},{28,20},{1,9},{5... | collective-permute-start | bytes 1671176 | tf_op jit(solution)/shard_map/ppermute | solution.py:434
  122.3 20.7 %collective-permute-start.22 = (bf16[128,2048]{1,0:T(8,128)(2,1)S(1)}, bf16[128,2048]{1,0:T(8,128)(2,1)S(1)}, u32[]{:S(2)}, u32[]{:S(2)}) collective-permute-start(bf16[128,2048]{1,0:T(8,128)(2,1)S(1)} %collective-permute-done.20.refs_1_), channel_id=1, source_target_pairs={{0,8},{4,12},{8,0},{12,4},{16,24},{20,28},{24,16},{28,20},{1,9},{5... | collective-permute-start | bytes 1572872 | tf_op jit(solution)/shard_map/ppermute | solution.py:434
  123.8 19.3 %collective-permute-start.24 = (bf16[128,2048]{1,0:T(8,128)(2,1)S(1)}, bf16[128,2048]{1,0:T(8,128)(2,1)S(1)}, u32[]{:S(2)}, u32[]{:S(2)}) collective-permute-start(bf16[128,2048]{1,0:T(8,128)(2,1)S(1)} %collective-permute-done.20.refs_1_), channel_id=1, source_target_pairs={{0,4},{4,0},{8,12},{12,8},{16,20},{20,16},{24,28},{28,24},{1,5},{5... | collective-permute-start | bytes 1572872 | tf_op jit(solution)/shard_map/ppermute | solution.py:434
  123.8 20.8 %collective-permute-start.25 = (bf16[128,2048]{1,0:T(8,128)(2,1)}, bf16[128,2048]{1,0:T(8,128)(2,1)S(1)}, u32[]{:S(2)}, u32[]{:S(2)}) collective-permute-start(bf16[128,2048]{1,0:T(8,128)(2,1)} %collective-permute-done.21.refs_2_), channel_id=1, source_target_pairs={{0,4},{4,0},{8,12},{12,8},{16,20},{20,16},{24,28},{28,24},{1,5},{5... | collective-permute-start | bytes 1572872 | tf_op jit(solution)/shard_map/ppermute | solution.py:434
  145.4 16.8 %collective-permute-start.15 = (bf16[128,2048]{1,0:T(8,128)(2,1)}, bf16[128,2048]{1,0:T(8,128)(2,1)S(1)}, u32[]{:S(2)}, u32[]{:S(2)}) collective-permute-start(bf16[128,2048]{1,0:T(8,128)(2,1)} %copy-done.55), channel_id=1, source_target_pairs={{0,4},{4,0},{8,12},{12,8},{16,20},{20,16},{24,28},{28,24},{1,5},{5... | collective-permute-start | bytes 1572872 | tf_op jit(solution)/shard_map/ppermute | solution.py:434
  147.1 17.3 %collective-permute-start.5 = (bf16[128,2176]{1,0:T(8,128)(2,1)}, bf16[128,2176]{1,0:T(8,128)(2,1)}, u32[]{:S(2)}, u32[]{:S(2)}) collective-permute-start(bf16[128,2176]{1,0:T(8,128)(2,1)} %collective-permute-done.3.refs_1_), channel_id=1, source_target_pairs={{0,8},{4,12},{8,0},{12,4},{16,24},{20,28},{24,16},{28,20},{1,9},{5... | collective-permute-start | bytes 1671176 | tf_op jit(solution)/shard_map/ppermute | solution.py:434
  162.2 44.0 %collective-permute-start.37 = (bf16[128,4096]{1,0:T(8,128)(2,1)}, bf16[128,4096]{1,0:T(8,128)(2,1)}, u32[]{:S(2)}, u32[]{:S(2)}) collective-permute-start(bf16[128,4096]{1,0:T(8,128)(2,1)} %place_rows.17.refs_0_), channel_id=1, source_target_pairs={{0,8},{4,12},{8,0},{12,4},{16,24},{20,28},{24,16},{28,20},{1,9},{5... | collective-permute-start | bytes 3145736 | tf_op jit(solution)/shard_map/ppermute | solution.py:434
  164.3 41.3 %collective-permute-start.6 = (bf16[128,2176]{1,0:T(8,128)(2,1)S(1)}, bf16[128,2176]{1,0:T(8,128)(2,1)}, u32[]{:S(2)}, u32[]{:S(2)}) collective-permute-start(bf16[128,2176]{1,0:T(8,128)(2,1)S(1)} %slice.342.refs_0_), channel_id=1, source_target_pairs={{0,4},{4,0},{8,12},{12,8},{16,20},{20,16},{24,28},{28,24},{1,5},{5... | collective-permute-start | bytes 1671176 | tf_op jit(solution)/shard_map/ppermute | solution.py:434
  164.4 41.8 %collective-permute-start.7 = (bf16[128,2176]{1,0:T(8,128)(2,1)}, bf16[128,2176]{1,0:T(8,128)(2,1)}, u32[]{:S(2)}, u32[]{:S(2)}) collective-permute-start(bf16[128,2176]{1,0:T(8,128)(2,1)} %collective-permute-done.3.refs_1_), channel_id=1, source_target_pairs={{0,4},{4,0},{8,12},{12,8},{16,20},{20,16},{24,28},{28,24},{1,5},{5... | collective-permute-start | bytes 1671176 | tf_op jit(solution)/shard_map/ppermute | solution.py:434
  164.9 42.9 %collective-permute-start.8 = (bf16[128,2176]{1,0:T(8,128)(2,1)}, bf16[128,2176]{1,0:T(8,128)(2,1)}, u32[]{:S(2)}, u32[]{:S(2)}) collective-permute-start(bf16[128,2176]{1,0:T(8,128)(2,1)} %collective-permute-done.4.refs_2_), channel_id=1, source_target_pairs={{0,4},{4,0},{8,12},{12,8},{16,20},{20,16},{24,28},{28,24},{1,5},{5... | collective-permute-start | bytes 1671176 | tf_op jit(solution)/shard_map/ppermute | solution.py:434
  165.0 43.3 %collective-permute-start.9 = (bf16[128,2176]{1,0:T(8,128)(2,1)}, bf16[128,2176]{1,0:T(8,128)(2,1)}, u32[]{:S(2)}, u32[]{:S(2)}) collective-permute-start(bf16[128,2176]{1,0:T(8,128)(2,1)} %collective-permute-done.5.refs_3_), channel_id=1, source_target_pairs={{0,4},{4,0},{8,12},{12,8},{16,20},{20,16},{24,28},{28,24},{1,5},{5... | collective-permute-start | bytes 1671176 | tf_op jit(solution)/shard_map/ppermute | solution.py:434
  205.7 49.3 %collective-permute-start.38 = (bf16[128,4096]{1,0:T(8,128)(2,1)S(1)}, bf16[128,4096]{1,0:T(8,128)(2,1)}, u32[]{:S(2)}, u32[]{:S(2)}) collective-permute-start(bf16[128,4096]{1,0:T(8,128)(2,1)S(1)} %copy-done.20), channel_id=1, source_target_pairs={{0,16},{4,20},{8,24},{12,28},{16,0},{20,4},{24,8},{28,12},{1,17},{... | collective-permute-start | bytes 3145736 | tf_op jit(solution)/shard_map/ppermute | solution.py:434
  206.2 48.8 %collective-permute-start.40 = (bf16[128,4096]{1,0:T(8,128)(2,1)S(1)}, bf16[128,4096]{1,0:T(8,128)(2,1)}, u32[]{:S(2)}, u32[]{:S(2)}) collective-permute-start(bf16[128,4096]{1,0:T(8,128)(2,1)S(1)} %copy-done.20), channel_id=1, source_target_pairs={{0,4},{4,0},{8,12},{12,8},{16,20},{20,16},{24,28},{28,24},{1,5},{5... | collective-permute-start | bytes 3145736 | tf_op jit(solution)/shard_map/ppermute | solution.py:434
  206.3 49.3 %collective-permute-start.47 = (bf16[512,1024]{1,0:T(8,128)(2,1)}, bf16[512,1024]{1,0:T(8,128)(2,1)}, u32[]{:S(2)}, u32[]{:S(2)}) collective-permute-start(bf16[512,1024]{1,0:T(8,128)(2,1)} %place_rows.19.refs_0_), channel_id=1, source_target_pairs={{0,16},{4,20},{8,24},{12,28},{16,0},{20,4},{24,8},{28,12},{1,17},{... | collective-permute-start | bytes 3145736 | tf_op jit(solution)/shard_map/ppermute | solution.py:434
  207.9 71.4 %collective-permute-start.48 = (bf16[512,1024]{1,0:T(8,128)(2,1)}, bf16[512,1024]{1,0:T(8,128)(2,1)}, u32[]{:S(2)}, u32[]{:S(2)}) collective-permute-start(bf16[512,1024]{1,0:T(8,128)(2,1)} %place_rows.19.refs_0_), channel_id=1, source_target_pairs={{0,8},{4,12},{8,0},{12,4},{16,24},{20,28},{24,16},{28,20},{1,9},{5... | collective-permute-start | bytes 3145736 | tf_op jit(solution)/shard_map/ppermute | solution.py:434
  208.3 71.0 %collective-permute-start.39 = (bf16[128,4096]{1,0:T(8,128)(2,1)}, bf16[128,4096]{1,0:T(8,128)(2,1)}, u32[]{:S(2)}, u32[]{:S(2)}) collective-permute-start(bf16[128,4096]{1,0:T(8,128)(2,1)} %collective-permute-done.37.refs_1_), channel_id=1, source_target_pairs={{0,16},{4,20},{8,24},{12,28},{16,0},{20,4},{24,8},{28,12},{1,17},{... | collective-permute-start | bytes 3145736 | tf_op jit(solution)/shard_map/ppermute | solution.py:434
  255.0 24.8 %collective-permute-start.41 = (bf16[128,4096]{1,0:T(8,128)(2,1)}, bf16[128,4096]{1,0:T(8,128)(2,1)S(1)}, u32[]{:S(2)}, u32[]{:S(2)}) collective-permute-start(bf16[128,4096]{1,0:T(8,128)(2,1)} %collective-permute-done.37.refs_1_), channel_id=1, source_target_pairs={{0,4},{4,0},{8,12},{12,8},{16,20},{20,16},{24,28},{28,24},{1,5},{5... | collective-permute-start | bytes 3145736 | tf_op jit(solution)/shard_map/ppermute | solution.py:434
  255.1 24.8 %collective-permute-start.42 = (bf16[128,4096]{1,0:T(8,128)(2,1)}, bf16[128,4096]{1,0:T(8,128)(2,1)S(1)}, u32[]{:S(2)}, u32[]{:S(2)}) collective-permute-start(bf16[128,4096]{1,0:T(8,128)(2,1)} %collective-permute-done.38.refs_2_), channel_id=1, source_target_pairs={{0,4},{4,0},{8,12},{12,8},{16,20},{20,16},{24,28},{28,24},{1,5},{5... | collective-permute-start | bytes 3145736 | tf_op jit(solution)/shard_map/ppermute | solution.py:434
  255.6 25.5 %collective-permute-start.49 = (bf16[512,1024]{1,0:T(8,128)(2,1)}, bf16[512,1024]{1,0:T(8,128)(2,1)}, u32[]{:S(2)}, u32[]{:S(2)}) collective-permute-start(bf16[512,1024]{1,0:T(8,128)(2,1)} %collective-permute-done.47.refs_1_), channel_id=1, source_target_pairs={{0,8},{4,12},{8,0},{12,4},{16,24},{20,28},{24,16},{28,20},{1,9},{5... | collective-permute-start | bytes 3145736 | tf_op jit(solution)/shard_map/ppermute | solution.py:434
  279.2 56.9 %collective-permute-start.50 = (bf16[512,1024]{1,0:T(8,128)(2,1)}, bf16[512,1024]{1,0:T(8,128)(2,1)}, u32[]{:S(2)}, u32[]{:S(2)}) collective-permute-start(bf16[512,1024]{1,0:T(8,128)(2,1)} %place_rows.19.refs_0_), channel_id=1, source_target_pairs={{0,4},{4,0},{8,12},{12,8},{16,20},{20,16},{24,28},{28,24},{1,5},{5... | collective-permute-start | bytes 3145736 | tf_op jit(solution)/shard_map/ppermute | solution.py:434
  279.3 56.9 %collective-permute-start.51 = (bf16[512,1024]{1,0:T(8,128)(2,1)}, bf16[512,1024]{1,0:T(8,128)(2,1)}, u32[]{:S(2)}, u32[]{:S(2)}) collective-permute-start(bf16[512,1024]{1,0:T(8,128)(2,1)} %collective-permute-done.47.refs_1_), channel_id=1, source_target_pairs={{0,4},{4,0},{8,12},{12,8},{16,20},{20,16},{24,28},{28,24},{1,5},{5... | collective-permute-start | bytes 3145736 | tf_op jit(solution)/shard_map/ppermute | solution.py:434
  279.8 56.4 %collective-permute-start.52 = (bf16[512,1024]{1,0:T(8,128)(2,1)}, bf16[512,1024]{1,0:T(8,128)(2,1)}, u32[]{:S(2)}, u32[]{:S(2)}) collective-permute-start(bf16[512,1024]{1,0:T(8,128)(2,1)} %collective-permute-done.48.refs_2_), channel_id=1, source_target_pairs={{0,4},{4,0},{8,12},{12,8},{16,20},{20,16},{24,28},{28,24},{1,5},{5... | collective-permute-start | bytes 3145736 | tf_op jit(solution)/shard_map/ppermute | solution.py:434
  279.9 47.3 %collective-permute-start.43 = (bf16[128,4096]{1,0:T(8,128)(2,1)}, bf16[128,4096]{1,0:T(8,128)(2,1)}, u32[]{:S(2)}, u32[]{:S(2)}) collective-permute-start(bf16[128,4096]{1,0:T(8,128)(2,1)} %collective-permute-done.39.refs_3_), channel_id=1, source_target_pairs={{0,4},{4,0},{8,12},{12,8},{16,20},{20,16},{24,28},{28,24},{1,5},{5... | collective-permute-start | bytes 3145736 | tf_op jit(solution)/shard_map/ppermute | solution.py:434
  281.0 55.2 %collective-permute-start.53 = (bf16[512,1024]{1,0:T(8,128)(2,1)}, bf16[512,1024]{1,0:T(8,128)(2,1)}, u32[]{:S(2)}, u32[]{:S(2)}) collective-permute-start(bf16[512,1024]{1,0:T(8,128)(2,1)} %collective-permute-done.49.refs_3_), channel_id=1, source_target_pairs={{0,4},{4,0},{8,12},{12,8},{16,20},{20,16},{24,28},{28,24},{1,5},{5... | collective-permute-start | bytes 3145736 | tf_op jit(solution)/shard_map/ppermute | solution.py:434
  531.2 39.9 %collective-permute-start.60 = (bf16[512,1024]{1,0:T(8,128)(2,1)}, bf16[512,1024]{1,0:T(8,128)(2,1)S(1)}, u32[]{:S(2)}, u32[]{:S(2)}) collective-permute-start(bf16[512,1024]{1,0:T(8,128)(2,1)} %slice.367), channel_id=1, source_target_pairs={{0,4},{4,0},{8,12},{12,8},{16,20},{20,16},{24,28},{28,24},{1,5},{5... | collective-permute-start | bytes 3145736 | tf_op jit(solution)/shard_map/ppermute | solution.py:434
  535.8 37.7 %collective-permute-start.66 = (bf16[512,1024]{1,0:T(8,128)(2,1)}, bf16[512,1024]{1,0:T(8,128)(2,1)}, u32[]{:S(2)}, u32[]{:S(2)}) collective-permute-start(bf16[512,1024]{1,0:T(8,128)(2,1)} %slice.373), channel_id=1, source_target_pairs={{0,4},{4,0},{8,12},{12,8},{16,20},{20,16},{24,28},{28,24},{1,5},{5... | collective-permute-start | bytes 3145736 | tf_op jit(solution)/shard_map/ppermute | solution.py:434
  536.0 33.2 %collective-permute-start.107 = (bf16[32,128]{1,0:T(8,128)(2,1)S(1)}, bf16[32,128]{1,0:T(8,128)(2,1)S(1)}, u32[]{:S(2)}, u32[]{:S(2)}) collective-permute-start(bf16[32,128]{1,0:T(8,128)(2,1)S(1)} %get-tuple-element.138), channel_id=1, source_target_pairs={{0,3},{1,2},{2,1},{3,0},{4,7},{5,6},{6,5},{7,4},{8,11},{9,10},{10,... | collective-permute-start | bytes 24584 | tf_op jit(solution)/shard_map/ppermute | solution.py:437
  538.6 30.6 %collective-permute-start.106 = (bf16[32,128]{1,0:T(8,128)(2,1)S(1)}, bf16[32,128]{1,0:T(8,128)(2,1)S(1)}, u32[]{:S(2)}, u32[]{:S(2)}) collective-permute-start(bf16[32,128]{1,0:T(8,128)(2,1)S(1)} %get-tuple-element.139), channel_id=1, source_target_pairs={{0,2},{1,3},{2,0},{3,1},{4,6},{5,7},{6,4},{7,5},{8,10},{9,11},{10,... | collective-permute-start | bytes 24584 | tf_op jit(solution)/shard_map/ppermute | solution.py:437
  553.0 16.7 %collective-permute-start.105 = (bf16[32,128]{1,0:T(8,128)(2,1)S(1)}, bf16[32,128]{1,0:T(8,128)(2,1)S(1)}, u32[]{:S(2)}, u32[]{:S(2)}) collective-permute-start(bf16[32,128]{1,0:T(8,128)(2,1)S(1)} %get-tuple-element.137), channel_id=1, source_target_pairs={{0,1},{1,0},{2,3},{3,2},{4,5},{5,4},{6,7},{7,6},{8,9},{9,8},{10,11... | collective-permute-start | bytes 24584 | tf_op jit(solution)/shard_map/ppermute | solution.py:437
  569.2 75.1 %collective-permute-start.54 = (bf16[512,2048]{1,0:T(8,128)(2,1)}, bf16[512,2048]{1,0:T(8,128)(2,1)S(1)}, u32[]{:S(2)}, u32[]{:S(2)}) collective-permute-start(bf16[512,2048]{1,0:T(8,128)(2,1)} %slice.361), channel_id=1, source_target_pairs={{0,4},{4,0},{8,12},{12,8},{16,20},{20,16},{24,28},{28,24},{1,5},{5... | collective-permute-start | bytes 6291464 | tf_op jit(solution)/shard_map/ppermute | solution.py:434
  571.2 79.7 %collective-permute-start.78 = (bf16[512,2048]{1,0:T(8,128)(2,1)}, bf16[512,2048]{1,0:T(8,128)(2,1)S(1)}, u32[]{:S(2)}, u32[]{:S(2)}) collective-permute-start(bf16[512,2048]{1,0:T(8,128)(2,1)} %slice.385), channel_id=1, source_target_pairs={{0,4},{4,0},{8,12},{12,8},{16,20},{20,16},{24,28},{28,24},{1,5},{5... | collective-permute-start | bytes 6291464 | tf_op jit(solution)/shard_map/ppermute | solution.py:434
  573.5 117.1 %collective-permute-start.90 = (bf16[512,4096]{1,0:T(8,128)(2,1)}, bf16[512,4096]{1,0:T(8,128)(2,1)S(1)}, u32[]{:S(2)}, u32[]{:S(2)}) collective-permute-start(bf16[512,4096]{1,0:T(8,128)(2,1)} %slice.315), channel_id=1, source_target_pairs={{0,4},{4,0},{8,12},{12,8},{16,20},{20,16},{24,28},{28,24},{1,5},{5... | collective-permute-start | bytes 12582920 | tf_op jit(solution)/shard_map/ppermute | solution.py:434
  594.1 22.5 %collective-permute-start.85 = (bf16[256,1024]{1,0:T(8,128)(2,1)S(1)}, bf16[256,1024]{1,0:T(8,128)(2,1)S(1)}, u32[]{:S(2)}, u32[]{:S(2)}) collective-permute-start(bf16[256,1024]{1,0:T(8,128)(2,1)S(1)} %slice.393), channel_id=1, source_target_pairs={{0,16},{4,20},{8,24},{12,28},{16,0},{20,4},{24,8},{28,12},{1,17},{... | collective-permute-start | bytes 1572872 | tf_op jit(solution)/shard_map/ppermute | solution.py:434
  650.9 20.0 %collective-permute-start.55 = (bf16[256,2048]{1,0:T(8,128)(2,1)S(1)}, bf16[256,2048]{1,0:T(8,128)(2,1)S(1)}, u32[]{:S(2)}, u32[]{:S(2)}) collective-permute-start(bf16[256,2048]{1,0:T(8,128)(2,1)S(1)} %slice.363), channel_id=1, source_target_pairs={{0,16},{4,20},{8,24},{12,28},{16,0},{20,4},{24,8},{28,12},{1,17},{... | collective-permute-start | bytes 3145736 | tf_op jit(solution)/shard_map/ppermute | solution.py:434
  657.9 24.3 %collective-permute-start.79 = (bf16[256,2048]{1,0:T(8,128)(2,1)S(1)}, bf16[256,2048]{1,0:T(8,128)(2,1)S(1)}, u32[]{:S(2)}, u32[]{:S(2)}) collective-permute-start(bf16[256,2048]{1,0:T(8,128)(2,1)S(1)} %slice.387), channel_id=1, source_target_pairs={{0,8},{4,12},{8,0},{12,4},{16,24},{20,28},{24,16},{28,20},{1,9},{5... | collective-permute-start | bytes 3145736 | tf_op jit(solution)/shard_map/ppermute | solution.py:434
  664.5 43.6 %collective-permute-start.96 = (bf16[2048,1024]{1,0:T(8,128)(2,1)}, bf16[2048,1024]{1,0:T(8,128)(2,1)}, u32[]{:S(2)}, u32[]{:S(2)}) collective-permute-start(bf16[2048,1024]{1,0:T(8,128)(2,1)} %slice.321), channel_id=1, source_target_pairs={{0,4},{4,0},{8,12},{12,8},{16,20},{20,16},{24,28},{28,24},{1,5},{5... | collective-permute-start | bytes 12582920 | tf_op jit(solution)/shard_map/ppermute | solution.py:434
  683.4 17.0 %collective-permute-start.80 = (bf16[128,2048]{1,0:T(8,128)(2,1)}, bf16[128,2048]{1,0:T(8,128)(2,1)}, u32[]{:S(2)}, u32[]{:S(2)}) collective-permute-start(bf16[128,2048]{1,0:T(8,128)(2,1)} %slice.389), channel_id=1, source_target_pairs={{0,16},{4,20},{8,24},{12,28},{16,0},{20,4},{24,8},{28,12},{1,17},{... | collective-permute-start | bytes 1572872 | tf_op jit(solution)/shard_map/ppermute | solution.py:434
  700.5 40.2 %collective-permute-start.91 = (bf16[256,4096]{1,0:T(8,128)(2,1)}, bf16[256,4096]{1,0:T(8,128)(2,1)S(1)}, u32[]{:S(2)}, u32[]{:S(2)}) collective-permute-start(bf16[256,4096]{1,0:T(8,128)(2,1)} %slice.397), channel_id=1, source_target_pairs={{0,8},{4,12},{8,0},{12,4},{16,24},{20,28},{24,16},{28,20},{1,9},{5... | collective-permute-start | bytes 6291464 | tf_op jit(solution)/shard_map/ppermute | solution.py:434
  712.6 48.6 %collective-permute-start.97 = (bf16[1024,1024]{1,0:T(8,128)(2,1)S(1)}, bf16[1024,1024]{1,0:T(8,128)(2,1)S(1)}, u32[]{:S(2)}, u32[]{:S(2)}) collective-permute-start(bf16[1024,1024]{1,0:T(8,128)(2,1)S(1)} %slice.401), channel_id=1, source_target_pairs={{0,16},{4,20},{8,24},{12,28},{16,0},{20,4},{24,8},{28,12},{1,17},{... | collective-permute-start | bytes 6291464 | tf_op jit(solution)/shard_map/ppermute | solution.py:434
  741.6 32.6 %collective-permute-start.92 = (bf16[128,4096]{1,0:T(8,128)(2,1)S(1)}, bf16[128,4096]{1,0:T(8,128)(2,1)S(1)}, u32[]{:S(2)}, u32[]{:S(2)}) collective-permute-start(bf16[128,4096]{1,0:T(8,128)(2,1)S(1)} %slice.399), channel_id=1, source_target_pairs={{0,16},{4,20},{8,24},{12,28},{16,0},{20,4},{24,8},{28,12},{1,17},{... | collective-permute-start | bytes 3145736 | tf_op jit(solution)/shard_map/ppermute | solution.py:434
  762.3 16.7 %collective-permute-start.98 = (bf16[512,1024]{1,0:T(8,128)(2,1)S(1)}, bf16[512,1024]{1,0:T(8,128)(2,1)S(1)}, u32[]{:S(2)}, u32[]{:S(2)}) collective-permute-start(bf16[512,1024]{1,0:T(8,128)(2,1)S(1)} %slice.403), channel_id=1, source_target_pairs={{0,8},{4,12},{8,0},{12,4},{16,24},{20,28},{24,16},{28,20},{1,9},{5... | collective-permute-start | bytes 3145736 | tf_op jit(solution)/shard_map/ppermute | solution.py:434
  776.5 29.6 %collective-permute-start.94 = (bf16[32,4096]{1,0:T(8,128)(2,1)S(1)}, bf16[32,4096]{1,0:T(8,128)(2,1)S(1)}, u32[]{:S(2)}, u32[]{:S(2)}) collective-permute-start(bf16[32,4096]{1,0:T(8,128)(2,1)S(1)} %get-tuple-element.108), channel_id=1, source_target_pairs={{0,2},{1,3},{2,0},{3,1},{4,6},{5,7},{6,4},{7,5},{8,10},{9,11},{10,... | collective-permute-start | bytes 786440 | tf_op jit(solution)/shard_map/ppermute | solution.py:437
  776.5 29.6 %collective-permute-start.93 = (bf16[32,4096]{1,0:T(8,128)(2,1)S(1)}, bf16[32,4096]{1,0:T(8,128)(2,1)S(1)}, u32[]{:S(2)}, u32[]{:S(2)}) collective-permute-start(bf16[32,4096]{1,0:T(8,128)(2,1)S(1)} %get-tuple-element.106), channel_id=1, source_target_pairs={{0,1},{1,0},{2,3},{3,2},{4,5},{5,4},{6,7},{7,6},{8,9},{9,8},{10,11... | collective-permute-start | bytes 786440 | tf_op jit(solution)/shard_map/ppermute | solution.py:437
  779.5 27.5 %collective-permute-start.101 = (bf16[128,1024]{1,0:T(8,128)(2,1)S(1)}, bf16[128,1024]{1,0:T(8,128)(2,1)S(1)}, u32[]{:S(2)}, u32[]{:S(2)}) collective-permute-start(bf16[128,1024]{1,0:T(8,128)(2,1)S(1)} %get-tuple-element.104), channel_id=1, source_target_pairs={{0,3},{1,2},{2,1},{3,0},{4,7},{5,6},{6,5},{7,4},{8,11},{9,10},{10,... | collective-permute-start | bytes 786440 | tf_op jit(solution)/shard_map/ppermute | solution.py:437
  781.4 31.4 %collective-permute-start.100 = (bf16[128,1024]{1,0:T(8,128)(2,1)S(1)}, bf16[128,1024]{1,0:T(8,128)(2,1)S(1)}, u32[]{:S(2)}, u32[]{:S(2)}) collective-permute-start(bf16[128,1024]{1,0:T(8,128)(2,1)S(1)} %get-tuple-element.105), channel_id=1, source_target_pairs={{0,2},{1,3},{2,0},{3,1},{4,6},{5,7},{6,4},{7,5},{8,10},{9,11},{10,... | collective-permute-start | bytes 786440 | tf_op jit(solution)/shard_map/ppermute | solution.py:437
  785.7 27.1 %collective-permute-start.99 = (bf16[128,1024]{1,0:T(8,128)(2,1)S(1)}, bf16[128,1024]{1,0:T(8,128)(2,1)S(1)}, u32[]{:S(2)}, u32[]{:S(2)}) collective-permute-start(bf16[128,1024]{1,0:T(8,128)(2,1)S(1)} %get-tuple-element.103), channel_id=1, source_target_pairs={{0,1},{1,0},{2,3},{3,2},{4,5},{5,4},{6,7},{7,6},{8,9},{9,8},{10,11... | collective-permute-start | bytes 786440 | tf_op jit(solution)/shard_map/ppermute | solution.py:437
  (139 other events, 2056.3 us)

commit v2 on v1

v2 whole, which is shorter than its diff:
```python
import functools

import jax
import jax.numpy as jnp
from jax import lax
from jax.experimental import pallas as pl
from jax.experimental.pallas import tpu as pltpu
from jax.sharding import Mesh
from jax.sharding import PartitionSpec as P

HEAD = 64
LANES = 128
BOTH = ("h", "c", "fsdp")
VMEM_BYTES = 60 * 1024 * 1024
SHORT = pl.CostEstimate(flops=1024, transcendentals=0, bytes_accessed=1024)
TAIL_RATE = 0.2316419
TAIL_POLY = (
    0.09252224973357535,
    0.09042007971374488,
    0.10265042640370807,
    0.013551821473999732,
    0.2252533241128307,
    -0.2016603378863937,
    0.24768663093443657,
    -0.07042413008644138,
)


def product(left, right):
    return jnp.dot(left, right, preferred_element_type=jnp.float32)


def contract_rows(left, right):
    return lax.dot_general(
        left, right, (((0,), (0,)), ((), ())), preferred_element_type=jnp.float32
    )


def times_transposed(left, right):
    return lax.dot_general(
        left, right, (((1,), (1,)), ((), ())), preferred_element_type=jnp.float32
    )


def layer_norm(values, gain_row, bias_row):
    centre = values - jnp.mean(values, axis=-1, keepdims=True)
    spread = jnp.mean(centre * centre, axis=-1, keepdims=True)
    return centre * lax.rsqrt(spread + 1e-05) * gain_row + bias_row


def norm_backward(values, gain_row, grad):
    centre = values - jnp.mean(values, axis=-1, keepdims=True)
    rate = lax.rsqrt(jnp.mean(centre * centre, axis=-1, keepdims=True) + 1e-05)
    normed = centre * rate
    scaled = grad * gain_row
    grad_input = rate * (
        scaled
        - jnp.mean(scaled, axis=-1, keepdims=True)
        - normed * jnp.mean(scaled * normed, axis=-1, keepdims=True)
    )
    return grad_input, jnp.sum(grad * normed, axis=0), jnp.sum(grad, axis=0)


def masked_scores(keys, queries, key_limit, causal, query_start):
    scores = times_transposed(keys, queries)
    key_count, query_count = scores.shape
    if not causal:
        row = lax.broadcasted_iota(jnp.int32, scores.shape, 0)
        return jnp.where(row < key_limit, scores, -1e30)
    row = query_start + lax.broadcasted_iota(jnp.int32, (query_count, query_count), 0)
    column = query_start + lax.broadcasted_iota(jnp.int32, (query_count, query_count), 1)
    diagonal = jnp.where(
        (row <= column) & (row < key_limit), scores[query_start:, :], -1e30
    )
    if query_start == 0:
        return diagonal
    below_row = lax.broadcasted_iota(jnp.int32, (query_start, query_count), 0)
    below = jnp.where(below_row < key_limit, scores[:query_start, :], -1e30)
    return jnp.concatenate([below, diagonal], axis=0)


def query_blocks(row_count, key_count, causal):
    width = 256 if row_count % 256 == 0 else row_count
    return [
        (start, width, start + width if causal else key_count)
        for start in range(0, row_count, width)
    ]


def head_lanes(head, shape):
    lane = lax.broadcasted_iota(jnp.int32, shape, 1)
    return (lane >= head * HEAD) & (lane < (head + 1) * HEAD)


def attention_forward_kernel(causal, limit_ref, q_ref, k_ref, v_ref, mixed_ref, total_ref, mixed_turned):
    key_limit = limit_ref[0]
    row_count, key_count = q_ref.shape[0], k_ref.shape[0]
    values_turned = v_ref[...].T
    scaled = q_ref[...] * jnp.bfloat16(HEAD**-0.5)
    for head in range(2):
        own = jnp.where(head_lanes(head, scaled.shape), scaled, jnp.zeros_like(scaled))
        lanes = slice(head * HEAD, (head + 1) * HEAD)
        for start, width, stop in query_blocks(row_count, key_count, causal):
            scores = masked_scores(
                k_ref[:stop, :], own[start : start + width, :], key_limit, causal, start
            )
            highest = jnp.max(scores, axis=0, keepdims=True)
            expanded = jnp.exp(scores - highest)
            total = jnp.sum(expanded, axis=0, keepdims=True)
            mixed = product(values_turned[lanes, :stop], expanded.astype(jnp.bfloat16))
            mixed_turned[lanes, start : start + width] = mixed / total
            total_ref[0, head : head + 1, start : start + width] = highest + jnp.log(total)
    mixed_ref[...] = mixed_turned[...].T.astype(jnp.bfloat16)


def attention_forward(limit, queries, q_at, keys, k_at, values, v_at, causal):
    row_count, key_count = queries.shape[0], keys.shape[0]
    width = 1024
    pairs = width // LANES
    return pl.pallas_call(
        functools.partial(attention_forward_kernel, causal),
        grid_spec=pltpu.PrefetchScalarGridSpec(
            num_scalar_prefetch=1,
            grid=(pairs,),
            in_specs=[
                pl.BlockSpec((row_count, LANES), lambda p, s: (0, q_at + p)),
                pl.BlockSpec((key_count, LANES), lambda p, s: (0, k_at + p)),
                pl.BlockSpec((key_count, LANES), lambda p, s: (0, v_at + p)),
            ],
            out_specs=[
                pl.BlockSpec((row_count, LANES), lambda p, s: (0, p)),
                pl.BlockSpec((1, 2, row_count), lambda p, s: (p, 0, 0)),
            ],
            scratch_shapes=[pltpu.VMEM((LANES, row_count), jnp.float32)],
        ),
        out_shape=[
            jax.ShapeDtypeStruct((row_count, width), jnp.bfloat16),
            jax.ShapeDtypeStruct((pairs, 2, row_count), jnp.float32),
        ],
        compiler_params=pltpu.CompilerParams(vmem_limit_bytes=VMEM_BYTES),
        cost_estimate=SHORT,
        name="attention_forward",
    )(limit, queries, keys, values)


def attention_backward_kernel(
    causal,
    limit_ref,
    q_ref,
    k_ref,
    v_ref,
    mixed_ref,
    grad_ref,
    total_ref,
    grad_q_ref,
    grad_k_ref,
    grad_v_ref,
    grad_q_turned,
    grad_k_sum,
    grad_v_sum,
):
    key_limit = limit_ref[0]
    row_count, key_count = q_ref.shape[0], k_ref.shape[0]
    keys_turned = k_ref[...].T
    scaled = q_ref[...] * jnp.bfloat16(HEAD**-0.5)
    grad = grad_ref[...]
    inner_turned = (grad.astype(jnp.float32) * mixed_ref[...].astype(jnp.float32)).T
    grad_k_sum[...] = jnp.zeros_like(grad_k_sum)
    grad_v_sum[...] = jnp.zeros_like(grad_v_sum)
    for head in range(2):
        mask = head_lanes(head, scaled.shape)
        own = jnp.where(mask, scaled, jnp.zeros_like(scaled))
        own_grad = jnp.where(mask, grad, jnp.zeros_like(grad))
        lanes = slice(head * HEAD, (head + 1) * HEAD)
        inner = jnp.sum(inner_turned[lanes, :], axis=0, keepdims=True)
        for start, width, stop in query_blocks(row_count, key_count, causal):
            columns = slice(start, start + width)
            queries, grads = own[columns, :], own_grad[columns, :]
            scores = masked_scores(k_ref[:stop, :], queries, key_limit, causal, start)
            probs = jnp.exp(scores - total_ref[0, head : head + 1, columns])
            grad_v_sum[:stop, :] += product(probs.astype(jnp.bfloat16), grads)
            grad_probs = times_transposed(v_ref[:stop, :], grads)
            grad_scores = (probs * (grad_probs - inner[:, columns])).astype(jnp.bfloat16)
            grad_k_sum[:stop, :] += product(grad_scores, queries)
            grad_q_turned[lanes, columns] = product(keys_turned[lanes, :stop], grad_scores)
    grad_q_ref[...] = (grad_q_turned[...].T * HEAD**-0.5).astype(jnp.bfloat16)
    grad_k_ref[...] = grad_k_sum[...].astype(jnp.bfloat16)
    grad_v_ref[...] = grad_v_sum[...].astype(jnp.bfloat16)


def attention_backward(limit, queries, q_at, keys, k_at, values, v_at, mixed, grad_mixed, totals, causal):
    row_count, key_count = queries.shape[0], keys.shape[0]
    width = 1024
    pairs = width // LANES
    row_block = pl.BlockSpec((row_count, LANES), lambda p, s: (0, p))
    key_block = pl.BlockSpec((key_count, LANES), lambda p, s: (0, p))
    return pl.pallas_call(
        functools.partial(attention_backward_kernel, causal),
        grid_spec=pltpu.PrefetchScalarGridSpec(
            num_scalar_prefetch=1,
            grid=(pairs,),
            in_specs=[
                pl.BlockSpec((row_count, LANES), lambda p, s: (0, q_at + p)),
                pl.BlockSpec((key_count, LANES), lambda p, s: (0, k_at + p)),
                pl.BlockSpec((key_count, LANES), lambda p, s: (0, v_at + p)),
                row_block,
                row_block,
                pl.BlockSpec((1, 2, row_count), lambda p, s: (p, 0, 0)),
            ],
            out_specs=[row_block, key_block, key_block],
            scratch_shapes=[
                pltpu.VMEM((LANES, row_count), jnp.float32),
                pltpu.VMEM((key_count, LANES), jnp.float32),
                pltpu.VMEM((key_count, LANES), jnp.float32),
            ],
        ),
        out_shape=[
            jax.ShapeDtypeStruct((row_count, width), jnp.bfloat16),
            jax.ShapeDtypeStruct((key_count, width), jnp.bfloat16),
            jax.ShapeDtypeStruct((key_count, width), jnp.bfloat16),
        ],
        compiler_params=pltpu.CompilerParams(vmem_limit_bytes=VMEM_BYTES),
        cost_estimate=SHORT,
        name="attention_backward",
    )(limit, queries, keys, values, mixed, grad_mixed, totals)


def gelu_and_slope(values):
    size = jnp.abs(values)
    bell = jnp.exp(-0.5 * values * values)
    t = 1.0 / (1.0 + TAIL_RATE * size)
    poly = TAIL_POLY[-1] * t + TAIL_POLY[-2]
    for coefficient in TAIL_POLY[-3::-1]:
        poly = poly * t + coefficient
    tail = poly * t * bell
    normal_cdf = jnp.where(values >= 0, 1.0 - tail, tail)
    return values * normal_cdf, normal_cdf + values * (bell * (2.0 * jnp.pi) ** (-0.5))


def unfold_rows(folded_ref, unfolded, rows):
    width = unfolded.shape[1]
    folds = folded_ref.shape[1] // width
    for shard in range(folded_ref.shape[0] // rows):
        for fold in range(folds):
            start = (shard * folds + fold) * rows
            unfolded[start : start + rows, :] = folded_ref[
                shard * rows : (shard + 1) * rows, fold * width : (fold + 1) * width
            ]


def fold_rows(unfolded, folded_ref, rows):
    width = unfolded.shape[1]
    folds = folded_ref.shape[1] // width
    for shard in range(folded_ref.shape[0] // rows):
        for fold in range(folds):
            start = (shard * folds + fold) * rows
            folded_ref[shard * rows : (shard + 1) * rows, fold * width : (fold + 1) * width] = unfolded[
                start : start + rows, :
            ]


def feed_forward_kernel(
    rows, normed_ref, input_ref, output_ref, base_ref, hidden_ref, slope_ref, after_ref, unfolded
):
    if rows:
        unfold_rows(output_ref, unfolded, rows)
        output_ref = unfolded

    @pl.when(pl.program_id(0) == 0)
    def _():
        after_ref[...] = base_ref[...]

    row_count = normed_ref.shape[0]
    step = 256 if row_count % 256 == 0 else row_count
    for start in range(0, row_count, step):
        rows = slice(start, start + step)
        hidden, slope = gelu_and_slope(product(normed_ref[rows, :], input_ref[...]))
        hidden = hidden.astype(jnp.bfloat16)
        hidden_ref[rows, :] = hidden
        slope_ref[rows, :] = slope.astype(jnp.bfloat16)
        after_ref[rows, :] += product(hidden, output_ref[...])


FEED_TILE = 512


def feed_weight_specs(folds, width, tile, index):
    first = pl.BlockSpec((width, tile), lambda *at: (0, index(*at)))
    if folds:
        return first, pl.BlockSpec((tile // folds, folds * width), lambda *at: (index(*at), 1))
    return first, pl.BlockSpec((tile, width), lambda *at: (index(*at), 0))


def feed_forward(rows, normed, input_low, output_low, after_cross):
    row_count, width = normed.shape
    hidden_width = 4 * width
    tile = FEED_TILE
    whole = pl.BlockSpec((row_count, width), lambda j: (0, 0))
    tall = pl.BlockSpec((row_count, tile), lambda j: (0, j))
    weight_specs = feed_weight_specs(hidden_width // width if rows else 0, width, tile, lambda j: j)
    return pl.pallas_call(
        functools.partial(feed_forward_kernel, rows),
        grid=(hidden_width // tile,),
        in_specs=[whole, *weight_specs, whole],
        out_specs=[tall, tall, whole],
        out_shape=[
            jax.ShapeDtypeStruct((row_count, hidden_width), jnp.bfloat16),
            jax.ShapeDtypeStruct((row_count, hidden_width), jnp.bfloat16),
            jax.ShapeDtypeStruct((row_count, width), jnp.float32),
        ],
        scratch_shapes=[pltpu.VMEM((tile, width), jnp.bfloat16)],
        compiler_params=pltpu.CompilerParams(vmem_limit_bytes=VMEM_BYTES),
        cost_estimate=SHORT,
        name="feed_forward",
    )(normed, input_low, output_low, after_cross)


def turn_rows(x_ref, turned, positions_ref):
    for j in range(x_ref.shape[1] // LANES):
        start = pl.multiple_of(positions_ref[j] * LANES, LANES)
        turned[pl.ds(start, LANES), :] = x_ref[:, j * LANES : (j + 1) * LANES].T


def feed_backward_kernel(
    rows,
    half_blocks,
    positions_ref,
    grad_ref,
    normed_ref,
    hidden_ref,
    slope_ref,
    input_ref,
    output_ref,
    in_send_ref,
    in_keep_ref,
    out_ref,
    grad_normed_ref,
    turned,
    unfolded,
):
    step = pl.program_id(0)
    if rows:
        unfold_rows(output_ref, unfolded, rows)
        output_ref = unfolded

    @pl.when(step == 0)
    def _():
        grad_normed_ref[...] = jnp.zeros_like(grad_normed_ref)
        turn_rows(normed_ref, turned, positions_ref)

    grad_hidden = times_transposed(grad_ref[...], output_ref[...])
    grad_pre = (grad_hidden * slope_ref[...].astype(jnp.float32)).astype(jnp.bfloat16)
    grad_out = contract_rows(hidden_ref[...], grad_ref[...]).astype(jnp.bfloat16)
    if rows:
        fold_rows(grad_out, out_ref, rows)
    else:
        out_ref[...] = grad_out
    half = turned.shape[0] // 2
    in_send_ref[...] = product(turned[:half, :], grad_pre).astype(jnp.bfloat16)
    in_keep_ref[...] = product(turned[half:, :], grad_pre).astype(jnp.bfloat16)
    grad_normed_ref[...] += times_transposed(grad_pre, input_ref[...])


def feed_backward(rows, positions, grad_branch, normed, hidden, slope, input_low, output_low):
    row_count, width = grad_branch.shape
    hidden_width = hidden.shape[1]
    count = positions.shape[0]
    tile = hidden_width // count
    whole = pl.BlockSpec((row_count, width), lambda j, p: (0, 0))
    tall = pl.BlockSpec((row_count, tile), lambda j, p: (0, j))
    in_half = pl.BlockSpec((width // 2, tile), lambda j, p: (0, j))
    folds = hidden_width // width if rows else 1
    weight_specs = feed_weight_specs(folds if rows else 0, width, tile, lambda j, p: j)
    return pl.pallas_call(
        functools.partial(feed_backward_kernel, rows, count // 2),
        grid_spec=pltpu.PrefetchScalarGridSpec(
            num_scalar_prefetch=1,
            grid=(count,),
            in_specs=[whole, whole, tall, tall, *weight_specs],
            out_specs=[
                in_half,
                in_half,
                pl.BlockSpec((tile // folds, folds * width), lambda j, p: (p[j], 0)),
                whole,
            ],
            scratch_shapes=[
                pltpu.VMEM((width, row_count), jnp.bfloat16),
                pltpu.VMEM((tile, width), jnp.bfloat16),
            ],
        ),
        out_shape=[
            jax.ShapeDtypeStruct((width // 2, hidden_width), jnp.bfloat16),
            jax.ShapeDtypeStruct((width // 2, hidden_width), jnp.bfloat16),
            jax.ShapeDtypeStruct((hidden_width // folds, folds * width), jnp.bfloat16),
            jax.ShapeDtypeStruct((row_count, width), jnp.float32),
        ],
        compiler_params=pltpu.CompilerParams(vmem_limit_bytes=VMEM_BYTES),
        cost_estimate=SHORT,
        name="feed_backward",
    )(positions, grad_branch, normed, hidden, slope, input_low, output_low)


def weight_gradient_kernel(starts, positions_ref, x_ref, *refs):
    turned = refs[-1]
    send_ref, keep_ref = refs[-3:-1]
    step = pl.program_id(0)

    @pl.when(step == 0)
    def _():
        turn_rows(x_ref, turned, positions_ref)

    half = turned.shape[0] // 2
    for index, grad_ref in enumerate(refs[:-3]):

        @pl.when((step >= starts[index]) & (step < starts[index + 1]))
        def _(grad_ref=grad_ref):
            send_ref[...] = product(turned[:half, :], grad_ref[...]).astype(jnp.bfloat16)
            keep_ref[...] = product(turned[half:, :], grad_ref[...]).astype(jnp.bfloat16)


def weight_gradient(positions, x, grads):
    row_count, width = x.shape
    tile = 512
    starts = [0]
    for grad in grads:
        starts.append(starts[-1] + grad.shape[1] // tile)
    columns = starts[-1] * tile

    def grad_spec(first, last):
        return pl.BlockSpec((row_count, tile), lambda j, p: (0, jnp.clip(j - first, 0, last - first - 1)))

    half = pl.BlockSpec((width // 2, tile), lambda j, p: (0, j))
    return pl.pallas_call(
        functools.partial(weight_gradient_kernel, starts),
        grid_spec=pltpu.PrefetchScalarGridSpec(
            num_scalar_prefetch=1,
            grid=(starts[-1],),
            in_specs=[pl.BlockSpec((row_count, width), lambda j, p: (0, 0))]
            + [grad_spec(starts[i], starts[i + 1]) for i in range(len(grads))],
            out_specs=[half, half],
            scratch_shapes=[pltpu.VMEM((width, row_count), jnp.bfloat16)],
        ),
        out_shape=[jax.ShapeDtypeStruct((width // 2, columns), jnp.bfloat16)] * 2,
        compiler_params=pltpu.CompilerParams(vmem_limit_bytes=VMEM_BYTES),
        cost_estimate=SHORT,
        name="weight_gradient",
    )(positions, x, *grads)


class Order:
    def __init__(self):
        self.last = ()

    def after(self, *values):
        values, _ = lax.optimization_barrier((values, self.last))
        return values if len(values) > 1 else values[0]

    def run(self, work, *values):
        values, _ = lax.optimization_barrier((values, self.last))
        result = work(*values)
        self.last = result
        return result


def place_rows_kernel(counts, rows, table_ref, *refs):
    pieces, out_ref, held, sems_in, sems_out = refs[:-4], *refs[-4:]
    loads, stores = [], []
    for piece, count in zip(pieces, counts):
        for block in range(count):
            at = len(loads)
            start = pl.multiple_of(table_ref[at] * rows, rows)
            loads.append(
                pltpu.make_async_copy(piece.at[pl.ds(block * rows, rows), :], held.at[at], sems_in.at[at])
            )
            stores.append(
                pltpu.make_async_copy(held.at[at], out_ref.at[pl.ds(start, rows), :], sems_out.at[at])
            )
    for load in loads:
        load.start()
    for load, store in zip(loads, stores):
        load.wait()
        store.start()
    for store in stores:
        store.wait()


def place_rows(table, pieces, rows):
    counts = [piece.shape[0] // rows for piece in pieces]
    total, columns = sum(counts), pieces[0].shape[1]
    anywhere = pl.BlockSpec(memory_space=pl.ANY)
    return pl.pallas_call(
        functools.partial(place_rows_kernel, counts, rows),
        grid_spec=pltpu.PrefetchScalarGridSpec(
            num_scalar_prefetch=1,
            grid=(1,),
            in_specs=[anywhere] * len(pieces),
            out_specs=anywhere,
            scratch_shapes=[
                pltpu.VMEM((total, rows, columns), pieces[0].dtype),
                pltpu.SemaphoreType.DMA((total,)),
                pltpu.SemaphoreType.DMA((total,)),
            ],
        ),
        out_shape=jax.ShapeDtypeStruct((total * rows, columns), pieces[0].dtype),
        compiler_params=pltpu.CompilerParams(vmem_limit_bytes=VMEM_BYTES),
        cost_estimate=SHORT,
        name="place_rows",
    )(table, *pieces)


class Links:
    def __init__(self, width):
        self.h_count, self.fsdp_count = lax.axis_size("h"), lax.axis_size("fsdp")
        self.core, self.h, self.fsdp = lax.axis_index("c"), lax.axis_index("h"), lax.axis_index("fsdp")
        dp_count = 2 * self.h_count
        self.pairwise = (
            (self.h_count & (self.h_count - 1)) == 0
            and (self.fsdp_count & (self.fsdp_count - 1)) == 0
            and width == dp_count * LANES
        )
        self.blocks = width // LANES
        self.bits = [1 << b for b in range(self.h_count.bit_length() - 1)]
        self.fsdp_table = (self.fsdp ^ jnp.arange(self.fsdp_count, dtype=jnp.int32)).astype(jnp.int32)

    def order(self, flip):
        return self.bits[::-1] if flip else self.bits

    def swap(self, array, bit):
        return lax.ppermute(array, "h", [(i, i ^ bit) for i in range(self.h_count)])

    def swap_core(self, array):
        return lax.ppermute(array, "c", [(0, 1), (1, 0)])

    def swap_fsdp(self, array, bit):
        return lax.ppermute(array, "fsdp", [(i, i ^ bit) for i in range(self.fsdp_count)])

    def gather(self, shard):
        return lax.all_gather(shard, BOTH, axis=0, tiled=True)

    def spread_fsdp(self, shard):
        return [shard] + [self.swap_fsdp(shard, k) for k in range(1, self.fsdp_count)]

    def place_fsdp(self, parts):
        return place_rows(self.fsdp_table, parts, parts[0].shape[0])

    def spread(self, block, at, flip):
        return jnp.concatenate([block, self.swap(block, self.order(flip)[at])], axis=0)

    def place(self, block, other, flip):
        masks = [0]
        for bit in self.order(flip):
            masks = masks + [mask ^ bit for mask in masks]
        h = self.h ^ jnp.asarray(masks, dtype=jnp.int32)
        table = jnp.concatenate([2 * h + self.core, 2 * h + 1 - self.core]).astype(jnp.int32)
        return place_rows(table, [block, other], block.shape[0] // self.h_count)

    def positions(self, flip=None):
        block = jnp.arange(self.blocks, dtype=jnp.int32)
        if not self.pairwise:
            return block
        place, own = block >> 1, (block & 1) == self.core
        if flip is not None:
            mask, place = place ^ self.h, jnp.zeros_like(place)
            for at, bit in enumerate(self.order(flip)):
                place = place + jnp.where((mask & bit) == 0, 1 << at, 0)
        return (place + jnp.where(own, self.h_count, 0)).astype(jnp.int32)

    def halves(self, rows, flip):
        blocks = rows.reshape(self.blocks, -1, rows.shape[1])
        place = self.positions(flip)
        order = jnp.sum(
            jnp.where(place[:, None] == jnp.arange(self.blocks)[None, :], jnp.arange(self.blocks)[:, None], 0),
            axis=0,
        )
        ordered = [lax.dynamic_index_in_dim(blocks, order[j], 0, keepdims=False) for j in range(self.blocks)]
        half = self.blocks // 2
        return jnp.concatenate(ordered[:half], axis=0), jnp.concatenate(ordered[half:], axis=0)

    def sum_cores(self, keep, other):
        return (keep.astype(jnp.float32) + other.astype(jnp.float32)).astype(jnp.bfloat16)

    def send_fsdp(self, grad):
        return lax.all_to_all(grad, "fsdp", 0, 0, tiled=True)

    def sum_fsdp(self, parts):
        rows = parts.shape[0] // self.fsdp_count
        parts = parts.astype(jnp.float32)
        return sum(parts[k * rows : (k + 1) * rows] for k in range(self.fsdp_count))

    def scatter_whole(self, send, keep):
        grad = jnp.concatenate([send, keep], axis=0).astype(jnp.float32)
        part = lax.psum_scatter(grad, ("h", "c"), scatter_dimension=0, tiled=True)
        return lax.psum_scatter(part, "fsdp", scatter_dimension=0, tiled=True)

    def sum_chips(self, grad):
        return lax.psum_scatter(grad, "h", scatter_dimension=0, tiled=True)

    def first_pair(self, keep, other):
        half = keep.shape[0] // 2
        return self.sum_cores(keep[:half], other[:half]), self.sum_cores(keep[half:], other[half:])

    def bit(self, at, flip):
        return self.order(flip)[::-1][at]


def body(
    unit_states,
    encoder_states,
    cotangent,
    unit_lengths,
    text_lengths,
    self_project,
    self_output,
    cross_project,
    cross_output,
    feed_input,
    feed_output,
    norm_gains,
    norm_biases,
):
    low = jnp.bfloat16
    layer_input = unit_states[0].astype(jnp.float32)
    encoded = encoder_states[0]
    row_count, width = layer_input.shape
    links = Links(width)

    tables = jnp.concatenate([norm_gains, norm_biases], axis=0).T
    tables = jnp.pad(tables, ((0, 0), (0, LANES - tables.shape[1])))
    self_shard = jnp.concatenate([self_project.astype(low), self_output.astype(low), tables], axis=1)
    cross_shard = jnp.concatenate(
        [cross_project[:, width:].astype(low), cross_project[:, :width].astype(low), cross_output.astype(low)],
        axis=1,
    )
    feed_shard = feed_input.astype(low)
    order = Order()
    flips = [False, True]
    split = 2 * width
    if links.pairwise:
        fold_count = feed_input.shape[0]
        folded = [
            feed_output[at : at + fold_count].astype(low) for at in range(0, feed_output.shape[0], fold_count)
        ]
        feed_shard = jnp.concatenate([feed_shard] + folded, axis=1)
        bits = [links.order(flip) for flip in flips]

        def send(sides, at):
            return [links.swap(side, bit[at]) for side, bit in zip(sides, bits)]

        def join(*arrays):
            half = len(arrays) // 2
            return [jnp.concatenate(pair, axis=0) for pair in zip(arrays[:half], arrays[half:])]

        def lay(*arrays):
            half = len(arrays) // 2
            return [links.place(*pair, flip) for pair, flip in zip(zip(arrays[:half], arrays[half:]), flips)]

        def lay_fsdp(*parts):
            return links.place_fsdp(parts)

        gathered = links.gather(jnp.concatenate([feed_shard, cross_shard], axis=1))
        feed_input_low, feed_output_low, cross_whole = gathered, gathered, gathered[:, 8 * width :]
        self_part = order.run(lay_fsdp, *links.spread_fsdp(self_shard))
        self_sides = [self_part[:, :split], self_part[:, split:]]
        self_swaps = send(self_sides, 0)
        self_sides = order.run(join, *self_sides, *self_swaps)
        self_swaps = send(self_sides, 1)
        self_sides = order.run(join, *self_sides, *self_swaps)
        self_others = [links.swap_core(side) for side in self_sides]
        self_first, self_second = order.run(lay, *self_sides, *self_others)
    else:
        fold_count = 0
        self_whole, cross_whole = links.gather(self_shard), links.gather(cross_shard)
        self_first, self_second = self_whole[:, :split], self_whole[:, split:]
        feed_input_low = links.gather(feed_shard)
        feed_output_low = links.gather(feed_output.astype(low))

    self_value, self_output_low = self_second[:, :width], self_second[:, width : 2 * width]
    norm_rows = self_second[:, 2 * width : 2 * width + 8].astype(jnp.float32).T
    gain_table, bias_table = norm_rows[:4], norm_rows[4:]

    def self_projections(layer_input, self_first, self_value, gain_row, bias_row):
        normed_self = layer_norm(layer_input, gain_row, bias_row).astype(low)
        return (
            normed_self,
            product(normed_self, self_first).astype(low),
            product(normed_self, self_value).astype(low),
        )

    normed_self, query_key, self_values = order.run(
        self_projections, layer_input, self_first, self_value, gain_table[0], bias_table[0]
    )
    self_mixed, self_totals = order.run(
        lambda query_key, self_values: attention_forward(
            unit_lengths, query_key, 0, query_key, width // LANES, self_values, 0, True
        ),
        query_key,
        self_values,
    )
    after_self, normed_cross = order.run(
        lambda self_mixed, self_output_low, gain_row, bias_row: (
            lambda after_self: (after_self, layer_norm(after_self, gain_row, bias_row).astype(low))
        )(layer_input + product(self_mixed, self_output_low)),
        self_mixed,
        self_output_low,
        gain_table[1],
        bias_table[1],
    )
    cross_first, cross_second = cross_whole[:, :split], cross_whole[:, split:]
    cross_query, cross_output_low = cross_second[:, :width], cross_second[:, width:]
    cross_queries = product(normed_cross, cross_query).astype(low)
    cross_kv = product(encoded, cross_first).astype(low)
    cross_mixed, cross_totals = attention_forward(
        text_lengths, cross_queries, 0, cross_kv, 0, cross_kv, width // LANES, False
    )
    after_cross = after_self + product(cross_mixed, cross_output_low)
    normed_feed = layer_norm(after_cross, gain_table[2], bias_table[2]).astype(low)
    hidden, slope, after_feed = feed_forward(
        fold_count, normed_feed, feed_input_low, feed_output_low, after_cross
    )
    block_output = layer_norm(after_feed, gain_table[3], bias_table[3]).astype(low)

    row_live = (jnp.arange(row_count, dtype=jnp.int32) < unit_lengths[0]).astype(jnp.float32)
    grad_y = cotangent[0] * row_live[:, None]
    grad_after_feed, grad_gain_3, grad_bias_3 = norm_backward(after_feed, gain_table[3], grad_y)
    positions = links.positions()
    in_send, in_keep, out_grad, grad_normed = order.run(
        lambda *arrays: feed_backward(fold_count, positions, *arrays),
        grad_after_feed.astype(low),
        normed_feed,
        hidden,
        slope,
        feed_input_low,
        feed_output_low,
    )
    if links.pairwise:
        out_half = out_grad.shape[0] // 2
        in_other, out_other = links.swap_core(in_send), links.swap_core(out_grad[:out_half])

    def cross_entry(grad_after_feed, after_cross, grad_normed, gain_row, cross_output_low, cross_mixed):
        grad_input, grad_gain, grad_bias = norm_backward(after_cross, gain_row, grad_normed)
        grad_after_cross = grad_after_feed + grad_input
        cross_branch = grad_after_cross.astype(low)
        return (
            grad_after_cross,
            grad_gain,
            grad_bias,
            times_transposed(cross_branch, cross_output_low).astype(low),
            weight_gradient(links.positions(True), cross_mixed, [cross_branch]),
        )

    grad_after_cross, grad_gain_2, grad_bias_2, grad_cross_mixed, cross_out = order.run(
        cross_entry, grad_after_feed, after_cross, grad_normed, gain_table[2], cross_output_low, cross_mixed
    )
    if links.pairwise:
        feed_sum = order.run(
            lambda *arrays: links.sum_cores(
                jnp.concatenate(arrays[:2], axis=1), jnp.concatenate(arrays[2:], axis=1)
            ),
            in_keep,
            out_grad[out_half:],
            in_other,
            out_other,
        )
        feed_chips = links.sum_chips(feed_sum)
    else:
        feed_in_part = links.scatter_whole(in_send, in_keep)
        feed_out_part = links.scatter_whole(out_grad[: out_grad.shape[0] // 2], out_grad[out_grad.shape[0] // 2 :])

    def cross_middle(cross_queries, cross_kv, cross_mixed, grad_cross_mixed, cross_totals):
        grad_q, grad_k, grad_v = attention_backward(
            text_lengths,
            cross_queries,
            0,
            cross_kv,
            0,
            cross_kv,
            width // LANES,
            cross_mixed,
            grad_cross_mixed,
            cross_totals,
            False,
        )
        return (
            grad_q,
            grad_k,
            grad_v,
            weight_gradient(links.positions(True), normed_cross, [grad_q]),
            weight_gradient(links.positions(False), encoded, [grad_k, grad_v]),
        )

    grad_q, grad_k, grad_v, cross_query_grad, cross_kv_grad = order.run(
        cross_middle, cross_queries, cross_kv, cross_mixed, grad_cross_mixed, cross_totals
    )
    cross_send, cross_keep = [
        [kv, jnp.concatenate([query, out], axis=1)]
        for kv, query, out in zip(cross_kv_grad, cross_query_grad, cross_out)
    ]
    if links.pairwise:
        cross_sides = list(zip(cross_keep, [links.swap_core(side) for side in cross_send]))

        def exchange(sides, at):
            halves = order.run(
                lambda *arrays: [links.first_pair(*arrays[i : i + 2]) for i in range(0, len(arrays), 2)],
                *[array for side in sides for array in side],
            )
            return [
                (stays, links.swap(goes, links.bit(at, flip))) for (goes, stays), flip in zip(halves, flips)
            ]

        def finish(sides):
            arrays = [array for side in sides for array in side]
            return links.send_fsdp(
                order.run(
                    lambda *arrays: jnp.concatenate(
                        [links.sum_cores(*arrays[i : i + 2]) for i in range(0, len(arrays), 2)], axis=1
                    ),
                    *arrays,
                )
            )

    def cross_exit(grad_q, grad_k, grad_v, cross_query, cross_first, after_self, gain_row, grad_after_cross):
        grad_kv = jnp.concatenate([grad_k, grad_v], axis=1)
        grad_normed = times_transposed(grad_q, cross_query)
        grad_encoded = times_transposed(grad_kv, cross_first)
        grad_input, grad_gain, grad_bias = norm_backward(after_self, gain_row, grad_normed)
        grad_after_self = grad_after_cross + grad_input
        return grad_after_self, grad_encoded, grad_gain, grad_bias

    grad_after_self, grad_encoded, grad_gain_1, grad_bias_1 = order.run(
        cross_exit, grad_q, grad_k, grad_v, cross_query, cross_first, after_self, gain_table[1], grad_after_cross
    )
    if links.pairwise:
        cross_sides = exchange(cross_sides, 0)
    else:
        cross_part = links.scatter_whole(*[jnp.concatenate(side, axis=1) for side in (cross_send, cross_keep)])

    def self_entry(grad_after_self, self_output_low, self_mixed):
        self_branch = grad_after_self.astype(low)
        return (
            times_transposed(self_branch, self_output_low).astype(low),
            weight_gradient(links.positions(True), self_mixed, [self_branch]),
        )

    grad_self_mixed, self_out = order.run(self_entry, grad_after_self, self_output_low, self_mixed)
    grad_q, grad_k, grad_v = order.run(
        lambda query_key, self_values, self_mixed, grad_self_mixed, self_totals: attention_backward(
            unit_lengths,
            query_key,
            0,
            query_key,
            width // LANES,
            self_values,
            0,
            self_mixed,
            grad_self_mixed,
            self_totals,
            True,
        ),
        query_key,
        self_values,
        self_mixed,
        grad_self_mixed,
        self_totals,
    )
    if links.pairwise:
        cross_sides = exchange(cross_sides, 1)
        feed_chips = order.after(feed_chips)
        feed_part = lax.psum_scatter(feed_chips, "fsdp", scatter_dimension=0, tiled=True)
    first_send, first_keep = order.run(
        lambda *grads: weight_gradient(links.positions(False), normed_self, list(grads)), grad_q, grad_k
    )
    if links.pairwise:
        first_other = links.swap_core(first_send)
    second_send, second_keep = order.run(
        lambda grad, *out: [
            jnp.concatenate(pair, axis=1)
            for pair in zip(weight_gradient(links.positions(True), normed_self, [grad]), out)
        ],
        grad_v,
        *self_out,
    )
    if links.pairwise:
        self_sides = [(first_keep, first_other), (second_keep, links.swap_core(second_send))]
        cross_parts = finish(cross_sides)
        self_sides = exchange(self_sides, 0)

    def self_exit(grad_q, grad_k, grad_v, self_first, self_value, gain_row, grad_after_self, *others):
        grad_qk = jnp.concatenate([grad_q, grad_k], axis=1)
        grad_normed = times_transposed(grad_qk, self_first) + times_transposed(grad_v, self_value)
        grad_input, grad_gain, grad_bias = norm_backward(layer_input, gain_row, grad_normed)
        grad_tables = jnp.stack([grad_gain, *others[:3], grad_bias, *others[3:]])
        return grad_after_self + grad_input, jnp.pad(grad_tables.T, ((0, 0), (0, LANES - 8))).astype(low)

    grad_states, grad_tables = order.run(
        self_exit,
        grad_q,
        grad_k,
        grad_v,
        self_first,
        self_value,
        gain_table[0],
        grad_after_self,
        grad_gain_1,
        grad_gain_2,
        grad_gain_3,
        grad_bias_1,
        grad_bias_2,
        grad_bias_3,
    )
    table_send, table_keep = links.halves(grad_tables, False)
    if links.pairwise:
        cross_part = order.run(links.sum_fsdp, cross_parts)
        table_goes, table_stays = links.first_pair(table_keep, links.swap_core(table_send))
        table_side = (table_stays, links.swap(table_goes, links.bit(0, False)))
        self_sides = exchange(self_sides, 1)
        feed_part = order.run(lambda part: part.astype(jnp.float32), feed_part)
        table_goes, table_stays = links.first_pair(*table_side)
        table_side = (table_stays, links.swap(table_goes, links.bit(1, False)))
        self_part = links.sum_fsdp(finish(self_sides + [table_side]))
        feed_in_part, feed_out_part = feed_part[:, : 4 * width], feed_part[:, 4 * width :]
        feed_out_part = jnp.concatenate(
            [feed_out_part[:, at * width : (at + 1) * width] for at in range(4)], axis=0
        )
    else:
        self_part = jnp.concatenate(
            [
                links.scatter_whole(*pair)
                for pair in ((first_send, first_keep), (second_send, second_keep), (table_send, table_keep))
            ],
            axis=1,
        )
    self_in_part, self_out_part = self_part[:, : 3 * width], self_part[:, 3 * width : 4 * width]
    table_part = self_part[:, 4 * width :]
    cross_in_part = jnp.concatenate([cross_part[:, split : 3 * width], cross_part[:, :split]], axis=1)
    cross_out_part = cross_part[:, 3 * width :]

    return (
        block_output[None],
        grad_states[None],
        grad_encoded[None],
        self_in_part,
        self_out_part,
        cross_in_part,
        cross_out_part,
        feed_in_part,
        feed_out_part,
        table_part[:, :4].T,
        table_part[:, 4:8].T,
    )


def solution(mesh):
    dp_count, fsdp_count = mesh.shape["dp"], mesh.shape["fsdp"]
    split = Mesh(mesh.devices.reshape(dp_count // 2, 2, fsdp_count), BOTH)
    return jax.shard_map(
        body,
        mesh=split,
        in_specs=(
            P(BOTH, None, None),
            P(BOTH, None, None),
            P(BOTH, None, None),
            P(BOTH),
            P(BOTH),
            P(BOTH, None),
            P(BOTH, None),
            P(BOTH, None),
            P(BOTH, None),
            P(BOTH, None),
            P(BOTH, None),
            P(None, BOTH),
            P(None, BOTH),
        ),
        out_specs=(
            P(BOTH, None, None),
            P(BOTH, None, None),
            P(BOTH, None, None),
            P(BOTH, None),
            P(BOTH, None),
            P(BOTH, None),
            P(BOTH, None),
            P(BOTH, None),
            P(BOTH, None),
            P(None, BOTH),
            P(None, BOTH),
        ),
        check_vma=False,
    )
```

time: 825 us -> 605 us (0.73)
  starting transfers between devices: 145 us -> 31.3 us
  waiting for transfers between devices: 228 us -> 159 us
  Pallas kernels: 257 us -> 202 us
  between operations: 9.13 us -> 32.2 us
  matrix products: 69.3 us -> 51.8 us
  other arithmetic: 61.8 us -> 76.1 us
    ppermute x69 -> x23, waiting for transfers between devices: 161 us -> 69.3 us  [the longest x14 68.1 us: swap(): return lax.ppermute(array, 'h', [(i, i ^ bit) for i in range(self.h_count)])]
    ppermute x39 -> x3, starting transfers between devices: 96.6 us -> 5.7 us  [swap_fsdp(): lax.ppermute(array, 'fsdp', [(i, i ^ bit) for i in range(self.fsdp_count)])]
    pallas_call x20 -> x11, Pallas kernels: 174 us -> 120 us  [the longest x6 39.3 us: weight_gradient(): pl.pallas_call(functools.partial(weight_gradient_kernel, starts), grid_sp...]
    ppermute x39 -> x3, waiting for transfers between devices: 67.4 us -> 24.9 us  [swap_fsdp(): lax.ppermute(array, 'fsdp', [(i, i ^ bit) for i in range(self.fsdp_count)])]
    all_gather x0 -> x1, waiting for transfers between devices: none -> 35 us  [gather(): return lax.all_gather(shard, BOTH, axis=0, tiled=True)]
    ppermute x69 -> x23, starting transfers between devices: 48.9 us -> 17.7 us  [the longest x14 15.7 us: swap(): return lax.ppermute(array, 'h', [(i, i ^ bit) for i in range(self.h_count)])]
    all_to_all x0 -> x2, waiting for transfers between devices: none -> 23.8 us  [send_fsdp(): return lax.all_to_all(grad, 'fsdp', 0, 0, tiled=True)]
    dot_general x12 -> x6, matrix products: 43.9 us -> 25 us  [product(): return jnp.dot(left, right, preferred_element_type=jnp.float32)]
  transfers between devices with their start and end apart: 108 -> 31, of which waited for: 38 -> 12; matrix products, arithmetic and copies ran while one was open for 13% -> 20% of each run, Pallas kernels for 16% -> 19%
where the time goes in v2:
time: 605 us; the launch traced here: 598 us
  Pallas kernels  202 us (33%)
  waiting for transfers between devices  159 us (26%)
  other arithmetic  76.1 us (13%)
  matrix products  51.8 us (9%)
  local copies, waits for them, and re-layouts  45.3 us (7%)
  between operations  32.2 us (5%)
  starting transfers between devices  31.3 us (5%)
    ppermute x14, waiting for transfers between devices, swap(): return lax.ppermute(array, 'h', [(i, i ^ bit) for i in range(self.h_count)])  68.1 us
    pallas_call x2, Pallas kernels, attention_backward(): pl.pallas_call(functools.partial(attention_backward_kernel, causal), grid...  43.8 us
    pallas_call x6, Pallas kernels, weight_gradient(): pl.pallas_call(functools.partial(weight_gradient_kernel, starts), grid_sp...  39.3 us
    pallas_call x2, Pallas kernels, attention_forward(): pl.pallas_call(functools.partial(attention_forward_kernel, causal), grid_...  38.7 us
    all_gather x1, waiting for transfers between devices, gather(): return lax.all_gather(shard, BOTH, axis=0, tiled=True)  35 us
    pallas_call x1, Pallas kernels, feed_backward(): pl.pallas_call(functools.partial(feed_backward_kernel, rows, count // 2),...  34.8 us
    pallas_call x1, Pallas kernels, feed_forward(): pl.pallas_call(functools.partial(feed_forward_kernel, rows), grid=(hidden...  34.2 us
    convert_element_type x16, other arithmetic, sum_cores(): (keep.astype(jnp.float32) + other.astype(jnp.float32)).astype(jnp.bfloat16)  33.8 us
  transfers between devices with their start and end apart: 31, of which 12 were waited for; matrix products, arithmetic and copies ran while one was open for 20% of the time, Pallas kernels for 19%

profile of v2, /device:TPU:0, one launch (start us, length us, event | category | flops | bytes accessed | tf_op | source)
XLA Modules:
  0.0 598.1 jit_solution(11715645747181638828)
XLA Ops:
  11.9 3.1 collective-permute-start
  15.0 2.6 collective-permute-start.1
  18.1 8.4 %collective-permute-done.refs_1_ = bf16[32,4224]{1,0:T(8,128)(2,1)S(1)} collective-permute-done((bf16[32,4224]{1,0:T(8,128)(2,1)S(1)}, bf16[32,4224]{1,0:T(8,128)(2,1)S(1)}, u32[]{:S(2)}, u32[]{:S(2)}) %collective-permute-start) | collective-permute-done | bytes 270368 | tf_op jit(solution)/shard_map/ppermute | solution.py:535
  26.5 14.5 %collective-permute-done.1.refs_2_ = bf16[32,4224]{1,0:T(8,128)(2,1)S(1)} collective-permute-done((bf16[32,4224]{1,0:T(8,128)(2,1)S(1)}, bf16[32,4224]{1,0:T(8,128)(2,1)S(1)}, u32[]{:S(2)}, u32[]{:S(2)}) %collective-permute-start.1) | collective-permute-done | bytes 270368 | tf_op jit(solution)/shard_map/ppermute | solution.py:535
  41.0 2.0 collective-permute-done.2.refs_3_
  43.7 2.7 place_rows.3
  51.7 10.3 %collective-permute-done.3 = bf16[128,2048]{1,0:T(8,128)(2,1)S(1)} collective-permute-done((bf16[128,2048]{1,0:T(8,128)(2,1)S(1)}, bf16[128,2048]{1,0:T(8,128)(2,1)S(1)}, u32[]{:S(2)}, u32[]{:S(2)}) %collective-permute-start.3) | collective-permute-done | bytes 524320 | tf_op jit(solution)/shard_map/ppermute | solution.py:529
  64.4 30.2 %collective-permute-done.5 = bf16[256,2048]{1,0:T(8,128)(2,1)S(1)} collective-permute-done((bf16[256,2048]{1,0:T(8,128)(2,1)S(1)}, bf16[256,2048]{1,0:T(8,128)(2,1)S(1)}, u32[]{:S(2)}, u32[]{:S(2)}) %collective-permute-start.5) | collective-permute-done | bytes 1048608 | tf_op jit(solution)/shard_map/ppermute | solution.py:529
  94.6 12.6 %collective-permute-done.6 = bf16[256,2176]{1,0:T(8,128)(2,1)S(1)} collective-permute-done((bf16[256,2176]{1,0:T(8,128)(2,1)S(1)}, bf16[256,2176]{1,0:T(8,128)(2,1)S(1)}, u32[]{:S(2)}, u32[]{:S(2)}) %collective-permute-start.6) | collective-permute-done | bytes 1114144 | tf_op jit(solution)/shard_map/ppermute | solution.py:529
  114.0 1.8 convert_bitcast_fusion
  117.0 4.2 place_rows.4
  121.2 4.6 place_rows.5
  126.9 2.1 slice_reduce_fusion.1
  129.1 3.0 fusion.38
  134.3 3.0 convolution_convert_fusion.5.v_ref
  137.3 4.9 convolution_convert_fusion.q_ref.k_ref
  142.2 21.3 %attention_forward.2 = (bf16[768,1024]{1,0:T(8,128)(2,1)}, f32[8,2,768]{2,1,0:T(2,128)}) custom-call(s32[1]{0:T(128)} %copy.85.limit_ref, bf16[768,2048]{1,0:T(8,128)(2,1)} %convolution_convert_fusion.q_ref.k_ref, bf16[768,2048]{1,0:T(8,128)(2,1)} %convolution_convert_fusion.q_ref.k_ref, bf16[768,1024]{1,0:T(8,128)(2,1)} %convolution_convert_fusion.5.v_ref), custom_call_target="tpu_custom_call" | custom-call | flops 1024 | bytes 1024 | tf_op jit(solution)/shard_map/attention_forward/pallas_call | solution.py:120
  163.6 3.3 fusion.42
  169.1 35.0 %all-gather.2.cloned.1.call-done.input_ref.output_ref = bf16[1024,12288]{1,0:T(8,128)(2,1)} async-done(((bf16[32,12288]{1,0:T(8,128)(2,1)}), bf16[1024,12288]{1,0:T(8,128)(2,1)}) %all-gather.2.cloned.1.call-update) | async-done | bytes 25165840 | tf_op jit(solution)/shard_map/all_gather | solution.py:538
  204.1 4.6 convolution_convert_fusion.4.q_ref
  208.7 4.4 fusion.6.k_ref.v_ref
  213.1 17.3 %attention_forward.3 = (bf16[768,1024]{1,0:T(8,128)(2,1)}, f32[8,2,768]{2,1,0:T(2,128)}) custom-call(s32[1]{0:T(128)S(6)} %copy.86.limit_ref, bf16[768,1024]{1,0:T(8,128)(2,1)} %convolution_convert_fusion.4.q_ref, bf16[256,2048]{1,0:T(8,128)(2,1)} %fusion.6.k_ref.v_ref, bf16[256,2048]{1,0:T(8,128)(2,1)} %fusion.6.k_ref.v_ref), custom_call_target="tpu_custom_call" | custom-call | flops 1024 | bytes 1024 | tf_op jit(solution)/shard_map/attention_forward/pallas_call | solution.py:120
  230.4 4.9 fusion.43
  238.0 34.2 %feed_forward.1 = (bf16[768,4096]{1,0:T(8,128)(2,1)}, bf16[768,4096]{1,0:T(8,128)(2,1)}, f32[768,1024]{1,0:T(8,128)}) custom-call(bf16[768,1024]{1,0:T(8,128)(2,1)} %add_convert_fusion.2.normed_ref, bf16[1024,12288]{1,0:T(8,128)(2,1)} %all-gather.2.cloned.1.call-done.input_ref.output_ref, ...), custom_call_target="tpu_custom_call" | custom-call | flops 1024 | bytes 1024 | tf_op jit(solution)/shard_map/feed_forward/pallas_call | solution.py:301
  272.3 2.3 reduce_sum.293
  276.6 1.8 multiply_reduce_fusion.3
  278.4 3.4 fusion.35
  281.8 34.8 %feed_backward.1 = (bf16[512,4096]{1,0:T(8,128)(2,1)}, bf16[512,4096]{1,0:T(8,128)(2,1)}, bf16[1024,4096]{1,0:T(8,128)(2,1)}, f32[768,1024]{1,0:T(8,128)}) custom-call(s32[8]{0:T(128)} %fusion.23.positions_ref, bf16[768,1024]{1,0:T(8,128)(2,1)} %get-tuple-element.184.grad_ref, bf16[768,1024]{1,0:T(8,128)(2,1)} %add_convert_fusion.2.normed_ref, ...), custom_call_target="tpu_custom_call" | custom-call | flops 1024 | bytes 1024 | tf_op jit(solution)/shard_map/feed_backward/pallas_call | solution.py:374
  316.7 6.1 %fusion.37 = (bf16[512,4096]{1,0:T(8,128)(2,1)}, bf16[512,4096]{1,0:T(8,128)(2,1)}) fusion(bf16[1024,4096]{1,0:T(8,128)(2,1)} %get-tuple-element.193), kind=kLoop, calls=%fused_computation.196 | loop fusion | bytes 16777216 | tf_op jit(solution)/shard_map/slice | solution.py:737
  323.8 4.8 fusion.36
  332.7 2.9 fusion.34
  335.6 5.9 weight_gradient.6
  341.6 4.7 convolution_convert_fusion.3.grad_ref
  346.3 7.7 %add_convert_fusion = bf16[512,8192]{1,0:T(8,128)(2,1)} fusion(bf16[512,4096]{1,0:T(8,128)(2,1)S(1)} %copy-done.10, bf16[512,4096]{1,0:T(8,128)(2,1)S(1)} %copy-done.23, bf16[512,4096]{1,0:T(8,128)(2,1)} %collective-permute-done.10, bf16[512,4096]{1,0:T(8,128)(2,1)} %collective-permute-done.9), kind=kLoop, calls=%fused_computation | loop fusion | flops 41943040 | bytes 25165824 | tf_op jit(solution)/shard_map/convert_element_type | solution.py:580
  354.0 17.8 %attention_backward.2 = (bf16[768,1024]{1,0:T(8,128)(2,1)}, bf16[256,1024]{1,0:T(8,128)(2,1)}, bf16[256,1024]{1,0:T(8,128)(2,1)}) custom-call(s32[1]{0:T(128)S(6)} %copy.86.limit_ref, bf16[768,1024]{1,0:T(8,128)(2,1)} %convolution_convert_fusion.4.q_ref, bf16[256,2048]{1,0:T(8,128)(2,1)} %fusion.6.k_ref.v_ref, bf16[256,2048]{1,0:T(8,128)(2,1)} %fusion.6.k_ref.v_ref, ...), custom_call_target="tpu_custom_call" | custom-call | flops 1024 | bytes 1024 | tf_op jit(solution)/shard_map/attention_backward/pallas_call | solution.py:197
  371.9 6.3 %weight_gradient.7 = (bf16[512,1024]{1,0:T(8,128)(2,1)}, bf16[512,1024]{1,0:T(8,128)(2,1)}) custom-call(s32[8]{0:T(128)} %get-tuple-element.422.positions_ref, bf16[768,1024]{1,0:T(8,128)(2,1)} %copy-done.17, bf16[768,1024]{1,0:T(8,128)(2,1)} %get-tuple-element.221.refs_0_), custom_call_target="tpu_custom_call" | custom-call | flops 1024 | bytes 1024 | tf_op jit(solution)/shard_map/weight_gradient/pallas_call | solution.py:433
  378.2 6.2 %weight_gradient.8 = (bf16[512,2048]{1,0:T(8,128)(2,1)}, bf16[512,2048]{1,0:T(8,128)(2,1)}) custom-call(s32[8]{0:T(128)} %get-tuple-element.423.positions_ref, bf16[256,1024]{1,0:T(8,128)(2,1)} %bitcast.96, bf16[256,1024]{1,0:T(8,128)(2,1)} %get-tuple-element.224.refs_0_, bf16[256,1024]{1,0:T(8,128)(2,1)} %get-tuple-element.225.refs_1_), custom_call_target="tpu_custom_call" | custom-call | flops 1024 | bytes 1024 | tf_op jit(solution)/shard_map/weight_gradient/pallas_call | solution.py:433
  384.7 1.9 pad_maximum_fusion.1
  387.6 2.4 multiply_reduce_fusion.4
  390.2 2.2 slice-done
  392.4 2.2 fusion.10
  396.2 4.3 add_convert_fusion.11
  402.0 1.8 add_convert_fusion.9
  406.5 6.0 weight_gradient.9
  412.5 4.6 convolution_convert_fusion.2.grad_ref
  417.1 26.0 %attention_backward.3 = (bf16[768,1024]{1,0:T(8,128)(2,1)}, bf16[768,1024]{1,0:T(8,128)(2,1)}, bf16[768,1024]{1,0:T(8,128)(2,1)}) custom-call(s32[1]{0:T(128)} %copy.85.limit_ref, bf16[768,2048]{1,0:T(8,128)(2,1)} %convolution_convert_fusion.q_ref.k_ref, bf16[768,2048]{1,0:T(8,128)(2,1)} %convolution_convert_fusion.q_ref.k_ref, ...), custom_call_target="tpu_custom_call" | custom-call | flops 1024 | bytes 1024 | tf_op jit(solution)/shard_map/attention_backward/pallas_call | solution.py:197
  443.2 2.6 add_convert_fusion.23
  445.7 2.6 add_convert_fusion.21
  448.3 8.7 %weight_gradient.10 = (bf16[512,2048]{1,0:T(8,128)(2,1)}, bf16[512,2048]{1,0:T(8,128)(2,1)}) custom-call(s32[8]{0:T(128)} %get-tuple-element.423.positions_ref, bf16[768,1024]{1,0:T(8,128)(2,1)} %copy-done.11, bf16[768,1024]{1,0:T(8,128)(2,1)} %get-tuple-element.266.refs_0_, bf16[768,1024]{1,0:T(8,128)(2,1)} %get-tuple-element.267.refs_1_), custom_call_target="tpu_custom_call" | custom-call | flops 1024 | bytes 1024 | tf_op jit(solution)/shard_map/weight_gradient/pallas_call | solution.py:433
  457.0 6.2 %weight_gradient.11 = (bf16[512,1024]{1,0:T(8,128)(2,1)}, bf16[512,1024]{1,0:T(8,128)(2,1)}) custom-call(s32[8]{0:T(128)} %get-tuple-element.422.positions_ref, bf16[768,1024]{1,0:T(8,128)(2,1)} %copy-done.11, bf16[768,1024]{1,0:T(8,128)(2,1)} %get-tuple-element.269.refs_0_), custom_call_target="tpu_custom_call" | custom-call | flops 1024 | bytes 1024 | tf_op jit(solution)/shard_map/weight_gradient/pallas_call | solution.py:433
  463.2 2.3 constant_dynamic-update-slice_fusion.11
  491.5 4.3 all-to-all-start
  495.9 4.5 add_convert_fusion.7
  501.9 3.8 add_convert_fusion.5
  506.2 5.1 fusion
  511.4 7.7 %multiply_reduce_fusion = (bf16[1024]{0:T(1024)(128)(2,1)S(1)}, f32[768]{0:T(1024)S(1)}, f32[768]{0:T(1024)S(1)}, bf16[1024]{0:T(1024)(128)(2,1)S(1)}, f32[768,1024]{1,0:T(8,128)}) fusion(bf16[1,768,1024]{2,1,0:T(8,128)(2,1)} %param.15, f32[768]{0:T(1024)S(1)} %add_rsqrt_fusion, f32[768]{0:T(1024)S(1)} %broadcast_multiply_fusion.2, f32[1024]{0:T(1024)S(1)} %copy-done.49, ...), kind=kOutput, calls=%fused_computation.9 | convolution fusion | flops 1619259904 | bytes 11554816 | tf_op jit(solution)/shard_map/dot_general | solution.py:40
  521.1 4.0 multiply_add_fusion
  526.9 3.7 collective-permute-done.20
  530.6 2.4 add_convert_fusion.17
  537.1 11.3 %collective-permute-done.24 = bf16[256,128]{1,0:T(8,128)(2,1)S(1)} collective-permute-done((bf16[256,128]{1,0:T(8,128)(2,1)S(1)}, bf16[256,128]{1,0:T(8,128)(2,1)S(1)}, u32[]{:S(2)}, u32[]{:S(2)}) %collective-permute-start.24) | collective-permute-done | bytes 65568 | tf_op jit(solution)/shard_map/ppermute | solution.py:529
  548.4 1.8 collective-permute-start.25
  550.2 5.9 reduce-scatter.5.cloned.1.call-done
  557.5 3.5 all-to-all-start.1
  564.3 23.8 %all-to-all-done.1 = bf16[4,32,4224]{2,1,0:T(8,128)(2,1)S(1)} async-done(((bf16[4,32,4224]{2,1,0:T(8,128)(2,1)}), bf16[4,32,4224]{2,1,0:T(8,128)(2,1)S(1)}, u32[]{:S(2)}, u32[]{:S(2)}) %all-to-all-start.1) | async-done | bytes 1081376 | tf_op jit(solution)/shard_map/all_to_all | solution.py:583
  (275 shorter events, 70.5 us)
Async XLA Ops:
  7.2 3.5 copy-start.46
  7.2 4.5 copy-start.51
  7.2 4.5 copy-start.52
  7.2 4.6 copy-start.47
  7.2 4.6 copy-start.42
  7.2 196.9 %all-gather.2.cloned.1.call-start = ((), (), s32[]{:S(2)}) async-start(), calls=%async_computation.4 | async-start | bytes 25952256 | tf_op jit(solution)/shard_map/all_gather | solution.py:538
  11.6 499.7 %reduce-scatter.3.cloned.1.call-start = ((), (), s32[]{:S(2)}) async-start(), calls=%async_computation.5 | async-start | bytes 10485760 | tf_op jit(solution)/shard_map/reduce_scatter | solution.py:596
  11.9 31.2 %copy-start.35 = (bf16[32,4224]{1,0:T(8,128)(2,1)}, bf16[32,4224]{1,0:T(8,128)(2,1)S(1)}, u32[]{:S(2)}) copy-start(bf16[32,4224]{1,0:T(8,128)(2,1)S(1)} %fusion.16.refs_0_) | copy-start | bytes 811012
  11.9 14.6 %collective-permute-start = (bf16[32,4224]{1,0:T(8,128)(2,1)S(1)}, bf16[32,4224]{1,0:T(8,128)(2,1)S(1)}, u32[]{:S(2)}, u32[]{:S(2)}) collective-permute-start(bf16[32,4224]{1,0:T(8,128)(2,1)S(1)} %fusion.16.refs_0_), channel_id=1, source_target_pairs={{0,1},{1,0},{2,3},{3,2},{4,5},{5,4},{6,7},{7,6},{8,9},{9,8},{10,11... | collective-permute-start | bytes 811016 | tf_op jit(solution)/shard_map/ppermute | solution.py:535
  15.0 26.1 %collective-permute-start.1 = (bf16[32,4224]{1,0:T(8,128)(2,1)S(1)}, bf16[32,4224]{1,0:T(8,128)(2,1)S(1)}, u32[]{:S(2)}, u32[]{:S(2)}) collective-permute-start(bf16[32,4224]{1,0:T(8,128)(2,1)S(1)} %fusion.16.refs_0_), channel_id=1, source_target_pairs={{0,2},{1,3},{2,0},{3,1},{4,6},{5,7},{6,4},{7,5},{8,10},{9,11},{10,... | collective-permute-start | bytes 811016 | tf_op jit(solution)/shard_map/ppermute | solution.py:535
  17.6 25.4 %collective-permute-start.2 = (bf16[32,4224]{1,0:T(8,128)(2,1)S(1)}, bf16[32,4224]{1,0:T(8,128)(2,1)S(1)}, u32[]{:S(2)}, u32[]{:S(2)}) collective-permute-start(bf16[32,4224]{1,0:T(8,128)(2,1)S(1)} %fusion.16.refs_0_), channel_id=1, source_target_pairs={{0,3},{1,2},{2,1},{3,0},{4,7},{5,6},{6,5},{7,4},{8,11},{9,10},{10,... | collective-permute-start | bytes 811016 | tf_op jit(solution)/shard_map/ppermute | solution.py:535
  26.5 16.5 %copy-start.43 = (bf16[32,4224]{1,0:T(8,128)(2,1)}, bf16[32,4224]{1,0:T(8,128)(2,1)S(1)}, u32[]{:S(2)}) copy-start(bf16[32,4224]{1,0:T(8,128)(2,1)S(1)} %collective-permute-done.refs_1_) | copy-start | bytes 811012
  47.5 14.5 %collective-permute-start.4 = (bf16[128,2176]{1,0:T(8,128)(2,1)S(1)}, bf16[128,2176]{1,0:T(8,128)(2,1)S(1)}, u32[]{:S(2)}, u32[]{:S(2)}) collective-permute-start(bf16[128,2176]{1,0:T(8,128)(2,1)S(1)} %slice.403), channel_id=1, source_target_pairs={{0,16},{8,24},{16,0},{24,8},{1,17},{9,25},{17,1},{25,9},{2,18},{10... | collective-permute-start | bytes 1671176 | tf_op jit(solution)/shard_map/ppermute | solution.py:529
  50.2 11.9 %collective-permute-start.3 = (bf16[128,2048]{1,0:T(8,128)(2,1)S(1)}, bf16[128,2048]{1,0:T(8,128)(2,1)S(1)}, u32[]{:S(2)}, u32[]{:S(2)}) collective-permute-start(bf16[128,2048]{1,0:T(8,128)(2,1)S(1)} %slice.402), channel_id=1, source_target_pairs={{0,8},{8,0},{16,24},{24,16},{1,9},{9,1},{17,25},{25,17},{2,10},{10... | collective-permute-start | bytes 1572872 | tf_op jit(solution)/shard_map/ppermute | solution.py:529
  62.2 45.0 %collective-permute-start.6 = (bf16[256,2176]{1,0:T(8,128)(2,1)S(1)}, bf16[256,2176]{1,0:T(8,128)(2,1)S(1)}, u32[]{:S(2)}, u32[]{:S(2)}) collective-permute-start(bf16[256,2176]{1,0:T(8,128)(2,1)S(1)} %constant_dynamic-update-slice_fusion.2), channel_id=1, source_target_pairs={{0,8},{8,0},{16,24},{24,16},{1,9},{9,1},{17,25},{25,17},{2,10},{10... | collective-permute-start | bytes 3342344 | tf_op jit(solution)/shard_map/ppermute | solution.py:529
  63.8 30.8 %collective-permute-start.5 = (bf16[256,2048]{1,0:T(8,128)(2,1)S(1)}, bf16[256,2048]{1,0:T(8,128)(2,1)S(1)}, u32[]{:S(2)}, u32[]{:S(2)}) collective-permute-start(bf16[256,2048]{1,0:T(8,128)(2,1)S(1)} %constant_dynamic-update-slice_fusion), channel_id=1, source_target_pairs={{0,16},{8,24},{16,0},{24,8},{1,17},{9,25},{17,1},{25,9},{2,18},{10... | collective-permute-start | bytes 3145736 | tf_op jit(solution)/shard_map/ppermute | solution.py:529
  108.2 5.2 copy-start.53
  109.3 7.7 %collective-permute-start.8 = (bf16[512,2176]{1,0:T(8,128)(2,1)}, bf16[512,2176]{1,0:T(8,128)(2,1)}, u32[]{:S(2)}, u32[]{:S(2)}) collective-permute-start(bf16[512,2176]{1,0:T(8,128)(2,1)} %constant_dynamic-update-slice_fusion.6.refs_0_), channel_id=1, source_target_pairs={{0,4},{4,0},{1,5},{5,1},{2,6},{6,2},{3,7},{7,3},{8,12},{12,8},{9,1... | collective-permute-start | bytes 6684680 | tf_op jit(solution)/shard_map/ppermute | solution.py:532
  111.5 5.4 collective-permute-start.7
  129.1 3.7 copy-start.48
  142.2 21.3 %copy-start.7 = (bf16[1,768,1024]{2,1,0:T(8,128)(2,1)S(1)}, bf16[1,768,1024]{2,1,0:T(8,128)(2,1)}, u32[]{:S(2)}) copy-start(bf16[1,768,1024]{2,1,0:T(8,128)(2,1)} %param.15) | copy-start | bytes 4718596
  142.2 21.3 %copy-start.29 = (bf16[1024,1024]{1,0:T(8,128)(2,1)S(1)}, bf16[1024,1024]{1,0:T(8,128)(2,1)}, u32[]{:S(2)}) copy-start(bf16[1024,1024]{1,0:T(8,128)(2,1)} %get-tuple-element.232) | copy-start | bytes 6291460
  169.1 39.6 %copy-start.17 = (bf16[768,1024]{1,0:T(8,128)(2,1)}, bf16[768,1024]{1,0:T(8,128)(2,1)S(1)}, u32[]{:S(2)}) copy-start(bf16[768,1024]{1,0:T(8,128)(2,1)S(1)} %add_convert_fusion.3.x_ref) | copy-start | bytes 4718596
  169.1 39.6 %copy-start.39 = (bf16[1,256,1024]{2,1,0:T(8,128)(2,1)S(1)}, bf16[1,256,1024]{2,1,0:T(8,128)(2,1)}, u32[]{:S(2)}) copy-start(bf16[1,256,1024]{2,1,0:T(8,128)(2,1)} %param.16) | copy-start | bytes 1572868
  322.8 23.5 %collective-permute-start.9 = (bf16[512,4096]{1,0:T(8,128)(2,1)}, bf16[512,4096]{1,0:T(8,128)(2,1)}, u32[]{:S(2)}, u32[]{:S(2)}) collective-permute-start(bf16[512,4096]{1,0:T(8,128)(2,1)} %get-tuple-element.191), channel_id=1, source_target_pairs={{0,4},{4,0},{1,5},{5,1},{2,6},{6,2},{3,7},{7,3},{8,12},{12,8},{9,1... | collective-permute-start | bytes 12582920 | tf_op jit(solution)/shard_map/ppermute | solution.py:532
  323.0 23.2 %collective-permute-start.10 = (bf16[512,4096]{1,0:T(8,128)(2,1)}, bf16[512,4096]{1,0:T(8,128)(2,1)}, u32[]{:S(2)}, u32[]{:S(2)}) collective-permute-start(bf16[512,4096]{1,0:T(8,128)(2,1)} %get-tuple-element.365), channel_id=1, source_target_pairs={{0,4},{4,0},{1,5},{5,1},{2,6},{6,2},{3,7},{7,3},{8,12},{12,8},{9,1... | collective-permute-start | bytes 12582920 | tf_op jit(solution)/shard_map/ppermute | solution.py:532
  323.8 4.8 copy-start.1
  335.6 6.0 copy-start.16
  341.5 4.7 copy-start.10
  341.5 4.7 copy-start.23
  371.9 12.6 %copy-start.3 = (f32[768,1024]{1,0:T(8,128)S(1)}, f32[768,1024]{1,0:T(8,128)}, u32[]{:S(2)}) copy-start(f32[768,1024]{1,0:T(8,128)} %copy-done.2) | copy-start | bytes 9437188
  384.4 11.6 %collective-permute-start.11 = (bf16[512,2048]{1,0:T(8,128)(2,1)}, bf16[512,2048]{1,0:T(8,128)(2,1)}, u32[]{:S(2)}, u32[]{:S(2)}) collective-permute-start(bf16[512,2048]{1,0:T(8,128)(2,1)} %get-tuple-element.217), channel_id=1, source_target_pairs={{0,4},{4,0},{1,5},{5,1},{2,6},{6,2},{3,7},{7,3},{8,12},{12,8},{9,1... | collective-permute-start | bytes 6291464 | tf_op jit(solution)/shard_map/ppermute | solution.py:532
  386.7 9.3 %collective-permute-start.12 = (bf16[512,2048]{1,0:T(8,128)(2,1)S(1)}, bf16[512,2048]{1,0:T(8,128)(2,1)S(1)}, u32[]{:S(2)}, u32[]{:S(2)}) collective-permute-start(bf16[512,2048]{1,0:T(8,128)(2,1)S(1)} %pad_maximum_fusion.1), channel_id=1, source_target_pairs={{0,4},{4,0},{1,5},{5,1},{2,6},{6,2},{3,7},{7,3},{8,12},{12,8},{9,1... | collective-permute-start | bytes 6291464 | tf_op jit(solution)/shard_map/ppermute | solution.py:532
  396.0 9.2 %copy-start.5 = (f32[768,1024]{1,0:T(8,128)}, f32[768,1024]{1,0:T(8,128)S(1)}, u32[]{:S(2)}) copy-start(f32[768,1024]{1,0:T(8,128)S(1)} %multiply_add_fusion.1) | copy-start | bytes 9437188
  400.5 3.8 copy-start.8
  400.5 42.7 %collective-permute-start.13 = (bf16[256,2048]{1,0:T(8,128)(2,1)}, bf16[256,2048]{1,0:T(8,128)(2,1)}, u32[]{:S(2)}, u32[]{:S(2)}) collective-permute-start(bf16[256,2048]{1,0:T(8,128)(2,1)} %get-tuple-element.376), channel_id=1, source_target_pairs={{0,16},{8,24},{16,0},{24,8},{1,17},{9,25},{17,1},{25,9},{2,18},{10... | collective-permute-start | bytes 3145736 | tf_op jit(solution)/shard_map/ppermute | solution.py:529
  403.7 39.4 %collective-permute-start.14 = (bf16[256,2048]{1,0:T(8,128)(2,1)}, bf16[256,2048]{1,0:T(8,128)(2,1)}, u32[]{:S(2)}, u32[]{:S(2)}) collective-permute-start(bf16[256,2048]{1,0:T(8,128)(2,1)} %get-tuple-element.374), channel_id=1, source_target_pairs={{0,8},{8,0},{16,24},{24,16},{1,9},{9,1},{17,25},{25,17},{2,10},{10... | collective-permute-start | bytes 3145736 | tf_op jit(solution)/shard_map/ppermute | solution.py:529
  406.5 6.0 copy-start.18
  457.0 8.5 %copy-start.36 = (bf16[512,1024]{1,0:T(8,128)(2,1)S(1)}, bf16[512,1024]{1,0:T(8,128)(2,1)}, u32[]{:S(2)}) copy-start(bf16[512,1024]{1,0:T(8,128)(2,1)} %get-tuple-element.256) | copy-start | bytes 3145732
  457.0 38.8 %collective-permute-start.15 = (bf16[512,2048]{1,0:T(8,128)(2,1)}, bf16[512,2048]{1,0:T(8,128)(2,1)}, u32[]{:S(2)}, u32[]{:S(2)}) collective-permute-start(bf16[512,2048]{1,0:T(8,128)(2,1)} %get-tuple-element.251), channel_id=1, source_target_pairs={{0,4},{4,0},{1,5},{5,1},{2,6},{6,2},{3,7},{7,3},{8,12},{12,8},{9,1... | collective-permute-start | bytes 6291464 | tf_op jit(solution)/shard_map/ppermute | solution.py:532
  457.0 10.0 %copy-start.50 = (s32[8]{0:T(128)S(1)}, s32[8]{0:T(128)}, u32[]{:S(2)}) copy-start(s32[8]{0:T(128)} %get-tuple-element.423.positions_ref) | copy-start | bytes 100
  465.5 22.5 %copy-start.27 = (bf16[128,2048]{1,0:T(8,128)(2,1)S(1)}, bf16[128,2048]{1,0:T(8,128)(2,1)}, u32[]{:S(2)}) copy-start(bf16[128,2048]{1,0:T(8,128)(2,1)} %get-tuple-element.259) | copy-start | bytes 1572868
  466.6 22.7 %copy-start.26 = (bf16[128,2048]{1,0:T(8,128)(2,1)S(1)}, bf16[128,2048]{1,0:T(8,128)(2,1)}, u32[]{:S(2)}) copy-start(bf16[128,2048]{1,0:T(8,128)(2,1)} %get-tuple-element.257) | copy-start | bytes 1572868
  466.6 29.3 %collective-permute-start.16 = (bf16[512,2048]{1,0:T(8,128)(2,1)}, bf16[512,2048]{1,0:T(8,128)(2,1)}, u32[]{:S(2)}, u32[]{:S(2)}) collective-permute-start(bf16[512,2048]{1,0:T(8,128)(2,1)} %constant_dynamic-update-slice_fusion.10), channel_id=1, source_target_pairs={{0,4},{4,0},{1,5},{5,1},{2,6},{6,2},{3,7},{7,3},{8,12},{12,8},{9,1... | collective-permute-start | bytes 6291464 | tf_op jit(solution)/shard_map/ppermute | solution.py:532
  467.1 20.9 %collective-permute-start.17 = (bf16[128,2048]{1,0:T(8,128)(2,1)}, bf16[128,2048]{1,0:T(8,128)(2,1)}, u32[]{:S(2)}, u32[]{:S(2)}) collective-permute-start(bf16[128,2048]{1,0:T(8,128)(2,1)} %get-tuple-element.385), channel_id=1, source_target_pairs={{0,8},{8,0},{16,24},{24,16},{1,9},{9,1},{17,25},{25,17},{2,10},{10... | collective-permute-start | bytes 1572872 | tf_op jit(solution)/shard_map/ppermute | solution.py:529
  468.8 19.3 %collective-permute-start.18 = (bf16[128,2048]{1,0:T(8,128)(2,1)}, bf16[128,2048]{1,0:T(8,128)(2,1)}, u32[]{:S(2)}, u32[]{:S(2)}) collective-permute-start(bf16[128,2048]{1,0:T(8,128)(2,1)} %get-tuple-element.383), channel_id=1, source_target_pairs={{0,16},{8,24},{16,0},{24,8},{1,17},{9,25},{17,1},{25,9},{2,18},{10... | collective-permute-start | bytes 1572872 | tf_op jit(solution)/shard_map/ppermute | solution.py:529
  491.5 33.6 %all-to-all-start = ((bf16[4,32,4096]{2,1,0:T(8,128)(2,1)}), bf16[4,32,4096]{2,1,0:T(8,128)(2,1)}, u32[]{:S(2)}, u32[]{:S(2)}) async-start(bf16[4,32,4096]{2,1,0:T(8,128)(2,1)} %bitcast.10), calls=%async_computation | async-start | bytes 2097152 | tf_op jit(solution)/shard_map/all_to_all | solution.py:583
  495.8 60.4 %reduce-scatter.5.cloned.1.call-start = ((), (), s32[]{:S(2)}) async-start(), calls=%async_computation.6 | async-start | bytes 2621440 | tf_op jit(solution)/shard_map/reduce_scatter | solution.py:868
  495.9 10.3 %copy-start.32 = (bf16[768,1024]{1,0:T(8,128)(2,1)S(1)}, bf16[768,1024]{1,0:T(8,128)(2,1)}, u32[]{:S(2)}) copy-start(bf16[768,1024]{1,0:T(8,128)(2,1)} %get-tuple-element.267.refs_1_) | copy-start | bytes 4718596
  500.4 5.8 copy-start.20
  500.4 5.8 copy-start.31
  500.4 26.6 %collective-permute-start.19 = (bf16[256,2048]{1,0:T(8,128)(2,1)}, bf16[256,2048]{1,0:T(8,128)(2,1)}, u32[]{:S(2)}, u32[]{:S(2)}) collective-permute-start(bf16[256,2048]{1,0:T(8,128)(2,1)} %get-tuple-element.372), channel_id=1, source_target_pairs={{0,16},{8,24},{16,0},{24,8},{1,17},{9,25},{17,1},{25,9},{2,18},{10... | collective-permute-start | bytes 3145736 | tf_op jit(solution)/shard_map/ppermute | solution.py:529
  505.7 24.8 %collective-permute-start.20 = (bf16[256,2048]{1,0:T(8,128)(2,1)}, bf16[256,2048]{1,0:T(8,128)(2,1)}, u32[]{:S(2)}, u32[]{:S(2)}) collective-permute-start(bf16[256,2048]{1,0:T(8,128)(2,1)} %get-tuple-element.370), channel_id=1, source_target_pairs={{0,8},{8,0},{16,24},{24,16},{1,9},{9,1},{17,25},{25,17},{2,10},{10... | collective-permute-start | bytes 3145736 | tf_op jit(solution)/shard_map/ppermute | solution.py:529
  506.2 5.1 copy-start.49
  511.4 9.7 %copy-start.6 = (f32[768,1024]{1,0:T(8,128)S(1)}, f32[768,1024]{1,0:T(8,128)}, u32[]{:S(2)}) copy-start(f32[768,1024]{1,0:T(8,128)} %copy-done.5) | copy-start | bytes 9437188
  525.1 5.5 copy-start.21
  526.7 6.6 %copy-start.22 = (bf16[256,2048]{1,0:T(8,128)(2,1)S(1)}, bf16[256,2048]{1,0:T(8,128)(2,1)}, u32[]{:S(2)}) copy-start(bf16[256,2048]{1,0:T(8,128)(2,1)} %get-tuple-element.281) | copy-start | bytes 3145732
  526.7 9.9 %collective-permute-start.23 = (bf16[512,128]{1,0:T(8,128)(2,1)S(1)}, bf16[512,128]{1,0:T(8,128)(2,1)S(1)}, u32[]{:S(2)}, u32[]{:S(2)}) collective-permute-start(bf16[512,128]{1,0:T(8,128)(2,1)S(1)} %pad_maximum_fusion.6), channel_id=1, source_target_pairs={{0,4},{4,0},{1,5},{5,1},{2,6},{6,2},{3,7},{7,3},{8,12},{12,8},{9,1... | collective-permute-start | bytes 393224 | tf_op jit(solution)/shard_map/ppermute | solution.py:532
  533.0 23.2 %collective-permute-start.21 = (bf16[128,2048]{1,0:T(8,128)(2,1)}, bf16[128,2048]{1,0:T(8,128)(2,1)S(1)}, u32[]{:S(2)}, u32[]{:S(2)}) collective-permute-start(bf16[128,2048]{1,0:T(8,128)(2,1)} %get-tuple-element.380), channel_id=1, source_target_pairs={{0,8},{8,0},{16,24},{24,16},{1,9},{9,1},{17,25},{25,17},{2,10},{10... | collective-permute-start | bytes 1572872 | tf_op jit(solution)/shard_map/ppermute | solution.py:529
  534.9 21.3 %collective-permute-start.22 = (bf16[128,2048]{1,0:T(8,128)(2,1)S(1)}, bf16[128,2048]{1,0:T(8,128)(2,1)S(1)}, u32[]{:S(2)}, u32[]{:S(2)}) collective-permute-start(bf16[128,2048]{1,0:T(8,128)(2,1)S(1)} %get-tuple-element.378), channel_id=1, source_target_pairs={{0,16},{8,24},{16,0},{24,8},{1,17},{9,25},{17,1},{25,9},{2,18},{10... | collective-permute-start | bytes 1572872 | tf_op jit(solution)/shard_map/ppermute | solution.py:529
  536.7 11.7 %collective-permute-start.24 = (bf16[256,128]{1,0:T(8,128)(2,1)S(1)}, bf16[256,128]{1,0:T(8,128)(2,1)S(1)}, u32[]{:S(2)}, u32[]{:S(2)}) collective-permute-start(bf16[256,128]{1,0:T(8,128)(2,1)S(1)} %get-tuple-element.405), channel_id=1, source_target_pairs={{0,16},{8,24},{16,0},{24,8},{1,17},{9,25},{17,1},{25,9},{2,18},{10... | collective-permute-start | bytes 196616 | tf_op jit(solution)/shard_map/ppermute | solution.py:529
  548.4 7.7 %collective-permute-start.25 = (bf16[128,128]{1,0:T(8,128)(2,1)S(1)}, bf16[128,128]{1,0:T(8,128)(2,1)S(1)}, u32[]{:S(2)}, u32[]{:S(2)}) collective-permute-start(bf16[128,128]{1,0:T(8,128)(2,1)S(1)} %get-tuple-element.402), channel_id=1, source_target_pairs={{0,8},{8,0},{16,24},{24,16},{1,9},{9,1},{17,25},{25,17},{2,10},{10... | collective-permute-start | bytes 98312 | tf_op jit(solution)/shard_map/ppermute | solution.py:529
  556.5 6.1 %copy-start.25 = (bf16[32,8192]{1,0:T(8,128)(2,1)S(1)}, bf16[32,8192]{1,0:T(8,128)(2,1)}, u32[]{:S(2)}) copy-start(bf16[32,8192]{1,0:T(8,128)(2,1)} %reduce-scatter.5.cloned.1.call-done) | copy-start | bytes 1572868
  557.5 30.5 %all-to-all-start.1 = ((bf16[4,32,4224]{2,1,0:T(8,128)(2,1)}), bf16[4,32,4224]{2,1,0:T(8,128)(2,1)S(1)}, u32[]{:S(2)}, u32[]{:S(2)}) async-start(bf16[4,32,4224]{2,1,0:T(8,128)(2,1)} %bitcast.29), calls=%async_computation.3 | async-start | bytes 2162688 | tf_op jit(solution)/shard_map/all_to_all | solution.py:583
  (22 other events, 48.9 us)
Sparse Core Ops, SparseCore 0:
  11.7 192.3 all-gather.1
  354.1 98.5 reduce-scatter.2
  511.5 44.6 reduce-scatter.4

commit v3 on v2

--- a/solution.py
+++ b/solution.py
@@ -10,20 +10,10 @@
 
 HEAD = 64
 LANES = 128
+AHEAD = 1
 BOTH = ("h", "c", "fsdp")
 VMEM_BYTES = 60 * 1024 * 1024
 SHORT = pl.CostEstimate(flops=1024, transcendentals=0, bytes_accessed=1024)
-TAIL_RATE = 0.2316419
-TAIL_POLY = (
-    0.09252224973357535,
-    0.09042007971374488,
-    0.10265042640370807,
-    0.013551821473999732,
-    0.2252533241128307,
-    -0.2016603378863937,
-    0.24768663093443657,
-    -0.07042413008644138,
-)
 
 
 def product(left, right):
@@ -61,26 +51,41 @@
     return grad_input, jnp.sum(grad * normed, axis=0), jnp.sum(grad, axis=0)
 
 
-def masked_scores(keys, queries, key_limit, causal, query_start):
+def with_bias_lane(matrix, head, bias):
+    lane = lax.broadcasted_iota(jnp.int32, matrix.shape, 1)
+    own = (lane >= head * HEAD) & (lane < (head + 1) * HEAD)
+    rest = jnp.where(lane == (1 - head) * HEAD, bias, 0.0).astype(matrix.dtype)
+    return jnp.where(own, matrix, rest)
+
+
+def key_bias(key_count, key_limit):
+    row = lax.broadcasted_iota(jnp.int32, (key_count, LANES), 0)
+    return jnp.where(row < key_limit, 0.0, -1e30)
+
+
+def masked_scores(keys, queries, diagonal_ref):
     scores = times_transposed(keys, queries)
-    key_count, query_count = scores.shape
-    if not causal:
-        row = lax.broadcasted_iota(jnp.int32, scores.shape, 0)
-        return jnp.where(row < key_limit, scores, -1e30)
-    row = query_start + lax.broadcasted_iota(jnp.int32, (query_count, query_count), 0)
-    column = query_start + lax.broadcasted_iota(jnp.int32, (query_count, query_count), 1)
-    diagonal = jnp.where(
-        (row <= column) & (row < key_limit), scores[query_start:, :], -1e30
-    )
-    if query_start == 0:
-        return diagonal
-    below_row = lax.broadcasted_iota(jnp.int32, (query_start, query_count), 0)
-    below = jnp.where(below_row < key_limit, scores[:query_start, :], -1e30)
-    return jnp.concatenate([below, diagonal], axis=0)
+    if diagonal_ref is None:
+        return scores
+    below = scores.shape[0] - scores.shape[1]
+    diagonal = scores[below:, :] + diagonal_ref[...]
+    return jnp.concatenate([scores[:below, :], diagonal], axis=0) if below else diagonal
+
+
+def set_diagonal(diagonal_ref):
+    @pl.when(pl.program_id(0) == 0)
+    def _():
+        row = lax.broadcasted_iota(jnp.int32, diagonal_ref.shape, 0)
+        column = lax.broadcasted_iota(jnp.int32, diagonal_ref.shape, 1)
+        diagonal_ref[...] = jnp.where(row <= column, 0.0, -1e30)
+
+
+def query_width(row_count, causal):
+    return 256 if causal and row_count % 256 == 0 else row_count
 
 
 def query_blocks(row_count, key_count, causal):
-    width = 256 if row_count % 256 == 0 else row_count
+    width = query_width(row_count, causal)
     return [
         (start, width, start + width if causal else key_count)
         for start in range(0, row_count, width)
@@ -92,24 +97,55 @@
     return (lane >= head * HEAD) & (lane < (head + 1) * HEAD)
 
 
-def attention_forward_kernel(causal, limit_ref, q_ref, k_ref, v_ref, mixed_ref, total_ref, mixed_turned):
-    key_limit = limit_ref[0]
+def staggered(items, first, middle, last, ahead):
+    begun = [first(item) for item in items[:ahead]]
+    waiting = None
+    for at, item in enumerate(items):
+        if at + ahead < len(items):
+            begun.append(first(items[at + ahead]))
+        done = middle(item, begun[at])
+        begun[at] = None
+        if waiting is not None:
+            last(*waiting)
+        waiting = (item, done)
+    last(*waiting)
+
+
+def attention_forward_kernel(
+    causal, limit_ref, q_ref, k_ref, v_ref, mixed_ref, total_ref, mixed_turned, diagonal_ref
+):
     row_count, key_count = q_ref.shape[0], k_ref.shape[0]
+    bias = key_bias(key_count, limit_ref[0])
+    if causal:
+        set_diagonal(diagonal_ref)
+    else:
+        diagonal_ref = None
     values_turned = v_ref[...].T
+    ones = jnp.ones((16, key_count), jnp.bfloat16)
     scaled = q_ref[...] * jnp.bfloat16(HEAD**-0.5)
-    for head in range(2):
-        own = jnp.where(head_lanes(head, scaled.shape), scaled, jnp.zeros_like(scaled))
-        lanes = slice(head * HEAD, (head + 1) * HEAD)
-        for start, width, stop in query_blocks(row_count, key_count, causal):
-            scores = masked_scores(
-                k_ref[:stop, :], own[start : start + width, :], key_limit, causal, start
-            )
-            highest = jnp.max(scores, axis=0, keepdims=True)
-            expanded = jnp.exp(scores - highest)
-            total = jnp.sum(expanded, axis=0, keepdims=True)
-            mixed = product(values_turned[lanes, :stop], expanded.astype(jnp.bfloat16))
-            mixed_turned[lanes, start : start + width] = mixed / total
-            total_ref[0, head : head + 1, start : start + width] = highest + jnp.log(total)
+    queries = [with_bias_lane(scaled, head, 1.0) for head in range(2)]
+    keys = [with_bias_lane(k_ref[...], head, bias) for head in range(2)]
+    lanes = [slice(head * HEAD, (head + 1) * HEAD) for head in range(2)]
+    values = [jnp.concatenate([values_turned[at, :], ones], axis=0) for at in lanes]
+
+    def scores_of(item):
+        head, (start, width, stop) = item
+        return masked_scores(keys[head][:stop, :], queries[head][start : start + width, :], diagonal_ref)
+
+    def expand(item, scores):
+        highest = jnp.max(scores, axis=0, keepdims=True)
+        return highest, jnp.exp(scores - highest).astype(jnp.bfloat16)
+
+    def mix(item, done):
+        head, (start, width, stop) = item
+        highest, expanded = done
+        mixed = product(values[head][:, :stop], expanded)
+        total = mixed[HEAD : HEAD + 1, :]
+        mixed_turned[lanes[head], start : start + width] = mixed[:HEAD, :] / total
+        total_ref[0, head : head + 1, start : start + width] = highest + jnp.log(total)
+
+    items = [(head, block) for block in query_blocks(row_count, key_count, causal) for head in range(2)]
+    staggered(items, scores_of, expand, mix, 2)
     mixed_ref[...] = mixed_turned[...].T.astype(jnp.bfloat16)
 
 
@@ -131,7 +167,10 @@
                 pl.BlockSpec((row_count, LANES), lambda p, s: (0, p)),
                 pl.BlockSpec((1, 2, row_count), lambda p, s: (p, 0, 0)),
             ],
-            scratch_shapes=[pltpu.VMEM((LANES, row_count), jnp.float32)],
+            scratch_shapes=[
+                pltpu.VMEM((LANES, row_count), jnp.float32),
+                pltpu.VMEM((query_width(row_count, causal),) * 2, jnp.float32),
+            ],
         ),
         out_shape=[
             jax.ShapeDtypeStruct((row_count, width), jnp.bfloat16),
@@ -158,31 +197,52 @@
     grad_q_turned,
     grad_k_sum,
     grad_v_sum,
+    diagonal_ref,
 ):
-    key_limit = limit_ref[0]
     row_count, key_count = q_ref.shape[0], k_ref.shape[0]
+    bias = key_bias(key_count, limit_ref[0])
+    if causal:
+        set_diagonal(diagonal_ref)
+    else:
+        diagonal_ref = None
     keys_turned = k_ref[...].T
     scaled = q_ref[...] * jnp.bfloat16(HEAD**-0.5)
     grad = grad_ref[...]
     inner_turned = (grad.astype(jnp.float32) * mixed_ref[...].astype(jnp.float32)).T
     grad_k_sum[...] = jnp.zeros_like(grad_k_sum)
     grad_v_sum[...] = jnp.zeros_like(grad_v_sum)
-    for head in range(2):
-        mask = head_lanes(head, scaled.shape)
-        own = jnp.where(mask, scaled, jnp.zeros_like(scaled))
-        own_grad = jnp.where(mask, grad, jnp.zeros_like(grad))
-        lanes = slice(head * HEAD, (head + 1) * HEAD)
-        inner = jnp.sum(inner_turned[lanes, :], axis=0, keepdims=True)
-        for start, width, stop in query_blocks(row_count, key_count, causal):
-            columns = slice(start, start + width)
-            queries, grads = own[columns, :], own_grad[columns, :]
-            scores = masked_scores(k_ref[:stop, :], queries, key_limit, causal, start)
-            probs = jnp.exp(scores - total_ref[0, head : head + 1, columns])
-            grad_v_sum[:stop, :] += product(probs.astype(jnp.bfloat16), grads)
-            grad_probs = times_transposed(v_ref[:stop, :], grads)
-            grad_scores = (probs * (grad_probs - inner[:, columns])).astype(jnp.bfloat16)
-            grad_k_sum[:stop, :] += product(grad_scores, queries)
-            grad_q_turned[lanes, columns] = product(keys_turned[lanes, :stop], grad_scores)
+    masks = [head_lanes(head, scaled.shape) for head in range(2)]
+    queries = [jnp.where(mask, scaled, jnp.zeros_like(scaled)) for mask in masks]
+    grads = [jnp.where(mask, grad, jnp.zeros_like(grad)) for mask in masks]
+    biased = [with_bias_lane(scaled, head, 1.0) for head in range(2)]
+    keys = [with_bias_lane(k_ref[...], head, bias) for head in range(2)]
+    lanes = [slice(head * HEAD, (head + 1) * HEAD) for head in range(2)]
+    inner = [jnp.sum(inner_turned[at, :], axis=0, keepdims=True) for at in lanes]
+
+    def scores_of(item):
+        head, (start, width, stop) = item
+        columns = slice(start, start + width)
+        scores = masked_scores(keys[head][:stop, :], biased[head][columns, :], diagonal_ref)
+        return scores, times_transposed(v_ref[:stop, :], grads[head][columns, :])
+
+    def differentiate(item, begun):
+        head, (start, width, stop) = item
+        columns = slice(start, start + width)
+        scores, grad_probs = begun
+        probs = jnp.exp(scores - total_ref[0, head : head + 1, columns])
+        grad_scores = probs * (grad_probs - inner[head][:, columns])
+        return probs.astype(jnp.bfloat16), grad_scores.astype(jnp.bfloat16)
+
+    def add(item, done):
+        head, (start, width, stop) = item
+        columns = slice(start, start + width)
+        probs, grad_scores = done
+        grad_v_sum[:stop, :] += product(probs, grads[head][columns, :])
+        grad_k_sum[:stop, :] += product(grad_scores, queries[head][columns, :])
+        grad_q_turned[lanes[head], columns] = product(keys_turned[lanes[head], :stop], grad_scores)
+
+    items = [(head, block) for block in query_blocks(row_count, key_count, causal) for head in range(2)]
+    staggered(items, scores_of, differentiate, add, AHEAD)
     grad_q_ref[...] = (grad_q_turned[...].T * HEAD**-0.5).astype(jnp.bfloat16)
     grad_k_ref[...] = grad_k_sum[...].astype(jnp.bfloat16)
     grad_v_ref[...] = grad_v_sum[...].astype(jnp.bfloat16)
@@ -212,6 +272,7 @@
                 pltpu.VMEM((LANES, row_count), jnp.float32),
                 pltpu.VMEM((key_count, LANES), jnp.float32),
                 pltpu.VMEM((key_count, LANES), jnp.float32),
+                pltpu.VMEM((query_width(row_count, causal),) * 2, jnp.float32),
             ],
         ),
         out_shape=[
@@ -226,15 +287,9 @@
 
 
 def gelu_and_slope(values):
-    size = jnp.abs(values)
-    bell = jnp.exp(-0.5 * values * values)
-    t = 1.0 / (1.0 + TAIL_RATE * size)
-    poly = TAIL_POLY[-1] * t + TAIL_POLY[-2]
-    for coefficient in TAIL_POLY[-3::-1]:
-        poly = poly * t + coefficient
-    tail = poly * t * bell
-    normal_cdf = jnp.where(values >= 0, 1.0 - tail, tail)
-    return values * normal_cdf, normal_cdf + values * (bell * (2.0 * jnp.pi) ** (-0.5))
+    normal_cdf = 0.5 + 0.5 * lax.erf(values * 2.0 ** (-0.5))
+    bell = jnp.exp(-0.5 * values * values) * (2.0 * jnp.pi) ** (-0.5)
+    return values * normal_cdf, normal_cdf + values * bell
 
 
 def unfold_rows(folded_ref, unfolded, rows):
@@ -272,13 +327,19 @@
 
     row_count = normed_ref.shape[0]
     step = 256 if row_count % 256 == 0 else row_count
-    for start in range(0, row_count, step):
-        rows = slice(start, start + step)
-        hidden, slope = gelu_and_slope(product(normed_ref[rows, :], input_ref[...]))
+    blocks = [slice(start, start + step) for start in range(0, row_count, step)]
+    hidden_pre = product(normed_ref[blocks[0], :], input_ref[...])
+    ready = None
+    for at, rows_at in enumerate(blocks):
+        following = product(normed_ref[blocks[at + 1], :], input_ref[...]) if at + 1 < len(blocks) else None
+        hidden, slope = gelu_and_slope(hidden_pre)
         hidden = hidden.astype(jnp.bfloat16)
-        hidden_ref[rows, :] = hidden
-        slope_ref[rows, :] = slope.astype(jnp.bfloat16)
-        after_ref[rows, :] += product(hidden, output_ref[...])
+        hidden_ref[rows_at, :] = hidden
+        slope_ref[rows_at, :] = slope.astype(jnp.bfloat16)
+        if ready is not None:
+            after_ref[blocks[at - 1], :] += product(ready, output_ref[...])
+        hidden_pre, ready = following, hidden
+    after_ref[blocks[-1], :] += product(ready, output_ref[...])
 
 
 FEED_TILE = 512

time: 605 us -> 574 us (0.949)
  Pallas kernels: 202 us -> 162 us
  waiting for transfers between devices: 159 us -> 168 us
    pallas_call x2, Pallas kernels: 38.7 us -> 22.2 us  [attention_forward(): pl.pallas_call(functools.partial(attention_forward_kernel, causal), grid_...]
    pallas_call x1, Pallas kernels: 34.2 us -> 21.2 us  [feed_forward(): pl.pallas_call(functools.partial(feed_forward_kernel, rows), grid=(hidden...]
    pallas_call x2, Pallas kernels: 43.8 us -> 32.7 us  [attention_backward(): pl.pallas_call(functools.partial(attention_backward_kernel, causal), grid...]
    all_gather x1, waiting for transfers between devices: 35 us -> 43.2 us  [gather(): return lax.all_gather(shard, BOTH, axis=0, tiled=True)]
  transfers between devices with their start and end apart: 31 -> 31, of which waited for: 12 -> 14; matrix products, arithmetic and copies ran while one was open for 20% -> 21% of each run, Pallas kernels for 19% -> 17%
where the time goes in v3:
time: 574 us; the launch traced here: 566 us
  waiting for transfers between devices  168 us (29%)
  Pallas kernels  162 us (28%)
  other arithmetic  76.1 us (13%)
  matrix products  51.8 us (9%)
  local copies, waits for them, and re-layouts  45.2 us (8%)
  between operations  32.2 us (6%)
  starting transfers between devices  31.4 us (5%)
    ppermute x14, waiting for transfers between devices, swap(): return lax.ppermute(array, 'h', [(i, i ^ bit) for i in range(self.h_count)])  68.2 us
    all_gather x1, waiting for transfers between devices, gather(): return lax.all_gather(shard, BOTH, axis=0, tiled=True)  43.2 us
    pallas_call x6, Pallas kernels, weight_gradient(): pl.pallas_call(functools.partial(weight_gradient_kernel, starts), grid_sp...  39.4 us
    pallas_call x1, Pallas kernels, feed_backward(): pl.pallas_call(functools.partial(feed_backward_kernel, rows, count // 2),...  34.8 us
    convert_element_type x16, other arithmetic, sum_cores(): (keep.astype(jnp.float32) + other.astype(jnp.float32)).astype(jnp.bfloat16)  34.1 us
    pallas_call x2, Pallas kernels, attention_backward(): pl.pallas_call(functools.partial(attention_backward_kernel, causal), grid...  32.7 us
    dot_general x6, matrix products, times_transposed(): lax.dot_general(left, right, (((1,), (1,)), ((), ())), preferred_element_...  26.7 us
    dot_general x6, matrix products, product(): return jnp.dot(left, right, preferred_element_type=jnp.float32)  25 us
  transfers between devices with their start and end apart: 31, of which 14 were waited for; matrix products, arithmetic and copies ran while one was open for 21% of the time, Pallas kernels for 17%

profile of v3, /device:TPU:0, one launch (start us, length us, event | category | flops | bytes accessed | tf_op | source)
XLA Modules:
  0.0 566.1 jit_solution(4324236347728675813)
XLA Ops:
  11.9 3.1 collective-permute-start
  15.0 2.6 collective-permute-start.1
  18.1 8.4 %collective-permute-done.refs_1_ = bf16[32,4224]{1,0:T(8,128)(2,1)S(1)} collective-permute-done((bf16[32,4224]{1,0:T(8,128)(2,1)S(1)}, bf16[32,4224]{1,0:T(8,128)(2,1)S(1)}, u32[]{:S(2)}, u32[]{:S(2)}) %collective-permute-start) | collective-permute-done | bytes 270368 | tf_op jit(solution)/shard_map/ppermute | solution.py:596
  26.5 14.5 %collective-permute-done.1.refs_2_ = bf16[32,4224]{1,0:T(8,128)(2,1)S(1)} collective-permute-done((bf16[32,4224]{1,0:T(8,128)(2,1)S(1)}, bf16[32,4224]{1,0:T(8,128)(2,1)S(1)}, u32[]{:S(2)}, u32[]{:S(2)}) %collective-permute-start.1) | collective-permute-done | bytes 270368 | tf_op jit(solution)/shard_map/ppermute | solution.py:596
  41.0 2.0 collective-permute-done.2.refs_3_
  43.7 2.7 place_rows.3
  51.7 10.3 %collective-permute-done.3 = bf16[128,2048]{1,0:T(8,128)(2,1)S(1)} collective-permute-done((bf16[128,2048]{1,0:T(8,128)(2,1)S(1)}, bf16[128,2048]{1,0:T(8,128)(2,1)S(1)}, u32[]{:S(2)}, u32[]{:S(2)}) %collective-permute-start.3) | collective-permute-done | bytes 524320 | tf_op jit(solution)/shard_map/ppermute | solution.py:590
  64.4 30.2 %collective-permute-done.5 = bf16[256,2048]{1,0:T(8,128)(2,1)S(1)} collective-permute-done((bf16[256,2048]{1,0:T(8,128)(2,1)S(1)}, bf16[256,2048]{1,0:T(8,128)(2,1)S(1)}, u32[]{:S(2)}, u32[]{:S(2)}) %collective-permute-start.5) | collective-permute-done | bytes 1048608 | tf_op jit(solution)/shard_map/ppermute | solution.py:590
  94.6 12.6 %collective-permute-done.6 = bf16[256,2176]{1,0:T(8,128)(2,1)S(1)} collective-permute-done((bf16[256,2176]{1,0:T(8,128)(2,1)S(1)}, bf16[256,2176]{1,0:T(8,128)(2,1)S(1)}, u32[]{:S(2)}, u32[]{:S(2)}) %collective-permute-start.6) | collective-permute-done | bytes 1114144 | tf_op jit(solution)/shard_map/ppermute | solution.py:590
  114.0 1.8 convert_bitcast_fusion
  117.0 4.2 place_rows.4
  121.2 4.6 place_rows.5
  126.9 2.1 slice_reduce_fusion.1
  129.1 3.0 fusion.38
  134.3 3.0 convolution_convert_fusion.5.v_ref
  137.3 4.9 convolution_convert_fusion.q_ref.k_ref
  142.2 13.1 %attention_forward.2 = (bf16[768,1024]{1,0:T(8,128)(2,1)}, f32[8,2,768]{2,1,0:T(2,128)}) custom-call(s32[1]{0:T(128)} %copy.85.limit_ref, bf16[768,2048]{1,0:T(8,128)(2,1)} %convolution_convert_fusion.q_ref.k_ref, bf16[768,2048]{1,0:T(8,128)(2,1)} %convolution_convert_fusion.q_ref.k_ref, bf16[768,1024]{1,0:T(8,128)(2,1)} %convolution_convert_fusion.5.v_ref), custom_call_target="tpu_custom_call" | custom-call | flops 1024 | bytes 1024 | tf_op jit(solution)/shard_map/attention_forward/pallas_call | solution.py:156
  155.4 3.3 fusion.42
  160.9 43.2 %all-gather.2.cloned.1.call-done.input_ref.output_ref = bf16[1024,12288]{1,0:T(8,128)(2,1)} async-done(((bf16[32,12288]{1,0:T(8,128)(2,1)}), bf16[1024,12288]{1,0:T(8,128)(2,1)}) %all-gather.2.cloned.1.call-update) | async-done | bytes 25165840 | tf_op jit(solution)/shard_map/all_gather | solution.py:599
  204.1 4.6 convolution_convert_fusion.4.q_ref
  208.7 4.4 fusion.6.k_ref.v_ref
  213.1 9.0 %attention_forward.3 = (bf16[768,1024]{1,0:T(8,128)(2,1)}, f32[8,2,768]{2,1,0:T(2,128)}) custom-call(s32[1]{0:T(128)S(6)} %copy.86.limit_ref, bf16[768,1024]{1,0:T(8,128)(2,1)} %convolution_convert_fusion.4.q_ref, bf16[256,2048]{1,0:T(8,128)(2,1)} %fusion.6.k_ref.v_ref, bf16[256,2048]{1,0:T(8,128)(2,1)} %fusion.6.k_ref.v_ref), custom_call_target="tpu_custom_call" | custom-call | flops 1024 | bytes 1024 | tf_op jit(solution)/shard_map/attention_forward/pallas_call | solution.py:156
  222.1 4.9 fusion.43
  229.7 21.2 %feed_forward.1 = (bf16[768,4096]{1,0:T(8,128)(2,1)}, bf16[768,4096]{1,0:T(8,128)(2,1)}, f32[768,1024]{1,0:T(8,128)}) custom-call(bf16[768,1024]{1,0:T(8,128)(2,1)} %add_convert_fusion.2.normed_ref, bf16[1024,12288]{1,0:T(8,128)(2,1)} %all-gather.2.cloned.1.call-done.input_ref.output_ref, ...), custom_call_target="tpu_custom_call" | custom-call | flops 1024 | bytes 1024 | tf_op jit(solution)/shard_map/feed_forward/pallas_call | solution.py:362
  251.0 2.3 reduce_sum.293
  255.3 1.8 multiply_reduce_fusion.3
  257.1 3.4 fusion.35
  260.5 34.8 %feed_backward.1 = (bf16[512,4096]{1,0:T(8,128)(2,1)}, bf16[512,4096]{1,0:T(8,128)(2,1)}, bf16[1024,4096]{1,0:T(8,128)(2,1)}, f32[768,1024]{1,0:T(8,128)}) custom-call(s32[8]{0:T(128)} %fusion.23.positions_ref, bf16[768,1024]{1,0:T(8,128)(2,1)} %get-tuple-element.184.grad_ref, bf16[768,1024]{1,0:T(8,128)(2,1)} %add_convert_fusion.2.normed_ref, ...), custom_call_target="tpu_custom_call" | custom-call | flops 1024 | bytes 1024 | tf_op jit(solution)/shard_map/feed_backward/pallas_call | solution.py:435
  295.4 6.1 %fusion.37 = (bf16[512,4096]{1,0:T(8,128)(2,1)}, bf16[512,4096]{1,0:T(8,128)(2,1)}) fusion(bf16[1024,4096]{1,0:T(8,128)(2,1)} %get-tuple-element.193), kind=kLoop, calls=%fused_computation.196 | loop fusion | bytes 16777216 | tf_op jit(solution)/shard_map/slice | solution.py:798
  302.5 4.8 fusion.36
  311.3 2.8 fusion.34
  314.1 6.1 %weight_gradient.6 = (bf16[512,1024]{1,0:T(8,128)(2,1)}, bf16[512,1024]{1,0:T(8,128)(2,1)}) custom-call(s32[8]{0:T(128)} %get-tuple-element.422.positions_ref, bf16[768,1024]{1,0:T(8,128)(2,1)} %get-tuple-element.209.x_ref.mixed_ref, bf16[768,1024]{1,0:T(8,128)(2,1)} %get-tuple-element.359.refs_0_), custom_call_target="tpu_custom_call" | custom-call | flops 1024 | bytes 1024 | tf_op jit(solution)/shard_map/weight_gradient/pallas_call | solution.py:494
  320.2 4.7 convolution_convert_fusion.3.grad_ref
  325.0 7.7 %add_convert_fusion = bf16[512,8192]{1,0:T(8,128)(2,1)} fusion(bf16[512,4096]{1,0:T(8,128)(2,1)S(1)} %copy-done.10, bf16[512,4096]{1,0:T(8,128)(2,1)S(1)} %copy-done.23, bf16[512,4096]{1,0:T(8,128)(2,1)} %collective-permute-done.10, bf16[512,4096]{1,0:T(8,128)(2,1)} %collective-permute-done.9), kind=kLoop, calls=%fused_computation | loop fusion | flops 41943040 | bytes 25165824 | tf_op jit(solution)/shard_map/convert_element_type | solution.py:641
  332.7 12.4 %attention_backward.2 = (bf16[768,1024]{1,0:T(8,128)(2,1)}, bf16[256,1024]{1,0:T(8,128)(2,1)}, bf16[256,1024]{1,0:T(8,128)(2,1)}) custom-call(s32[1]{0:T(128)S(6)} %copy.86.limit_ref, bf16[768,1024]{1,0:T(8,128)(2,1)} %convolution_convert_fusion.4.q_ref, bf16[256,2048]{1,0:T(8,128)(2,1)} %fusion.6.k_ref.v_ref, bf16[256,2048]{1,0:T(8,128)(2,1)} %fusion.6.k_ref.v_ref, ...), custom_call_target="tpu_custom_call" | custom-call | flops 1024 | bytes 1024 | tf_op jit(solution)/shard_map/attention_backward/pallas_call | solution.py:257
  345.2 6.4 %weight_gradient.7 = (bf16[512,1024]{1,0:T(8,128)(2,1)}, bf16[512,1024]{1,0:T(8,128)(2,1)}) custom-call(s32[8]{0:T(128)} %get-tuple-element.422.positions_ref, bf16[768,1024]{1,0:T(8,128)(2,1)} %copy-done.17, bf16[768,1024]{1,0:T(8,128)(2,1)} %get-tuple-element.221.refs_0_), custom_call_target="tpu_custom_call" | custom-call | flops 1024 | bytes 1024 | tf_op jit(solution)/shard_map/weight_gradient/pallas_call | solution.py:494
  351.5 6.1 %weight_gradient.8 = (bf16[512,2048]{1,0:T(8,128)(2,1)}, bf16[512,2048]{1,0:T(8,128)(2,1)}) custom-call(s32[8]{0:T(128)} %get-tuple-element.423.positions_ref, bf16[256,1024]{1,0:T(8,128)(2,1)} %bitcast.96, bf16[256,1024]{1,0:T(8,128)(2,1)} %get-tuple-element.224.refs_0_, bf16[256,1024]{1,0:T(8,128)(2,1)} %get-tuple-element.225.refs_1_), custom_call_target="tpu_custom_call" | custom-call | flops 1024 | bytes 1024 | tf_op jit(solution)/shard_map/weight_gradient/pallas_call | solution.py:494
  358.0 1.9 pad_maximum_fusion.1
  360.9 2.4 multiply_reduce_fusion.4
  363.5 2.1 slice-done
  365.6 2.3 fusion.10
  369.5 4.2 add_convert_fusion.11
  375.0 1.8 add_convert_fusion.9
  379.8 6.0 %weight_gradient.9 = (bf16[512,1024]{1,0:T(8,128)(2,1)}, bf16[512,1024]{1,0:T(8,128)(2,1)}) custom-call(s32[8]{0:T(128)} %get-tuple-element.422.positions_ref, bf16[768,1024]{1,0:T(8,128)(2,1)} %get-tuple-element.238.x_ref.mixed_ref, bf16[768,1024]{1,0:T(8,128)(2,1)} %convert_element_type.356.refs_0_), custom_call_target="tpu_custom_call" | custom-call | flops 1024 | bytes 1024 | tf_op jit(solution)/shard_map/weight_gradient/pallas_call | solution.py:494
  385.7 4.6 convolution_convert_fusion.2.grad_ref
  390.4 20.3 %attention_backward.3 = (bf16[768,1024]{1,0:T(8,128)(2,1)}, bf16[768,1024]{1,0:T(8,128)(2,1)}, bf16[768,1024]{1,0:T(8,128)(2,1)}) custom-call(s32[1]{0:T(128)} %copy.85.limit_ref, bf16[768,2048]{1,0:T(8,128)(2,1)} %convolution_convert_fusion.q_ref.k_ref, bf16[768,2048]{1,0:T(8,128)(2,1)} %convolution_convert_fusion.q_ref.k_ref, ...), custom_call_target="tpu_custom_call" | custom-call | flops 1024 | bytes 1024 | tf_op jit(solution)/shard_map/attention_backward/pallas_call | solution.py:257
  411.3 2.6 add_convert_fusion.23
  413.8 2.7 add_convert_fusion.21
  416.5 8.7 %weight_gradient.10 = (bf16[512,2048]{1,0:T(8,128)(2,1)}, bf16[512,2048]{1,0:T(8,128)(2,1)}) custom-call(s32[8]{0:T(128)} %get-tuple-element.423.positions_ref, bf16[768,1024]{1,0:T(8,128)(2,1)} %copy-done.11, bf16[768,1024]{1,0:T(8,128)(2,1)} %get-tuple-element.266.refs_0_, bf16[768,1024]{1,0:T(8,128)(2,1)} %get-tuple-element.267.refs_1_), custom_call_target="tpu_custom_call" | custom-call | flops 1024 | bytes 1024 | tf_op jit(solution)/shard_map/weight_gradient/pallas_call | solution.py:494
  425.2 6.2 %weight_gradient.11 = (bf16[512,1024]{1,0:T(8,128)(2,1)}, bf16[512,1024]{1,0:T(8,128)(2,1)}) custom-call(s32[8]{0:T(128)} %get-tuple-element.422.positions_ref, bf16[768,1024]{1,0:T(8,128)(2,1)} %copy-done.11, bf16[768,1024]{1,0:T(8,128)(2,1)} %get-tuple-element.269.refs_0_), custom_call_target="tpu_custom_call" | custom-call | flops 1024 | bytes 1024 | tf_op jit(solution)/shard_map/weight_gradient/pallas_call | solution.py:494
  431.4 2.3 constant_dynamic-update-slice_fusion.11
  459.6 4.5 all-to-all-start
  464.1 4.5 add_convert_fusion.7
  470.0 4.0 add_convert_fusion.5
  474.6 5.1 fusion
  479.8 7.7 %multiply_reduce_fusion = (bf16[1024]{0:T(1024)(128)(2,1)S(1)}, f32[768]{0:T(1024)S(1)}, f32[768]{0:T(1024)S(1)}, bf16[1024]{0:T(1024)(128)(2,1)S(1)}, f32[768,1024]{1,0:T(8,128)}) fusion(bf16[1,768,1024]{2,1,0:T(8,128)(2,1)} %param.15, f32[768]{0:T(1024)S(1)} %add_rsqrt_fusion, f32[768]{0:T(1024)S(1)} %broadcast_multiply_fusion.2, f32[1024]{0:T(1024)S(1)} %copy-done.49, ...), kind=kOutput, calls=%fused_computation.9 | convolution fusion | flops 1619259904 | bytes 11554816 | tf_op jit(solution)/shard_map/dot_general | solution.py:30
  489.5 4.0 multiply_add_fusion
  495.3 3.3 collective-permute-done.20
  498.6 2.4 add_convert_fusion.17
  502.9 1.8 collective-permute-start.22
  505.1 11.2 %collective-permute-done.24 = bf16[256,128]{1,0:T(8,128)(2,1)S(1)} collective-permute-done((bf16[256,128]{1,0:T(8,128)(2,1)S(1)}, bf16[256,128]{1,0:T(8,128)(2,1)S(1)}, u32[]{:S(2)}, u32[]{:S(2)}) %collective-permute-start.24) | collective-permute-done | bytes 65568 | tf_op jit(solution)/shard_map/ppermute | solution.py:590
  518.1 6.3 %reduce-scatter.5.cloned.1.call-done = bf16[32,8192]{1,0:T(8,128)(2,1)} async-done(((bf16[128,8192]{1,0:T(8,128)(2,1)}), bf16[32,8192]{1,0:T(8,128)(2,1)}) %reduce-scatter.5.cloned.1.call-update) | async-done | bytes 524304 | tf_op jit(solution)/shard_map/reduce_scatter | solution.py:929
  525.7 3.5 all-to-all-start.1
  532.4 23.6 %all-to-all-done.1 = bf16[4,32,4224]{2,1,0:T(8,128)(2,1)S(1)} async-done(((bf16[4,32,4224]{2,1,0:T(8,128)(2,1)}), bf16[4,32,4224]{2,1,0:T(8,128)(2,1)S(1)}, u32[]{:S(2)}, u32[]{:S(2)}) %all-to-all-start.1) | async-done | bytes 1081376 | tf_op jit(solution)/shard_map/all_to_all | solution.py:644
  (275 shorter events, 71.0 us)
Async XLA Ops:
  7.2 3.5 copy-start.46
  7.2 4.5 copy-start.51
  7.2 4.5 copy-start.52
  7.2 4.6 copy-start.47
  7.2 4.6 copy-start.42
  7.2 196.9 %all-gather.2.cloned.1.call-start = ((), (), s32[]{:S(2)}) async-start(), calls=%async_computation.4 | async-start | bytes 25952256 | tf_op jit(solution)/shard_map/all_gather | solution.py:599
  11.6 468.2 %reduce-scatter.3.cloned.1.call-start = ((), (), s32[]{:S(2)}) async-start(), calls=%async_computation.5 | async-start | bytes 10485760 | tf_op jit(solution)/shard_map/reduce_scatter | solution.py:657
  11.9 31.2 %copy-start.35 = (bf16[32,4224]{1,0:T(8,128)(2,1)}, bf16[32,4224]{1,0:T(8,128)(2,1)S(1)}, u32[]{:S(2)}) copy-start(bf16[32,4224]{1,0:T(8,128)(2,1)S(1)} %fusion.16.refs_0_) | copy-start | bytes 811012
  11.9 14.6 %collective-permute-start = (bf16[32,4224]{1,0:T(8,128)(2,1)S(1)}, bf16[32,4224]{1,0:T(8,128)(2,1)S(1)}, u32[]{:S(2)}, u32[]{:S(2)}) collective-permute-start(bf16[32,4224]{1,0:T(8,128)(2,1)S(1)} %fusion.16.refs_0_), channel_id=1, source_target_pairs={{0,1},{1,0},{2,3},{3,2},{4,5},{5,4},{6,7},{7,6},{8,9},{9,8},{10,11... | collective-permute-start | bytes 811016 | tf_op jit(solution)/shard_map/ppermute | solution.py:596
  15.0 26.1 %collective-permute-start.1 = (bf16[32,4224]{1,0:T(8,128)(2,1)S(1)}, bf16[32,4224]{1,0:T(8,128)(2,1)S(1)}, u32[]{:S(2)}, u32[]{:S(2)}) collective-permute-start(bf16[32,4224]{1,0:T(8,128)(2,1)S(1)} %fusion.16.refs_0_), channel_id=1, source_target_pairs={{0,2},{1,3},{2,0},{3,1},{4,6},{5,7},{6,4},{7,5},{8,10},{9,11},{10,... | collective-permute-start | bytes 811016 | tf_op jit(solution)/shard_map/ppermute | solution.py:596
  17.6 25.4 %collective-permute-start.2 = (bf16[32,4224]{1,0:T(8,128)(2,1)S(1)}, bf16[32,4224]{1,0:T(8,128)(2,1)S(1)}, u32[]{:S(2)}, u32[]{:S(2)}) collective-permute-start(bf16[32,4224]{1,0:T(8,128)(2,1)S(1)} %fusion.16.refs_0_), channel_id=1, source_target_pairs={{0,3},{1,2},{2,1},{3,0},{4,7},{5,6},{6,5},{7,4},{8,11},{9,10},{10,... | collective-permute-start | bytes 811016 | tf_op jit(solution)/shard_map/ppermute | solution.py:596
  26.5 16.5 %copy-start.43 = (bf16[32,4224]{1,0:T(8,128)(2,1)}, bf16[32,4224]{1,0:T(8,128)(2,1)S(1)}, u32[]{:S(2)}) copy-start(bf16[32,4224]{1,0:T(8,128)(2,1)S(1)} %collective-permute-done.refs_1_) | copy-start | bytes 811012
  47.5 14.5 %collective-permute-start.4 = (bf16[128,2176]{1,0:T(8,128)(2,1)S(1)}, bf16[128,2176]{1,0:T(8,128)(2,1)S(1)}, u32[]{:S(2)}, u32[]{:S(2)}) collective-permute-start(bf16[128,2176]{1,0:T(8,128)(2,1)S(1)} %slice.403), channel_id=1, source_target_pairs={{0,16},{8,24},{16,0},{24,8},{1,17},{9,25},{17,1},{25,9},{2,18},{10... | collective-permute-start | bytes 1671176 | tf_op jit(solution)/shard_map/ppermute | solution.py:590
  50.2 11.9 %collective-permute-start.3 = (bf16[128,2048]{1,0:T(8,128)(2,1)S(1)}, bf16[128,2048]{1,0:T(8,128)(2,1)S(1)}, u32[]{:S(2)}, u32[]{:S(2)}) collective-permute-start(bf16[128,2048]{1,0:T(8,128)(2,1)S(1)} %slice.402), channel_id=1, source_target_pairs={{0,8},{8,0},{16,24},{24,16},{1,9},{9,1},{17,25},{25,17},{2,10},{10... | collective-permute-start | bytes 1572872 | tf_op jit(solution)/shard_map/ppermute | solution.py:590
  62.2 45.0 %collective-permute-start.6 = (bf16[256,2176]{1,0:T(8,128)(2,1)S(1)}, bf16[256,2176]{1,0:T(8,128)(2,1)S(1)}, u32[]{:S(2)}, u32[]{:S(2)}) collective-permute-start(bf16[256,2176]{1,0:T(8,128)(2,1)S(1)} %constant_dynamic-update-slice_fusion.2), channel_id=1, source_target_pairs={{0,8},{8,0},{16,24},{24,16},{1,9},{9,1},{17,25},{25,17},{2,10},{10... | collective-permute-start | bytes 3342344 | tf_op jit(solution)/shard_map/ppermute | solution.py:590
  63.8 30.8 %collective-permute-start.5 = (bf16[256,2048]{1,0:T(8,128)(2,1)S(1)}, bf16[256,2048]{1,0:T(8,128)(2,1)S(1)}, u32[]{:S(2)}, u32[]{:S(2)}) collective-permute-start(bf16[256,2048]{1,0:T(8,128)(2,1)S(1)} %constant_dynamic-update-slice_fusion), channel_id=1, source_target_pairs={{0,16},{8,24},{16,0},{24,8},{1,17},{9,25},{17,1},{25,9},{2,18},{10... | collective-permute-start | bytes 3145736 | tf_op jit(solution)/shard_map/ppermute | solution.py:590
  108.2 5.2 copy-start.53
  109.3 7.7 %collective-permute-start.8 = (bf16[512,2176]{1,0:T(8,128)(2,1)}, bf16[512,2176]{1,0:T(8,128)(2,1)}, u32[]{:S(2)}, u32[]{:S(2)}) collective-permute-start(bf16[512,2176]{1,0:T(8,128)(2,1)} %constant_dynamic-update-slice_fusion.6.refs_0_), channel_id=1, source_target_pairs={{0,4},{4,0},{1,5},{5,1},{2,6},{6,2},{3,7},{7,3},{8,12},{12,8},{9,1... | collective-permute-start | bytes 6684680 | tf_op jit(solution)/shard_map/ppermute | solution.py:593
  111.5 5.4 collective-permute-start.7
  129.1 3.7 copy-start.48
  142.2 13.1 %copy-start.7 = (bf16[1,768,1024]{2,1,0:T(8,128)(2,1)S(1)}, bf16[1,768,1024]{2,1,0:T(8,128)(2,1)}, u32[]{:S(2)}) copy-start(bf16[1,768,1024]{2,1,0:T(8,128)(2,1)} %param.15) | copy-start | bytes 4718596
  142.2 13.1 %copy-start.29 = (bf16[1024,1024]{1,0:T(8,128)(2,1)S(1)}, bf16[1024,1024]{1,0:T(8,128)(2,1)}, u32[]{:S(2)}) copy-start(bf16[1024,1024]{1,0:T(8,128)(2,1)} %get-tuple-element.232) | copy-start | bytes 6291460
  160.9 47.8 %copy-start.17 = (bf16[768,1024]{1,0:T(8,128)(2,1)}, bf16[768,1024]{1,0:T(8,128)(2,1)S(1)}, u32[]{:S(2)}) copy-start(bf16[768,1024]{1,0:T(8,128)(2,1)S(1)} %add_convert_fusion.3.x_ref) | copy-start | bytes 4718596
  160.9 47.8 %copy-start.39 = (bf16[1,256,1024]{2,1,0:T(8,128)(2,1)S(1)}, bf16[1,256,1024]{2,1,0:T(8,128)(2,1)}, u32[]{:S(2)}) copy-start(bf16[1,256,1024]{2,1,0:T(8,128)(2,1)} %param.16) | copy-start | bytes 1572868
  301.5 23.5 %collective-permute-start.9 = (bf16[512,4096]{1,0:T(8,128)(2,1)}, bf16[512,4096]{1,0:T(8,128)(2,1)}, u32[]{:S(2)}, u32[]{:S(2)}) collective-permute-start(bf16[512,4096]{1,0:T(8,128)(2,1)} %get-tuple-element.191), channel_id=1, source_target_pairs={{0,4},{4,0},{1,5},{5,1},{2,6},{6,2},{3,7},{7,3},{8,12},{12,8},{9,1... | collective-permute-start | bytes 12582920 | tf_op jit(solution)/shard_map/ppermute | solution.py:593
  301.7 23.2 %collective-permute-start.10 = (bf16[512,4096]{1,0:T(8,128)(2,1)}, bf16[512,4096]{1,0:T(8,128)(2,1)}, u32[]{:S(2)}, u32[]{:S(2)}) collective-permute-start(bf16[512,4096]{1,0:T(8,128)(2,1)} %get-tuple-element.365), channel_id=1, source_target_pairs={{0,4},{4,0},{1,5},{5,1},{2,6},{6,2},{3,7},{7,3},{8,12},{12,8},{9,1... | collective-permute-start | bytes 12582920 | tf_op jit(solution)/shard_map/ppermute | solution.py:593
  302.5 4.8 copy-start.1
  314.1 6.1 %copy-start.16 = (bf16[768,1024]{1,0:T(8,128)(2,1)S(1)}, bf16[768,1024]{1,0:T(8,128)(2,1)}, u32[]{:S(2)}) copy-start(bf16[768,1024]{1,0:T(8,128)(2,1)} %get-tuple-element.359.refs_0_) | copy-start | bytes 4718596
  320.2 4.7 copy-start.10
  320.2 4.7 copy-start.23
  345.2 12.6 %copy-start.3 = (f32[768,1024]{1,0:T(8,128)S(1)}, f32[768,1024]{1,0:T(8,128)}, u32[]{:S(2)}) copy-start(f32[768,1024]{1,0:T(8,128)} %copy-done.2) | copy-start | bytes 9437188
  357.7 11.5 %collective-permute-start.11 = (bf16[512,2048]{1,0:T(8,128)(2,1)}, bf16[512,2048]{1,0:T(8,128)(2,1)}, u32[]{:S(2)}, u32[]{:S(2)}) collective-permute-start(bf16[512,2048]{1,0:T(8,128)(2,1)} %get-tuple-element.217), channel_id=1, source_target_pairs={{0,4},{4,0},{1,5},{5,1},{2,6},{6,2},{3,7},{7,3},{8,12},{12,8},{9,1... | collective-permute-start | bytes 6291464 | tf_op jit(solution)/shard_map/ppermute | solution.py:593
  359.9 9.4 %collective-permute-start.12 = (bf16[512,2048]{1,0:T(8,128)(2,1)S(1)}, bf16[512,2048]{1,0:T(8,128)(2,1)S(1)}, u32[]{:S(2)}, u32[]{:S(2)}) collective-permute-start(bf16[512,2048]{1,0:T(8,128)(2,1)S(1)} %pad_maximum_fusion.1), channel_id=1, source_target_pairs={{0,4},{4,0},{1,5},{5,1},{2,6},{6,2},{3,7},{7,3},{8,12},{12,8},{9,1... | collective-permute-start | bytes 6291464 | tf_op jit(solution)/shard_map/ppermute | solution.py:593
  369.2 9.2 %copy-start.5 = (f32[768,1024]{1,0:T(8,128)}, f32[768,1024]{1,0:T(8,128)S(1)}, u32[]{:S(2)}) copy-start(f32[768,1024]{1,0:T(8,128)S(1)} %multiply_add_fusion.1) | copy-start | bytes 9437188
  373.7 3.8 copy-start.8
  373.7 37.5 %collective-permute-start.13 = (bf16[256,2048]{1,0:T(8,128)(2,1)}, bf16[256,2048]{1,0:T(8,128)(2,1)}, u32[]{:S(2)}, u32[]{:S(2)}) collective-permute-start(bf16[256,2048]{1,0:T(8,128)(2,1)} %get-tuple-element.376), channel_id=1, source_target_pairs={{0,16},{8,24},{16,0},{24,8},{1,17},{9,25},{17,1},{25,9},{2,18},{10... | collective-permute-start | bytes 3145736 | tf_op jit(solution)/shard_map/ppermute | solution.py:590
  376.8 34.5 %collective-permute-start.14 = (bf16[256,2048]{1,0:T(8,128)(2,1)}, bf16[256,2048]{1,0:T(8,128)(2,1)}, u32[]{:S(2)}, u32[]{:S(2)}) collective-permute-start(bf16[256,2048]{1,0:T(8,128)(2,1)} %get-tuple-element.374), channel_id=1, source_target_pairs={{0,8},{8,0},{16,24},{24,16},{1,9},{9,1},{17,25},{25,17},{2,10},{10... | collective-permute-start | bytes 3145736 | tf_op jit(solution)/shard_map/ppermute | solution.py:590
  379.8 6.0 %copy-start.18 = (bf16[768,1024]{1,0:T(8,128)(2,1)S(1)}, bf16[768,1024]{1,0:T(8,128)(2,1)}, u32[]{:S(2)}) copy-start(bf16[768,1024]{1,0:T(8,128)(2,1)} %convert_element_type.356.refs_0_) | copy-start | bytes 4718596
  425.2 8.5 %copy-start.36 = (bf16[512,1024]{1,0:T(8,128)(2,1)S(1)}, bf16[512,1024]{1,0:T(8,128)(2,1)}, u32[]{:S(2)}) copy-start(bf16[512,1024]{1,0:T(8,128)(2,1)} %get-tuple-element.256) | copy-start | bytes 3145732
  425.2 39.0 %collective-permute-start.15 = (bf16[512,2048]{1,0:T(8,128)(2,1)}, bf16[512,2048]{1,0:T(8,128)(2,1)}, u32[]{:S(2)}, u32[]{:S(2)}) collective-permute-start(bf16[512,2048]{1,0:T(8,128)(2,1)} %get-tuple-element.251), channel_id=1, source_target_pairs={{0,4},{4,0},{1,5},{5,1},{2,6},{6,2},{3,7},{7,3},{8,12},{12,8},{9,1... | collective-permute-start | bytes 6291464 | tf_op jit(solution)/shard_map/ppermute | solution.py:593
  425.2 10.0 %copy-start.50 = (s32[8]{0:T(128)S(1)}, s32[8]{0:T(128)}, u32[]{:S(2)}) copy-start(s32[8]{0:T(128)} %get-tuple-element.423.positions_ref) | copy-start | bytes 100
  433.7 22.5 %copy-start.27 = (bf16[128,2048]{1,0:T(8,128)(2,1)S(1)}, bf16[128,2048]{1,0:T(8,128)(2,1)}, u32[]{:S(2)}) copy-start(bf16[128,2048]{1,0:T(8,128)(2,1)} %get-tuple-element.259) | copy-start | bytes 1572868
  434.7 22.6 %copy-start.26 = (bf16[128,2048]{1,0:T(8,128)(2,1)S(1)}, bf16[128,2048]{1,0:T(8,128)(2,1)}, u32[]{:S(2)}) copy-start(bf16[128,2048]{1,0:T(8,128)(2,1)} %get-tuple-element.257) | copy-start | bytes 1572868
  434.7 29.4 %collective-permute-start.16 = (bf16[512,2048]{1,0:T(8,128)(2,1)}, bf16[512,2048]{1,0:T(8,128)(2,1)}, u32[]{:S(2)}, u32[]{:S(2)}) collective-permute-start(bf16[512,2048]{1,0:T(8,128)(2,1)} %constant_dynamic-update-slice_fusion.10), channel_id=1, source_target_pairs={{0,4},{4,0},{1,5},{5,1},{2,6},{6,2},{3,7},{7,3},{8,12},{12,8},{9,1... | collective-permute-start | bytes 6291464 | tf_op jit(solution)/shard_map/ppermute | solution.py:593
  435.3 20.9 %collective-permute-start.17 = (bf16[128,2048]{1,0:T(8,128)(2,1)}, bf16[128,2048]{1,0:T(8,128)(2,1)}, u32[]{:S(2)}, u32[]{:S(2)}) collective-permute-start(bf16[128,2048]{1,0:T(8,128)(2,1)} %get-tuple-element.385), channel_id=1, source_target_pairs={{0,8},{8,0},{16,24},{24,16},{1,9},{9,1},{17,25},{25,17},{2,10},{10... | collective-permute-start | bytes 1572872 | tf_op jit(solution)/shard_map/ppermute | solution.py:590
  436.7 19.5 %collective-permute-start.18 = (bf16[128,2048]{1,0:T(8,128)(2,1)}, bf16[128,2048]{1,0:T(8,128)(2,1)}, u32[]{:S(2)}, u32[]{:S(2)}) collective-permute-start(bf16[128,2048]{1,0:T(8,128)(2,1)} %get-tuple-element.383), channel_id=1, source_target_pairs={{0,16},{8,24},{16,0},{24,8},{1,17},{9,25},{17,1},{25,9},{2,18},{10... | collective-permute-start | bytes 1572872 | tf_op jit(solution)/shard_map/ppermute | solution.py:590
  459.6 34.0 %all-to-all-start = ((bf16[4,32,4096]{2,1,0:T(8,128)(2,1)}), bf16[4,32,4096]{2,1,0:T(8,128)(2,1)}, u32[]{:S(2)}, u32[]{:S(2)}) async-start(bf16[4,32,4096]{2,1,0:T(8,128)(2,1)} %bitcast.10), calls=%async_computation | async-start | bytes 2097152 | tf_op jit(solution)/shard_map/all_to_all | solution.py:644
  464.1 60.2 %reduce-scatter.5.cloned.1.call-start = ((), (), s32[]{:S(2)}) async-start(), calls=%async_computation.6 | async-start | bytes 2621440 | tf_op jit(solution)/shard_map/reduce_scatter | solution.py:929
  464.1 10.5 %copy-start.32 = (bf16[768,1024]{1,0:T(8,128)(2,1)S(1)}, bf16[768,1024]{1,0:T(8,128)(2,1)}, u32[]{:S(2)}) copy-start(bf16[768,1024]{1,0:T(8,128)(2,1)} %get-tuple-element.267.refs_1_) | copy-start | bytes 4718596
  468.6 6.0 %copy-start.20 = (bf16[1024,2048]{1,0:T(8,128)(2,1)S(1)}, bf16[1024,2048]{1,0:T(8,128)(2,1)}, u32[]{:S(2)}) copy-start(bf16[1024,2048]{1,0:T(8,128)(2,1)} %place_rows.4) | copy-start | bytes 12582916
  468.6 6.0 %copy-start.31 = (bf16[768,1024]{1,0:T(8,128)(2,1)S(1)}, bf16[768,1024]{1,0:T(8,128)(2,1)}, u32[]{:S(2)}) copy-start(bf16[768,1024]{1,0:T(8,128)(2,1)} %get-tuple-element.266.refs_0_) | copy-start | bytes 4718596
  468.6 26.7 %collective-permute-start.19 = (bf16[256,2048]{1,0:T(8,128)(2,1)}, bf16[256,2048]{1,0:T(8,128)(2,1)}, u32[]{:S(2)}, u32[]{:S(2)}) collective-permute-start(bf16[256,2048]{1,0:T(8,128)(2,1)} %get-tuple-element.372), channel_id=1, source_target_pairs={{0,16},{8,24},{16,0},{24,8},{1,17},{9,25},{17,1},{25,9},{2,18},{10... | collective-permute-start | bytes 3145736 | tf_op jit(solution)/shard_map/ppermute | solution.py:590
  474.0 24.6 %collective-permute-start.20 = (bf16[256,2048]{1,0:T(8,128)(2,1)}, bf16[256,2048]{1,0:T(8,128)(2,1)}, u32[]{:S(2)}, u32[]{:S(2)}) collective-permute-start(bf16[256,2048]{1,0:T(8,128)(2,1)} %get-tuple-element.370), channel_id=1, source_target_pairs={{0,8},{8,0},{16,24},{24,16},{1,9},{9,1},{17,25},{25,17},{2,10},{10... | collective-permute-start | bytes 3145736 | tf_op jit(solution)/shard_map/ppermute | solution.py:590
  474.6 5.2 copy-start.49
  479.8 9.7 %copy-start.6 = (f32[768,1024]{1,0:T(8,128)S(1)}, f32[768,1024]{1,0:T(8,128)}, u32[]{:S(2)}) copy-start(f32[768,1024]{1,0:T(8,128)} %copy-done.5) | copy-start | bytes 9437188
  493.6 5.1 copy-start.21
  495.1 6.2 %copy-start.22 = (bf16[256,2048]{1,0:T(8,128)(2,1)S(1)}, bf16[256,2048]{1,0:T(8,128)(2,1)}, u32[]{:S(2)}) copy-start(bf16[256,2048]{1,0:T(8,128)(2,1)} %get-tuple-element.281) | copy-start | bytes 3145732
  495.1 9.6 %collective-permute-start.23 = (bf16[512,128]{1,0:T(8,128)(2,1)S(1)}, bf16[512,128]{1,0:T(8,128)(2,1)S(1)}, u32[]{:S(2)}, u32[]{:S(2)}) collective-permute-start(bf16[512,128]{1,0:T(8,128)(2,1)S(1)} %pad_maximum_fusion.6), channel_id=1, source_target_pairs={{0,4},{4,0},{1,5},{5,1},{2,6},{6,2},{3,7},{7,3},{8,12},{12,8},{9,1... | collective-permute-start | bytes 393224 | tf_op jit(solution)/shard_map/ppermute | solution.py:593
  501.0 23.3 %collective-permute-start.21 = (bf16[128,2048]{1,0:T(8,128)(2,1)}, bf16[128,2048]{1,0:T(8,128)(2,1)S(1)}, u32[]{:S(2)}, u32[]{:S(2)}) collective-permute-start(bf16[128,2048]{1,0:T(8,128)(2,1)} %get-tuple-element.380), channel_id=1, source_target_pairs={{0,8},{8,0},{16,24},{24,16},{1,9},{9,1},{17,25},{25,17},{2,10},{10... | collective-permute-start | bytes 1572872 | tf_op jit(solution)/shard_map/ppermute | solution.py:590
  502.9 21.4 %collective-permute-start.22 = (bf16[128,2048]{1,0:T(8,128)(2,1)S(1)}, bf16[128,2048]{1,0:T(8,128)(2,1)S(1)}, u32[]{:S(2)}, u32[]{:S(2)}) collective-permute-start(bf16[128,2048]{1,0:T(8,128)(2,1)S(1)} %get-tuple-element.378), channel_id=1, source_target_pairs={{0,16},{8,24},{16,0},{24,8},{1,17},{9,25},{17,1},{25,9},{2,18},{10... | collective-permute-start | bytes 1572872 | tf_op jit(solution)/shard_map/ppermute | solution.py:590
  504.8 11.5 %collective-permute-start.24 = (bf16[256,128]{1,0:T(8,128)(2,1)S(1)}, bf16[256,128]{1,0:T(8,128)(2,1)S(1)}, u32[]{:S(2)}, u32[]{:S(2)}) collective-permute-start(bf16[256,128]{1,0:T(8,128)(2,1)S(1)} %get-tuple-element.405), channel_id=1, source_target_pairs={{0,16},{8,24},{16,0},{24,8},{1,17},{9,25},{17,1},{25,9},{2,18},{10... | collective-permute-start | bytes 196616 | tf_op jit(solution)/shard_map/ppermute | solution.py:590
  516.3 8.0 %collective-permute-start.25 = (bf16[128,128]{1,0:T(8,128)(2,1)S(1)}, bf16[128,128]{1,0:T(8,128)(2,1)S(1)}, u32[]{:S(2)}, u32[]{:S(2)}) collective-permute-start(bf16[128,128]{1,0:T(8,128)(2,1)S(1)} %get-tuple-element.402), channel_id=1, source_target_pairs={{0,8},{8,0},{16,24},{24,16},{1,9},{9,1},{17,25},{25,17},{2,10},{10... | collective-permute-start | bytes 98312 | tf_op jit(solution)/shard_map/ppermute | solution.py:590
  524.6 6.1 %copy-start.25 = (bf16[32,8192]{1,0:T(8,128)(2,1)S(1)}, bf16[32,8192]{1,0:T(8,128)(2,1)}, u32[]{:S(2)}) copy-start(bf16[32,8192]{1,0:T(8,128)(2,1)} %reduce-scatter.5.cloned.1.call-done) | copy-start | bytes 1572868
  525.7 30.4 %all-to-all-start.1 = ((bf16[4,32,4224]{2,1,0:T(8,128)(2,1)}), bf16[4,32,4224]{2,1,0:T(8,128)(2,1)S(1)}, u32[]{:S(2)}, u32[]{:S(2)}) async-start(bf16[4,32,4224]{2,1,0:T(8,128)(2,1)} %bitcast.29), calls=%async_computation.3 | async-start | bytes 2162688 | tf_op jit(solution)/shard_map/all_to_all | solution.py:644
  (22 other events, 49.0 us)
Sparse Core Ops, SparseCore 0:
  11.7 192.3 all-gather.1
  332.8 98.1 reduce-scatter.2
  479.9 44.3 reduce-scatter.4

commit v4 on v3

--- a/solution.py
+++ b/solution.py
@@ -38,17 +38,37 @@
     return centre * lax.rsqrt(spread + 1e-05) * gain_row + bias_row
 
 
-def norm_backward(values, gain_row, grad):
-    centre = values - jnp.mean(values, axis=-1, keepdims=True)
-    rate = lax.rsqrt(jnp.mean(centre * centre, axis=-1, keepdims=True) + 1e-05)
-    normed = centre * rate
-    scaled = grad * gain_row
-    grad_input = rate * (
-        scaled
-        - jnp.mean(scaled, axis=-1, keepdims=True)
-        - normed * jnp.mean(scaled * normed, axis=-1, keepdims=True)
-    )
-    return grad_input, jnp.sum(grad * normed, axis=0), jnp.sum(grad, axis=0)
+def row_blocks(row_count, step):
+    step = step if row_count % step == 0 else row_count
+    return [slice(start, start + step) for start in range(0, row_count, step)]
+
+
+def norm_backward_rows(norm, values_ref, grad_of, base_ref, rows_ref, grad_ref, low_ref, sums_ref, normed_ref=None):
+    gain, bias = rows_ref[norm : norm + 1, :], rows_ref[4 + norm : 5 + norm, :]
+    gain_sum, bias_sum = jnp.zeros_like(gain), jnp.zeros_like(gain)
+    for rows in row_blocks(values_ref.shape[0], LANES):
+        values = values_ref[rows, :].astype(jnp.float32)
+        grad = grad_of(rows)
+        centre = values - jnp.mean(values, axis=-1, keepdims=True)
+        rate = lax.rsqrt(jnp.mean(centre * centre, axis=-1, keepdims=True) + 1e-05)
+        normed = centre * rate
+        if normed_ref is not None:
+            normed_ref[rows, :] = (normed * gain + bias).astype(normed_ref.dtype)
+        scaled = grad * gain
+        total = rate * (
+            scaled
+            - jnp.mean(scaled, axis=-1, keepdims=True)
+            - normed * jnp.mean(scaled * normed, axis=-1, keepdims=True)
+        )
+        if base_ref is not None:
+            total = base_ref[rows, :] + total
+        grad_ref[rows, :] = total
+        if low_ref is not None:
+            low_ref[rows, :] = total.astype(jnp.bfloat16)
+        gain_sum += jnp.sum(grad * normed, axis=0, keepdims=True)
+        bias_sum += jnp.sum(grad, axis=0, keepdims=True)
+    sums_ref[0:1, :] = gain_sum
+    sums_ref[1:2, :] = bias_sum
 
 
 def with_bias_lane(matrix, head, bias):
@@ -315,7 +335,22 @@
 
 
 def feed_forward_kernel(
-    rows, normed_ref, input_ref, output_ref, base_ref, hidden_ref, slope_ref, after_ref, unfolded
+    rows,
+    limit_ref,
+    normed_ref,
+    input_ref,
+    output_ref,
+    base_ref,
+    cotangent_ref,
+    rows_ref,
+    hidden_ref,
+    slope_ref,
+    block_ref,
+    grad_ref,
+    low_ref,
+    sums_ref,
+    after_ref,
+    unfolded,
 ):
     if rows:
         unfold_rows(output_ref, unfolded, rows)
@@ -341,6 +376,15 @@
         hidden_pre, ready = following, hidden
     after_ref[blocks[-1], :] += product(ready, output_ref[...])
 
+    @pl.when(pl.program_id(0) == pl.num_programs(0) - 1)
+    def _():
+        def live_grad(rows_at):
+            shape = (rows_at.stop - rows_at.start, after_ref.shape[1])
+            row = rows_at.start + lax.broadcasted_iota(jnp.int32, shape, 0)
+            return jnp.where(row < limit_ref[0], cotangent_ref[rows_at, :], 0.0)
+
+        norm_backward_rows(3, after_ref, live_grad, None, rows_ref, grad_ref, low_ref, sums_ref, block_ref)
+
 
 FEED_TILE = 512
 
@@ -352,28 +396,34 @@
     return first, pl.BlockSpec((tile, width), lambda *at: (index(*at), 0))
 
 
-def feed_forward(rows, normed, input_low, output_low, after_cross):
+def feed_forward(rows, limit, normed, input_low, output_low, after_cross, cotangent, norm_rows):
     row_count, width = normed.shape
     hidden_width = 4 * width
     tile = FEED_TILE
-    whole = pl.BlockSpec((row_count, width), lambda j: (0, 0))
-    tall = pl.BlockSpec((row_count, tile), lambda j: (0, j))
-    weight_specs = feed_weight_specs(hidden_width // width if rows else 0, width, tile, lambda j: j)
+    whole = pl.BlockSpec((row_count, width), lambda j, s: (0, 0))
+    tall = pl.BlockSpec((row_count, tile), lambda j, s: (0, j))
+    weight_specs = feed_weight_specs(hidden_width // width if rows else 0, width, tile, lambda j, s: j)
     return pl.pallas_call(
         functools.partial(feed_forward_kernel, rows),
-        grid=(hidden_width // tile,),
-        in_specs=[whole, *weight_specs, whole],
-        out_specs=[tall, tall, whole],
+        grid_spec=pltpu.PrefetchScalarGridSpec(
+            num_scalar_prefetch=1,
+            grid=(hidden_width // tile,),
+            in_specs=[whole, *weight_specs, whole, whole, pl.BlockSpec((8, width), lambda j, s: (0, 0))],
+            out_specs=[tall, tall, whole, whole, whole, pl.BlockSpec((2, width), lambda j, s: (0, 0))],
+            scratch_shapes=[pltpu.VMEM((row_count, width), jnp.float32), pltpu.VMEM((tile, width), jnp.bfloat16)],
+        ),
         out_shape=[
             jax.ShapeDtypeStruct((row_count, hidden_width), jnp.bfloat16),
             jax.ShapeDtypeStruct((row_count, hidden_width), jnp.bfloat16),
+            jax.ShapeDtypeStruct((row_count, width), jnp.bfloat16),
             jax.ShapeDtypeStruct((row_count, width), jnp.float32),
+            jax.ShapeDtypeStruct((row_count, width), jnp.bfloat16),
+            jax.ShapeDtypeStruct((2, width), jnp.float32),
         ],
-        scratch_shapes=[pltpu.VMEM((tile, width), jnp.bfloat16)],
         compiler_params=pltpu.CompilerParams(vmem_limit_bytes=VMEM_BYTES),
         cost_estimate=SHORT,
         name="feed_forward",
-    )(normed, input_low, output_low, after_cross)
+    )(limit, normed, input_low, output_low, after_cross, cotangent, norm_rows)
 
 
 def turn_rows(x_ref, turned, positions_ref):
@@ -384,7 +434,7 @@
 
 def feed_backward_kernel(
     rows,
-    half_blocks,
+    tiles_ref,
     positions_ref,
     grad_ref,
     normed_ref,
@@ -392,9 +442,16 @@
     slope_ref,
     input_ref,
     output_ref,
+    values_ref,
+    base_ref,
+    rows_ref,
     in_send_ref,
     in_keep_ref,
-    out_ref,
+    out_send_ref,
+    out_keep_ref,
+    total_ref,
+    low_ref,
+    sums_ref,
     grad_normed_ref,
     turned,
     unfolded,
@@ -412,39 +469,73 @@
     grad_hidden = times_transposed(grad_ref[...], output_ref[...])
     grad_pre = (grad_hidden * slope_ref[...].astype(jnp.float32)).astype(jnp.bfloat16)
     grad_out = contract_rows(hidden_ref[...], grad_ref[...]).astype(jnp.bfloat16)
-    if rows:
-        fold_rows(grad_out, out_ref, rows)
-    else:
-        out_ref[...] = grad_out
+    for out_ref, first in ((out_send_ref, True), (out_keep_ref, False)):
+
+        @pl.when((step < pl.num_programs(0) // 2) == first)
+        def _(out_ref=out_ref):
+            if rows:
+                fold_rows(grad_out, out_ref, rows)
+            else:
+                out_ref[...] = grad_out
+
     half = turned.shape[0] // 2
     in_send_ref[...] = product(turned[:half, :], grad_pre).astype(jnp.bfloat16)
     in_keep_ref[...] = product(turned[half:, :], grad_pre).astype(jnp.bfloat16)
     grad_normed_ref[...] += times_transposed(grad_pre, input_ref[...])
 
-
-def feed_backward(rows, positions, grad_branch, normed, hidden, slope, input_low, output_low):
+    @pl.when(step == pl.num_programs(0) - 1)
+    def _():
+        norm_backward_rows(
+            2,
+            values_ref,
+            lambda rows_at: grad_normed_ref[rows_at, :],
+            base_ref,
+            rows_ref,
+            total_ref,
+            low_ref,
+            sums_ref,
+        )
+
+
+def feed_backward(
+    rows, tiles, positions, grad_branch, normed, hidden, slope, input_low, output_low, after_cross, grad_after, norm_rows
+):
     row_count, width = grad_branch.shape
     hidden_width = hidden.shape[1]
-    count = positions.shape[0]
+    count = tiles.shape[0]
+    half = count // 2
     tile = hidden_width // count
-    whole = pl.BlockSpec((row_count, width), lambda j, p: (0, 0))
-    tall = pl.BlockSpec((row_count, tile), lambda j, p: (0, j))
-    in_half = pl.BlockSpec((width // 2, tile), lambda j, p: (0, j))
+    whole = pl.BlockSpec((row_count, width), lambda j, t, p: (0, 0))
+    tall = pl.BlockSpec((row_count, tile), lambda j, t, p: (0, t[j]))
+    in_half = pl.BlockSpec((width // 2, tile), lambda j, t, p: (0, t[j]))
     folds = hidden_width // width if rows else 1
-    weight_specs = feed_weight_specs(folds if rows else 0, width, tile, lambda j, p: j)
+    weight_specs = feed_weight_specs(folds if rows else 0, width, tile, lambda j, t, p: t[j])
     return pl.pallas_call(
-        functools.partial(feed_backward_kernel, rows, count // 2),
+        functools.partial(feed_backward_kernel, rows),
         grid_spec=pltpu.PrefetchScalarGridSpec(
-            num_scalar_prefetch=1,
+            num_scalar_prefetch=2,
             grid=(count,),
-            in_specs=[whole, whole, tall, tall, *weight_specs],
+            in_specs=[
+                whole,
+                whole,
+                tall,
+                tall,
+                *weight_specs,
+                whole,
+                whole,
+                pl.BlockSpec((8, width), lambda j, t, p: (0, 0)),
+            ],
             out_specs=[
                 in_half,
                 in_half,
-                pl.BlockSpec((tile // folds, folds * width), lambda j, p: (p[j], 0)),
+                pl.BlockSpec((tile // folds, folds * width), lambda j, t, p: (jnp.minimum(j, half - 1), 0)),
+                pl.BlockSpec((tile // folds, folds * width), lambda j, t, p: (jnp.maximum(j - half, 0), 0)),
                 whole,
+                whole,
+                pl.BlockSpec((2, width), lambda j, t, p: (0, 0)),
             ],
             scratch_shapes=[
+                pltpu.VMEM((row_count, width), jnp.float32),
                 pltpu.VMEM((width, row_count), jnp.bfloat16),
                 pltpu.VMEM((tile, width), jnp.bfloat16),
             ],
@@ -452,18 +543,38 @@
         out_shape=[
             jax.ShapeDtypeStruct((width // 2, hidden_width), jnp.bfloat16),
             jax.ShapeDtypeStruct((width // 2, hidden_width), jnp.bfloat16),
-            jax.ShapeDtypeStruct((hidden_width // folds, folds * width), jnp.bfloat16),
+            jax.ShapeDtypeStruct((hidden_width // folds // 2, folds * width), jnp.bfloat16),
+            jax.ShapeDtypeStruct((hidden_width // folds // 2, folds * width), jnp.bfloat16),
             jax.ShapeDtypeStruct((row_count, width), jnp.float32),
+            jax.ShapeDtypeStruct((row_count, width), jnp.bfloat16),
+            jax.ShapeDtypeStruct((2, width), jnp.float32),
         ],
         compiler_params=pltpu.CompilerParams(vmem_limit_bytes=VMEM_BYTES),
         cost_estimate=SHORT,
         name="feed_backward",
-    )(positions, grad_branch, normed, hidden, slope, input_low, output_low)
-
-
-def weight_gradient_kernel(starts, positions_ref, x_ref, *refs):
-    turned = refs[-1]
-    send_ref, keep_ref = refs[-3:-1]
+    )(
+        tiles, positions, grad_branch, normed, hidden, slope, input_low, output_low, after_cross, grad_after, norm_rows
+    )
+
+
+WEIGHT_TILE = 512
+
+
+def tile_starts(arrays):
+    starts = [0]
+    for array in arrays:
+        starts.append(starts[-1] + array.shape[1] // WEIGHT_TILE)
+    return starts
+
+
+def tile_spec(rows, first, last, offset=0):
+    return pl.BlockSpec(
+        (rows, WEIGHT_TILE), lambda j, *_: (0, offset + jnp.clip(j - first, 0, last - first - 1))
+    )
+
+
+def weight_gradient_kernel(starts, groups, crossed, positions_ref, x_ref, *refs):
+    grads, outs, turned = refs[: len(starts) - 1], refs[len(starts) - 1 : -1], refs[-1]
     step = pl.program_id(0)
 
     @pl.when(step == 0)
@@ -471,41 +582,99 @@
         turn_rows(x_ref, turned, positions_ref)
 
     half = turned.shape[0] // 2
-    for index, grad_ref in enumerate(refs[:-3]):
+    for index, grad_ref in enumerate(grads):
+        group = groups[index]
 
         @pl.when((step >= starts[index]) & (step < starts[index + 1]))
-        def _(grad_ref=grad_ref):
-            send_ref[...] = product(turned[:half, :], grad_ref[...]).astype(jnp.bfloat16)
-            keep_ref[...] = product(turned[half:, :], grad_ref[...]).astype(jnp.bfloat16)
-
-
-def weight_gradient(positions, x, grads):
+        def _(grad_ref=grad_ref, group=group):
+            for out_ref, rows in ((outs[2 * group], slice(0, half)), (outs[2 * group + 1], slice(half, 2 * half))):
+                result = product(turned[rows, :], grad_ref[...]).astype(jnp.bfloat16)
+                if crossed[group]:
+                    for block, place in enumerate((0, 2, 1, 3)):
+                        out_ref[place * LANES : (place + 1) * LANES, :] = result[
+                            block * LANES : (block + 1) * LANES, :
+                        ]
+                else:
+                    out_ref[...] = result
+
+
+def weight_gradient(positions, x, *groups):
     row_count, width = x.shape
-    tile = 512
-    starts = [0]
-    for grad in grads:
-        starts.append(starts[-1] + grad.shape[1] // tile)
-    columns = starts[-1] * tile
-
-    def grad_spec(first, last):
-        return pl.BlockSpec((row_count, tile), lambda j, p: (0, jnp.clip(j - first, 0, last - first - 1)))
-
-    half = pl.BlockSpec((width // 2, tile), lambda j, p: (0, j))
+    grads = [grad for group, _ in groups for grad in group]
+    group_of = [index for index, (group, _) in enumerate(groups) for _ in group]
+    starts = tile_starts(grads)
+    half = width // 2
+    out_specs, out_shape = [], []
+    for index in range(len(groups)):
+        own = [at for at, group in enumerate(group_of) if group == index]
+        first, last = starts[own[0]], starts[own[-1] + 1]
+        out_specs += [tile_spec(half, first, last)] * 2
+        out_shape += [jax.ShapeDtypeStruct((half, (last - first) * WEIGHT_TILE), jnp.bfloat16)] * 2
     return pl.pallas_call(
-        functools.partial(weight_gradient_kernel, starts),
+        functools.partial(weight_gradient_kernel, starts, group_of, [crossed for _, crossed in groups]),
         grid_spec=pltpu.PrefetchScalarGridSpec(
             num_scalar_prefetch=1,
             grid=(starts[-1],),
             in_specs=[pl.BlockSpec((row_count, width), lambda j, p: (0, 0))]
-            + [grad_spec(starts[i], starts[i + 1]) for i in range(len(grads))],
-            out_specs=[half, half],
+            + [tile_spec(row_count, starts[i], starts[i + 1]) for i in range(len(grads))],
+            out_specs=out_specs,
             scratch_shapes=[pltpu.VMEM((width, row_count), jnp.bfloat16)],
         ),
-        out_shape=[jax.ShapeDtypeStruct((width // 2, columns), jnp.bfloat16)] * 2,
+        out_shape=out_shape,
         compiler_params=pltpu.CompilerParams(vmem_limit_bytes=VMEM_BYTES),
         cost_estimate=SHORT,
         name="weight_gradient",
     )(positions, x, *grads)
+
+
+def input_gradient_kernel(norm, starts, has_low, *refs):
+    count = len(starts) - 1
+    grads, weights = refs[:count], refs[count : 2 * count]
+    values_ref, base_ref, rows_ref, total_ref = refs[2 * count : 2 * count + 4]
+    low_ref = refs[2 * count + 4] if has_low else None
+    sums_ref, summed = refs[-2:]
+    step = pl.program_id(0)
+
+    @pl.when(step == 0)
+    def _():
+        summed[...] = jnp.zeros_like(summed)
+
+    for index in range(count):
+
+        @pl.when((step >= starts[index]) & (step < starts[index + 1]))
+        def _(index=index):
+            summed[...] += times_transposed(grads[index][...], weights[index][...])
+
+    @pl.when(step == starts[-1] - 1)
+    def _():
+        norm_backward_rows(
+            norm, values_ref, lambda rows: summed[rows, :], base_ref, rows_ref, total_ref, low_ref, sums_ref
+        )
+
+
+def input_gradient(norm, grads, weights, values, base, norm_rows, has_low):
+    row_count, width = values.shape
+    starts = tile_starts(grads)
+    whole = pl.BlockSpec((row_count, width), lambda j: (0, 0))
+    spans = [(starts[i], starts[i + 1]) for i in range(len(grads))]
+    lows = [jax.ShapeDtypeStruct((row_count, width), jnp.bfloat16)] if has_low else []
+    return pl.pallas_call(
+        functools.partial(input_gradient_kernel, norm, starts, has_low),
+        grid=(starts[-1],),
+        in_specs=[tile_spec(row_count, *span) for span in spans]
+        + [
+            tile_spec(width, *span, offset=column // WEIGHT_TILE) for span, (_, column) in zip(spans, weights)
+        ]
+        + [whole, whole, pl.BlockSpec((8, width), lambda j: (0, 0))],
+        out_specs=[whole] * (1 + len(lows)) + [pl.BlockSpec((2, width), lambda j: (0, 0))],
+        out_shape=[jax.ShapeDtypeStruct((row_count, width), jnp.float32)]
+        + lows
+        + [jax.ShapeDtypeStruct((2, width), jnp.float32)],
+        scratch_shapes=[pltpu.VMEM((row_count, width), jnp.float32)],
+        compiler_params=pltpu.CompilerParams(vmem_limit_bytes=VMEM_BYTES),
+        cost_estimate=SHORT,
+        name="input_gradient",
+    )(*grads, *[array for array, _ in weights], values, base, norm_rows)
 
 
 class Order:
@@ -615,6 +784,12 @@
         table = jnp.concatenate([2 * h + self.core, 2 * h + 1 - self.core]).astype(jnp.int32)
         return place_rows(table, [block, other], block.shape[0] // self.h_count)
 
+    def tiles(self):
+        if not self.pairwise:
+            return jnp.arange(self.blocks, dtype=jnp.int32)
+        h = 2 * jnp.arange(self.h_count, dtype=jnp.int32)
+        return jnp.concatenate([h + 1 - self.core, h + self.core]).astype(jnp.int32)
+
     def positions(self, flip=None):
         block = jnp.arange(self.blocks, dtype=jnp.int32)
         if not self.pairwise:
@@ -627,15 +802,9 @@
         return (place + jnp.where(own, self.h_count, 0)).astype(jnp.int32)
 
     def halves(self, rows, flip):
-        blocks = rows.reshape(self.blocks, -1, rows.shape[1])
-        place = self.positions(flip)
-        order = jnp.sum(
-            jnp.where(place[:, None] == jnp.arange(self.blocks)[None, :], jnp.arange(self.blocks)[:, None], 0),
-            axis=0,
-        )
-        ordered = [lax.dynamic_index_in_dim(blocks, order[j], 0, keepdims=False) for j in range(self.blocks)]
-        half = self.blocks // 2
-        return jnp.concatenate(ordered[:half], axis=0), jnp.concatenate(ordered[half:], axis=0)
+        ordered = place_rows(self.positions(flip), [rows], rows.shape[0] // self.blocks)
+        half = rows.shape[0] // 2
+        return ordered[:half], ordered[half:]
 
     def sum_cores(self, keep, other):
         return (keep.astype(jnp.float32) + other.astype(jnp.float32)).astype(jnp.bfloat16)
@@ -647,6 +816,13 @@
         rows = parts.shape[0] // self.fsdp_count
         parts = parts.astype(jnp.float32)
         return sum(parts[k * rows : (k + 1) * rows] for k in range(self.fsdp_count))
+
+    def sum_all_fsdp(self, grad):
+        grad = grad.astype(jnp.float32)
+        for bit in range(self.fsdp_count.bit_length() - 1):
+            grad = grad + self.swap_fsdp(grad, 1 << bit)
+        rows = grad.shape[0] // self.fsdp_count
+        return lax.dynamic_slice_in_dim(grad, self.fsdp * rows, rows, 0)
 
     def scatter_whole(self, send, keep):
         grad = jnp.concatenate([send, keep], axis=0).astype(jnp.float32)
@@ -720,6 +896,7 @@
 
         gathered = links.gather(jnp.concatenate([feed_shard, cross_shard], axis=1))
         feed_input_low, feed_output_low, cross_whole = gathered, gathered, gathered[:, 8 * width :]
+        cross_held, cross_at = gathered, 8 * width
         self_part = order.run(lay_fsdp, *links.spread_fsdp(self_shard))
         self_sides = [self_part[:, :split], self_part[:, split:]]
         self_swaps = send(self_sides, 0)
@@ -732,6 +909,7 @@
         fold_count = 0
         self_whole, cross_whole = links.gather(self_shard), links.gather(cross_shard)
         self_first, self_second = self_whole[:, :split], self_whole[:, split:]
+        cross_held, cross_at = cross_whole, 0
         feed_input_low = links.gather(feed_shard)
         feed_output_low = links.gather(feed_output.astype(low))
 
@@ -775,42 +953,42 @@
     )
     after_cross = after_self + product(cross_mixed, cross_output_low)
     normed_feed = layer_norm(after_cross, gain_table[2], bias_table[2]).astype(low)
-    hidden, slope, after_feed = feed_forward(
-        fold_count, normed_feed, feed_input_low, feed_output_low, after_cross
-    )
-    block_output = layer_norm(after_feed, gain_table[3], bias_table[3]).astype(low)
-
-    row_live = (jnp.arange(row_count, dtype=jnp.int32) < unit_lengths[0]).astype(jnp.float32)
-    grad_y = cotangent[0] * row_live[:, None]
-    grad_after_feed, grad_gain_3, grad_bias_3 = norm_backward(after_feed, gain_table[3], grad_y)
+    hidden, slope, block_output, grad_after_feed, feed_branch, sums_3 = feed_forward(
+        fold_count,
+        unit_lengths,
+        normed_feed,
+        feed_input_low,
+        feed_output_low,
+        after_cross,
+        cotangent[0],
+        norm_rows,
+    )
+
     positions = links.positions()
-    in_send, in_keep, out_grad, grad_normed = order.run(
-        lambda *arrays: feed_backward(fold_count, positions, *arrays),
-        grad_after_feed.astype(low),
+    in_send, in_keep, down_send, down_keep, grad_after_cross, cross_branch, sums_2 = order.run(
+        lambda *arrays: feed_backward(fold_count, links.tiles(), positions, *arrays),
+        feed_branch,
         normed_feed,
         hidden,
         slope,
         feed_input_low,
         feed_output_low,
+        after_cross,
+        grad_after_feed,
+        norm_rows,
     )
     if links.pairwise:
-        out_half = out_grad.shape[0] // 2
-        in_other, out_other = links.swap_core(in_send), links.swap_core(out_grad[:out_half])
-
-    def cross_entry(grad_after_feed, after_cross, grad_normed, gain_row, cross_output_low, cross_mixed):
-        grad_input, grad_gain, grad_bias = norm_backward(after_cross, gain_row, grad_normed)
-        grad_after_cross = grad_after_feed + grad_input
-        cross_branch = grad_after_cross.astype(low)
-        return (
-            grad_after_cross,
-            grad_gain,
-            grad_bias,
-            times_transposed(cross_branch, cross_output_low).astype(low),
-            weight_gradient(links.positions(True), cross_mixed, [cross_branch]),
-        )
-
-    grad_after_cross, grad_gain_2, grad_bias_2, grad_cross_mixed, cross_out = order.run(
-        cross_entry, grad_after_feed, after_cross, grad_normed, gain_table[2], cross_output_low, cross_mixed
+        in_other, down_other = links.swap_core(in_send), links.swap_core(down_send)
+
+    crossed, straight = links.positions(True), links.positions(False)
+    grad_cross_mixed, cross_out = order.run(
+        lambda branch, weights, mixed: (
+            times_transposed(branch, weights).astype(low),
+            weight_gradient(crossed, mixed, ([branch], False)),
+        ),
+        cross_branch,
+        cross_output_low,
+        cross_mixed,
     )
     if links.pairwise:
         feed_sum = order.run(
@@ -818,14 +996,14 @@
                 jnp.concatenate(arrays[:2], axis=1), jnp.concatenate(arrays[2:], axis=1)
             ),
             in_keep,
-            out_grad[out_half:],
+            down_keep,
             in_other,
-            out_other,
+            down_other,
         )
         feed_chips = links.sum_chips(feed_sum)
     else:
         feed_in_part = links.scatter_whole(in_send, in_keep)
-        feed_out_part = links.scatter_whole(out_grad[: out_grad.shape[0] // 2], out_grad[out_grad.shape[0] // 2 :])
+        feed_out_part = links.scatter_whole(down_send, down_keep)
 
     def cross_middle(cross_queries, cross_kv, cross_mixed, grad_cross_mixed, cross_totals):
         grad_q, grad_k, grad_v = attention_backward(
@@ -845,8 +1023,8 @@
             grad_q,
             grad_k,
             grad_v,
-            weight_gradient(links.positions(True), normed_cross, [grad_q]),
-            weight_gradient(links.positions(False), encoded, [grad_k, grad_v]),
+            weight_gradient(crossed, normed_cross, ([grad_q], False)),
+            weight_gradient(straight, encoded, ([grad_k, grad_v], False)),
         )
 
     grad_q, grad_k, grad_v, cross_query_grad, cross_kv_grad = order.run(
@@ -859,13 +1037,14 @@
     if links.pairwise:
         cross_sides = list(zip(cross_keep, [links.swap_core(side) for side in cross_send]))
 
-        def exchange(sides, at):
+        def exchange(sides, ats, flips):
             halves = order.run(
                 lambda *arrays: [links.first_pair(*arrays[i : i + 2]) for i in range(0, len(arrays), 2)],
                 *[array for side in sides for array in side],
             )
             return [
-                (stays, links.swap(goes, links.bit(at, flip))) for (goes, stays), flip in zip(halves, flips)
+                (stays, links.swap(goes, links.bit(at, flip)))
+                for (goes, stays), at, flip in zip(halves, ats, flips)
             ]
 
         def finish(sides):
@@ -879,30 +1058,29 @@
                 )
             )
 
-    def cross_exit(grad_q, grad_k, grad_v, cross_query, cross_first, after_self, gain_row, grad_after_cross):
-        grad_kv = jnp.concatenate([grad_k, grad_v], axis=1)
-        grad_normed = times_transposed(grad_q, cross_query)
-        grad_encoded = times_transposed(grad_kv, cross_first)
-        grad_input, grad_gain, grad_bias = norm_backward(after_self, gain_row, grad_normed)
-        grad_after_self = grad_after_cross + grad_input
-        return grad_after_self, grad_encoded, grad_gain, grad_bias
-
-    grad_after_self, grad_encoded, grad_gain_1, grad_bias_1 = order.run(
-        cross_exit, grad_q, grad_k, grad_v, cross_query, cross_first, after_self, gain_table[1], grad_after_cross
+    grad_after_self, self_branch, sums_1 = order.run(
+        lambda grad_q, held, *arrays: input_gradient(1, [grad_q], [(held, cross_at + split)], *arrays, True),
+        grad_q,
+        cross_held,
+        after_self,
+        grad_after_cross,
+        norm_rows,
     )
     if links.pairwise:
-        cross_sides = exchange(cross_sides, 0)
+        cross_sides = exchange(cross_sides, [0, 0], flips)
     else:
         cross_part = links.scatter_whole(*[jnp.concatenate(side, axis=1) for side in (cross_send, cross_keep)])
-
-    def self_entry(grad_after_self, self_output_low, self_mixed):
-        self_branch = grad_after_self.astype(low)
-        return (
-            times_transposed(self_branch, self_output_low).astype(low),
-            weight_gradient(links.positions(True), self_mixed, [self_branch]),
-        )
-
-    grad_self_mixed, self_out = order.run(self_entry, grad_after_self, self_output_low, self_mixed)
+    grad_k_cross, grad_v_cross = grad_k, grad_v
+
+    grad_self_mixed, self_out = order.run(
+        lambda branch, weights, mixed: (
+            times_transposed(branch, weights).astype(low),
+            weight_gradient(crossed, mixed, ([branch], False)),
+        ),
+        self_branch,
+        self_output_low,
+        self_mixed,
+    )
     grad_q, grad_k, grad_v = order.run(
         lambda query_key, self_values, self_mixed, grad_self_mixed, self_totals: attention_backward(
             unit_lengths,
@@ -924,74 +1102,65 @@
         self_totals,
     )
     if links.pairwise:
-        cross_sides = exchange(cross_sides, 1)
-        feed_chips = order.after(feed_chips)
-        feed_part = lax.psum_scatter(feed_chips, "fsdp", scatter_dimension=0, tiled=True)
-    first_send, first_keep = order.run(
-        lambda *grads: weight_gradient(links.positions(False), normed_self, list(grads)), grad_q, grad_k
-    )
+        cross_sides = exchange(cross_sides, [1, 1], flips)
+        feed_part = lax.psum_scatter(order.after(feed_chips), "fsdp", scatter_dimension=0, tiled=True)
+    first_send, first_keep, second_send, second_keep = order.run(
+        lambda normed, grad_q, grad_k, grad_v: weight_gradient(
+            straight, normed, ([grad_q, grad_k], False), ([grad_v], links.pairwise)
+        ),
+        normed_self,
+        grad_q,
+        grad_k,
+        grad_v,
+    )
+    second_send, second_keep = [
+        jnp.concatenate(pair, axis=1) for pair in zip((second_send, second_keep), self_out)
+    ]
     if links.pairwise:
-        first_other = links.swap_core(first_send)
-    second_send, second_keep = order.run(
-        lambda grad, *out: [
-            jnp.concatenate(pair, axis=1)
-            for pair in zip(weight_gradient(links.positions(True), normed_self, [grad]), out)
-        ],
-        grad_v,
-        *self_out,
-    )
-    if links.pairwise:
-        self_sides = [(first_keep, first_other), (second_keep, links.swap_core(second_send))]
+        self_sides = [(first_keep, links.swap_core(first_send)), (second_keep, links.swap_core(second_send))]
+        self_sides = exchange(self_sides, [0, 0], flips)
         cross_parts = finish(cross_sides)
-        self_sides = exchange(self_sides, 0)
-
-    def self_exit(grad_q, grad_k, grad_v, self_first, self_value, gain_row, grad_after_self, *others):
-        grad_qk = jnp.concatenate([grad_q, grad_k], axis=1)
-        grad_normed = times_transposed(grad_qk, self_first) + times_transposed(grad_v, self_value)
-        grad_input, grad_gain, grad_bias = norm_backward(layer_input, gain_row, grad_normed)
-        grad_tables = jnp.stack([grad_gain, *others[:3], grad_bias, *others[3:]])
-        return grad_after_self + grad_input, jnp.pad(grad_tables.T, ((0, 0), (0, LANES - 8))).astype(low)
-
-    grad_states, grad_tables = order.run(
-        self_exit,
+
+    grad_states, sums_0 = order.run(
+        lambda grad_q, grad_k, grad_v, first, value, *arrays: input_gradient(
+            0, [grad_q, grad_k, grad_v], [(first, 0), (first, width), (value, 0)], *arrays, False
+        ),
         grad_q,
         grad_k,
         grad_v,
         self_first,
-        self_value,
-        gain_table[0],
+        self_second,
+        unit_states[0],
         grad_after_self,
-        grad_gain_1,
-        grad_gain_2,
-        grad_gain_3,
-        grad_bias_1,
-        grad_bias_2,
-        grad_bias_3,
-    )
+        norm_rows,
+    )
+    sums = [sums_0, sums_1, sums_2, sums_3]
+    grad_tables = jnp.stack([part[0] for part in sums] + [part[1] for part in sums])
+    grad_tables = jnp.pad(grad_tables.T, ((0, 0), (0, LANES - 8))).astype(low)
     table_send, table_keep = links.halves(grad_tables, False)
+    grad_encoded = times_transposed(jnp.concatenate([grad_k_cross, grad_v_cross], axis=1), cross_first)
     if links.pairwise:
+        self_sides = exchange(self_sides, [1, 1], flips)
+        table_other = links.swap_core(table_send)
         cross_part = order.run(links.sum_fsdp, cross_parts)
-        table_goes, table_stays = links.first_pair(table_keep, links.swap_core(table_send))
+        table_goes, table_stays = order.run(links.first_pair, table_keep, table_other)
         table_side = (table_stays, links.swap(table_goes, links.bit(0, False)))
-        self_sides = exchange(self_sides, 1)
         feed_part = order.run(lambda part: part.astype(jnp.float32), feed_part)
-        table_goes, table_stays = links.first_pair(*table_side)
+        self_parts = finish(self_sides)
+        table_goes, table_stays = order.run(links.first_pair, *table_side)
         table_side = (table_stays, links.swap(table_goes, links.bit(1, False)))
-        self_part = links.sum_fsdp(finish(self_sides + [table_side]))
+        table_part = links.sum_all_fsdp(links.sum_cores(*table_side))
+        self_part = links.sum_fsdp(self_parts)
         feed_in_part, feed_out_part = feed_part[:, : 4 * width], feed_part[:, 4 * width :]
         feed_out_part = jnp.concatenate(
             [feed_out_part[:, at * width : (at + 1) * width] for at in range(4)], axis=0
         )
     else:
         self_part = jnp.concatenate(
-            [
-                links.scatter_whole(*pair)
-                for pair in ((first_send, first_keep), (second_send, second_keep), (table_send, table_keep))
-            ],
-            axis=1,
+            [links.scatter_whole(first_send, first_keep), links.scatter_whole(second_send, second_keep)], axis=1
         )
-    self_in_part, self_out_part = self_part[:, : 3 * width], self_part[:, 3 * width : 4 * width]
-    table_part = self_part[:, 4 * width :]
+        table_part = links.scatter_whole(table_send, table_keep)
+    self_in_part, self_out_part = self_part[:, : 3 * width], self_part[:, 3 * width :]
     cross_in_part = jnp.concatenate([cross_part[:, split : 3 * width], cross_part[:, :split]], axis=1)
     cross_out_part = cross_part[:, 3 * width :]
 

time: 574 us -> 554 us (0.965)
  Pallas kernels: 162 us -> 200 us
  local copies, waits for them, and re-layouts: 45.2 us -> 25.6 us
  other arithmetic: 76.1 us -> 57.8 us
  between operations: 32.2 us -> 16.1 us
  matrix products: 51.8 us -> 39.3 us
  starting transfers between devices: 31.4 us -> 41.6 us
    pallas_call x8 -> x9, Pallas kernels: 95.5 us -> 131 us  [the longest x1 43 us: feed_backward(): pl.pallas_call(functools.partial(feed_backward_kernel, rows), grid_spec=p...]
    slice x7 -> x11, local copies, waits for them, and re-layouts: 16.5 us -> 1.73 us  [the longest x1 0.99 us: halves(): return (ordered[:half], ordered[half:])]
    ppermute x3 -> x5, waiting for transfers between devices: 24.9 us -> 39.7 us  [swap_fsdp(): lax.ppermute(array, 'fsdp', [(i, i ^ bit) for i in range(self.fsdp_count)])]
    dot_general x6 -> x3, matrix products: 26.7 us -> 14 us  [times_transposed(): lax.dot_general(left, right, (((1,), (1,)), ((), ())), preferred_element_...]
    ppermute x14, waiting for transfers between devices: 68.2 us -> 56.9 us  [swap(): return lax.ppermute(array, 'h', [(i, i ^ bit) for i in range(self.h_count)])]
    convert_element_type x4 -> x1, other arithmetic: 7.57 us -> 0.01 us  [sum_all_fsdp(): grad = grad.astype(jnp.float32)]
    ppermute x3 -> x5, starting transfers between devices: 5.7 us -> 12.7 us  [swap_fsdp(): lax.ppermute(array, 'fsdp', [(i, i ^ bit) for i in range(self.fsdp_count)])]
    reduce_scatter x1, waiting for transfers between devices: 6.28 us -> 0.01 us  [body(): lax.psum_scatter(order.after(feed_chips), 'fsdp', scatter_dimension=0, ti...]
  transfers between devices with their start and end apart: 31 -> 33, of which waited for: 14 -> 17; matrix products, arithmetic and copies ran while one was open for 21% -> 16% of each run, Pallas kernels for 17% -> 22%
where the time goes in v4:
time: 554 us; the launch traced here: 547 us
  Pallas kernels  200 us (36%)
  waiting for transfers between devices  167 us (30%)
  other arithmetic  57.8 us (10%)
  starting transfers between devices  41.6 us (8%)
  matrix products  39.3 us (7%)
  local copies, waits for them, and re-layouts  25.6 us (5%)
  between operations  16.1 us (3%)
    ppermute x14, waiting for transfers between devices, swap(): return lax.ppermute(array, 'h', [(i, i ^ bit) for i in range(self.h_count)])  56.9 us
    all_gather x1, waiting for transfers between devices, gather(): return lax.all_gather(shard, BOTH, axis=0, tiled=True)  44 us
    pallas_call x1, Pallas kernels, feed_backward(): pl.pallas_call(functools.partial(feed_backward_kernel, rows), grid_spec=p...  43 us
    ppermute x5, waiting for transfers between devices, swap_fsdp(): lax.ppermute(array, 'fsdp', [(i, i ^ bit) for i in range(self.fsdp_count)])  39.7 us
    pallas_call x5, Pallas kernels, weight_gradient(): pl.pallas_call(functools.partial(weight_gradient_kernel, starts, group_of...  35.6 us
    pallas_call x2, Pallas kernels, attention_backward(): pl.pallas_call(functools.partial(attention_backward_kernel, causal), grid...  33.4 us
    convert_element_type x15, other arithmetic, sum_cores(): (keep.astype(jnp.float32) + other.astype(jnp.float32)).astype(jnp.bfloat16)  32.1 us
    pallas_call x1, Pallas kernels, feed_forward(): pl.pallas_call(functools.partial(feed_forward_kernel, rows), grid_spec=pl...  26.3 us
  transfers between devices with their start and end apart: 33, of which 17 were waited for; matrix products, arithmetic and copies ran while one was open for 16% of the time, Pallas kernels for 22%

profile of v4, /device:TPU:0, one launch (start us, length us, event | category | flops | bytes accessed | tf_op | source)
XLA Modules:
  0.0 547.2 jit_solution(14303838396591219873)
XLA Ops:
  10.9 3.1 collective-permute-start
  14.0 2.6 collective-permute-start.1
  17.1 8.4 %collective-permute-done.refs_1_ = bf16[32,4224]{1,0:T(8,128)(2,1)S(1)} collective-permute-done((bf16[32,4224]{1,0:T(8,128)(2,1)S(1)}, bf16[32,4224]{1,0:T(8,128)(2,1)S(1)}, u32[]{:S(2)}, u32[]{:S(2)}) %collective-permute-start) | collective-permute-done | bytes 270368 | tf_op jit(solution)/shard_map/ppermute | solution.py:765
  25.5 14.9 %collective-permute-done.1.refs_2_ = bf16[32,4224]{1,0:T(8,128)(2,1)S(1)} collective-permute-done((bf16[32,4224]{1,0:T(8,128)(2,1)S(1)}, bf16[32,4224]{1,0:T(8,128)(2,1)S(1)}, u32[]{:S(2)}, u32[]{:S(2)}) %collective-permute-start.1) | collective-permute-done | bytes 270368 | tf_op jit(solution)/shard_map/ppermute | solution.py:765
  42.3 2.7 place_rows.4
  46.1 1.6 collective-permute-start.4
  48.8 1.6 collective-permute-start.3
  50.4 10.3 %collective-permute-done.3 = bf16[128,2048]{1,0:T(8,128)(2,1)S(1)} collective-permute-done((bf16[128,2048]{1,0:T(8,128)(2,1)S(1)}, bf16[128,2048]{1,0:T(8,128)(2,1)S(1)}, u32[]{:S(2)}, u32[]{:S(2)}) %collective-permute-start.3) | collective-permute-done | bytes 524320 | tf_op jit(solution)/shard_map/ppermute | solution.py:759
  60.8 1.6 collective-permute-start.6
  63.0 29.5 %collective-permute-done.5 = bf16[256,2048]{1,0:T(8,128)(2,1)S(1)} collective-permute-done((bf16[256,2048]{1,0:T(8,128)(2,1)S(1)}, bf16[256,2048]{1,0:T(8,128)(2,1)S(1)}, u32[]{:S(2)}, u32[]{:S(2)}) %collective-permute-start.5) | collective-permute-done | bytes 1048608 | tf_op jit(solution)/shard_map/ppermute | solution.py:759
  92.5 12.9 %collective-permute-done.6 = bf16[256,2176]{1,0:T(8,128)(2,1)S(1)} collective-permute-done((bf16[256,2176]{1,0:T(8,128)(2,1)S(1)}, bf16[256,2176]{1,0:T(8,128)(2,1)S(1)}, u32[]{:S(2)}, u32[]{:S(2)}) %collective-permute-start.6) | collective-permute-done | bytes 1114144 | tf_op jit(solution)/shard_map/ppermute | solution.py:759
  113.3 1.8 bitcast_convert_fusion
  115.3 4.5 place_rows.6.refs_5_
  119.8 4.4 place_rows.5.refs_3_.refs_4_
  124.4 5.5 fusion.39
  132.3 3.0 convolution_convert_fusion.3.v_ref
  135.2 5.3 convolution_convert_fusion.q_ref.k_ref
  140.5 13.1 %attention_forward.2 = (bf16[768,1024]{1,0:T(8,128)(2,1)}, f32[8,2,768]{2,1,0:T(2,128)}) custom-call(s32[1]{0:T(128)S(6)} %copy.59.limit_ref, bf16[768,2048]{1,0:T(8,128)(2,1)} %convolution_convert_fusion.q_ref.k_ref, bf16[768,2048]{1,0:T(8,128)(2,1)} %convolution_convert_fusion.q_ref.k_ref, bf16[768,1024]{1,0:T(8,128)(2,1)} %convolution_convert_fusion.3.v_ref), custom_call_target="tpu_custom_call" | custom-call | flops 1024 | bytes 1024 | tf_op jit(solution)/shard_map/attention_forward/pallas_call | solution.py:176
  153.7 3.3 fusion.48
  159.2 44.0 %all-gather.2.cloned.1.call-done.input_ref.output_ref.refs_1_ = bf16[1024,12288]{1,0:T(8,128)(2,1)} async-done(((bf16[32,12288]{1,0:T(8,128)(2,1)}), bf16[1024,12288]{1,0:T(8,128)(2,1)}) %all-gather.2.cloned.1.call-update) | async-done | bytes 25165840 | tf_op jit(solution)/shard_map/all_gather | solution.py:768
  203.2 4.5 fusion.12.q_ref
  207.7 4.4 fusion.7.k_ref.v_ref
  212.7 9.1 %attention_forward.3 = (bf16[768,1024]{1,0:T(8,128)(2,1)}, f32[8,2,768]{2,1,0:T(2,128)}) custom-call(s32[1]{0:T(128)S(6)} %copy.60.limit_ref, bf16[768,1024]{1,0:T(8,128)(2,1)} %fusion.12.q_ref, bf16[256,2048]{1,0:T(8,128)(2,1)} %fusion.7.k_ref.v_ref, bf16[256,2048]{1,0:T(8,128)(2,1)} %fusion.7.k_ref.v_ref), custom_call_target="tpu_custom_call" | custom-call | flops 1024 | bytes 1024 | tf_op jit(solution)/shard_map/attention_forward/pallas_call | solution.py:176
  221.8 4.9 fusion.49
  227.1 1.8 add_convert_fusion.1.normed_ref
  228.9 26.3 %feed_forward.1 = (bf16[768,4096]{1,0:T(8,128)(2,1)}, bf16[768,4096]{1,0:T(8,128)(2,1)}, bf16[768,1024]{1,0:T(8,128)(2,1)}, f32[768,1024]{1,0:T(8,128)}, bf16[768,1024]{1,0:T(8,128)(2,1)}, /*index=5*/f32[2,1024]{1,0:T(2,128)}) custom-call(s32[1]{0:T(128)S(6)} %copy.59.limit_ref, bf16[768,1024]{1,0:T(8,128)(2,1)} %add_convert_fusion.1.normed_ref, ...), custom_call_target="tpu_custom_call" | custom-call | flops 1024 | bytes 1024 | tf_op jit(solution)/shard_map/feed_forward/pallas_call | solution.py:406
  255.2 43.0 %feed_backward.1 = (bf16[512,4096]{1,0:T(8,128)(2,1)}, bf16[512,4096]{1,0:T(8,128)(2,1)}, bf16[512,4096]{1,0:T(8,128)(2,1)}, bf16[512,4096]{1,0:T(8,128)(2,1)}, ...) custom-call(s32[8]{0:T(128)} %pad_add_fusion.2.tiles_ref, s32[8]{0:T(128)} %fusion.30.positions_ref, ...), custom_call_target="tpu_custom_call" | custom-call | flops 1024 | bytes 1024 | tf_op jit(solution)/shard_map/feed_backward/pallas_call | solution.py:513
  299.3 6.0 %weight_gradient.5 = (bf16[512,1024]{1,0:T(8,128)(2,1)}, bf16[512,1024]{1,0:T(8,128)(2,1)}) custom-call(s32[8]{0:T(128)} %get-tuple-element.371.positions_ref, bf16[768,1024]{1,0:T(8,128)(2,1)} %get-tuple-element.218.x_ref.mixed_ref, bf16[768,1024]{1,0:T(8,128)(2,1)} %get-tuple-element.206.refs_0_), custom_call_target="tpu_custom_call" | custom-call | flops 1024 | bytes 1024 | tf_op jit(solution)/shard_map/weight_gradient/pallas_call | solution.py:613
  305.3 4.6 convolution_convert_fusion.2.grad_ref
  309.9 1.8 collective-permute-done.9
  311.8 7.7 %add_convert_fusion = bf16[512,8192]{1,0:T(8,128)(2,1)} fusion(bf16[512,4096]{1,0:T(8,128)(2,1)S(1)} %copy-done.7, bf16[512,4096]{1,0:T(8,128)(2,1)S(1)} %copy-done.6, bf16[512,4096]{1,0:T(8,128)(2,1)} %collective-permute-done.10, bf16[512,4096]{1,0:T(8,128)(2,1)} %collective-permute-done.9), kind=kLoop, calls=%fused_computation | loop fusion | flops 41943040 | bytes 25165824 | tf_op jit(solution)/shard_map/convert_element_type | solution.py:810
  319.5 12.7 %attention_backward.2 = (bf16[768,1024]{1,0:T(8,128)(2,1)}, bf16[256,1024]{1,0:T(8,128)(2,1)}, bf16[256,1024]{1,0:T(8,128)(2,1)}) custom-call(s32[1]{0:T(128)S(6)} %copy.60.limit_ref, bf16[768,1024]{1,0:T(8,128)(2,1)} %fusion.12.q_ref, bf16[256,2048]{1,0:T(8,128)(2,1)} %fusion.7.k_ref.v_ref, bf16[256,2048]{1,0:T(8,128)(2,1)} %fusion.7.k_ref.v_ref, ...), custom_call_target="tpu_custom_call" | custom-call | flops 1024 | bytes 1024 | tf_op jit(solution)/shard_map/attention_backward/pallas_call | solution.py:277
  332.2 6.1 %weight_gradient.6 = (bf16[512,1024]{1,0:T(8,128)(2,1)}, bf16[512,1024]{1,0:T(8,128)(2,1)}) custom-call(s32[8]{0:T(128)} %get-tuple-element.371.positions_ref, bf16[768,1024]{1,0:T(8,128)(2,1)} %copy-done.4, bf16[768,1024]{1,0:T(8,128)(2,1)} %get-tuple-element.228.refs_0_), custom_call_target="tpu_custom_call" | custom-call | flops 1024 | bytes 1024 | tf_op jit(solution)/shard_map/weight_gradient/pallas_call | solution.py:613
  338.4 2.8 pad_maximum_fusion.1
  341.4 6.0 %weight_gradient.7 = (bf16[512,2048]{1,0:T(8,128)(2,1)}, bf16[512,2048]{1,0:T(8,128)(2,1)}) custom-call(s32[8]{0:T(128)} %get-tuple-element.372.positions_ref.table_ref, bf16[256,1024]{1,0:T(8,128)(2,1)} %bitcast.49, bf16[256,1024]{1,0:T(8,128)(2,1)} %get-tuple-element.222.refs_0_, bf16[256,1024]{1,0:T(8,128)(2,1)} %get-tuple-element.223.refs_1_), custom_call_target="tpu_custom_call" | custom-call | flops 1024 | bytes 1024 | tf_op jit(solution)/shard_map/weight_gradient/pallas_call | solution.py:613
  347.7 10.4 %input_gradient.2 = (f32[768,1024]{1,0:T(8,128)}, bf16[768,1024]{1,0:T(8,128)(2,1)}, f32[2,1024]{1,0:T(2,128)}) custom-call(bf16[768,1024]{1,0:T(8,128)(2,1)} %get-tuple-element.228.refs_0_, bf16[1024,12288]{1,0:T(8,128)(2,1)} %all-gather.2.cloned.1.call-done.input_ref.output_ref.refs_1_, f32[768,1024]{1,0:T(8,128)} %copy-done.2, ...), custom_call_target="tpu_custom_call" | custom-call | flops 1024 | bytes 1024 | tf_op jit(solution)/shard_map/input_gradient/pallas_call | solution.py:661
  358.2 1.5 pad_maximum_fusion
  361.1 3.6 add_convert_fusion.8
  365.9 1.8 add_convert_fusion.10
  368.5 5.8 %weight_gradient.8 = (bf16[512,1024]{1,0:T(8,128)(2,1)}, bf16[512,1024]{1,0:T(8,128)(2,1)}) custom-call(s32[8]{0:T(128)} %get-tuple-element.371.positions_ref, bf16[768,1024]{1,0:T(8,128)(2,1)} %get-tuple-element.247.x_ref.mixed_ref, bf16[768,1024]{1,0:T(8,128)(2,1)} %get-tuple-element.240.refs_0_), custom_call_target="tpu_custom_call" | custom-call | flops 1024 | bytes 1024 | tf_op jit(solution)/shard_map/weight_gradient/pallas_call | solution.py:613
  374.3 4.6 convolution_convert_fusion.1.grad_ref
  378.9 20.7 %attention_backward.3 = (bf16[768,1024]{1,0:T(8,128)(2,1)}, bf16[768,1024]{1,0:T(8,128)(2,1)}, bf16[768,1024]{1,0:T(8,128)(2,1)}) custom-call(s32[1]{0:T(128)S(6)} %copy.59.limit_ref, bf16[768,2048]{1,0:T(8,128)(2,1)} %convolution_convert_fusion.q_ref.k_ref, bf16[768,2048]{1,0:T(8,128)(2,1)} %convolution_convert_fusion.q_ref.k_ref, ...), custom_call_target="tpu_custom_call" | custom-call | flops 1024 | bytes 1024 | tf_op jit(solution)/shard_map/attention_backward/pallas_call | solution.py:277
  399.6 2.0 collective-permute-done.14
  401.7 2.6 add_convert_fusion.20
  404.2 2.6 add_convert_fusion.22
  406.8 11.6 %weight_gradient.9 = (bf16[512,2048]{1,0:T(8,128)(2,1)}, bf16[512,2048]{1,0:T(8,128)(2,1)}, bf16[512,1024]{1,0:T(8,128)(2,1)}, bf16[512,1024]{1,0:T(8,128)(2,1)}) custom-call(s32[8]{0:T(128)} %get-tuple-element.372.positions_ref.table_ref, bf16[768,1024]{1,0:T(8,128)(2,1)} %copy-done.3, bf16[768,1024]{1,0:T(8,128)(2,1)} %get-tuple-element.273.refs_0_, ...), custom_call_target="tpu_custom_call" | custom-call | flops 1024 | bytes 1024 | tf_op jit(solution)/shard_map/weight_gradient/pallas_call | solution.py:613
  418.5 2.8 pad_maximum_fusion.3
  425.5 3.3 collective-permute-done.18
  430.1 3.4 add_convert_fusion.4
  435.1 1.8 add_convert_fusion.6
  441.4 4.7 all-to-all-start
  446.1 15.6 %input_gradient.3 = (f32[768,1024]{1,0:T(8,128)}, f32[2,1024]{1,0:T(2,128)}) custom-call(bf16[768,1024]{1,0:T(8,128)(2,1)} %get-tuple-element.273.refs_0_, bf16[768,1024]{1,0:T(8,128)(2,1)} %get-tuple-element.274.refs_1_, bf16[768,1024]{1,0:T(8,128)(2,1)} %get-tuple-element.275.refs_2_, bf16[1024,2048]{1,0:T(8,128)(2,1)} %place_rows.5.refs_3_.refs_4_, ...), custom_call_target="tpu_custom_call" | custom-call | flops 1024 | bytes 1024 | tf_op jit(solution)/shard_map/input_gradient/pallas_call | solution.py:661
  463.4 4.8 fusion.15
  468.2 2.3 place_rows.7
  471.6 2.6 add_convert_fusion.14
  475.2 2.4 add_convert_fusion.16
  478.7 20.6 %all-to-all-done = bf16[4,32,4096]{2,1,0:T(8,128)(2,1)S(1)} async-done(((bf16[4,32,4096]{2,1,0:T(8,128)(2,1)}), bf16[4,32,4096]{2,1,0:T(8,128)(2,1)S(1)}, u32[]{:S(2)}, u32[]{:S(2)}) %all-to-all-start) | async-done | bytes 1048608 | tf_op jit(solution)/shard_map/all_to_all | solution.py:813
  503.2 5.5 %all-to-all-start.1 = ((bf16[4,32,4096]{2,1,0:T(8,128)(2,1)}), bf16[4,32,4096]{2,1,0:T(8,128)(2,1)S(1)}, u32[]{:S(2)}, u32[]{:S(2)}) async-start(bf16[4,32,4096]{2,1,0:T(8,128)(2,1)} %bitcast.18), calls=%async_computation.3 | async-start | bytes 2097152 | tf_op jit(solution)/shard_map/all_to_all | solution.py:813
  509.5 1.6 collective-permute-start.25
  511.8 1.7 collective-permute-done.25
  513.5 2.3 collective-permute-start.26
  516.6 10.6 %collective-permute-done.26 = f32[128,128]{1,0:T(8,128)S(1)} collective-permute-done((f32[128,128]{1,0:T(8,128)S(1)}, f32[128,128]{1,0:T(8,128)S(1)}, u32[]{:S(2)}, u32[]{:S(2)}) %collective-permute-start.26) | collective-permute-done | bytes 65568 | tf_op jit(solution)/shard_map/ppermute | solution.py:765
  527.3 4.7 collective-permute-start.27
  532.8 4.6 collective-permute-done.27
  (222 shorter events, 53.0 us)
Async XLA Ops:
  7.2 2.5 copy-start.29
  7.2 2.5 copy-start.34
  7.2 3.5 copy-start.30
  7.2 196.0 %all-gather.2.cloned.1.call-start = ((), (), s32[]{:S(2)}) async-start(), calls=%async_computation.4 | async-start | bytes 25952256 | tf_op jit(solution)/shard_map/all_gather | solution.py:768
  8.4 2.3 copy-start.39
  10.6 427.2 %reduce-scatter.3.cloned.1.call-start = ((), (), s32[]{:S(2)}) async-start(), calls=%async_computation.5 | async-start | bytes 10485760 | tf_op jit(solution)/shard_map/reduce_scatter | solution.py:833
  10.9 30.7 %copy-start.23 = (bf16[32,4224]{1,0:T(8,128)(2,1)}, bf16[32,4224]{1,0:T(8,128)(2,1)S(1)}, u32[]{:S(2)}) copy-start(bf16[32,4224]{1,0:T(8,128)(2,1)S(1)} %fusion.23.refs_0_) | copy-start | bytes 811012
  10.9 14.6 %collective-permute-start = (bf16[32,4224]{1,0:T(8,128)(2,1)S(1)}, bf16[32,4224]{1,0:T(8,128)(2,1)S(1)}, u32[]{:S(2)}, u32[]{:S(2)}) collective-permute-start(bf16[32,4224]{1,0:T(8,128)(2,1)S(1)} %fusion.23.refs_0_), channel_id=1, source_target_pairs={{0,1},{1,0},{2,3},{3,2},{4,5},{5,4},{6,7},{7,6},{8,9},{9,8},{10,11... | collective-permute-start | bytes 811016 | tf_op jit(solution)/shard_map/ppermute | solution.py:765
  14.0 26.4 %collective-permute-start.1 = (bf16[32,4224]{1,0:T(8,128)(2,1)S(1)}, bf16[32,4224]{1,0:T(8,128)(2,1)S(1)}, u32[]{:S(2)}, u32[]{:S(2)}) collective-permute-start(bf16[32,4224]{1,0:T(8,128)(2,1)S(1)} %fusion.23.refs_0_), channel_id=1, source_target_pairs={{0,2},{1,3},{2,0},{3,1},{4,6},{5,7},{6,4},{7,5},{8,10},{9,11},{10,... | collective-permute-start | bytes 811016 | tf_op jit(solution)/shard_map/ppermute | solution.py:765
  16.6 25.0 %collective-permute-start.2 = (bf16[32,4224]{1,0:T(8,128)(2,1)S(1)}, bf16[32,4224]{1,0:T(8,128)(2,1)S(1)}, u32[]{:S(2)}, u32[]{:S(2)}) collective-permute-start(bf16[32,4224]{1,0:T(8,128)(2,1)S(1)} %fusion.23.refs_0_), channel_id=1, source_target_pairs={{0,3},{1,2},{2,1},{3,0},{4,7},{5,6},{6,5},{7,4},{8,11},{9,10},{10,... | collective-permute-start | bytes 811016 | tf_op jit(solution)/shard_map/ppermute | solution.py:765
  25.5 16.1 %copy-start.31 = (bf16[32,4224]{1,0:T(8,128)(2,1)}, bf16[32,4224]{1,0:T(8,128)(2,1)S(1)}, u32[]{:S(2)}) copy-start(bf16[32,4224]{1,0:T(8,128)(2,1)S(1)} %collective-permute-done.refs_1_) | copy-start | bytes 811012
  46.1 14.6 %collective-permute-start.4 = (bf16[128,2176]{1,0:T(8,128)(2,1)S(1)}, bf16[128,2176]{1,0:T(8,128)(2,1)S(1)}, u32[]{:S(2)}, u32[]{:S(2)}) collective-permute-start(bf16[128,2176]{1,0:T(8,128)(2,1)S(1)} %slice.398), channel_id=1, source_target_pairs={{0,16},{8,24},{16,0},{24,8},{1,17},{9,25},{17,1},{25,9},{2,18},{10... | collective-permute-start | bytes 1671176 | tf_op jit(solution)/shard_map/ppermute | solution.py:759
  48.8 11.9 %collective-permute-start.3 = (bf16[128,2048]{1,0:T(8,128)(2,1)S(1)}, bf16[128,2048]{1,0:T(8,128)(2,1)S(1)}, u32[]{:S(2)}, u32[]{:S(2)}) collective-permute-start(bf16[128,2048]{1,0:T(8,128)(2,1)S(1)} %slice.397), channel_id=1, source_target_pairs={{0,8},{8,0},{16,24},{24,16},{1,9},{9,1},{17,25},{25,17},{2,10},{10... | collective-permute-start | bytes 1572872 | tf_op jit(solution)/shard_map/ppermute | solution.py:759
  60.8 44.6 %collective-permute-start.6 = (bf16[256,2176]{1,0:T(8,128)(2,1)S(1)}, bf16[256,2176]{1,0:T(8,128)(2,1)S(1)}, u32[]{:S(2)}, u32[]{:S(2)}) collective-permute-start(bf16[256,2176]{1,0:T(8,128)(2,1)S(1)} %constant_dynamic-update-slice_fusion.2), channel_id=1, source_target_pairs={{0,8},{8,0},{16,24},{24,16},{1,9},{9,1},{17,25},{25,17},{2,10},{10... | collective-permute-start | bytes 3342344 | tf_op jit(solution)/shard_map/ppermute | solution.py:759
  62.5 30.0 %collective-permute-start.5 = (bf16[256,2048]{1,0:T(8,128)(2,1)S(1)}, bf16[256,2048]{1,0:T(8,128)(2,1)S(1)}, u32[]{:S(2)}, u32[]{:S(2)}) collective-permute-start(bf16[256,2048]{1,0:T(8,128)(2,1)S(1)} %constant_dynamic-update-slice_fusion), channel_id=1, source_target_pairs={{0,16},{8,24},{16,0},{24,8},{1,17},{9,25},{17,1},{25,9},{2,18},{10... | collective-permute-start | bytes 3145736 | tf_op jit(solution)/shard_map/ppermute | solution.py:759
  107.6 4.5 copy-start.41
  107.6 7.7 %collective-permute-start.8 = (bf16[512,2176]{1,0:T(8,128)(2,1)}, bf16[512,2176]{1,0:T(8,128)(2,1)}, u32[]{:S(2)}, u32[]{:S(2)}) collective-permute-start(bf16[512,2176]{1,0:T(8,128)(2,1)} %constant_dynamic-update-slice_fusion.6.refs_0_), channel_id=1, source_target_pairs={{0,4},{4,0},{1,5},{5,1},{2,6},{6,2},{3,7},{7,3},{8,12},{12,8},{9,1... | collective-permute-start | bytes 6684680 | tf_op jit(solution)/shard_map/ppermute | solution.py:762
  109.8 5.5 %collective-permute-start.7 = (bf16[512,2048]{1,0:T(8,128)(2,1)}, bf16[512,2048]{1,0:T(8,128)(2,1)}, u32[]{:S(2)}, u32[]{:S(2)}) collective-permute-start(bf16[512,2048]{1,0:T(8,128)(2,1)} %constant_dynamic-update-slice_fusion.4.refs_0_), channel_id=1, source_target_pairs={{0,4},{4,0},{1,5},{5,1},{2,6},{6,2},{3,7},{7,3},{8,12},{12,8},{9,1... | collective-permute-start | bytes 6291464 | tf_op jit(solution)/shard_map/ppermute | solution.py:762
  119.8 4.4 slice-start.1
  124.4 5.5 %copy-start.22 = (f32[8,1024]{1,0:T(8,128)}, f32[8,1024]{1,0:T(8,128)S(1)}, u32[]{:S(2)}) copy-start(f32[8,1024]{1,0:T(8,128)S(1)} %convert_bitcast_fusion.rows_ref.refs_4_.refs_8_) | copy-start | bytes 98308
  132.3 3.0 copy-start.3
  132.3 3.0 copy-start.1
  140.5 13.2 %copy-start.5 = (bf16[1,768,1024]{2,1,0:T(8,128)(2,1)S(1)}, bf16[1,768,1024]{2,1,0:T(8,128)(2,1)}, u32[]{:S(2)}) copy-start(bf16[1,768,1024]{2,1,0:T(8,128)(2,1)} %param.15) | copy-start | bytes 4718596
  140.5 13.2 %copy-start.18 = (bf16[1024,1024]{1,0:T(8,128)(2,1)S(1)}, bf16[1024,1024]{1,0:T(8,128)(2,1)}, u32[]{:S(2)}) copy-start(bf16[1024,1024]{1,0:T(8,128)(2,1)} %get-tuple-element.241) | copy-start | bytes 6291460
  159.2 48.5 %copy-start.4 = (bf16[768,1024]{1,0:T(8,128)(2,1)}, bf16[768,1024]{1,0:T(8,128)(2,1)S(1)}, u32[]{:S(2)}) copy-start(bf16[768,1024]{1,0:T(8,128)(2,1)S(1)} %add_convert_fusion.2.x_ref) | copy-start | bytes 4718596
  159.2 48.5 %copy-start.28 = (bf16[1,256,1024]{2,1,0:T(8,128)(2,1)S(1)}, bf16[1,256,1024]{2,1,0:T(8,128)(2,1)}, u32[]{:S(2)}) copy-start(bf16[1,256,1024]{2,1,0:T(8,128)(2,1)} %param.16) | copy-start | bytes 1572868
  298.2 11.7 %collective-permute-start.10 = (bf16[512,4096]{1,0:T(8,128)(2,1)}, bf16[512,4096]{1,0:T(8,128)(2,1)}, u32[]{:S(2)}, u32[]{:S(2)}) collective-permute-start(bf16[512,4096]{1,0:T(8,128)(2,1)} %get-tuple-element.202), channel_id=1, source_target_pairs={{0,4},{4,0},{1,5},{5,1},{2,6},{6,2},{3,7},{7,3},{8,12},{12,8},{9,1... | collective-permute-start | bytes 12582920 | tf_op jit(solution)/shard_map/ppermute | solution.py:762
  298.6 13.2 %collective-permute-start.9 = (bf16[512,4096]{1,0:T(8,128)(2,1)}, bf16[512,4096]{1,0:T(8,128)(2,1)}, u32[]{:S(2)}, u32[]{:S(2)}) collective-permute-start(bf16[512,4096]{1,0:T(8,128)(2,1)} %get-tuple-element.200), channel_id=1, source_target_pairs={{0,4},{4,0},{1,5},{5,1},{2,6},{6,2},{3,7},{7,3},{8,12},{12,8},{9,1... | collective-permute-start | bytes 12582920 | tf_op jit(solution)/shard_map/ppermute | solution.py:762
  299.3 6.0 %slice-start = ((bf16[1024,12288]{1,0:T(8,128)(2,1)}), bf16[1024,1024]{1,0:T(8,128)(2,1)S(1)}, s32[]{:S(2)}) async-start(bf16[1024,12288]{1,0:T(8,128)(2,1)} %all-gather.2.cloned.1.call-done.input_ref.output_ref.refs_1_), calls=%async_computation.7 | async-start | bytes 4194304 | tf_op jit(solution)/shard_map/slice | solution.py:948
  305.3 6.5 %copy-start.6 = (bf16[512,4096]{1,0:T(8,128)(2,1)S(1)}, bf16[512,4096]{1,0:T(8,128)(2,1)}, u32[]{:S(2)}) copy-start(bf16[512,4096]{1,0:T(8,128)(2,1)} %get-tuple-element.212) | copy-start | bytes 12582916
  305.3 6.5 %copy-start.7 = (bf16[512,4096]{1,0:T(8,128)(2,1)S(1)}, bf16[512,4096]{1,0:T(8,128)(2,1)}, u32[]{:S(2)}) copy-start(bf16[512,4096]{1,0:T(8,128)(2,1)} %get-tuple-element.213) | copy-start | bytes 12582916
  319.5 181.4 %reduce-scatter.5.cloned.1.call-start = ((), (), s32[]{:S(2)}) async-start(), calls=%async_computation.6 | async-start | bytes 2621440 | tf_op jit(solution)/shard_map/reduce_scatter | solution.py:1106
  332.2 6.1 %copy-start.26 = (bf16[512,1024]{1,0:T(8,128)(2,1)S(1)}, bf16[512,1024]{1,0:T(8,128)(2,1)}, u32[]{:S(2)}) copy-start(bf16[512,1024]{1,0:T(8,128)(2,1)} %get-tuple-element.210) | copy-start | bytes 3145732
  341.2 18.5 %collective-permute-start.12 = (bf16[512,2048]{1,0:T(8,128)(2,1)}, bf16[512,2048]{1,0:T(8,128)(2,1)}, u32[]{:S(2)}, u32[]{:S(2)}) collective-permute-start(bf16[512,2048]{1,0:T(8,128)(2,1)} %pad_maximum_fusion.1), channel_id=1, source_target_pairs={{0,4},{4,0},{1,5},{5,1},{2,6},{6,2},{3,7},{7,3},{8,12},{12,8},{9,1... | collective-permute-start | bytes 6291464 | tf_op jit(solution)/shard_map/ppermute | solution.py:762
  347.4 12.3 %collective-permute-start.11 = (bf16[512,2048]{1,0:T(8,128)(2,1)}, bf16[512,2048]{1,0:T(8,128)(2,1)S(1)}, u32[]{:S(2)}, u32[]{:S(2)}) collective-permute-start(bf16[512,2048]{1,0:T(8,128)(2,1)} %get-tuple-element.226), channel_id=1, source_target_pairs={{0,4},{4,0},{1,5},{5,1},{2,6},{6,2},{3,7},{7,3},{8,12},{12,8},{9,1... | collective-permute-start | bytes 6291464 | tf_op jit(solution)/shard_map/ppermute | solution.py:762
  347.7 10.4 %copy-start.25 = (bf16[512,1024]{1,0:T(8,128)(2,1)S(1)}, bf16[512,1024]{1,0:T(8,128)(2,1)}, u32[]{:S(2)}) copy-start(bf16[512,1024]{1,0:T(8,128)(2,1)} %get-tuple-element.211) | copy-start | bytes 3145732
  361.1 4.8 copy-start.11
  361.1 4.8 copy-start.13
  364.7 36.9 %collective-permute-start.14 = (bf16[256,2048]{1,0:T(8,128)(2,1)}, bf16[256,2048]{1,0:T(8,128)(2,1)}, u32[]{:S(2)}, u32[]{:S(2)}) collective-permute-start(bf16[256,2048]{1,0:T(8,128)(2,1)} %get-tuple-element.328), channel_id=1, source_target_pairs={{0,8},{8,0},{16,24},{24,16},{1,9},{9,1},{17,25},{25,17},{2,10},{10... | collective-permute-start | bytes 3145736 | tf_op jit(solution)/shard_map/ppermute | solution.py:759
  367.7 6.6 %copy-start.20 = (bf16[768,1024]{1,0:T(8,128)(2,1)S(1)}, bf16[768,1024]{1,0:T(8,128)(2,1)}, u32[]{:S(2)}) copy-start(bf16[768,1024]{1,0:T(8,128)(2,1)} %get-tuple-element.240.refs_0_) | copy-start | bytes 4718596
  367.7 34.0 %collective-permute-start.13 = (bf16[256,2048]{1,0:T(8,128)(2,1)}, bf16[256,2048]{1,0:T(8,128)(2,1)}, u32[]{:S(2)}, u32[]{:S(2)}) collective-permute-start(bf16[256,2048]{1,0:T(8,128)(2,1)} %get-tuple-element.330), channel_id=1, source_target_pairs={{0,16},{8,24},{16,0},{24,8},{1,17},{9,25},{17,1},{25,9},{2,18},{10... | collective-permute-start | bytes 3145736 | tf_op jit(solution)/shard_map/ppermute | solution.py:759
  406.8 11.6 %copy-start.27 = (bf16[512,1024]{1,0:T(8,128)(2,1)S(1)}, bf16[512,1024]{1,0:T(8,128)(2,1)}, u32[]{:S(2)}) copy-start(bf16[512,1024]{1,0:T(8,128)(2,1)} %get-tuple-element.243) | copy-start | bytes 3145732
  418.4 3.4 copy-start.37
  418.4 3.4 copy-start.36
  418.5 3.4 copy-start.38
  418.5 5.6 %copy-start.24 = (bf16[512,1024]{1,0:T(8,128)(2,1)S(1)}, bf16[512,1024]{1,0:T(8,128)(2,1)}, u32[]{:S(2)}) copy-start(bf16[512,1024]{1,0:T(8,128)(2,1)} %get-tuple-element.244) | copy-start | bytes 3145732
  421.3 7.5 %collective-permute-start.18 = (bf16[512,2048]{1,0:T(8,128)(2,1)}, bf16[512,2048]{1,0:T(8,128)(2,1)}, u32[]{:S(2)}, u32[]{:S(2)}) collective-permute-start(bf16[512,2048]{1,0:T(8,128)(2,1)} %pad_maximum_fusion.3), channel_id=1, source_target_pairs={{0,4},{4,0},{1,5},{5,1},{2,6},{6,2},{3,7},{7,3},{8,12},{12,8},{9,1... | collective-permute-start | bytes 6291464 | tf_op jit(solution)/shard_map/ppermute | solution.py:762
  421.3 7.5 %collective-permute-start.17 = (bf16[512,2048]{1,0:T(8,128)(2,1)}, bf16[512,2048]{1,0:T(8,128)(2,1)S(1)}, u32[]{:S(2)}, u32[]{:S(2)}) collective-permute-start(bf16[512,2048]{1,0:T(8,128)(2,1)} %get-tuple-element.262), channel_id=1, source_target_pairs={{0,4},{4,0},{1,5},{5,1},{2,6},{6,2},{3,7},{7,3},{8,12},{12,8},{9,1... | collective-permute-start | bytes 6291464 | tf_op jit(solution)/shard_map/ppermute | solution.py:762
  421.9 15.5 %collective-permute-start.16 = (bf16[128,2048]{1,0:T(8,128)(2,1)}, bf16[128,2048]{1,0:T(8,128)(2,1)}, u32[]{:S(2)}, u32[]{:S(2)}) collective-permute-start(bf16[128,2048]{1,0:T(8,128)(2,1)} %get-tuple-element.335), channel_id=1, source_target_pairs={{0,16},{8,24},{16,0},{24,8},{1,17},{9,25},{17,1},{25,9},{2,18},{10... | collective-permute-start | bytes 1572872 | tf_op jit(solution)/shard_map/ppermute | solution.py:759
  423.4 14.5 %collective-permute-start.15 = (bf16[128,2048]{1,0:T(8,128)(2,1)}, bf16[128,2048]{1,0:T(8,128)(2,1)}, u32[]{:S(2)}, u32[]{:S(2)}) collective-permute-start(bf16[128,2048]{1,0:T(8,128)(2,1)} %get-tuple-element.337), channel_id=1, source_target_pairs={{0,8},{8,0},{16,24},{24,16},{1,9},{9,1},{17,25},{25,17},{2,10},{10... | collective-permute-start | bytes 1572872 | tf_op jit(solution)/shard_map/ppermute | solution.py:759
  430.1 5.0 copy-start.8
  430.1 5.0 copy-start.10
  433.6 38.0 %collective-permute-start.20 = (bf16[256,2048]{1,0:T(8,128)(2,1)}, bf16[256,2048]{1,0:T(8,128)(2,1)}, u32[]{:S(2)}, u32[]{:S(2)}) collective-permute-start(bf16[256,2048]{1,0:T(8,128)(2,1)} %get-tuple-element.324), channel_id=1, source_target_pairs={{0,8},{8,0},{16,24},{24,16},{1,9},{9,1},{17,25},{25,17},{2,10},{10... | collective-permute-start | bytes 3145736 | tf_op jit(solution)/shard_map/ppermute | solution.py:759
  436.9 34.7 %collective-permute-start.19 = (bf16[256,2048]{1,0:T(8,128)(2,1)}, bf16[256,2048]{1,0:T(8,128)(2,1)}, u32[]{:S(2)}, u32[]{:S(2)}) collective-permute-start(bf16[256,2048]{1,0:T(8,128)(2,1)} %get-tuple-element.326), channel_id=1, source_target_pairs={{0,16},{8,24},{16,0},{24,8},{1,17},{9,25},{17,1},{25,9},{2,18},{10... | collective-permute-start | bytes 3145736 | tf_op jit(solution)/shard_map/ppermute | solution.py:759
  441.4 58.0 %all-to-all-start = ((bf16[4,32,4096]{2,1,0:T(8,128)(2,1)}), bf16[4,32,4096]{2,1,0:T(8,128)(2,1)S(1)}, u32[]{:S(2)}, u32[]{:S(2)}) async-start(bf16[4,32,4096]{2,1,0:T(8,128)(2,1)} %bitcast.46), calls=%async_computation.2 | async-start | bytes 2097152 | tf_op jit(solution)/shard_map/all_to_all | solution.py:813
  471.5 28.2 %collective-permute-start.23 = (bf16[512,128]{1,0:T(8,128)(2,1)S(1)}, bf16[512,128]{1,0:T(8,128)(2,1)S(1)}, u32[]{:S(2)}, u32[]{:S(2)}) collective-permute-start(bf16[512,128]{1,0:T(8,128)(2,1)S(1)} %get-tuple-element.347), channel_id=1, source_target_pairs={{0,4},{4,0},{1,5},{5,1},{2,6},{6,2},{3,7},{7,3},{8,12},{12,8},{9,1... | collective-permute-start | bytes 393224 | tf_op jit(solution)/shard_map/ppermute | solution.py:762
  474.1 26.7 %collective-permute-start.22 = (bf16[128,2048]{1,0:T(8,128)(2,1)}, bf16[128,2048]{1,0:T(8,128)(2,1)}, u32[]{:S(2)}, u32[]{:S(2)}) collective-permute-start(bf16[128,2048]{1,0:T(8,128)(2,1)} %get-tuple-element.331), channel_id=1, source_target_pairs={{0,16},{8,24},{16,0},{24,8},{1,17},{9,25},{17,1},{25,9},{2,18},{10... | collective-permute-start | bytes 1572872 | tf_op jit(solution)/shard_map/ppermute | solution.py:759
  477.6 23.3 %collective-permute-start.21 = (bf16[128,2048]{1,0:T(8,128)(2,1)}, bf16[128,2048]{1,0:T(8,128)(2,1)S(1)}, u32[]{:S(2)}, u32[]{:S(2)}) collective-permute-start(bf16[128,2048]{1,0:T(8,128)(2,1)} %get-tuple-element.333), channel_id=1, source_target_pairs={{0,8},{8,0},{16,24},{24,16},{1,9},{9,1},{17,25},{25,17},{2,10},{10... | collective-permute-start | bytes 1572872 | tf_op jit(solution)/shard_map/ppermute | solution.py:759
  499.7 9.7 %collective-permute-start.24 = (bf16[256,128]{1,0:T(8,128)(2,1)S(1)}, bf16[256,128]{1,0:T(8,128)(2,1)S(1)}, u32[]{:S(2)}, u32[]{:S(2)}) collective-permute-start(bf16[256,128]{1,0:T(8,128)(2,1)S(1)} %get-tuple-element.346), channel_id=1, source_target_pairs={{0,16},{8,24},{16,0},{24,8},{1,17},{9,25},{17,1},{25,9},{2,18},{10... | collective-permute-start | bytes 196616 | tf_op jit(solution)/shard_map/ppermute | solution.py:759
  503.2 12.6 %copy-start.14 = (bf16[32,8192]{1,0:T(8,128)(2,1)S(1)}, bf16[32,8192]{1,0:T(8,128)(2,1)}, u32[]{:S(2)}) copy-start(bf16[32,8192]{1,0:T(8,128)(2,1)} %reduce-scatter.5.cloned.1.call-done) | copy-start | bytes 1572868
  503.2 35.5 %all-to-all-start.1 = ((bf16[4,32,4096]{2,1,0:T(8,128)(2,1)}), bf16[4,32,4096]{2,1,0:T(8,128)(2,1)S(1)}, u32[]{:S(2)}, u32[]{:S(2)}) async-start(bf16[4,32,4096]{2,1,0:T(8,128)(2,1)} %bitcast.18), calls=%async_computation.3 | async-start | bytes 2097152 | tf_op jit(solution)/shard_map/all_to_all | solution.py:813
  509.5 4.0 collective-permute-start.25
  513.5 13.8 %collective-permute-start.26 = (f32[128,128]{1,0:T(8,128)S(1)}, f32[128,128]{1,0:T(8,128)S(1)}, u32[]{:S(2)}, u32[]{:S(2)}) collective-permute-start(f32[128,128]{1,0:T(8,128)S(1)} %fusion.24), channel_id=1, source_target_pairs={{0,1},{1,0},{2,3},{3,2},{4,5},{5,4},{6,7},{7,6},{8,9},{9,8},{10,11... | collective-permute-start | bytes 196616 | tf_op jit(solution)/shard_map/ppermute | solution.py:765
  527.3 10.1 %collective-permute-start.27 = (f32[128,128]{1,0:T(8,128)S(1)}, f32[128,128]{1,0:T(8,128)S(1)}, u32[]{:S(2)}, u32[]{:S(2)}) collective-permute-start(f32[128,128]{1,0:T(8,128)S(1)} %add.271), channel_id=1, source_target_pairs={{0,2},{1,3},{2,0},{3,1},{4,6},{5,7},{6,4},{7,5},{8,10},{9,11},{10,... | collective-permute-start | bytes 196616 | tf_op jit(solution)/shard_map/ppermute | solution.py:765
  (13 other events, 20.4 us)
Sparse Core Ops, SparseCore 0:
  11.5 191.6 all-gather.1
  319.6 98.1 reduce-scatter.2
  438.0 62.1 reduce-scatter.4

commit v5 on v4

--- a/solution.py
+++ b/solution.py
@@ -427,9 +427,10 @@
 
 
 def turn_rows(x_ref, turned, positions_ref):
-    for j in range(x_ref.shape[1] // LANES):
+    for j in range(turned.shape[0] // LANES):
         start = pl.multiple_of(positions_ref[j] * LANES, LANES)
-        turned[pl.ds(start, LANES), :] = x_ref[:, j * LANES : (j + 1) * LANES].T
+        block = slice(j * LANES, (j + 1) * LANES)
+        turned[pl.ds(start, LANES), :] = x_ref[block, :] if x_ref.shape == turned.shape else x_ref[:, block].T
 
 
 def feed_backward_kernel(
@@ -599,8 +600,9 @@
 
 
 def weight_gradient(positions, x, *groups):
-    row_count, width = x.shape
     grads = [grad for group, _ in groups for grad in group]
+    row_count = grads[0].shape[0]
+    width = x.size // row_count
     group_of = [index for index, (group, _) in enumerate(groups) for _ in group]
     starts = tile_starts(grads)
     half = width // 2
@@ -615,7 +617,7 @@
         grid_spec=pltpu.PrefetchScalarGridSpec(
             num_scalar_prefetch=1,
             grid=(starts[-1],),
-            in_specs=[pl.BlockSpec((row_count, width), lambda j, p: (0, 0))]
+            in_specs=[pl.BlockSpec(x.shape, lambda j, p: (0, 0))]
             + [tile_spec(row_count, starts[i], starts[i + 1]) for i in range(len(grads))],
             out_specs=out_specs,
             scratch_shapes=[pltpu.VMEM((width, row_count), jnp.bfloat16)],
@@ -625,6 +627,88 @@
         cost_estimate=SHORT,
         name="weight_gradient",
     )(positions, x, *grads)
+
+
+def output_backward_kernel(positions_ref, x_ref, grad_ref, weight_ref, send_ref, keep_ref, mixed_ref, turned, summed):
+    step = pl.program_id(0)
+
+    @pl.when(step == 0)
+    def _():
+        turn_rows(x_ref, turned, positions_ref)
+        summed[...] = jnp.zeros_like(summed)
+
+    half = turned.shape[0] // 2
+    summed[...] += times_transposed(grad_ref[...], weight_ref[...])
+    send_ref[...] = product(turned[:half, :], grad_ref[...]).astype(jnp.bfloat16)
+    keep_ref[...] = product(turned[half:, :], grad_ref[...]).astype(jnp.bfloat16)
+
+    @pl.when(step == pl.num_programs(0) - 1)
+    def _():
+        mixed_ref[...] = summed[...].astype(jnp.bfloat16)
+
+
+def output_backward(positions, x, grad, weights, column):
+    row_count, width = grad.shape
+    half = width // 2
+    last = width // WEIGHT_TILE
+    return pl.pallas_call(
+        output_backward_kernel,
+        grid_spec=pltpu.PrefetchScalarGridSpec(
+            num_scalar_prefetch=1,
+            grid=(last,),
+            in_specs=[
+                pl.BlockSpec(x.shape, lambda j, p: (0, 0)),
+                tile_spec(row_count, 0, last),
+                tile_spec(width, 0, last, offset=column // WEIGHT_TILE),
+            ],
+            out_specs=[
+                tile_spec(half, 0, last),
+                tile_spec(half, 0, last),
+                pl.BlockSpec((row_count, width), lambda j, p: (0, 0)),
+            ],
+            scratch_shapes=[
+                pltpu.VMEM((width, row_count), jnp.bfloat16),
+                pltpu.VMEM((row_count, width), jnp.float32),
+            ],
+        ),
+        out_shape=[jax.ShapeDtypeStruct((half, width), jnp.bfloat16)] * 2
+        + [jax.ShapeDtypeStruct((row_count, width), jnp.bfloat16)],
+        compiler_params=pltpu.CompilerParams(vmem_limit_bytes=VMEM_BYTES),
+        cost_estimate=SHORT,
+        name="output_backward",
+    )(positions, x, grad, weights)
+
+
+def weights_back_kernel(starts, *refs):
+    count = len(starts) - 1
+    grads, weights_ref, total_ref = refs[:count], refs[count], refs[-1]
+    step = pl.program_id(0)
+
+    @pl.when(step == 0)
+    def _():
+        total_ref[...] = jnp.zeros_like(total_ref)
+
+    for index in range(count):
+
+        @pl.when((step >= starts[index]) & (step < starts[index + 1]))
+        def _(index=index):
+            total_ref[...] += times_transposed(grads[index][...], weights_ref[...])
+
+
+def weights_back(grads, weights, column):
+    row_count, width = grads[0].shape[0], weights.shape[0]
+    starts = tile_starts(grads)
+    return pl.pallas_call(
+        functools.partial(weights_back_kernel, starts),
+        grid=(starts[-1],),
+        in_specs=[tile_spec(row_count, starts[i], starts[i + 1]) for i in range(len(grads))]
+        + [tile_spec(width, 0, starts[-1], offset=column // WEIGHT_TILE)],
+        out_specs=pl.BlockSpec((row_count, width), lambda j: (0, 0)),
+        out_shape=jax.ShapeDtypeStruct((row_count, width), jnp.float32),
+        compiler_params=pltpu.CompilerParams(vmem_limit_bytes=VMEM_BYTES),
+        cost_estimate=SHORT,
+        name="weights_back",
+    )(*grads, weights)
 
 
 def input_gradient_kernel(norm, starts, has_low, *refs):
@@ -817,13 +901,6 @@
         parts = parts.astype(jnp.float32)
         return sum(parts[k * rows : (k + 1) * rows] for k in range(self.fsdp_count))
 
-    def sum_all_fsdp(self, grad):
-        grad = grad.astype(jnp.float32)
-        for bit in range(self.fsdp_count.bit_length() - 1):
-            grad = grad + self.swap_fsdp(grad, 1 << bit)
-        rows = grad.shape[0] // self.fsdp_count
-        return lax.dynamic_slice_in_dim(grad, self.fsdp * rows, rows, 0)
-
     def scatter_whole(self, send, keep):
         grad = jnp.concatenate([send, keep], axis=0).astype(jnp.float32)
         part = lax.psum_scatter(grad, ("h", "c"), scatter_dimension=0, tiled=True)
@@ -945,6 +1022,9 @@
         bias_table[1],
     )
     cross_first, cross_second = cross_whole[:, :split], cross_whole[:, split:]
+    normed_self_turned, self_mixed_turned, encoded_turned = order.run(
+        lambda *arrays: [array.T for array in arrays], normed_self, self_mixed, encoded
+    )
     cross_query, cross_output_low = cross_second[:, :width], cross_second[:, width:]
     cross_queries = product(normed_cross, cross_query).astype(low)
     cross_kv = product(encoded, cross_first).astype(low)
@@ -981,14 +1061,8 @@
         in_other, down_other = links.swap_core(in_send), links.swap_core(down_send)
 
     crossed, straight = links.positions(True), links.positions(False)
-    grad_cross_mixed, cross_out = order.run(
-        lambda branch, weights, mixed: (
-            times_transposed(branch, weights).astype(low),
-            weight_gradient(crossed, mixed, ([branch], False)),
-        ),
-        cross_branch,
-        cross_output_low,
-        cross_mixed,
+    *cross_out, grad_cross_mixed = order.run(
+        lambda *arrays: output_backward(crossed, *arrays, cross_at + 3 * width), cross_mixed, cross_branch, cross_held
     )
     if links.pairwise:
         feed_sum = order.run(
@@ -1024,7 +1098,7 @@
             grad_k,
             grad_v,
             weight_gradient(crossed, normed_cross, ([grad_q], False)),
-            weight_gradient(straight, encoded, ([grad_k, grad_v], False)),
+            weight_gradient(straight, encoded_turned, ([grad_k, grad_v], False)),
         )
 
     grad_q, grad_k, grad_v, cross_query_grad, cross_kv_grad = order.run(
@@ -1072,14 +1146,8 @@
         cross_part = links.scatter_whole(*[jnp.concatenate(side, axis=1) for side in (cross_send, cross_keep)])
     grad_k_cross, grad_v_cross = grad_k, grad_v
 
-    grad_self_mixed, self_out = order.run(
-        lambda branch, weights, mixed: (
-            times_transposed(branch, weights).astype(low),
-            weight_gradient(crossed, mixed, ([branch], False)),
-        ),
-        self_branch,
-        self_output_low,
-        self_mixed,
+    *self_out, grad_self_mixed = order.run(
+        lambda *arrays: output_backward(crossed, *arrays, width), self_mixed_turned, self_branch, self_second
     )
     grad_q, grad_k, grad_v = order.run(
         lambda query_key, self_values, self_mixed, grad_self_mixed, self_totals: attention_backward(
@@ -1103,23 +1171,23 @@
     )
     if links.pairwise:
         cross_sides = exchange(cross_sides, [1, 1], flips)
-        feed_part = lax.psum_scatter(order.after(feed_chips), "fsdp", scatter_dimension=0, tiled=True)
     first_send, first_keep, second_send, second_keep = order.run(
         lambda normed, grad_q, grad_k, grad_v: weight_gradient(
             straight, normed, ([grad_q, grad_k], False), ([grad_v], links.pairwise)
         ),
-        normed_self,
+        normed_self_turned,
         grad_q,
         grad_k,
         grad_v,
     )
+    if links.pairwise:
+        feed_part = lax.psum_scatter(order.after(feed_chips), "fsdp", scatter_dimension=0, tiled=True)
     second_send, second_keep = [
         jnp.concatenate(pair, axis=1) for pair in zip((second_send, second_keep), self_out)
     ]
     if links.pairwise:
         self_sides = [(first_keep, links.swap_core(first_send)), (second_keep, links.swap_core(second_send))]
         self_sides = exchange(self_sides, [0, 0], flips)
-        cross_parts = finish(cross_sides)
 
     grad_states, sums_0 = order.run(
         lambda grad_q, grad_k, grad_v, first, value, *arrays: input_gradient(
@@ -1134,23 +1202,25 @@
         grad_after_self,
         norm_rows,
     )
-    sums = [sums_0, sums_1, sums_2, sums_3]
-    grad_tables = jnp.stack([part[0] for part in sums] + [part[1] for part in sums])
-    grad_tables = jnp.pad(grad_tables.T, ((0, 0), (0, LANES - 8))).astype(low)
-    table_send, table_keep = links.halves(grad_tables, False)
-    grad_encoded = times_transposed(jnp.concatenate([grad_k_cross, grad_v_cross], axis=1), cross_first)
     if links.pairwise:
+        cross_parts = finish(cross_sides)
         self_sides = exchange(self_sides, [1, 1], flips)
+        feed_part = order.run(lambda part: part.astype(jnp.float32), feed_part)
+
+    def table_halves(*sums):
+        tables = jnp.stack([part[0] for part in sums] + [part[1] for part in sums])
+        return links.halves(jnp.pad(tables.T, ((0, 0), (0, LANES - 8))).astype(low), False)
+
+    table_send, table_keep = order.run(table_halves, sums_0, sums_1, sums_2, sums_3)
+    if links.pairwise:
         table_other = links.swap_core(table_send)
-        cross_part = order.run(links.sum_fsdp, cross_parts)
+    if links.pairwise:
         table_goes, table_stays = order.run(links.first_pair, table_keep, table_other)
         table_side = (table_stays, links.swap(table_goes, links.bit(0, False)))
-        feed_part = order.run(lambda part: part.astype(jnp.float32), feed_part)
-        self_parts = finish(self_sides)
         table_goes, table_stays = order.run(links.first_pair, *table_side)
         table_side = (table_stays, links.swap(table_goes, links.bit(1, False)))
-        table_part = links.sum_all_fsdp(links.sum_cores(*table_side))
-        self_part = links.sum_fsdp(self_parts)
+        cross_part = order.run(links.sum_fsdp, cross_parts)
+        self_parts = finish([*self_sides, table_side])
         feed_in_part, feed_out_part = feed_part[:, : 4 * width], feed_part[:, 4 * width :]
         feed_out_part = jnp.concatenate(
             [feed_out_part[:, at * width : (at + 1) * width] for at in range(4)], axis=0
@@ -1160,6 +1230,15 @@
             [links.scatter_whole(first_send, first_keep), links.scatter_whole(second_send, second_keep)], axis=1
         )
         table_part = links.scatter_whole(table_send, table_keep)
+    grad_encoded = order.run(
+        lambda grad_k, grad_v, weights: weights_back([grad_k, grad_v], weights, cross_at),
+        grad_k_cross,
+        grad_v_cross,
+        cross_held,
+    )
+    if links.pairwise:
+        self_part = order.run(links.sum_fsdp, self_parts)
+        self_part, table_part = self_part[:, : 4 * width], self_part[:, 4 * width :]
     self_in_part, self_out_part = self_part[:, : 3 * width], self_part[:, 3 * width :]
     cross_in_part = jnp.concatenate([cross_part[:, split : 3 * width], cross_part[:, :split]], axis=1)
     cross_out_part = cross_part[:, 3 * width :]

time: 554 us -> 539 us (0.973)
  matrix products: 39.3 us -> 26 us
  Pallas kernels: 200 us -> 211 us
  waiting for transfers between devices: 167 us -> 156 us
  starting transfers between devices: 41.6 us -> 33.6 us
    all_gather x1, waiting for transfers between devices: 44 us -> 21.3 us  [gather(): return lax.all_gather(shard, BOTH, axis=0, tiled=True)]
    pallas_call x0 -> x3, Pallas kernels: none -> 22.5 us  [the longest x2 17.2 us: output_backward(): pl.pallas_call(output_backward_kernel, grid_spec=pltpu.PrefetchScalarGrid...]
    dot_general x3 -> x0, matrix products: 14 us -> none  [times_transposed(): lax.dot_general(left, right, (((1,), (1,)), ((), ())), preferred_element_...]
    pallas_call x5 -> x3, Pallas kernels: 35.6 us -> 23.3 us  [weight_gradient(): pl.pallas_call(functools.partial(weight_gradient_kernel, starts, group_of...]
    ppermute x5 -> x3, starting transfers between devices: 12.7 us -> 5.76 us  [swap_fsdp(): lax.ppermute(array, 'fsdp', [(i, i ^ bit) for i in range(self.fsdp_count)])]
    ppermute x5 -> x3, waiting for transfers between devices: 39.7 us -> 38.7 us  [swap_fsdp(): lax.ppermute(array, 'fsdp', [(i, i ^ bit) for i in range(self.fsdp_count)])]
    convert_element_type x15 -> x16, other arithmetic: 32.1 us -> 32 us  [sum_cores(): (keep.astype(jnp.float32) + other.astype(jnp.float32)).astype(jnp.bfloat16)]
  transfers between devices with their start and end apart: 33 -> 31, of which waited for: 17 -> 18; matrix products, arithmetic and copies ran while one was open for 16% -> 14% of each run, Pallas kernels for 22% -> 25%
where the time goes in v5:
time: 539 us; the launch traced here: 532 us
  Pallas kernels  211 us (39%)
  waiting for transfers between devices  156 us (29%)
  other arithmetic  59 us (11%)
  starting transfers between devices  33.6 us (6%)
  local copies, waits for them, and re-layouts  30.3 us (6%)
  matrix products  26 us (5%)
  between operations  16.3 us (3%)
    ppermute x14, waiting for transfers between devices, swap(): return lax.ppermute(array, 'h', [(i, i ^ bit) for i in range(self.h_count)])  60.3 us
    pallas_call x1, Pallas kernels, feed_backward(): pl.pallas_call(functools.partial(feed_backward_kernel, rows), grid_spec=p...  43.1 us
    ppermute x3, waiting for transfers between devices, swap_fsdp(): lax.ppermute(array, 'fsdp', [(i, i ^ bit) for i in range(self.fsdp_count)])  38.7 us
    pallas_call x2, Pallas kernels, attention_backward(): pl.pallas_call(functools.partial(attention_backward_kernel, causal), grid...  32.9 us
    convert_element_type x16, other arithmetic, sum_cores(): (keep.astype(jnp.float32) + other.astype(jnp.float32)).astype(jnp.bfloat16)  32 us
    pallas_call x1, Pallas kernels, feed_forward(): pl.pallas_call(functools.partial(feed_forward_kernel, rows), grid_spec=pl...  26.6 us
    pallas_call x2, Pallas kernels, input_gradient(): pl.pallas_call(functools.partial(input_gradient_kernel, norm, starts, has...  26.4 us
    dot_general x6, matrix products, product(): return jnp.dot(left, right, preferred_element_type=jnp.float32)  26 us
  transfers between devices with their start and end apart: 31, of which 18 were waited for; matrix products, arithmetic and copies ran while one was open for 14% of the time, Pallas kernels for 25%

profile of v5, /device:TPU:0, one launch (start us, length us, event | category | flops | bytes accessed | tf_op | source)
XLA Modules:
  0.0 532.1 jit_solution(12601544741301393873)
XLA Ops:
  11.9 5.1 collective-permute-start.2
  18.1 6.3 %collective-permute-done.2.refs_3_ = bf16[32,4224]{1,0:T(8,128)(2,1)S(1)} collective-permute-done((bf16[32,4224]{1,0:T(8,128)(2,1)S(1)}, bf16[32,4224]{1,0:T(8,128)(2,1)S(1)}, u32[]{:S(2)}, u32[]{:S(2)}) %collective-permute-start.2) | collective-permute-done | bytes 270368 | tf_op jit(solution)/shard_map/ppermute | solution.py:849
  24.4 32.4 %collective-permute-done.1.refs_2_ = bf16[32,4224]{1,0:T(8,128)(2,1)S(1)} collective-permute-done((bf16[32,4224]{1,0:T(8,128)(2,1)S(1)}, bf16[32,4224]{1,0:T(8,128)(2,1)S(1)}, u32[]{:S(2)}, u32[]{:S(2)}) %collective-permute-start.1) | collective-permute-done | bytes 270368 | tf_op jit(solution)/shard_map/ppermute | solution.py:849
  58.3 2.7 place_rows.4
  62.1 1.5 collective-permute-start.4
  64.7 1.6 collective-permute-start.3
  66.3 23.8 %collective-permute-done.3 = bf16[128,2048]{1,0:T(8,128)(2,1)S(1)} collective-permute-done((bf16[128,2048]{1,0:T(8,128)(2,1)S(1)}, bf16[128,2048]{1,0:T(8,128)(2,1)S(1)}, u32[]{:S(2)}, u32[]{:S(2)}) %collective-permute-start.3) | collective-permute-done | bytes 524320 | tf_op jit(solution)/shard_map/ppermute | solution.py:843
  90.2 1.6 collective-permute-start.6
  92.4 22.4 %collective-permute-done.5 = bf16[256,2048]{1,0:T(8,128)(2,1)S(1)} collective-permute-done((bf16[256,2048]{1,0:T(8,128)(2,1)S(1)}, bf16[256,2048]{1,0:T(8,128)(2,1)S(1)}, u32[]{:S(2)}, u32[]{:S(2)}) %collective-permute-start.5) | collective-permute-done | bytes 1048608 | tf_op jit(solution)/shard_map/ppermute | solution.py:843
  114.9 6.6 %collective-permute-done.6 = bf16[256,2176]{1,0:T(8,128)(2,1)S(1)} collective-permute-done((bf16[256,2176]{1,0:T(8,128)(2,1)S(1)}, bf16[256,2176]{1,0:T(8,128)(2,1)S(1)}, u32[]{:S(2)}, u32[]{:S(2)}) %collective-permute-start.6) | collective-permute-done | bytes 1114144 | tf_op jit(solution)/shard_map/ppermute | solution.py:843
  131.1 1.8 bitcast_convert_fusion
  132.9 1.8 collective-permute-done.7.refs_1_
  134.7 4.3 place_rows.5.refs_3_.refs_4_
  139.0 4.9 place_rows.6.weight_ref.refs_5_
  145.1 4.7 fusion.32
  152.1 3.0 convolution_convert_fusion.1.v_ref
  155.1 4.9 convolution_convert_fusion.q_ref.k_ref
  160.1 12.9 %attention_forward.2 = (bf16[768,1024]{1,0:T(8,128)(2,1)}, f32[8,2,768]{2,1,0:T(2,128)}) custom-call(s32[1]{0:T(128)S(6)} %copy.83.limit_ref, bf16[768,2048]{1,0:T(8,128)(2,1)} %convolution_convert_fusion.q_ref.k_ref, bf16[768,2048]{1,0:T(8,128)(2,1)} %convolution_convert_fusion.q_ref.k_ref, bf16[768,1024]{1,0:T(8,128)(2,1)} %convolution_convert_fusion.1.v_ref), custom_call_target="tpu_custom_call" | custom-call | flops 1024 | bytes 1024 | tf_op jit(solution)/shard_map/attention_forward/pallas_call | solution.py:176
  173.0 4.9 fusion.41
  178.3 1.8 add_convert_fusion.2.x_ref
  180.1 21.3 %all-gather.2.cloned.1.call-done.input_ref.output_ref.weight_ref.refs_1_.refs_2_ = bf16[1024,12288]{1,0:T(8,128)(2,1)} async-done(((bf16[32,12288]{1,0:T(8,128)(2,1)}), bf16[1024,12288]{1,0:T(8,128)(2,1)}) %all-gather.2.cloned.1.call-update) | async-done | bytes 25165840 | tf_op jit(solution)/shard_map/all_gather | solution.py:852
  201.4 4.7 fusion.5.k_ref.v_ref
  206.1 4.5 fusion.15.q_ref
  210.7 2.6 copy.65
  213.3 9.1 %attention_forward.3 = (bf16[768,1024]{1,0:T(8,128)(2,1)}, f32[8,2,768]{2,1,0:T(2,128)}) custom-call(s32[1]{0:T(128)S(6)} %copy.84.limit_ref, bf16[768,1024]{1,0:T(8,128)(2,1)} %fusion.15.q_ref, bf16[256,2048]{1,0:T(8,128)(2,1)} %fusion.5.k_ref.v_ref, bf16[256,2048]{1,0:T(8,128)(2,1)} %fusion.5.k_ref.v_ref), custom_call_target="tpu_custom_call" | custom-call | flops 1024 | bytes 1024 | tf_op jit(solution)/shard_map/attention_forward/pallas_call | solution.py:176
  222.4 3.9 fusion.42
  226.8 1.8 add_convert_fusion.1.normed_ref
  228.5 26.6 %feed_forward.1 = (bf16[768,4096]{1,0:T(8,128)(2,1)}, bf16[768,4096]{1,0:T(8,128)(2,1)}, bf16[768,1024]{1,0:T(8,128)(2,1)}, f32[768,1024]{1,0:T(8,128)}, bf16[768,1024]{1,0:T(8,128)(2,1)}, /*index=5*/f32[2,1024]{1,0:T(2,128)}) custom-call(s32[1]{0:T(128)S(6)} %copy.83.limit_ref, bf16[768,1024]{1,0:T(8,128)(2,1)} %add_convert_fusion.1.normed_ref, ...), custom_call_target="tpu_custom_call" | custom-call | flops 1024 | bytes 1024 | tf_op jit(solution)/shard_map/feed_forward/pallas_call | solution.py:406
  255.1 43.1 %feed_backward.1 = (bf16[512,4096]{1,0:T(8,128)(2,1)}, bf16[512,4096]{1,0:T(8,128)(2,1)}, bf16[512,4096]{1,0:T(8,128)(2,1)}, bf16[512,4096]{1,0:T(8,128)(2,1)}, ...) custom-call(s32[8]{0:T(128)} %pad_add_fusion.2.tiles_ref, s32[8]{0:T(128)} %fusion.26.positions_ref, ...), custom_call_target="tpu_custom_call" | custom-call | flops 1024 | bytes 1024 | tf_op jit(solution)/shard_map/feed_backward/pallas_call | solution.py:514
  299.3 8.9 %output_backward.2 = (bf16[512,1024]{1,0:T(8,128)(2,1)}, bf16[512,1024]{1,0:T(8,128)(2,1)}, bf16[768,1024]{1,0:T(8,128)(2,1)}) custom-call(s32[8]{0:T(128)} %get-tuple-element.414.positions_ref, bf16[768,1024]{1,0:T(8,128)(2,1)} %get-tuple-element.237.x_ref.mixed_ref, bf16[768,1024]{1,0:T(8,128)(2,1)} %get-tuple-element.225.grad_ref, ...), custom_call_target="tpu_custom_call" | custom-call | flops 1024 | bytes 1024 | tf_op jit(solution)/shard_map/output_backward/pallas_call | solution.py:654
  308.2 3.5 collective-permute-done.10
  311.8 9.4 %add_convert_fusion = bf16[512,8192]{1,0:T(8,128)(2,1)} fusion(bf16[512,4096]{1,0:T(8,128)(2,1)} %get-tuple-element.232, bf16[512,4096]{1,0:T(8,128)(2,1)} %get-tuple-element.231, bf16[512,4096]{1,0:T(8,128)(2,1)} %collective-permute-done.10, bf16[512,4096]{1,0:T(8,128)(2,1)} %collective-permute-done.9), kind=kLoop, calls=%fused_computation | loop fusion | flops 41943040 | bytes 25165824 | tf_op jit(solution)/shard_map/convert_element_type | solution.py:894
  321.3 12.4 %attention_backward.2 = (bf16[768,1024]{1,0:T(8,128)(2,1)}, bf16[256,1024]{1,0:T(8,128)(2,1)}, bf16[256,1024]{1,0:T(8,128)(2,1)}) custom-call(s32[1]{0:T(128)S(6)} %copy.84.limit_ref, bf16[768,1024]{1,0:T(8,128)(2,1)} %fusion.15.q_ref, bf16[256,2048]{1,0:T(8,128)(2,1)} %fusion.5.k_ref.v_ref, bf16[256,2048]{1,0:T(8,128)(2,1)} %fusion.5.k_ref.v_ref, ...), custom_call_target="tpu_custom_call" | custom-call | flops 1024 | bytes 1024 | tf_op jit(solution)/shard_map/attention_backward/pallas_call | solution.py:277
  333.7 6.2 %weight_gradient.3 = (bf16[512,1024]{1,0:T(8,128)(2,1)}, bf16[512,1024]{1,0:T(8,128)(2,1)}) custom-call(s32[8]{0:T(128)} %get-tuple-element.414.positions_ref, bf16[768,1024]{1,0:T(8,128)(2,1)} %add_convert_fusion.2.x_ref, bf16[768,1024]{1,0:T(8,128)(2,1)} %get-tuple-element.247.refs_0_), custom_call_target="tpu_custom_call" | custom-call | flops 1024 | bytes 1024 | tf_op jit(solution)/shard_map/weight_gradient/pallas_call | solution.py:615
  339.9 2.7 pad_maximum_fusion.1
  342.9 5.9 %weight_gradient.4 = (bf16[512,2048]{1,0:T(8,128)(2,1)}, bf16[512,2048]{1,0:T(8,128)(2,1)}) custom-call(s32[8]{0:T(128)} %get-tuple-element.415.positions_ref.table_ref, bf16[1024,256]{1,0:T(8,128)(2,1)} %bitcast.48, bf16[256,1024]{1,0:T(8,128)(2,1)} %get-tuple-element.325.refs_0_, bf16[256,1024]{1,0:T(8,128)(2,1)} %get-tuple-element.326.refs_1_), custom_call_target="tpu_custom_call" | custom-call | flops 1024 | bytes 1024 | tf_op jit(solution)/shard_map/weight_gradient/pallas_call | solution.py:615
  348.9 10.5 %input_gradient.2 = (f32[768,1024]{1,0:T(8,128)}, bf16[768,1024]{1,0:T(8,128)(2,1)}, f32[2,1024]{1,0:T(2,128)}) custom-call(bf16[768,1024]{1,0:T(8,128)(2,1)} %get-tuple-element.247.refs_0_, bf16[1024,12288]{1,0:T(8,128)(2,1)} %all-gather.2.cloned.1.call-done.input_ref.output_ref.weight_ref.refs_1_.refs_2_, f32[768,1024]{1,0:T(8,128)} %copy-done.2, ...), custom_call_target="tpu_custom_call" | custom-call | flops 1024 | bytes 1024 | tf_op jit(solution)/shard_map/input_gradient/pallas_call | solution.py:745
  359.3 1.6 pad_maximum_fusion
  362.2 3.6 add_convert_fusion.10
  367.0 1.8 add_convert_fusion.8
  369.6 8.3 %output_backward.3 = (bf16[512,1024]{1,0:T(8,128)(2,1)}, bf16[512,1024]{1,0:T(8,128)(2,1)}, bf16[768,1024]{1,0:T(8,128)(2,1)}) custom-call(s32[8]{0:T(128)} %get-tuple-element.414.positions_ref, bf16[1024,768]{1,0:T(8,128)(2,1)} %bitcast.43, bf16[768,1024]{1,0:T(8,128)(2,1)} %get-tuple-element.260.grad_ref, bf16[1024,2176]{1,0:T(8,128)(2,1)} %place_rows.6.weight_ref.refs_5_), custom_call_target="tpu_custom_call" | custom-call | flops 1024 | bytes 1024 | tf_op jit(solution)/shard_map/output_backward/pallas_call | solution.py:654
  377.9 20.5 %attention_backward.3 = (bf16[768,1024]{1,0:T(8,128)(2,1)}, bf16[768,1024]{1,0:T(8,128)(2,1)}, bf16[768,1024]{1,0:T(8,128)(2,1)}) custom-call(s32[1]{0:T(128)S(6)} %copy.83.limit_ref, bf16[768,2048]{1,0:T(8,128)(2,1)} %convolution_convert_fusion.q_ref.k_ref, bf16[768,2048]{1,0:T(8,128)(2,1)} %convolution_convert_fusion.q_ref.k_ref, ...), custom_call_target="tpu_custom_call" | custom-call | flops 1024 | bytes 1024 | tf_op jit(solution)/shard_map/attention_backward/pallas_call | solution.py:277
  398.4 4.4 collective-permute-done.13
  403.0 1.5 add_convert_fusion.22
  404.4 2.8 add_convert_fusion.20
  407.2 1.6 copy.66.x_ref
  408.8 11.3 %weight_gradient.5 = (bf16[512,2048]{1,0:T(8,128)(2,1)}, bf16[512,2048]{1,0:T(8,128)(2,1)}, bf16[512,1024]{1,0:T(8,128)(2,1)}, bf16[512,1024]{1,0:T(8,128)(2,1)}) custom-call(s32[8]{0:T(128)} %get-tuple-element.415.positions_ref.table_ref, bf16[1024,768]{1,0:T(8,128)(2,1)} %copy.66.x_ref, bf16[768,1024]{1,0:T(8,128)(2,1)} %get-tuple-element.289.refs_0_, ...), custom_call_target="tpu_custom_call" | custom-call | flops 1024 | bytes 1024 | tf_op jit(solution)/shard_map/weight_gradient/pallas_call | solution.py:615
  420.0 2.7 pad_maximum_fusion.3
  425.4 1.4 pad_maximum_fusion.2
  426.8 3.3 collective-permute-done.16
  431.4 3.5 add_convert_fusion.6
  434.9 1.6 collective-permute-start.17
  436.4 1.8 add_convert_fusion.4
  438.7 15.9 %input_gradient.3 = (f32[768,1024]{1,0:T(8,128)}, f32[2,1024]{1,0:T(2,128)}) custom-call(bf16[768,1024]{1,0:T(8,128)(2,1)} %get-tuple-element.289.refs_0_, bf16[768,1024]{1,0:T(8,128)(2,1)} %get-tuple-element.290.refs_1_, bf16[768,1024]{1,0:T(8,128)(2,1)} %get-tuple-element.291.refs_2_, bf16[1024,2048]{1,0:T(8,128)(2,1)} %place_rows.5.refs_3_.refs_4_, ...), custom_call_target="tpu_custom_call" | custom-call | flops 1024 | bytes 1024 | tf_op jit(solution)/shard_map/input_gradient/pallas_call | solution.py:745
  458.1 4.8 all-to-all-start
  463.4 2.5 add_convert_fusion.16
  466.0 2.6 add_convert_fusion.14
  469.8 2.3 place_rows.7
  473.1 1.3 collective-permute-done.23
  477.6 1.3 collective-permute-done.24
  480.2 8.6 %all-to-all-done = bf16[4,32,4096]{2,1,0:T(8,128)(2,1)S(1)} async-done(((bf16[4,32,4096]{2,1,0:T(8,128)(2,1)}), bf16[4,32,4096]{2,1,0:T(8,128)(2,1)S(1)}, u32[]{:S(2)}, u32[]{:S(2)}) %all-to-all-start) | async-done | bytes 1048608 | tf_op jit(solution)/shard_map/all_to_all | solution.py:897
  491.5 5.0 all-to-all-start.1
  499.7 5.3 weights_back.1
  505.0 17.1 %all-to-all-done.1 = bf16[4,32,4224]{2,1,0:T(8,128)(2,1)S(1)} async-done(((bf16[4,32,4224]{2,1,0:T(8,128)(2,1)}), bf16[4,32,4224]{2,1,0:T(8,128)(2,1)S(1)}, u32[]{:S(2)}, u32[]{:S(2)}) %all-to-all-start.1) | async-done | bytes 1081376 | tf_op jit(solution)/shard_map/all_to_all | solution.py:897
  (210 shorter events, 51.5 us)
Async XLA Ops:
  7.2 3.5 copy-start.31
  7.2 4.5 copy-start.37
  7.2 4.5 copy-start.38
  7.2 4.6 copy-start.32
  7.2 4.6 copy-start.27
  7.2 194.2 %all-gather.2.cloned.1.call-start = ((), (), s32[]{:S(2)}) async-start(), calls=%async_computation.4 | async-start | bytes 25952256 | tf_op jit(solution)/shard_map/all_gather | solution.py:852
  11.6 411.7 %reduce-scatter.3.cloned.1.call-start = ((), (), s32[]{:S(2)}) async-start(), calls=%async_computation.5 | async-start | bytes 10485760 | tf_op jit(solution)/shard_map/reduce_scatter | solution.py:910
  11.9 45.0 %copy-start.20 = (bf16[32,4224]{1,0:T(8,128)(2,1)}, bf16[32,4224]{1,0:T(8,128)(2,1)S(1)}, u32[]{:S(2)}) copy-start(bf16[32,4224]{1,0:T(8,128)(2,1)S(1)} %fusion.20.refs_0_) | copy-start | bytes 811012
  11.9 12.6 %collective-permute-start.2 = (bf16[32,4224]{1,0:T(8,128)(2,1)S(1)}, bf16[32,4224]{1,0:T(8,128)(2,1)S(1)}, u32[]{:S(2)}, u32[]{:S(2)}) collective-permute-start(bf16[32,4224]{1,0:T(8,128)(2,1)S(1)} %fusion.20.refs_0_), channel_id=1, source_target_pairs={{0,3},{1,2},{2,1},{3,0},{4,7},{5,6},{6,5},{7,4},{8,11},{9,10},{10,... | collective-permute-start | bytes 811016 | tf_op jit(solution)/shard_map/ppermute | solution.py:849
  17.0 39.9 %collective-permute-start.1 = (bf16[32,4224]{1,0:T(8,128)(2,1)S(1)}, bf16[32,4224]{1,0:T(8,128)(2,1)S(1)}, u32[]{:S(2)}, u32[]{:S(2)}) collective-permute-start(bf16[32,4224]{1,0:T(8,128)(2,1)S(1)} %fusion.20.refs_0_), channel_id=1, source_target_pairs={{0,2},{1,3},{2,0},{3,1},{4,6},{5,7},{6,4},{7,5},{8,10},{9,11},{10,... | collective-permute-start | bytes 811016 | tf_op jit(solution)/shard_map/ppermute | solution.py:849
  17.0 39.9 %collective-permute-start = (bf16[32,4224]{1,0:T(8,128)(2,1)S(1)}, bf16[32,4224]{1,0:T(8,128)(2,1)S(1)}, u32[]{:S(2)}, u32[]{:S(2)}) collective-permute-start(bf16[32,4224]{1,0:T(8,128)(2,1)S(1)} %fusion.20.refs_0_), channel_id=1, source_target_pairs={{0,1},{1,0},{2,3},{3,2},{4,5},{5,4},{6,7},{7,6},{8,9},{9,8},{10,11... | collective-permute-start | bytes 811016 | tf_op jit(solution)/shard_map/ppermute | solution.py:849
  24.4 32.4 %copy-start.28 = (bf16[32,4224]{1,0:T(8,128)(2,1)}, bf16[32,4224]{1,0:T(8,128)(2,1)S(1)}, u32[]{:S(2)}) copy-start(bf16[32,4224]{1,0:T(8,128)(2,1)S(1)} %collective-permute-done.2.refs_3_) | copy-start | bytes 811012
  62.1 28.0 %collective-permute-start.4 = (bf16[128,2176]{1,0:T(8,128)(2,1)S(1)}, bf16[128,2176]{1,0:T(8,128)(2,1)S(1)}, u32[]{:S(2)}, u32[]{:S(2)}) collective-permute-start(bf16[128,2176]{1,0:T(8,128)(2,1)S(1)} %slice.400), channel_id=1, source_target_pairs={{0,16},{8,24},{16,0},{24,8},{1,17},{9,25},{17,1},{25,9},{2,18},{10... | collective-permute-start | bytes 1671176 | tf_op jit(solution)/shard_map/ppermute | solution.py:843
  64.7 25.4 %collective-permute-start.3 = (bf16[128,2048]{1,0:T(8,128)(2,1)S(1)}, bf16[128,2048]{1,0:T(8,128)(2,1)S(1)}, u32[]{:S(2)}, u32[]{:S(2)}) collective-permute-start(bf16[128,2048]{1,0:T(8,128)(2,1)S(1)} %slice.399), channel_id=1, source_target_pairs={{0,8},{8,0},{16,24},{24,16},{1,9},{9,1},{17,25},{25,17},{2,10},{10... | collective-permute-start | bytes 1572872 | tf_op jit(solution)/shard_map/ppermute | solution.py:843
  90.2 31.3 %collective-permute-start.6 = (bf16[256,2176]{1,0:T(8,128)(2,1)S(1)}, bf16[256,2176]{1,0:T(8,128)(2,1)S(1)}, u32[]{:S(2)}, u32[]{:S(2)}) collective-permute-start(bf16[256,2176]{1,0:T(8,128)(2,1)S(1)} %constant_dynamic-update-slice_fusion.2), channel_id=1, source_target_pairs={{0,8},{8,0},{16,24},{24,16},{1,9},{9,1},{17,25},{25,17},{2,10},{10... | collective-permute-start | bytes 3342344 | tf_op jit(solution)/shard_map/ppermute | solution.py:843
  91.8 23.0 %collective-permute-start.5 = (bf16[256,2048]{1,0:T(8,128)(2,1)S(1)}, bf16[256,2048]{1,0:T(8,128)(2,1)S(1)}, u32[]{:S(2)}, u32[]{:S(2)}) collective-permute-start(bf16[256,2048]{1,0:T(8,128)(2,1)S(1)} %constant_dynamic-update-slice_fusion), channel_id=1, source_target_pairs={{0,16},{8,24},{16,0},{24,8},{1,17},{9,25},{17,1},{25,9},{2,18},{10... | collective-permute-start | bytes 3145736 | tf_op jit(solution)/shard_map/ppermute | solution.py:843
  123.6 4.0 copy-start.25
  123.6 11.1 %collective-permute-start.8 = (bf16[512,2176]{1,0:T(8,128)(2,1)}, bf16[512,2176]{1,0:T(8,128)(2,1)}, u32[]{:S(2)}, u32[]{:S(2)}) collective-permute-start(bf16[512,2176]{1,0:T(8,128)(2,1)} %constant_dynamic-update-slice_fusion.6.refs_0_), channel_id=1, source_target_pairs={{0,4},{4,0},{1,5},{5,1},{2,6},{6,2},{3,7},{7,3},{8,12},{12,8},{9,1... | collective-permute-start | bytes 6684680 | tf_op jit(solution)/shard_map/ppermute | solution.py:846
  124.7 4.5 copy-start.39
  125.8 8.9 %collective-permute-start.7 = (bf16[512,2048]{1,0:T(8,128)(2,1)}, bf16[512,2048]{1,0:T(8,128)(2,1)}, u32[]{:S(2)}, u32[]{:S(2)}) collective-permute-start(bf16[512,2048]{1,0:T(8,128)(2,1)} %constant_dynamic-update-slice_fusion.4.refs_0_), channel_id=1, source_target_pairs={{0,4},{4,0},{1,5},{5,1},{2,6},{6,2},{3,7},{7,3},{8,12},{12,8},{9,1... | collective-permute-start | bytes 6291464 | tf_op jit(solution)/shard_map/ppermute | solution.py:846
  145.0 4.7 copy-start.19
  150.4 1.7 copy-start.17
  152.1 3.0 copy-start.3
  152.1 3.1 copy-start.1
  177.9 44.5 %copy-start.2 = (f32[768,1024]{1,0:T(8,128)}, f32[768,1024]{1,0:T(8,128)S(1)}, u32[]{:S(2)}) copy-start(f32[768,1024]{1,0:T(8,128)S(1)} %get-tuple-element.249.refs_2_) | copy-start | bytes 9437188
  201.4 4.7 copy-start.5
  226.3 2.2 copy-start
  298.2 10.0 %collective-permute-start.9 = (bf16[512,4096]{1,0:T(8,128)(2,1)}, bf16[512,4096]{1,0:T(8,128)(2,1)}, u32[]{:S(2)}, u32[]{:S(2)}) collective-permute-start(bf16[512,4096]{1,0:T(8,128)(2,1)} %get-tuple-element.218), channel_id=1, source_target_pairs={{0,4},{4,0},{1,5},{5,1},{2,6},{6,2},{3,7},{7,3},{8,12},{12,8},{9,1... | collective-permute-start | bytes 12582920 | tf_op jit(solution)/shard_map/ppermute | solution.py:846
  298.7 13.1 %collective-permute-start.10 = (bf16[512,4096]{1,0:T(8,128)(2,1)}, bf16[512,4096]{1,0:T(8,128)(2,1)}, u32[]{:S(2)}, u32[]{:S(2)}) collective-permute-start(bf16[512,4096]{1,0:T(8,128)(2,1)} %get-tuple-element.220), channel_id=1, source_target_pairs={{0,4},{4,0},{1,5},{5,1},{2,6},{6,2},{3,7},{7,3},{8,12},{12,8},{9,1... | collective-permute-start | bytes 12582920 | tf_op jit(solution)/shard_map/ppermute | solution.py:846
  321.2 147.4 %reduce-scatter.5.cloned.1.call-start = ((), (), s32[]{:S(2)}) async-start(), calls=%async_computation.6 | async-start | bytes 2621440 | tf_op jit(solution)/shard_map/reduce_scatter | solution.py:1184
  333.7 6.2 %copy-start.24 = (bf16[512,1024]{1,0:T(8,128)(2,1)S(1)}, bf16[512,1024]{1,0:T(8,128)(2,1)}, u32[]{:S(2)}) copy-start(bf16[512,1024]{1,0:T(8,128)(2,1)} %get-tuple-element.229) | copy-start | bytes 3145732
  342.6 18.3 %collective-permute-start.12 = (bf16[512,2048]{1,0:T(8,128)(2,1)}, bf16[512,2048]{1,0:T(8,128)(2,1)S(1)}, u32[]{:S(2)}, u32[]{:S(2)}) collective-permute-start(bf16[512,2048]{1,0:T(8,128)(2,1)} %pad_maximum_fusion.1), channel_id=1, source_target_pairs={{0,4},{4,0},{1,5},{5,1},{2,6},{6,2},{3,7},{7,3},{8,12},{12,8},{9,1... | collective-permute-start | bytes 6291464 | tf_op jit(solution)/shard_map/ppermute | solution.py:846
  348.8 12.1 %collective-permute-start.11 = (bf16[512,2048]{1,0:T(8,128)(2,1)}, bf16[512,2048]{1,0:T(8,128)(2,1)}, u32[]{:S(2)}, u32[]{:S(2)}) collective-permute-start(bf16[512,2048]{1,0:T(8,128)(2,1)} %get-tuple-element.245), channel_id=1, source_target_pairs={{0,4},{4,0},{1,5},{5,1},{2,6},{6,2},{3,7},{7,3},{8,12},{12,8},{9,1... | collective-permute-start | bytes 6291464 | tf_op jit(solution)/shard_map/ppermute | solution.py:846
  348.9 10.5 %copy-start.22 = (bf16[512,1024]{1,0:T(8,128)(2,1)S(1)}, bf16[512,1024]{1,0:T(8,128)(2,1)}, u32[]{:S(2)}) copy-start(bf16[512,1024]{1,0:T(8,128)(2,1)} %get-tuple-element.230) | copy-start | bytes 3145732
  359.3 2.9 copy-start.11
  362.2 4.8 copy-start.10
  365.7 37.1 %collective-permute-start.13 = (bf16[256,2048]{1,0:T(8,128)(2,1)}, bf16[256,2048]{1,0:T(8,128)(2,1)S(1)}, u32[]{:S(2)}, u32[]{:S(2)}) collective-permute-start(bf16[256,2048]{1,0:T(8,128)(2,1)} %get-tuple-element.371), channel_id=1, source_target_pairs={{0,16},{8,24},{16,0},{24,8},{1,17},{9,25},{17,1},{25,9},{2,18},{10... | collective-permute-start | bytes 3145736 | tf_op jit(solution)/shard_map/ppermute | solution.py:843
  368.8 34.2 %collective-permute-start.14 = (bf16[256,2048]{1,0:T(8,128)(2,1)}, bf16[256,2048]{1,0:T(8,128)(2,1)}, u32[]{:S(2)}, u32[]{:S(2)}) collective-permute-start(bf16[256,2048]{1,0:T(8,128)(2,1)} %get-tuple-element.369), channel_id=1, source_target_pairs={{0,8},{8,0},{16,24},{24,16},{1,9},{9,1},{17,25},{25,17},{2,10},{10... | collective-permute-start | bytes 3145736 | tf_op jit(solution)/shard_map/ppermute | solution.py:843
  404.4 2.8 copy-start.4
  408.8 11.3 %copy-start.23 = (bf16[512,1024]{1,0:T(8,128)(2,1)S(1)}, bf16[512,1024]{1,0:T(8,128)(2,1)}, u32[]{:S(2)}) copy-start(bf16[512,1024]{1,0:T(8,128)(2,1)} %get-tuple-element.263) | copy-start | bytes 3145732
  422.8 2.7 copy-start.21
  422.8 7.3 %collective-permute-start.16 = (bf16[512,2048]{1,0:T(8,128)(2,1)}, bf16[512,2048]{1,0:T(8,128)(2,1)S(1)}, u32[]{:S(2)}, u32[]{:S(2)}) collective-permute-start(bf16[512,2048]{1,0:T(8,128)(2,1)} %pad_maximum_fusion.3), channel_id=1, source_target_pairs={{0,4},{4,0},{1,5},{5,1},{2,6},{6,2},{3,7},{7,3},{8,12},{12,8},{9,1... | collective-permute-start | bytes 6291464 | tf_op jit(solution)/shard_map/ppermute | solution.py:846
  422.8 8.6 %collective-permute-start.15 = (bf16[512,2048]{1,0:T(8,128)(2,1)}, bf16[512,2048]{1,0:T(8,128)(2,1)}, u32[]{:S(2)}, u32[]{:S(2)}) collective-permute-start(bf16[512,2048]{1,0:T(8,128)(2,1)} %get-tuple-element.282), channel_id=1, source_target_pairs={{0,4},{4,0},{1,5},{5,1},{2,6},{6,2},{3,7},{7,3},{8,12},{12,8},{9,1... | collective-permute-start | bytes 6291464 | tf_op jit(solution)/shard_map/ppermute | solution.py:846
  423.3 8.1 %copy-start.8 = (bf16[512,2048]{1,0:T(8,128)(2,1)S(1)}, bf16[512,2048]{1,0:T(8,128)(2,1)}, u32[]{:S(2)}) copy-start(bf16[512,2048]{1,0:T(8,128)(2,1)} %get-tuple-element.285) | copy-start | bytes 6291460
  423.3 31.3 %collective-permute-start.19 = (bf16[128,2048]{1,0:T(8,128)(2,1)}, bf16[128,2048]{1,0:T(8,128)(2,1)}, u32[]{:S(2)}, u32[]{:S(2)}) collective-permute-start(bf16[128,2048]{1,0:T(8,128)(2,1)} %get-tuple-element.379), channel_id=1, source_target_pairs={{0,8},{8,0},{16,24},{24,16},{1,9},{9,1},{17,25},{25,17},{2,10},{10... | collective-permute-start | bytes 1572872 | tf_op jit(solution)/shard_map/ppermute | solution.py:843
  424.6 30.0 %collective-permute-start.20 = (bf16[128,2048]{1,0:T(8,128)(2,1)}, bf16[128,2048]{1,0:T(8,128)(2,1)}, u32[]{:S(2)}, u32[]{:S(2)}) collective-permute-start(bf16[128,2048]{1,0:T(8,128)(2,1)} %get-tuple-element.377), channel_id=1, source_target_pairs={{0,16},{8,24},{16,0},{24,8},{1,17},{9,25},{17,1},{25,9},{2,18},{10... | collective-permute-start | bytes 1572872 | tf_op jit(solution)/shard_map/ppermute | solution.py:843
  431.4 5.0 copy-start.7
  434.9 28.1 %collective-permute-start.17 = (bf16[256,2048]{1,0:T(8,128)(2,1)}, bf16[256,2048]{1,0:T(8,128)(2,1)}, u32[]{:S(2)}, u32[]{:S(2)}) collective-permute-start(bf16[256,2048]{1,0:T(8,128)(2,1)} %get-tuple-element.367), channel_id=1, source_target_pairs={{0,16},{8,24},{16,0},{24,8},{1,17},{9,25},{17,1},{25,9},{2,18},{10... | collective-permute-start | bytes 3145736 | tf_op jit(solution)/shard_map/ppermute | solution.py:843
  438.2 25.2 %collective-permute-start.18 = (bf16[256,2048]{1,0:T(8,128)(2,1)}, bf16[256,2048]{1,0:T(8,128)(2,1)}, u32[]{:S(2)}, u32[]{:S(2)}) collective-permute-start(bf16[256,2048]{1,0:T(8,128)(2,1)} %get-tuple-element.365), channel_id=1, source_target_pairs={{0,8},{8,0},{16,24},{24,16},{1,9},{9,1},{17,25},{25,17},{2,10},{10... | collective-permute-start | bytes 3145736 | tf_op jit(solution)/shard_map/ppermute | solution.py:843
  438.7 15.9 %copy-start.15 = (bf16[128,2048]{1,0:T(8,128)(2,1)S(1)}, bf16[128,2048]{1,0:T(8,128)(2,1)}, u32[]{:S(2)}) copy-start(bf16[128,2048]{1,0:T(8,128)(2,1)} %get-tuple-element.299) | copy-start | bytes 1572868
  438.7 17.1 %copy-start.16 = (bf16[128,2048]{1,0:T(8,128)(2,1)S(1)}, bf16[128,2048]{1,0:T(8,128)(2,1)}, u32[]{:S(2)}) copy-start(bf16[128,2048]{1,0:T(8,128)(2,1)} %get-tuple-element.301) | copy-start | bytes 1572868
  458.1 30.7 %all-to-all-start = ((bf16[4,32,4096]{2,1,0:T(8,128)(2,1)}), bf16[4,32,4096]{2,1,0:T(8,128)(2,1)S(1)}, u32[]{:S(2)}, u32[]{:S(2)}) async-start(bf16[4,32,4096]{2,1,0:T(8,128)(2,1)} %bitcast.18), calls=%async_computation.2 | async-start | bytes 2097152 | tf_op jit(solution)/shard_map/all_to_all | solution.py:897
  466.0 2.6 copy-start.33
  466.0 2.7 copy-start.36
  466.0 2.7 copy-start.35
  466.0 2.7 copy-start.34
  468.6 8.1 %copy-start.26 = (bf16[128,2048]{1,0:T(8,128)(2,1)S(1)}, bf16[128,2048]{1,0:T(8,128)(2,1)}, u32[]{:S(2)}) copy-start(bf16[128,2048]{1,0:T(8,128)(2,1)} %get-tuple-element.372) | copy-start | bytes 1572868
  473.1 1.4 collective-permute-start.23
  474.5 4.4 collective-permute-start.24
  475.4 14.3 %collective-permute-start.21 = (bf16[128,2048]{1,0:T(8,128)(2,1)}, bf16[128,2048]{1,0:T(8,128)(2,1)S(1)}, u32[]{:S(2)}, u32[]{:S(2)}) collective-permute-start(bf16[128,2048]{1,0:T(8,128)(2,1)} %get-tuple-element.374), channel_id=1, source_target_pairs={{0,8},{8,0},{16,24},{24,16},{1,9},{9,1},{17,25},{25,17},{2,10},{10... | collective-permute-start | bytes 1572872 | tf_op jit(solution)/shard_map/ppermute | solution.py:843
  476.7 13.4 %collective-permute-start.22 = (bf16[128,2048]{1,0:T(8,128)(2,1)S(1)}, bf16[128,2048]{1,0:T(8,128)(2,1)S(1)}, u32[]{:S(2)}, u32[]{:S(2)}) collective-permute-start(bf16[128,2048]{1,0:T(8,128)(2,1)S(1)} %copy-done.26), channel_id=1, source_target_pairs={{0,16},{8,24},{16,0},{24,8},{1,17},{9,25},{17,1},{25,9},{2,18},{10... | collective-permute-start | bytes 1572872 | tf_op jit(solution)/shard_map/ppermute | solution.py:843
  478.9 11.2 %collective-permute-start.25 = (bf16[128,128]{1,0:T(8,128)(2,1)S(1)}, bf16[128,128]{1,0:T(8,128)(2,1)S(1)}, u32[]{:S(2)}, u32[]{:S(2)}) collective-permute-start(bf16[128,128]{1,0:T(8,128)(2,1)S(1)} %get-tuple-element.392), channel_id=1, source_target_pairs={{0,8},{8,0},{16,24},{24,16},{1,9},{9,1},{17,25},{25,17},{2,10},{10... | collective-permute-start | bytes 98312 | tf_op jit(solution)/shard_map/ppermute | solution.py:843
  490.4 6.1 %copy-start.12 = (bf16[32,8192]{1,0:T(8,128)(2,1)S(1)}, bf16[32,8192]{1,0:T(8,128)(2,1)}, u32[]{:S(2)}) copy-start(bf16[32,8192]{1,0:T(8,128)(2,1)} %reduce-scatter.5.cloned.1.call-done) | copy-start | bytes 1572868
  491.5 30.6 %all-to-all-start.1 = ((bf16[4,32,4224]{2,1,0:T(8,128)(2,1)}), bf16[4,32,4224]{2,1,0:T(8,128)(2,1)S(1)}, u32[]{:S(2)}, u32[]{:S(2)}) async-start(bf16[4,32,4224]{2,1,0:T(8,128)(2,1)} %bitcast.21), calls=%async_computation.3 | async-start | bytes 2162688 | tf_op jit(solution)/shard_map/all_to_all | solution.py:897
  (7 other events, 7.5 us)
Sparse Core Ops, SparseCore 0:
  11.7 189.6 all-gather.1
  321.4 98.1 reduce-scatter.2
  423.4 44.1 reduce-scatter.4

commit v6 on v5

--- a/solution.py
+++ b/solution.py
@@ -574,6 +574,25 @@
     )
 
 
+def turn_kernel(count, *refs):
+    for x_ref, turned_ref in zip(refs[:count], refs[count:]):
+        for block in row_blocks(x_ref.shape[1], LANES):
+            turned_ref[block, :] = x_ref[:, block].T
+
+
+def turn(*arrays):
+    return pl.pallas_call(
+        functools.partial(turn_kernel, len(arrays)),
+        grid=(1,),
+        in_specs=[pl.BlockSpec(array.shape, lambda j: (0, 0)) for array in arrays],
+        out_specs=[pl.BlockSpec(array.shape[::-1], lambda j: (0, 0)) for array in arrays],
+        out_shape=[jax.ShapeDtypeStruct(array.shape[::-1], array.dtype) for array in arrays],
+        compiler_params=pltpu.CompilerParams(vmem_limit_bytes=VMEM_BYTES),
+        cost_estimate=SHORT,
+        name="turn",
+    )(*arrays)
+
+
 def weight_gradient_kernel(starts, groups, crossed, positions_ref, x_ref, *refs):
     grads, outs, turned = refs[: len(starts) - 1], refs[len(starts) - 1 : -1], refs[-1]
     step = pl.program_id(0)
@@ -1021,10 +1040,14 @@
         gain_table[1],
         bias_table[1],
     )
+    normed_self_turned, self_mixed_turned, encoded_turned = order.run(
+        turn, normed_self, self_mixed, encoded
+    )
+    if links.pairwise:
+        gathered = order.after(gathered)
+        feed_input_low, feed_output_low, cross_held = gathered, gathered, gathered
+        cross_whole = gathered[:, 8 * width :]
     cross_first, cross_second = cross_whole[:, :split], cross_whole[:, split:]
-    normed_self_turned, self_mixed_turned, encoded_turned = order.run(
-        lambda *arrays: [array.T for array in arrays], normed_self, self_mixed, encoded
-    )
     cross_query, cross_output_low = cross_second[:, :width], cross_second[:, width:]
     cross_queries = product(normed_cross, cross_query).astype(low)
     cross_kv = product(encoded, cross_first).astype(low)

time: 539 us -> 534 us (level)
  transfers between devices with their start and end apart: 31 -> 31, of which waited for: 18 -> 18; matrix products, arithmetic and copies ran while one was open for 14% -> 13% of each run, Pallas kernels for 25% -> 26%
where the time goes in v6:
time: 534 us; the launch traced here: 528 us
  Pallas kernels  215 us (40%)
  waiting for transfers between devices  153 us (29%)
  other arithmetic  58.8 us (11%)
  starting transfers between devices  33.4 us (6%)
  matrix products  26.1 us (5%)
  local copies, waits for them, and re-layouts  25.1 us (5%)
  between operations  16.1 us (3%)
    ppermute x14, waiting for transfers between devices, swap(): return lax.ppermute(array, 'h', [(i, i ^ bit) for i in range(self.h_count)])  60.2 us
    pallas_call x1, Pallas kernels, feed_backward(): pl.pallas_call(functools.partial(feed_backward_kernel, rows), grid_spec=p...  43 us
    ppermute x3, waiting for transfers between devices, swap_fsdp(): lax.ppermute(array, 'fsdp', [(i, i ^ bit) for i in range(self.fsdp_count)])  38.7 us
    pallas_call x2, Pallas kernels, attention_backward(): pl.pallas_call(functools.partial(attention_backward_kernel, causal), grid...  33.1 us
    convert_element_type x16, other arithmetic, sum_cores(): (keep.astype(jnp.float32) + other.astype(jnp.float32)).astype(jnp.bfloat16)  31.9 us
    pallas_call x2, Pallas kernels, input_gradient(): pl.pallas_call(functools.partial(input_gradient_kernel, norm, starts, has...  26.4 us
    pallas_call x1, Pallas kernels, feed_forward(): pl.pallas_call(functools.partial(feed_forward_kernel, rows), grid_spec=pl...  26.3 us
    dot_general x6, matrix products, product(): return jnp.dot(left, right, preferred_element_type=jnp.float32)  26.1 us
  transfers between devices with their start and end apart: 31, of which 18 were waited for; matrix products, arithmetic and copies ran while one was open for 13% of the time, Pallas kernels for 26%

profile of v6, /device:TPU:0, one launch (start us, length us, event | category | flops | bytes accessed | tf_op | source)
XLA Modules:
  0.0 527.9 jit_solution(7309193511383847248)
XLA Ops:
  11.9 5.1 collective-permute-start.2
  18.1 6.3 %collective-permute-done.2.refs_3_ = bf16[32,4224]{1,0:T(8,128)(2,1)S(1)} collective-permute-done((bf16[32,4224]{1,0:T(8,128)(2,1)S(1)}, bf16[32,4224]{1,0:T(8,128)(2,1)S(1)}, u32[]{:S(2)}, u32[]{:S(2)}) %collective-permute-start.2) | collective-permute-done | bytes 270368 | tf_op jit(solution)/shard_map/ppermute | solution.py:868
  24.4 32.4 %collective-permute-done.1.refs_2_ = bf16[32,4224]{1,0:T(8,128)(2,1)S(1)} collective-permute-done((bf16[32,4224]{1,0:T(8,128)(2,1)S(1)}, bf16[32,4224]{1,0:T(8,128)(2,1)S(1)}, u32[]{:S(2)}, u32[]{:S(2)}) %collective-permute-start.1) | collective-permute-done | bytes 270368 | tf_op jit(solution)/shard_map/ppermute | solution.py:868
  58.3 2.7 place_rows.4
  62.1 1.5 collective-permute-start.4
  64.7 1.6 collective-permute-start.3
  66.3 23.8 %collective-permute-done.3 = bf16[128,2048]{1,0:T(8,128)(2,1)S(1)} collective-permute-done((bf16[128,2048]{1,0:T(8,128)(2,1)S(1)}, bf16[128,2048]{1,0:T(8,128)(2,1)S(1)}, u32[]{:S(2)}, u32[]{:S(2)}) %collective-permute-start.3) | collective-permute-done | bytes 524320 | tf_op jit(solution)/shard_map/ppermute | solution.py:862
  90.2 1.6 collective-permute-start.6
  92.4 22.4 %collective-permute-done.5 = bf16[256,2048]{1,0:T(8,128)(2,1)S(1)} collective-permute-done((bf16[256,2048]{1,0:T(8,128)(2,1)S(1)}, bf16[256,2048]{1,0:T(8,128)(2,1)S(1)}, u32[]{:S(2)}, u32[]{:S(2)}) %collective-permute-start.5) | collective-permute-done | bytes 1048608 | tf_op jit(solution)/shard_map/ppermute | solution.py:862
  114.9 6.6 %collective-permute-done.6 = bf16[256,2176]{1,0:T(8,128)(2,1)S(1)} collective-permute-done((bf16[256,2176]{1,0:T(8,128)(2,1)S(1)}, bf16[256,2176]{1,0:T(8,128)(2,1)S(1)}, u32[]{:S(2)}, u32[]{:S(2)}) %collective-permute-start.6) | collective-permute-done | bytes 1114144 | tf_op jit(solution)/shard_map/ppermute | solution.py:862
  129.4 1.8 bitcast_convert_fusion
  131.2 3.5 collective-permute-done.7.refs_1_
  134.7 4.3 place_rows.5.refs_3_.refs_4_
  139.0 4.9 place_rows.6.weight_ref.refs_5_
  145.1 4.7 fusion.32
  152.1 3.0 convolution_convert_fusion.1.v_ref
  155.1 5.3 convolution_convert_fusion.q_ref.k_ref
  160.4 12.9 %attention_forward.2 = (bf16[768,1024]{1,0:T(8,128)(2,1)}, f32[8,2,768]{2,1,0:T(2,128)}) custom-call(s32[1]{0:T(128)S(6)} %copy.74.limit_ref, bf16[768,2048]{1,0:T(8,128)(2,1)} %convolution_convert_fusion.q_ref.k_ref, bf16[768,2048]{1,0:T(8,128)(2,1)} %convolution_convert_fusion.q_ref.k_ref, bf16[768,1024]{1,0:T(8,128)(2,1)} %convolution_convert_fusion.1.v_ref), custom_call_target="tpu_custom_call" | custom-call | flops 1024 | bytes 1024 | tf_op jit(solution)/shard_map/attention_forward/pallas_call | solution.py:176
  173.3 4.7 fusion.41
  178.5 1.7 add_convert_fusion.2.x_ref
  180.2 4.3 turn.1
  184.5 17.0 %all-gather.2.cloned.1.call-done.input_ref.output_ref.weight_ref.refs_1_.refs_2_ = bf16[1024,12288]{1,0:T(8,128)(2,1)} async-done(((bf16[32,12288]{1,0:T(8,128)(2,1)}), bf16[1024,12288]{1,0:T(8,128)(2,1)}) %all-gather.2.cloned.1.call-update) | async-done | bytes 25165840 | tf_op jit(solution)/shard_map/all_gather | solution.py:871
  201.4 4.7 fusion.5.k_ref.v_ref
  206.1 4.5 fusion.15.q_ref
  211.3 9.1 %attention_forward.3 = (bf16[768,1024]{1,0:T(8,128)(2,1)}, f32[8,2,768]{2,1,0:T(2,128)}) custom-call(s32[1]{0:T(128)S(6)} %copy.75.limit_ref, bf16[768,1024]{1,0:T(8,128)(2,1)} %fusion.15.q_ref, bf16[256,2048]{1,0:T(8,128)(2,1)} %fusion.5.k_ref.v_ref, bf16[256,2048]{1,0:T(8,128)(2,1)} %fusion.5.k_ref.v_ref), custom_call_target="tpu_custom_call" | custom-call | flops 1024 | bytes 1024 | tf_op jit(solution)/shard_map/attention_forward/pallas_call | solution.py:176
  220.3 3.9 fusion.42
  224.8 1.7 add_convert_fusion.1.normed_ref
  226.5 26.3 %feed_forward.1 = (bf16[768,4096]{1,0:T(8,128)(2,1)}, bf16[768,4096]{1,0:T(8,128)(2,1)}, bf16[768,1024]{1,0:T(8,128)(2,1)}, f32[768,1024]{1,0:T(8,128)}, bf16[768,1024]{1,0:T(8,128)(2,1)}, /*index=5*/f32[2,1024]{1,0:T(2,128)}) custom-call(s32[1]{0:T(128)S(6)} %copy.74.limit_ref, bf16[768,1024]{1,0:T(8,128)(2,1)} %add_convert_fusion.1.normed_ref, ...), custom_call_target="tpu_custom_call" | custom-call | flops 1024 | bytes 1024 | tf_op jit(solution)/shard_map/feed_forward/pallas_call | solution.py:406
  252.8 43.0 %feed_backward.1 = (bf16[512,4096]{1,0:T(8,128)(2,1)}, bf16[512,4096]{1,0:T(8,128)(2,1)}, bf16[512,4096]{1,0:T(8,128)(2,1)}, bf16[512,4096]{1,0:T(8,128)(2,1)}, ...) custom-call(s32[8]{0:T(128)} %pad_add_fusion.2.tiles_ref, s32[8]{0:T(128)} %fusion.25.positions_ref, ...), custom_call_target="tpu_custom_call" | custom-call | flops 1024 | bytes 1024 | tf_op jit(solution)/shard_map/feed_backward/pallas_call | solution.py:514
  297.0 9.0 %output_backward.2 = (bf16[512,1024]{1,0:T(8,128)(2,1)}, bf16[512,1024]{1,0:T(8,128)(2,1)}, bf16[768,1024]{1,0:T(8,128)(2,1)}) custom-call(s32[8]{0:T(128)} %get-tuple-element.422.positions_ref, bf16[768,1024]{1,0:T(8,128)(2,1)} %get-tuple-element.245.x_ref.mixed_ref, bf16[768,1024]{1,0:T(8,128)(2,1)} %get-tuple-element.233.grad_ref, ...), custom_call_target="tpu_custom_call" | custom-call | flops 1024 | bytes 1024 | tf_op jit(solution)/shard_map/output_backward/pallas_call | solution.py:673
  306.0 3.6 collective-permute-done.10
  309.5 9.4 %add_convert_fusion = bf16[512,8192]{1,0:T(8,128)(2,1)} fusion(bf16[512,4096]{1,0:T(8,128)(2,1)} %get-tuple-element.240, bf16[512,4096]{1,0:T(8,128)(2,1)} %get-tuple-element.239, bf16[512,4096]{1,0:T(8,128)(2,1)} %collective-permute-done.10, bf16[512,4096]{1,0:T(8,128)(2,1)} %collective-permute-done.9), kind=kLoop, calls=%fused_computation | loop fusion | flops 41943040 | bytes 25165824 | tf_op jit(solution)/shard_map/convert_element_type | solution.py:913
  319.0 12.4 %attention_backward.2 = (bf16[768,1024]{1,0:T(8,128)(2,1)}, bf16[256,1024]{1,0:T(8,128)(2,1)}, bf16[256,1024]{1,0:T(8,128)(2,1)}) custom-call(s32[1]{0:T(128)S(6)} %copy.75.limit_ref, bf16[768,1024]{1,0:T(8,128)(2,1)} %fusion.15.q_ref, bf16[256,2048]{1,0:T(8,128)(2,1)} %fusion.5.k_ref.v_ref, bf16[256,2048]{1,0:T(8,128)(2,1)} %fusion.5.k_ref.v_ref, ...), custom_call_target="tpu_custom_call" | custom-call | flops 1024 | bytes 1024 | tf_op jit(solution)/shard_map/attention_backward/pallas_call | solution.py:277
  331.4 6.2 %weight_gradient.3 = (bf16[512,1024]{1,0:T(8,128)(2,1)}, bf16[512,1024]{1,0:T(8,128)(2,1)}) custom-call(s32[8]{0:T(128)} %get-tuple-element.422.positions_ref, bf16[768,1024]{1,0:T(8,128)(2,1)} %add_convert_fusion.2.x_ref, bf16[768,1024]{1,0:T(8,128)(2,1)} %get-tuple-element.255.refs_0_), custom_call_target="tpu_custom_call" | custom-call | flops 1024 | bytes 1024 | tf_op jit(solution)/shard_map/weight_gradient/pallas_call | solution.py:634
  337.6 2.7 pad_maximum_fusion.1
  340.7 5.9 %weight_gradient.4 = (bf16[512,2048]{1,0:T(8,128)(2,1)}, bf16[512,2048]{1,0:T(8,128)(2,1)}) custom-call(s32[8]{0:T(128)} %get-tuple-element.423.positions_ref.table_ref, bf16[1024,256]{1,0:T(8,128)(2,1)} %get-tuple-element.208.x_ref, bf16[256,1024]{1,0:T(8,128)(2,1)} %get-tuple-element.333.refs_0_, bf16[256,1024]{1,0:T(8,128)(2,1)} %get-tuple-element.334.refs_1_), custom_call_target="tpu_custom_call" | custom-call | flops 1024 | bytes 1024 | tf_op jit(solution)/shard_map/weight_gradient/pallas_call | solution.py:634
  346.6 10.5 %input_gradient.2 = (f32[768,1024]{1,0:T(8,128)}, bf16[768,1024]{1,0:T(8,128)(2,1)}, f32[2,1024]{1,0:T(2,128)}) custom-call(bf16[768,1024]{1,0:T(8,128)(2,1)} %get-tuple-element.255.refs_0_, bf16[1024,12288]{1,0:T(8,128)(2,1)} %all-gather.2.cloned.1.call-done.input_ref.output_ref.weight_ref.refs_1_.refs_2_, f32[768,1024]{1,0:T(8,128)} %copy-done.2, ...), custom_call_target="tpu_custom_call" | custom-call | flops 1024 | bytes 1024 | tf_op jit(solution)/shard_map/input_gradient/pallas_call | solution.py:764
  357.1 1.6 pad_maximum_fusion
  359.9 3.6 add_convert_fusion.10
  364.8 1.8 add_convert_fusion.8
  367.3 8.3 %output_backward.3 = (bf16[512,1024]{1,0:T(8,128)(2,1)}, bf16[512,1024]{1,0:T(8,128)(2,1)}, bf16[768,1024]{1,0:T(8,128)(2,1)}) custom-call(s32[8]{0:T(128)} %get-tuple-element.422.positions_ref, bf16[1024,768]{1,0:T(8,128)(2,1)} %get-tuple-element.267.x_ref, bf16[768,1024]{1,0:T(8,128)(2,1)} %get-tuple-element.268.grad_ref, ...), custom_call_target="tpu_custom_call" | custom-call | flops 1024 | bytes 1024 | tf_op jit(solution)/shard_map/output_backward/pallas_call | solution.py:673
  375.7 20.7 %attention_backward.3 = (bf16[768,1024]{1,0:T(8,128)(2,1)}, bf16[768,1024]{1,0:T(8,128)(2,1)}, bf16[768,1024]{1,0:T(8,128)(2,1)}) custom-call(s32[1]{0:T(128)S(6)} %copy.74.limit_ref, bf16[768,2048]{1,0:T(8,128)(2,1)} %convolution_convert_fusion.q_ref.k_ref, bf16[768,2048]{1,0:T(8,128)(2,1)} %convolution_convert_fusion.q_ref.k_ref, ...), custom_call_target="tpu_custom_call" | custom-call | flops 1024 | bytes 1024 | tf_op jit(solution)/shard_map/attention_backward/pallas_call | solution.py:277
  396.4 4.3 collective-permute-done.13
  400.8 1.5 add_convert_fusion.22
  402.3 2.6 add_convert_fusion.20
  404.9 11.3 %weight_gradient.5 = (bf16[512,2048]{1,0:T(8,128)(2,1)}, bf16[512,2048]{1,0:T(8,128)(2,1)}, bf16[512,1024]{1,0:T(8,128)(2,1)}, bf16[512,1024]{1,0:T(8,128)(2,1)}) custom-call(s32[8]{0:T(128)} %get-tuple-element.423.positions_ref.table_ref, bf16[1024,768]{1,0:T(8,128)(2,1)} %get-tuple-element.285.x_ref, bf16[768,1024]{1,0:T(8,128)(2,1)} %get-tuple-element.297.refs_0_, ...), custom_call_target="tpu_custom_call" | custom-call | flops 1024 | bytes 1024 | tf_op jit(solution)/shard_map/weight_gradient/pallas_call | solution.py:634
  416.2 2.7 pad_maximum_fusion.3
  419.5 1.3 collective-permute-start.19
  421.5 1.4 pad_maximum_fusion.2
  423.0 3.3 collective-permute-done.16
  427.5 3.5 add_convert_fusion.6
  431.0 1.5 collective-permute-start.17
  432.5 1.8 add_convert_fusion.4
  434.8 15.9 %input_gradient.3 = (f32[768,1024]{1,0:T(8,128)}, f32[2,1024]{1,0:T(2,128)}) custom-call(bf16[768,1024]{1,0:T(8,128)(2,1)} %get-tuple-element.297.refs_0_, bf16[768,1024]{1,0:T(8,128)(2,1)} %get-tuple-element.298.refs_1_, bf16[768,1024]{1,0:T(8,128)(2,1)} %get-tuple-element.299.refs_2_, bf16[1024,2048]{1,0:T(8,128)(2,1)} %place_rows.5.refs_3_.refs_4_, ...), custom_call_target="tpu_custom_call" | custom-call | flops 1024 | bytes 1024 | tf_op jit(solution)/shard_map/input_gradient/pallas_call | solution.py:764
  454.2 4.8 all-to-all-start
  459.5 2.6 add_convert_fusion.16
  462.1 2.6 add_convert_fusion.14
  465.9 2.3 place_rows.7
  469.3 1.3 collective-permute-done.23
  471.4 1.4 collective-permute-start.21
  476.3 8.6 %all-to-all-done = bf16[4,32,4096]{2,1,0:T(8,128)(2,1)S(1)} async-done(((bf16[4,32,4096]{2,1,0:T(8,128)(2,1)}), bf16[4,32,4096]{2,1,0:T(8,128)(2,1)S(1)}, u32[]{:S(2)}, u32[]{:S(2)}) %all-to-all-start) | async-done | bytes 1048608 | tf_op jit(solution)/shard_map/all_to_all | solution.py:916
  487.7 4.9 all-to-all-start.1
  495.8 5.3 %weights_back.1 = f32[256,1024]{1,0:T(8,128)} custom-call(bf16[256,1024]{1,0:T(8,128)(2,1)} %get-tuple-element.333.refs_0_, bf16[256,1024]{1,0:T(8,128)(2,1)} %get-tuple-element.334.refs_1_, bf16[1024,12288]{1,0:T(8,128)(2,1)} %all-gather.2.cloned.1.call-done.input_ref.output_ref.weight_ref.refs_1_.refs_2_), custom_call_target="tpu_custom_call" | custom-call | flops 1024 | bytes 1024 | tf_op jit(solution)/shard_map/weights_back/pallas_call | solution.py:720
  501.0 17.1 %all-to-all-done.1 = bf16[4,32,4224]{2,1,0:T(8,128)(2,1)S(1)} async-done(((bf16[4,32,4224]{2,1,0:T(8,128)(2,1)}), bf16[4,32,4224]{2,1,0:T(8,128)(2,1)S(1)}, u32[]{:S(2)}, u32[]{:S(2)}) %all-to-all-start.1) | async-done | bytes 1081376 | tf_op jit(solution)/shard_map/all_to_all | solution.py:916
  (204 shorter events, 49.1 us)
Async XLA Ops:
  7.2 3.5 copy-start.29
  7.2 4.5 copy-start.35
  7.2 4.5 copy-start.36
  7.2 4.6 copy-start.30
  7.2 4.6 copy-start.25
  7.2 194.2 %all-gather.2.cloned.1.call-start = ((), (), s32[]{:S(2)}) async-start(), calls=%async_computation.4 | async-start | bytes 25952256 | tf_op jit(solution)/shard_map/all_gather | solution.py:871
  11.6 407.8 %reduce-scatter.3.cloned.1.call-start = ((), (), s32[]{:S(2)}) async-start(), calls=%async_computation.5 | async-start | bytes 10485760 | tf_op jit(solution)/shard_map/reduce_scatter | solution.py:929
  11.9 45.0 %copy-start.19 = (bf16[32,4224]{1,0:T(8,128)(2,1)}, bf16[32,4224]{1,0:T(8,128)(2,1)S(1)}, u32[]{:S(2)}) copy-start(bf16[32,4224]{1,0:T(8,128)(2,1)S(1)} %fusion.19.refs_0_) | copy-start | bytes 811012
  11.9 12.6 %collective-permute-start.2 = (bf16[32,4224]{1,0:T(8,128)(2,1)S(1)}, bf16[32,4224]{1,0:T(8,128)(2,1)S(1)}, u32[]{:S(2)}, u32[]{:S(2)}) collective-permute-start(bf16[32,4224]{1,0:T(8,128)(2,1)S(1)} %fusion.19.refs_0_), channel_id=1, source_target_pairs={{0,3},{1,2},{2,1},{3,0},{4,7},{5,6},{6,5},{7,4},{8,11},{9,10},{10,... | collective-permute-start | bytes 811016 | tf_op jit(solution)/shard_map/ppermute | solution.py:868
  17.0 39.9 %collective-permute-start.1 = (bf16[32,4224]{1,0:T(8,128)(2,1)S(1)}, bf16[32,4224]{1,0:T(8,128)(2,1)S(1)}, u32[]{:S(2)}, u32[]{:S(2)}) collective-permute-start(bf16[32,4224]{1,0:T(8,128)(2,1)S(1)} %fusion.19.refs_0_), channel_id=1, source_target_pairs={{0,2},{1,3},{2,0},{3,1},{4,6},{5,7},{6,4},{7,5},{8,10},{9,11},{10,... | collective-permute-start | bytes 811016 | tf_op jit(solution)/shard_map/ppermute | solution.py:868
  17.0 39.9 %collective-permute-start = (bf16[32,4224]{1,0:T(8,128)(2,1)S(1)}, bf16[32,4224]{1,0:T(8,128)(2,1)S(1)}, u32[]{:S(2)}, u32[]{:S(2)}) collective-permute-start(bf16[32,4224]{1,0:T(8,128)(2,1)S(1)} %fusion.19.refs_0_), channel_id=1, source_target_pairs={{0,1},{1,0},{2,3},{3,2},{4,5},{5,4},{6,7},{7,6},{8,9},{9,8},{10,11... | collective-permute-start | bytes 811016 | tf_op jit(solution)/shard_map/ppermute | solution.py:868
  24.4 32.4 %copy-start.26 = (bf16[32,4224]{1,0:T(8,128)(2,1)}, bf16[32,4224]{1,0:T(8,128)(2,1)S(1)}, u32[]{:S(2)}) copy-start(bf16[32,4224]{1,0:T(8,128)(2,1)S(1)} %collective-permute-done.2.refs_3_) | copy-start | bytes 811012
  62.1 28.0 %collective-permute-start.4 = (bf16[128,2176]{1,0:T(8,128)(2,1)S(1)}, bf16[128,2176]{1,0:T(8,128)(2,1)S(1)}, u32[]{:S(2)}, u32[]{:S(2)}) collective-permute-start(bf16[128,2176]{1,0:T(8,128)(2,1)S(1)} %slice.400), channel_id=1, source_target_pairs={{0,16},{8,24},{16,0},{24,8},{1,17},{9,25},{17,1},{25,9},{2,18},{10... | collective-permute-start | bytes 1671176 | tf_op jit(solution)/shard_map/ppermute | solution.py:862
  64.7 25.4 %collective-permute-start.3 = (bf16[128,2048]{1,0:T(8,128)(2,1)S(1)}, bf16[128,2048]{1,0:T(8,128)(2,1)S(1)}, u32[]{:S(2)}, u32[]{:S(2)}) collective-permute-start(bf16[128,2048]{1,0:T(8,128)(2,1)S(1)} %slice.399), channel_id=1, source_target_pairs={{0,8},{8,0},{16,24},{24,16},{1,9},{9,1},{17,25},{25,17},{2,10},{10... | collective-permute-start | bytes 1572872 | tf_op jit(solution)/shard_map/ppermute | solution.py:862
  90.2 31.3 %collective-permute-start.6 = (bf16[256,2176]{1,0:T(8,128)(2,1)S(1)}, bf16[256,2176]{1,0:T(8,128)(2,1)S(1)}, u32[]{:S(2)}, u32[]{:S(2)}) collective-permute-start(bf16[256,2176]{1,0:T(8,128)(2,1)S(1)} %constant_dynamic-update-slice_fusion.2), channel_id=1, source_target_pairs={{0,8},{8,0},{16,24},{24,16},{1,9},{9,1},{17,25},{25,17},{2,10},{10... | collective-permute-start | bytes 3342344 | tf_op jit(solution)/shard_map/ppermute | solution.py:862
  91.8 23.0 %collective-permute-start.5 = (bf16[256,2048]{1,0:T(8,128)(2,1)S(1)}, bf16[256,2048]{1,0:T(8,128)(2,1)S(1)}, u32[]{:S(2)}, u32[]{:S(2)}) collective-permute-start(bf16[256,2048]{1,0:T(8,128)(2,1)S(1)} %constant_dynamic-update-slice_fusion), channel_id=1, source_target_pairs={{0,16},{8,24},{16,0},{24,8},{1,17},{9,25},{17,1},{25,9},{2,18},{10... | collective-permute-start | bytes 3145736 | tf_op jit(solution)/shard_map/ppermute | solution.py:862
  123.6 4.6 copy-start.37
  123.6 11.1 %collective-permute-start.8 = (bf16[512,2176]{1,0:T(8,128)(2,1)}, bf16[512,2176]{1,0:T(8,128)(2,1)}, u32[]{:S(2)}, u32[]{:S(2)}) collective-permute-start(bf16[512,2176]{1,0:T(8,128)(2,1)} %constant_dynamic-update-slice_fusion.6.refs_0_), channel_id=1, source_target_pairs={{0,4},{4,0},{1,5},{5,1},{2,6},{6,2},{3,7},{7,3},{8,12},{12,8},{9,1... | collective-permute-start | bytes 6684680 | tf_op jit(solution)/shard_map/ppermute | solution.py:865
  125.8 8.9 %collective-permute-start.7 = (bf16[512,2048]{1,0:T(8,128)(2,1)}, bf16[512,2048]{1,0:T(8,128)(2,1)}, u32[]{:S(2)}, u32[]{:S(2)}) collective-permute-start(bf16[512,2048]{1,0:T(8,128)(2,1)} %constant_dynamic-update-slice_fusion.4.refs_0_), channel_id=1, source_target_pairs={{0,4},{4,0},{1,5},{5,1},{2,6},{6,2},{3,7},{7,3},{8,12},{12,8},{9,1... | collective-permute-start | bytes 6291464 | tf_op jit(solution)/shard_map/ppermute | solution.py:865
  145.0 4.7 copy-start.18
  150.4 1.7 copy-start.16
  152.1 3.0 copy-start.3
  152.1 3.0 copy-start.1
  178.0 42.4 %copy-start.2 = (f32[768,1024]{1,0:T(8,128)}, f32[768,1024]{1,0:T(8,128)S(1)}, u32[]{:S(2)}) copy-start(f32[768,1024]{1,0:T(8,128)S(1)} %get-tuple-element.257.refs_2_) | copy-start | bytes 9437188
  201.4 4.7 copy-start.4
  224.3 2.2 copy-start
  295.8 10.1 %collective-permute-start.9 = (bf16[512,4096]{1,0:T(8,128)(2,1)}, bf16[512,4096]{1,0:T(8,128)(2,1)}, u32[]{:S(2)}, u32[]{:S(2)}) collective-permute-start(bf16[512,4096]{1,0:T(8,128)(2,1)} %get-tuple-element.226), channel_id=1, source_target_pairs={{0,4},{4,0},{1,5},{5,1},{2,6},{6,2},{3,7},{7,3},{8,12},{12,8},{9,1... | collective-permute-start | bytes 12582920 | tf_op jit(solution)/shard_map/ppermute | solution.py:865
  296.4 13.1 %collective-permute-start.10 = (bf16[512,4096]{1,0:T(8,128)(2,1)}, bf16[512,4096]{1,0:T(8,128)(2,1)}, u32[]{:S(2)}, u32[]{:S(2)}) collective-permute-start(bf16[512,4096]{1,0:T(8,128)(2,1)} %get-tuple-element.228), channel_id=1, source_target_pairs={{0,4},{4,0},{1,5},{5,1},{2,6},{6,2},{3,7},{7,3},{8,12},{12,8},{9,1... | collective-permute-start | bytes 12582920 | tf_op jit(solution)/shard_map/ppermute | solution.py:865
  319.0 145.8 %reduce-scatter.5.cloned.1.call-start = ((), (), s32[]{:S(2)}) async-start(), calls=%async_computation.6 | async-start | bytes 2621440 | tf_op jit(solution)/shard_map/reduce_scatter | solution.py:1207
  331.4 6.2 %copy-start.23 = (bf16[512,1024]{1,0:T(8,128)(2,1)S(1)}, bf16[512,1024]{1,0:T(8,128)(2,1)}, u32[]{:S(2)}) copy-start(bf16[512,1024]{1,0:T(8,128)(2,1)} %get-tuple-element.237) | copy-start | bytes 3145732
  340.3 18.4 %collective-permute-start.12 = (bf16[512,2048]{1,0:T(8,128)(2,1)}, bf16[512,2048]{1,0:T(8,128)(2,1)S(1)}, u32[]{:S(2)}, u32[]{:S(2)}) collective-permute-start(bf16[512,2048]{1,0:T(8,128)(2,1)} %pad_maximum_fusion.1), channel_id=1, source_target_pairs={{0,4},{4,0},{1,5},{5,1},{2,6},{6,2},{3,7},{7,3},{8,12},{12,8},{9,1... | collective-permute-start | bytes 6291464 | tf_op jit(solution)/shard_map/ppermute | solution.py:865
  346.6 12.1 %collective-permute-start.11 = (bf16[512,2048]{1,0:T(8,128)(2,1)}, bf16[512,2048]{1,0:T(8,128)(2,1)}, u32[]{:S(2)}, u32[]{:S(2)}) collective-permute-start(bf16[512,2048]{1,0:T(8,128)(2,1)} %get-tuple-element.253), channel_id=1, source_target_pairs={{0,4},{4,0},{1,5},{5,1},{2,6},{6,2},{3,7},{7,3},{8,12},{12,8},{9,1... | collective-permute-start | bytes 6291464 | tf_op jit(solution)/shard_map/ppermute | solution.py:865
  346.6 10.5 %copy-start.21 = (bf16[512,1024]{1,0:T(8,128)(2,1)S(1)}, bf16[512,1024]{1,0:T(8,128)(2,1)}, u32[]{:S(2)}) copy-start(bf16[512,1024]{1,0:T(8,128)(2,1)} %get-tuple-element.238) | copy-start | bytes 3145732
  357.1 2.9 copy-start.10
  359.9 4.8 copy-start.9
  363.5 37.1 %collective-permute-start.13 = (bf16[256,2048]{1,0:T(8,128)(2,1)}, bf16[256,2048]{1,0:T(8,128)(2,1)S(1)}, u32[]{:S(2)}, u32[]{:S(2)}) collective-permute-start(bf16[256,2048]{1,0:T(8,128)(2,1)} %get-tuple-element.379), channel_id=1, source_target_pairs={{0,16},{8,24},{16,0},{24,8},{1,17},{9,25},{17,1},{25,9},{2,18},{10... | collective-permute-start | bytes 3145736 | tf_op jit(solution)/shard_map/ppermute | solution.py:862
  366.6 34.2 %collective-permute-start.14 = (bf16[256,2048]{1,0:T(8,128)(2,1)}, bf16[256,2048]{1,0:T(8,128)(2,1)}, u32[]{:S(2)}, u32[]{:S(2)}) collective-permute-start(bf16[256,2048]{1,0:T(8,128)(2,1)} %get-tuple-element.377), channel_id=1, source_target_pairs={{0,8},{8,0},{16,24},{24,16},{1,9},{9,1},{17,25},{25,17},{2,10},{10... | collective-permute-start | bytes 3145736 | tf_op jit(solution)/shard_map/ppermute | solution.py:862
  404.9 11.3 %copy-start.22 = (bf16[512,1024]{1,0:T(8,128)(2,1)S(1)}, bf16[512,1024]{1,0:T(8,128)(2,1)}, u32[]{:S(2)}) copy-start(bf16[512,1024]{1,0:T(8,128)(2,1)} %get-tuple-element.271) | copy-start | bytes 3145732
  418.9 2.6 copy-start.20
  418.9 7.3 %collective-permute-start.16 = (bf16[512,2048]{1,0:T(8,128)(2,1)}, bf16[512,2048]{1,0:T(8,128)(2,1)S(1)}, u32[]{:S(2)}, u32[]{:S(2)}) collective-permute-start(bf16[512,2048]{1,0:T(8,128)(2,1)} %pad_maximum_fusion.3), channel_id=1, source_target_pairs={{0,4},{4,0},{1,5},{5,1},{2,6},{6,2},{3,7},{7,3},{8,12},{12,8},{9,1... | collective-permute-start | bytes 6291464 | tf_op jit(solution)/shard_map/ppermute | solution.py:865
  418.9 8.6 %collective-permute-start.15 = (bf16[512,2048]{1,0:T(8,128)(2,1)}, bf16[512,2048]{1,0:T(8,128)(2,1)}, u32[]{:S(2)}, u32[]{:S(2)}) collective-permute-start(bf16[512,2048]{1,0:T(8,128)(2,1)} %get-tuple-element.290), channel_id=1, source_target_pairs={{0,4},{4,0},{1,5},{5,1},{2,6},{6,2},{3,7},{7,3},{8,12},{12,8},{9,1... | collective-permute-start | bytes 6291464 | tf_op jit(solution)/shard_map/ppermute | solution.py:865
  419.4 8.1 %copy-start.7 = (bf16[512,2048]{1,0:T(8,128)(2,1)S(1)}, bf16[512,2048]{1,0:T(8,128)(2,1)}, u32[]{:S(2)}) copy-start(bf16[512,2048]{1,0:T(8,128)(2,1)} %get-tuple-element.293) | copy-start | bytes 6291460
  419.5 31.3 %collective-permute-start.19 = (bf16[128,2048]{1,0:T(8,128)(2,1)}, bf16[128,2048]{1,0:T(8,128)(2,1)}, u32[]{:S(2)}, u32[]{:S(2)}) collective-permute-start(bf16[128,2048]{1,0:T(8,128)(2,1)} %get-tuple-element.387), channel_id=1, source_target_pairs={{0,8},{8,0},{16,24},{24,16},{1,9},{9,1},{17,25},{25,17},{2,10},{10... | collective-permute-start | bytes 1572872 | tf_op jit(solution)/shard_map/ppermute | solution.py:862
  420.8 29.9 %collective-permute-start.20 = (bf16[128,2048]{1,0:T(8,128)(2,1)}, bf16[128,2048]{1,0:T(8,128)(2,1)}, u32[]{:S(2)}, u32[]{:S(2)}) collective-permute-start(bf16[128,2048]{1,0:T(8,128)(2,1)} %get-tuple-element.385), channel_id=1, source_target_pairs={{0,16},{8,24},{16,0},{24,8},{1,17},{9,25},{17,1},{25,9},{2,18},{10... | collective-permute-start | bytes 1572872 | tf_op jit(solution)/shard_map/ppermute | solution.py:862
  427.5 5.0 copy-start.6
  431.0 28.0 %collective-permute-start.17 = (bf16[256,2048]{1,0:T(8,128)(2,1)}, bf16[256,2048]{1,0:T(8,128)(2,1)}, u32[]{:S(2)}, u32[]{:S(2)}) collective-permute-start(bf16[256,2048]{1,0:T(8,128)(2,1)} %get-tuple-element.375), channel_id=1, source_target_pairs={{0,16},{8,24},{16,0},{24,8},{1,17},{9,25},{17,1},{25,9},{2,18},{10... | collective-permute-start | bytes 3145736 | tf_op jit(solution)/shard_map/ppermute | solution.py:862
  434.3 25.2 %collective-permute-start.18 = (bf16[256,2048]{1,0:T(8,128)(2,1)}, bf16[256,2048]{1,0:T(8,128)(2,1)}, u32[]{:S(2)}, u32[]{:S(2)}) collective-permute-start(bf16[256,2048]{1,0:T(8,128)(2,1)} %get-tuple-element.373), channel_id=1, source_target_pairs={{0,8},{8,0},{16,24},{24,16},{1,9},{9,1},{17,25},{25,17},{2,10},{10... | collective-permute-start | bytes 3145736 | tf_op jit(solution)/shard_map/ppermute | solution.py:862
  434.8 15.9 %copy-start.14 = (bf16[128,2048]{1,0:T(8,128)(2,1)S(1)}, bf16[128,2048]{1,0:T(8,128)(2,1)}, u32[]{:S(2)}) copy-start(bf16[128,2048]{1,0:T(8,128)(2,1)} %get-tuple-element.307) | copy-start | bytes 1572868
  434.8 17.1 %copy-start.15 = (bf16[128,2048]{1,0:T(8,128)(2,1)S(1)}, bf16[128,2048]{1,0:T(8,128)(2,1)}, u32[]{:S(2)}) copy-start(bf16[128,2048]{1,0:T(8,128)(2,1)} %get-tuple-element.309) | copy-start | bytes 1572868
  454.2 30.7 %all-to-all-start = ((bf16[4,32,4096]{2,1,0:T(8,128)(2,1)}), bf16[4,32,4096]{2,1,0:T(8,128)(2,1)S(1)}, u32[]{:S(2)}, u32[]{:S(2)}) async-start(bf16[4,32,4096]{2,1,0:T(8,128)(2,1)} %bitcast.15), calls=%async_computation.2 | async-start | bytes 2097152 | tf_op jit(solution)/shard_map/all_to_all | solution.py:916
  462.1 2.6 copy-start.31
  462.1 2.7 copy-start.34
  462.1 2.7 copy-start.33
  462.1 2.7 copy-start.32
  464.7 8.1 %copy-start.24 = (bf16[128,2048]{1,0:T(8,128)(2,1)S(1)}, bf16[128,2048]{1,0:T(8,128)(2,1)}, u32[]{:S(2)}) copy-start(bf16[128,2048]{1,0:T(8,128)(2,1)} %get-tuple-element.380) | copy-start | bytes 1572868
  469.2 1.4 collective-permute-start.23
  470.6 4.3 collective-permute-start.24
  471.4 14.3 %collective-permute-start.21 = (bf16[128,2048]{1,0:T(8,128)(2,1)}, bf16[128,2048]{1,0:T(8,128)(2,1)S(1)}, u32[]{:S(2)}, u32[]{:S(2)}) collective-permute-start(bf16[128,2048]{1,0:T(8,128)(2,1)} %get-tuple-element.382), channel_id=1, source_target_pairs={{0,8},{8,0},{16,24},{24,16},{1,9},{9,1},{17,25},{25,17},{2,10},{10... | collective-permute-start | bytes 1572872 | tf_op jit(solution)/shard_map/ppermute | solution.py:862
  472.9 13.4 %collective-permute-start.22 = (bf16[128,2048]{1,0:T(8,128)(2,1)S(1)}, bf16[128,2048]{1,0:T(8,128)(2,1)S(1)}, u32[]{:S(2)}, u32[]{:S(2)}) collective-permute-start(bf16[128,2048]{1,0:T(8,128)(2,1)S(1)} %copy-done.24), channel_id=1, source_target_pairs={{0,16},{8,24},{16,0},{24,8},{1,17},{9,25},{17,1},{25,9},{2,18},{10... | collective-permute-start | bytes 1572872 | tf_op jit(solution)/shard_map/ppermute | solution.py:862
  475.0 11.3 %collective-permute-start.25 = (bf16[128,128]{1,0:T(8,128)(2,1)S(1)}, bf16[128,128]{1,0:T(8,128)(2,1)S(1)}, u32[]{:S(2)}, u32[]{:S(2)}) collective-permute-start(bf16[128,128]{1,0:T(8,128)(2,1)S(1)} %get-tuple-element.400), channel_id=1, source_target_pairs={{0,8},{8,0},{16,24},{24,16},{1,9},{9,1},{17,25},{25,17},{2,10},{10... | collective-permute-start | bytes 98312 | tf_op jit(solution)/shard_map/ppermute | solution.py:862
  484.9 1.4 copy-start.13
  485.1 1.3 copy-start.12
  486.6 6.0 %copy-start.11 = (bf16[32,8192]{1,0:T(8,128)(2,1)S(1)}, bf16[32,8192]{1,0:T(8,128)(2,1)}, u32[]{:S(2)}) copy-start(bf16[32,8192]{1,0:T(8,128)(2,1)} %reduce-scatter.5.cloned.1.call-done) | copy-start | bytes 1572868
  487.7 30.5 %all-to-all-start.1 = ((bf16[4,32,4224]{2,1,0:T(8,128)(2,1)}), bf16[4,32,4224]{2,1,0:T(8,128)(2,1)S(1)}, u32[]{:S(2)}, u32[]{:S(2)}) async-start(bf16[4,32,4224]{2,1,0:T(8,128)(2,1)} %bitcast.18), calls=%async_computation.3 | async-start | bytes 2162688 | tf_op jit(solution)/shard_map/all_to_all | solution.py:916
  (5 other events, 4.9 us)
Sparse Core Ops, SparseCore 0:
  11.7 189.6 all-gather.1
  319.1 98.2 reduce-scatter.2
  419.8 43.9 reduce-scatter.4
